TPU v7x, 128 devices: a whole 4x4x4 slice. The times are simulated.
128 devices in a mesh: row: 8 (over y, z_lo), col: 16 (over z_hi, x, core).
Axes of the slice: x: 4, y: 4, z: 4 (z_hi: 2, z_lo: 2; z = z_hi * 2 + z_lo), core: 2. Of those that a mesh axis runs over, the one named last changes fastest.
Arguments:
- latents: bfloat16 [256, 256, 512], P('row', 'col'), may hold values from -6 to 6
- cotangent: bfloat16 [256, 256, 512], P('row', 'col'), may hold values from -6 to 6
- w_row: bfloat16 [4, 512, 512], replicated, may hold values from -6.6733202 to 6.6733202, as said below
- w_col: bfloat16 [4, 512, 512], replicated, may hold values from -6.6733202 to 6.6733202, as said below
- keep_heads: int32 [2, 8], replicated, may hold values 0 or 1
Outputs:
- output: bfloat16 [256, 256, 512], P('row', 'col')
- grad_latents: bfloat16 [256, 256, 512], P('row', 'col')
- grad_row: float32 [4, 512, 512], replicated
- grad_col: float32 [4, 512, 512], replicated
Inputs may be any that keep to these rules, and one draw needn't show every extreme that they name: `w_row`: projection weights. `w_col`: projection weights.
All inputs are finite; a program needn't handle non-finite values.
Results may differ from a plain program's by a relative error of at most 0.033.
Values may be sent and summed in bfloat16 or wider, within the bound.
No kernel may reach another device: no remote copies, remote signals or barrier semaphores. Data moves between devices by JAX's collectives and lax.ppermute only.
A program may use at most 128 MiB of HBM per device.

v0:
```python
import jax
import jax.numpy as jnp
from jax import lax
from jax.experimental import pallas as pl
from jax.experimental.pallas import tpu as pltpu
from jax.sharding import Mesh, PartitionSpec as P


HEAD = 64
D = 512
PAIR = 128
N_PAIR = D // PAIR
LINE = 256
TOK = 512
N_ROW = 8
N_COL = 16
N_DEV = N_ROW * N_COL
EPSILON = 1e-06
SCALE = HEAD ** (-0.5)

F32 = jnp.float32
BF16 = jnp.bfloat16

ROW = ("y", "zl")
COL = ("zh", "x", "c")
BOTH = COL + ROW
CHIPS = ("y", "zl", "zh", "x")


def dot(left, right):
    return lax.dot_general(left, right, (((1,), (0,)), ((), ())), preferred_element_type=F32)


def dot_nt(left, right):
    return lax.dot_general(left, right, (((1,), (1,)), ((), ())), preferred_element_type=F32)


def dot_tn(left, right):
    return lax.dot_general(left, right, (((0,), (0,)), ((), ())), preferred_element_type=F32)


def halves(value):
    lane = lax.broadcasted_iota(jnp.int32, value.shape, 1)
    zero = jnp.zeros_like(value)
    return (jnp.where(lane < HEAD, value, zero), jnp.where(lane >= HEAD, value, zero))


def inverse_rms(values_f):
    return lax.rsqrt(jnp.mean(values_f * values_f, axis=-1, keepdims=True) + EPSILON)


def softmax(q_half, k_pair):
    scores = dot_nt(q_half, k_pair)
    peak = jnp.max(scores, axis=-1, keepdims=True)
    grown = jnp.exp(scores - peak)
    return grown * (1.0 / jnp.sum(grown, axis=-1, keepdims=True))


def slot(col_local, group, row_local):
    return col_local * 8 + group * 2 + row_local


def copies_of(source, target, sems, count):
    return [pltpu.make_async_copy(source.at[i], target.at[i], sems.at[i]) for i in range(count)]


def start_all(copies):
    for copy in copies:
        copy.start()


def wait_all(copies):
    for copy in copies:
        copy.wait()


def project(normed, qkv_ref, w_s, copies):
    copies[0].wait()
    qkv_ref[0] = (dot(normed, w_s[0]).astype(BF16).astype(F32) * SCALE).astype(BF16)
    copies[1].wait()
    qkv_ref[1] = dot(normed, w_s[1]).astype(BF16)
    copies[2].wait()
    qkv_ref[2] = dot(normed, w_s[2]).astype(BF16)


PER_STEP = 2


def each_pair(visit):
    def step(index, carry):
        line = index // (N_PAIR // PER_STEP)
        first = lax.rem(index, N_PAIR // PER_STEP) * PER_STEP
        rows = pl.ds(pl.multiple_of(line * LINE, LINE), LINE)
        for offset in range(PER_STEP):
            pair = first + offset
            lanes = pl.ds(pl.multiple_of(pair * PAIR, PAIR), PAIR)
            visit(rows, lanes, (line * N_PAIR + pair) * 2)
        return carry

    lax.fori_loop(0, 2 * N_PAIR // PER_STEP, step, 0)


def row_forward_kernel(
    x_ref, gain_ref, w_ref, mid_ref, qkv_ref, left_ref,
    mix_s, mid_s, qkv_s, left_s, w_s, w_sem, mid_sem, qkv_sem, left_sem,
):
    weights = copies_of(w_ref, w_s, w_sem, 4)
    start_all(weights)
    saved = copies_of(qkv_s, qkv_ref, qkv_sem, 3)
    lefts = copies_of(left_s, left_ref, left_sem, 2)
    for rr in range(2):
        u = x_ref[:, rr].astype(F32).reshape(LINE, D)
        left_s[0, rr * LINE : (rr + 1) * LINE, :] = (u * inverse_rms(u)).astype(BF16)
    project(left_s[0], qkv_s, w_s, weights)
    lefts[0].start()
    start_all(saved)

    def visit(rows, lanes, head):
        q_half = halves(qkv_s[0, rows, lanes])
        v_half = halves(qkv_s[2, rows, lanes])
        k_pair = qkv_s[1, rows, lanes]
        probs = [softmax(q_half[h], k_pair).astype(BF16) for h in range(2)]
        mixed = dot(probs[0], v_half[0]) + dot(probs[1], v_half[1])
        left_s[1, rows, lanes] = (mixed * gain_ref[:, lanes]).astype(BF16)

    each_pair(visit)
    lefts[1].start()
    weights[3].wait()
    added = dot(left_s[1], w_s[3])
    for rr in range(2):
        u = x_ref[:, rr].astype(F32).reshape(LINE, D)
        mid = (u + added[rr * LINE : (rr + 1) * LINE]).reshape(16, 2, 8, D)
        for cc in range(2):
            for group in range(4):
                piece = mid[:, cc, :, group * 128 : (group + 1) * 128].reshape(128, 128)
                mix_s[pl.ds(slot(cc, group, rr), 128, stride=16), :] = piece
    sends = []
    for part in range(4):
        rows = slice(part * 32, (part + 1) * 32)
        mid_s[rows] = mix_s[part * 512 : (part + 1) * 512, :].reshape(32, 16, 128).astype(BF16)
        sends.append(pltpu.make_async_copy(mid_s.at[rows], mid_ref.at[rows], mid_sem.at[part]))
        sends[-1].start()
    wait_all(saved + lefts + sends)


def row_prepare_kernel(qkv_ref, left_ref, probs_ref, turned_ref):
    def visit(rows, lanes, head):
        q_half = halves(qkv_ref[0, rows, lanes])
        k_pair = qkv_ref[1, rows, lanes]
        for h in range(2):
            probs_ref[head + h] = softmax(q_half[h], k_pair)

    each_pair(visit)
    for which in range(2):
        turned_ref[which] = left_ref[which].T


def attention_backward(rows, lanes, qkv, da_ref, probs_of, right_ref):
    q_half = halves(qkv[0, rows, lanes])
    k_pair = qkv[1, rows, lanes]
    k_half = halves(k_pair)
    v_pair = qkv[2, rows, lanes]
    da_half = halves(da_ref[rows, lanes])
    grads = []
    lows = []
    for h in range(2):
        probs = probs_of(h, q_half, k_pair)
        lows.append(probs.astype(BF16))
        grad_probs = dot_nt(da_half[h], v_pair)
        total = jnp.sum(probs * grad_probs, axis=-1, keepdims=True)
        grads.append((probs * (grad_probs - total)).astype(BF16))
    right_ref[0, rows, lanes] = (
        (dot(grads[0], k_half[0]) + dot(grads[1], k_half[1])) * SCALE
    ).astype(BF16)
    right_ref[1, rows, lanes] = (
        dot_tn(grads[0], q_half[0]) + dot_tn(grads[1], q_half[1])
    ).astype(BF16)
    right_ref[2, rows, lanes] = (
        dot_tn(lows[0], da_half[0]) + dot_tn(lows[1], da_half[1])
    ).astype(BF16)
    return lows


def input_gradient(u, right_ref, w_s, rows):
    inv = inverse_rms(u)
    dn = (
        dot_nt(right_ref[0, rows, :], w_s[0])
        + dot_nt(right_ref[1, rows, :], w_s[1])
        + dot_nt(right_ref[2, rows, :], w_s[2])
    )
    mean = jnp.mean(dn * u, axis=-1, keepdims=True)
    return right_ref[3, rows, :].astype(F32) + inv * dn - u * (inv * inv * inv * mean)


def recomputed(h, q_half, k_pair):
    return softmax(q_half[h], k_pair)


def weight_gradients(side, turned, right_ref, target):
    for j in range(2):
        which = side * 2 + j
        target[j] = dot(turned[which // 3], right_ref[which]).astype(BF16)


def row_backward_kernel(
    where_ref, g_ref, gain_ref, qkv_ref, turned_ref, probs_ref, w_ref,
    keep_ref, send_ref, right_ref,
    mix_s, da_s, wo_s, qkv_s, turned_s, probs_s, keep_s, send_s, right_s,
    wo_sem, qkv_sem, turned_sem, probs_sem, half_sem, right_sem,
):
    weight = pltpu.make_async_copy(w_ref.at[3], wo_s, wo_sem)
    weight.start()
    saved = copies_of(qkv_ref, qkv_s, qkv_sem, 3)
    start_all(saved)
    probs = [
        pltpu.make_async_copy(
            probs_ref.at[i * 4 : (i + 1) * 4], probs_s.at[i * 4 : (i + 1) * 4], probs_sem.at[i]
        )
        for i in range(4)
    ]
    start_all(probs)
    turned = copies_of(turned_ref, turned_s, turned_sem, 2)
    start_all(turned)
    mix_s[...] = g_ref[...].astype(F32).reshape(N_DEV * 16, 128)
    for rr in range(2):
        for group in range(4):
            sides = [
                mix_s[pl.ds(slot(cc, group, rr), 128, stride=16), :].reshape(16, 8, 128)
                for cc in range(2)
            ]
            right_s[3, rr * LINE : (rr + 1) * LINE, group * 128 : (group + 1) * 128] = (
                jnp.stack(sides, axis=1).reshape(LINE, 128).astype(BF16)
            )
    weight.wait()
    da_s[...] = (dot_nt(right_s[3], wo_s[...]) * gain_ref[...]).astype(BF16)
    wait_all(saved + probs)

    def visit(rows, lanes, head):
        attention_backward(
            rows, lanes, qkv_s, da_s, lambda h, q, k: probs_s[head + h], right_s
        )

    each_pair(visit)
    rights = copies_of(right_s, right_ref, right_sem, 4)
    start_all(rights)
    wait_all(turned)
    core = where_ref[2]
    weight_gradients(1 - core, turned_s, right_s, send_s)
    sent = pltpu.make_async_copy(send_s, send_ref, half_sem.at[0])
    sent.start()
    weight_gradients(core, turned_s, right_s, keep_s)
    kept = pltpu.make_async_copy(keep_s, keep_ref, half_sem.at[1])
    kept.start()
    wait_all(rights + [sent, kept])


def row_input_gradient_kernel(where_ref, x_ref, right_ref, w_ref, *refs):
    outs, w_s, sems = refs[:8], refs[8], refs[9]
    gin_s = refs[10]
    chip = where_ref[1]
    copies = copies_of(w_ref, w_s, sems, 3)
    start_all(copies)
    wait_all(copies)
    for rr in range(2):
        rows = slice(rr * LINE, (rr + 1) * LINE)
        u = x_ref[:, rr].astype(F32).reshape(LINE, D)
        grad_in = input_gradient(u, right_ref, w_s, rows)
        gin_s[:, :, rr] = grad_in.astype(BF16).reshape(8, 2, 16, D)
    for shift in range(8):
        outs[shift][...] = gin_s[lax.rem(chip + shift, 8)]


def col_kernel(where_ref, m_ref, gain_ref, w_ref, *refs):
    parts, refs = refs[:8], refs[8:]
    gmid_ref, left_ref, right_ref, u_ref = refs[:4]
    mix_s, u_s, ulow_s, left_s, right_s, qkv_s, da_s, w_s = refs[4:12]
    w_sem, left_sem, right_sem, u_sem = refs[12:]
    me = where_ref[0]
    weights = copies_of(w_ref, w_s, w_sem, 4)
    for i in (3, 0, 1, 2):
        weights[i].start()
    lefts = copies_of(left_s, left_ref, left_sem, 2)
    rights = copies_of(right_s, right_ref, right_sem, 4)
    for shift in range(8):
        start = lax.rem(me + (8 - shift), 8) * 16
        for cc in range(2):
            for rr in range(2):
                at = pl.multiple_of(start + (cc * LINE + rr * 128), 16)
                right_s[3, pl.ds(at, 16), :] = parts[shift][cc, rr * 16 : (rr + 1) * 16, :]
    rights[3].start()
    weights[3].wait()
    da_s[...] = (dot_nt(right_s[3], w_s[3]) * gain_ref[...]).astype(BF16)
    mix_s[...] = m_ref[...].astype(F32).reshape(N_DEV * 16, 128)
    for cc in range(2):
        for rr in range(2):
            base = cc * LINE + rr * 128
            for group in range(4):
                for grid_row in range(N_ROW):
                    start = base + grid_row * 16
                    u_s[start : start + 16, group * 128 : (group + 1) * 128] = mix_s[
                        pl.ds(grid_row * 16 + slot(cc, group, rr), 16, stride=128), :
                    ]
    u = u_s[...]
    ulow_s[...] = u.astype(BF16)
    kept_u = pltpu.make_async_copy(ulow_s, u_ref, u_sem)
    kept_u.start()
    left_s[0] = (u * inverse_rms(u)).astype(BF16)
    lefts[0].start()
    project(left_s[0], qkv_s, w_s, weights)

    def visit(rows, lanes, head):
        lows = attention_backward(rows, lanes, qkv_s, da_s, recomputed, right_s)
        v_half = halves(qkv_s[2, rows, lanes])
        mixed = dot(lows[0], v_half[0]) + dot(lows[1], v_half[1])
        left_s[1, rows, lanes] = (mixed * gain_ref[:, lanes]).astype(BF16)

    each_pair(visit)
    lefts[1].start()
    start_all(rights[:3])
    for cc in range(2):
        rows = slice(cc * LINE, (cc + 1) * LINE)
        grad_in = input_gradient(u_s[rows, :], right_s, w_s, rows)
        for rr in range(2):
            for group in range(4):
                for grid_row in range(N_ROW):
                    start = rr * 128 + grid_row * 16
                    mix_s[pl.ds(grid_row * 16 + slot(cc, group, rr), 16, stride=128), :] = grad_in[
                        start : start + 16, group * 128 : (group + 1) * 128
                    ]
    gmid_ref[...] = mix_s[...].reshape(N_DEV, 16, 128).astype(BF16)
    wait_all(lefts + rights + [kept_u])


def col_output_kernel(where_ref, left_ref, right_ref, u_ref, w_ref, *refs):
    keep_ref, send_ref, outs = refs[0], refs[1], refs[2:10]
    turned_s, out_s, wo_s, sem = refs[10:]
    me, core = where_ref[0], where_ref[2]
    copy = pltpu.make_async_copy(w_ref.at[3], wo_s, sem)
    copy.start()
    for which in range(2):
        turned_s[which] = left_ref[which].T
    weight_gradients(1 - core, turned_s, right_ref, send_ref)
    weight_gradients(core, turned_s, right_ref, keep_ref)
    copy.wait()
    out_s[...] = (u_ref[...].astype(F32) + dot(left_ref[1], wo_s[...])).astype(BF16)
    for shift in range(8):
        start = lax.rem(me + shift, 8) * 16
        for cc in range(2):
            for rr in range(2):
                at = pl.multiple_of(start + (cc * LINE + rr * 128), 16)
                outs[shift][cc, rr * 16 : (rr + 1) * 16, :] = out_s[pl.ds(at, 16), :]


def tile_to_lines_kernel(where_ref, tile_ref, *refs):
    outs, mix_s = refs[:8], refs[8]
    me = where_ref[0]
    tile = tile_ref[...].astype(F32).reshape(TOK, D)
    for group in range(4):
        lanes = slice(group * 128, (group + 1) * 128)
        mix_s[group] = tile[:, lanes]
        for shift in range(8):
            peer = lax.rem(me + shift, 8)
            for cc in range(2):
                for rr in range(2):
                    piece = mix_s[group, pl.ds(peer + (rr * 16 + cc * 8), 16, stride=32), :]
                    outs[shift][cc, rr * 16 : (rr + 1) * 16, lanes] = piece.astype(BF16)


def lines_to_tile_kernel(where_ref, *refs):
    parts, tile_ref, mix_s = refs[:8], refs[8], refs[9]
    me = where_ref[0]
    for group in range(4):
        lanes = slice(group * 128, (group + 1) * 128)
        for shift in range(8):
            peer = lax.rem(me + (8 - shift), 8)
            for cc in range(2):
                for rr in range(2):
                    piece = parts[shift][cc, rr * 16 : (rr + 1) * 16, lanes].astype(F32)
                    mix_s[group, pl.ds(peer + (rr * 16 + cc * 8), 16, stride=32), :] = piece
        tile_ref[:, :, lanes] = mix_s[group].astype(BF16).reshape(32, 16, 128)


def forward_kernel(where_ref, *refs):
    parts, pass_ref, mine_ref = refs[:8], refs[8], refs[9]
    chip, core = where_ref[1], where_ref[2]
    for shift in range(8):
        source = lax.rem(chip + (8 - shift), 8)
        pass_ref[source] = parts[shift][1 - core]
        mine_ref[source] = parts[shift][core]


def join_kernel(where_ref, mine_ref, passed_ref, tile_ref):
    core = where_ref[2]
    for source in range(8):
        tile_ref[source, core] = mine_ref[source]
        tile_ref[source, 1 - core] = passed_ref[source]


def pair_sum_kernel(keep_ref, got_ref, sum_ref):
    total = keep_ref[...].astype(F32) + got_ref[...].astype(F32)
    sum_ref[...] = total.astype(BF16).reshape(64, 16, D)


def chip_sum(parts_ref, first):
    total = parts_ref[0, first : first + 16, :].astype(F32)
    for chip in range(1, 64):
        total = total + parts_ref[chip, first : first + 16, :].astype(F32)
    return total.astype(BF16)


def pair_sum_first_kernel(keep_ref, got_ref, both_ref, sum_s, sem):
    total = keep_ref[...].astype(F32) + got_ref[...].astype(F32)
    sum_s[...] = total.astype(BF16).reshape(64, 16, D)
    copy = pltpu.make_async_copy(sum_s, both_ref.at[:, 0:16, :], sem)
    copy.start()
    copy.wait()


def spread_second_kernel(parts_ref, first_ref, both_ref, sum_s, sem):
    sum_s[...] = jnp.broadcast_to(chip_sum(parts_ref, 0)[None], (64, 16, D))
    copy = pltpu.make_async_copy(sum_s, both_ref.at[:, 16:32, :], sem)
    copy.start()
    copy.wait()


def spread_kernel(both_ref, spread_ref):
    spread_ref[...] = jnp.broadcast_to(chip_sum(both_ref, 0)[None], (64, 16, D))


def pick_kernel(both_ref, half_ref):
    half_ref[...] = both_ref[:, 16:32, :]


def widen_kernel(where_ref, own_ref, got_ref, out_ref):
    core = where_ref[2]
    out_ref[core] = own_ref[...].reshape(256, D).astype(F32)
    out_ref[1 - core] = got_ref[...].reshape(256, D).astype(F32)


MIB = 1 << 20
SMEM = pl.BlockSpec(memory_space=pltpu.SMEM)
VMEM = pl.BlockSpec(memory_space=pltpu.VMEM)
HBM = pl.BlockSpec(memory_space=pltpu.HBM)


SPACE = {"s": SMEM, "v": VMEM, "h": HBM}


def call(kernel, ins, out_kinds, outs, scratch, flops, moved, limit=24, aliases=None):
    spaces = tuple(SPACE[kind] for kind in out_kinds)
    return pl.pallas_call(
        kernel,
        in_specs=[SPACE[kind] for kind in ins],
        out_specs=spaces if isinstance(outs, tuple) else spaces[0],
        out_shape=outs,
        scratch_shapes=scratch,
        input_output_aliases=aliases or {},
        compiler_params=pltpu.CompilerParams(vmem_limit_bytes=limit * MIB),
        cost_estimate=pl.CostEstimate(flops=flops, bytes_accessed=moved, transcendentals=0),
    )


def shape(*dims, dtype=BF16):
    return jax.ShapeDtypeStruct(dims, dtype)


MATMUL = 2 * TOK * D * D
ATTEND = 2 * 16 * LINE * LINE * HEAD
MIX = pltpu.VMEM((N_DEV * 16, 128), F32)
MIX_TILE = pltpu.VMEM((4, TOK, 128), F32)
DMA = pltpu.SemaphoreType.DMA
WEIGHTS = [pltpu.VMEM((4, D, D), BF16), DMA((4,))]
WEIGHT = [pltpu.VMEM((D, D), BF16), DMA]
PIECE = shape(2, 32, D)
HALF = shape(2, D, D)
HALF_S = pltpu.VMEM((2, D, D), BF16)


def token_scratch(*lead, dtype=BF16):
    return pltpu.VMEM((*lead, TOK, D), dtype)


row_forward = call(
    row_forward_kernel,
    "vvh",
    "hhh",
    (shape(N_DEV, 16, 128), shape(3, TOK, D), shape(2, TOK, D)),
    [
        MIX, pltpu.VMEM((N_DEV, 16, 128), BF16), token_scratch(3), token_scratch(2), *WEIGHTS,
        DMA((4,)), DMA((3,)), DMA((2,)),
    ],
    4 * MATMUL + 2 * ATTEND,
    6 * MIB,
)
row_prepare = call(
    row_prepare_kernel,
    "vv",
    "vv",
    (shape(16, LINE, LINE, dtype=F32), shape(2, D, TOK)),
    [],
    ATTEND,
    8 * MIB,
)
row_backward = call(
    row_backward_kernel,
    "svvhhhh",
    "hhh",
    (HALF, HALF, shape(4, TOK, D)),
    [
        MIX, token_scratch(), pltpu.VMEM((D, D), BF16), token_scratch(3),
        pltpu.VMEM((2, D, TOK), BF16), pltpu.VMEM((16, LINE, LINE), F32), HALF_S, HALF_S,
        token_scratch(4), DMA, DMA((3,)), DMA((2,)), DMA((4,)), DMA((2,)), DMA((4,)),
    ],
    5 * MATMUL + 5 * ATTEND,
    12 * MIB,
    limit=32,
)
row_input_gradient = call(
    row_input_gradient_kernel,
    "svvh",
    "v" * 8,
    (shape(2, 2, 16, D),) * 8,
    [*WEIGHTS, pltpu.VMEM((8, 2, 2, 16, D), BF16)],
    3 * MATMUL,
    5 * MIB,
)
col_grad = call(
    col_kernel,
    "svvh" + "v" * 8,
    "vhhh",
    (shape(N_DEV, 16, 128), shape(2, TOK, D), shape(4, TOK, D), shape(TOK, D)),
    [
        MIX, token_scratch(dtype=F32), token_scratch(), token_scratch(2), token_scratch(4),
        token_scratch(3), token_scratch(), *WEIGHTS, DMA((2,)), DMA((4,)), DMA,
    ],
    8 * MATMUL + 6 * ATTEND,
    8 * MIB,
    limit=32,
)
col_output = call(
    col_output_kernel,
    "svvvh",
    "v" * 10,
    (HALF, HALF) + (PIECE,) * 8,
    [pltpu.VMEM((2, D, TOK), BF16), token_scratch(), *WEIGHT],
    5 * MATMUL,
    7 * MIB,
)
tile_to_lines = call(tile_to_lines_kernel, "sv", "v" * 8, (PIECE,) * 8, [MIX_TILE], 0, MIB)
lines_to_tile = call(lines_to_tile_kernel, "s" + "v" * 8, "v", shape(32, 16, D), [MIX_TILE], 0, MIB)
forward = call(
    forward_kernel, "s" + "v" * 8, "vv", (shape(8, 2, 16, D), shape(8, 2, 16, D)), [], 0, MIB
)
join = call(join_kernel, "svv", "v", shape(8, 2, 2, 16, D), [], 0, MIB)
CHUNKS = pltpu.VMEM((64, 16, D), BF16)
pair_sum = call(pair_sum_kernel, "vv", "v", shape(64, 16, D), [], 0, 3 * MIB)
pair_sum_first = call(pair_sum_first_kernel, "vv", "h", shape(64, 32, D), [CHUNKS, DMA], 0, 3 * MIB)
spread_second = call(
    spread_second_kernel, "vh", "h", shape(64, 32, D), [CHUNKS, DMA], 0, 2 * MIB,
    aliases={1: 0},
)
spread = call(spread_kernel, "v", "v", shape(64, 16, D), [], 0, 3 * MIB)
pick = call(pick_kernel, "v", "v", shape(64, 16, D), [], 0, 3 * MIB)


def widen(where, own, got):
    block = pl.BlockSpec((16, 16, D), lambda i: (i, 0, 0))
    return pl.pallas_call(
        widen_kernel,
        grid=(4,),
        in_specs=[SMEM, block, block],
        out_specs=pl.BlockSpec((2, 256, D), lambda i: (0, i, 0)),
        out_shape=shape(2, 1024, D, dtype=F32),
        name="widen",
        compiler_params=pltpu.CompilerParams(vmem_limit_bytes=8 * MIB),
        cost_estimate=pl.CostEstimate(flops=0, bytes_accessed=6 * MIB, transcendentals=0),
    )(where, own, got).reshape(4, D, D)


def exchange(values, axes):
    return lax.all_to_all(values, axes, split_axis=0, concat_axis=0, tiled=True)


def shifted(pieces, axes):
    n = len(pieces)
    return [pieces[0]] + [
        lax.ppermute(pieces[k], axes, [(i, (i + k) % n) for i in range(n)]) for k in range(1, n)
    ]


def swap(value):
    return lax.ppermute(value, "c", [(0, 1), (1, 0)])


def layer(latents, cotangent, w_row, w_col, keep_heads):
    where = jnp.stack(
        [lax.axis_index(ROW), lax.axis_index(("zh", "x")), lax.axis_index("c")]
    ).astype(jnp.int32)
    gain = jnp.repeat(keep_heads.astype(F32), HEAD, axis=1)
    gain_row, gain_col = gain[0:1], gain[1:2]
    rows_in = exchange(latents.reshape(16, 2, 16, D), COL)
    grad_pieces = tile_to_lines(where, cotangent)
    grad_parts = shifted(grad_pieces, ROW)
    mid_send, qkv_row, left_row = row_forward(rows_in, gain_row, w_row)
    mid_lines = exchange(mid_send, BOTH)
    probs_row, turned_row = row_prepare(qkv_row, left_row)
    grad_send, left_col, right_col, u_col = col_grad(where, mid_lines, gain_col, w_col, *grad_parts)
    grad_rows = exchange(grad_send, BOTH)
    keep_col, send_col, *out_pieces = col_output(where, left_col, right_col, u_col, w_col)
    got_col = swap(send_col)
    paired_col = pair_sum(keep_col, got_col)
    sums_col = exchange(paired_col, CHIPS)
    keep_row, send_row, right_row = row_backward(
        where, grad_rows, gain_row, qkv_row, turned_row, probs_row, w_row
    )
    got_row = swap(send_row)
    first = pair_sum_first(keep_row, got_row)
    merged = spread_second(sums_col, first)
    both = exchange(merged, CHIPS)
    spread_row = spread(both)
    own_row = exchange(spread_row, CHIPS)
    gin_pieces = row_input_gradient(where, rows_in, right_row, w_row)
    gin_parts = shifted(gin_pieces, ("zh", "x"))
    passed, mine = forward(where, *gin_parts)
    passed = swap(passed)
    grad_latents = join(where, mine, passed).reshape(32, 16, D)
    out_parts = shifted(out_pieces, ROW)
    output = lines_to_tile(where, *out_parts)
    own_col = pick(both)
    other_col = swap(own_col)
    grad_col = widen(where, own_col, other_col)
    other_row = swap(own_row)
    grad_row = widen(where, own_row, other_row)
    return (output, grad_latents, grad_row, grad_col)


def solution(mesh):
    fine = Mesh(mesh.devices.reshape(4, 2, 2, 4, 2), ("y", "zl", "zh", "x", "c"))
    tile = P(ROW, COL, None)
    return jax.shard_map(
        layer,
        mesh=fine,
        in_specs=(tile, tile, P(), P(), P()),
        out_specs=(tile, tile, P(), P()),
        check_vma=False,
    )
```

profile of v0, /device:TPU:1, one launch (start us, length us, event | category | flops | bytes accessed | tf_op | source)
XLA Modules:
  0.0 254.6 jit_solution(11217980800571755652)
XLA Ops:
  0.6 9.1 %all-to-all-start = ((bf16[16,2,16,512]{3,2,1,0:T(8,128)(2,1)}), bf16[16,2,16,512]{3,2,1,0:T(8,128)(2,1)S(1)}, u32[]{:S(2)}, u32[]{:S(2)}) async-start(bf16[16,2,16,512]{3,2,1,0:T(8,128)(2,1)} %bitcast.13), calls=%async_computation | async-start | bytes 1048576 | tf_op jit(solution)/shard_map/all_to_all | solution.py:581
  10.6 10.2 %all-to-all-done.x_ref = bf16[16,2,16,512]{3,2,1,0:T(8,128)(2,1)S(1)} async-done(((bf16[16,2,16,512]{3,2,1,0:T(8,128)(2,1)}), bf16[16,2,16,512]{3,2,1,0:T(8,128)(2,1)S(1)}, u32[]{:S(2)}, u32[]{:S(2)}) %all-to-all-start) | async-done | bytes 524320 | tf_op jit(solution)/shard_map/all_to_all | solution.py:581
  20.8 1.6 copy-done.2
  22.4 7.1 %shard_map.84 = (bf16[128,16,128]{2,1,0:T(8,128)(2,1)S(1)}, bf16[3,512,512]{2,1,0:T(8,128)(2,1)S(1)}, bf16[2,512,512]{2,1,0:T(8,128)(2,1)S(1)}) custom-call(bf16[16,2,16,512]{3,2,1,0:T(8,128)(2,1)S(1)} %all-to-all-done.x_ref, f32[1,512]{1,0:T(1,128)S(1)} %broadcast_in_dim.10.gain_ref, bf16[4,512,512]{2,1,0:T(8,128)(2,1)S(1)} %copy-done.2), custom_call_target="tpu_custom_call" | custom-call | flops 1342177280 | bytes 6291456 | tf_op jit(solution)/shard_map/pallas_call | solution.py:604
  29.4 1.1 copy-done.5
  32.3 6.0 %all-to-all-start.1 = ((bf16[128,16,128]{2,1,0:T(8,128)(2,1)}), bf16[128,16,128]{2,1,0:T(8,128)(2,1)S(1)}, u32[]{:S(2)}, u32[]{:S(2)}) async-start(bf16[128,16,128]{2,1,0:T(8,128)(2,1)} %copy-done.26), calls=%async_computation.1 | async-start | bytes 1048576 | tf_op jit(solution)/shard_map/all_to_all | solution.py:581
  38.4 1.3 shard_map.85
  39.7 1.6 collective-permute-start
  41.2 1.2 collective-permute-start.1
  42.5 1.7 collective-permute-start.2
  44.1 1.7 collective-permute-start.3
  45.9 3.0 %collective-permute-start.4 = (bf16[2,32,512]{2,1,0:T(8,128)(2,1)S(1)}, bf16[2,32,512]{2,1,0:T(8,128)(2,1)S(1)}, u32[]{:S(2)}, u32[]{:S(2)}) collective-permute-start(bf16[2,32,512]{2,1,0:T(8,128)(2,1)S(1)} %get-tuple-element.50), channel_id=1, source_target_pairs={{0,80},{16,96},{32,112},{48,0},{64,16},{80,32},{96,48},{112,64},{1... | collective-permute-start | bytes 196616 | tf_op jit(solution)/shard_map/ppermute | solution.py:587
  48.9 2.1 collective-permute-start.5
  51.0 1.3 collective-permute-start.6
  52.4 1.0 collective-permute-done.2.refs_3_
  53.4 1.1 collective-permute-done.6.refs_7_
  54.5 13.5 %shard_map.86 = (bf16[128,16,128]{2,1,0:T(8,128)(2,1)}, bf16[2,512,512]{2,1,0:T(8,128)(2,1)S(1)}, bf16[4,512,512]{2,1,0:T(8,128)(2,1)S(1)}, bf16[512,512]{1,0:T(8,128)(2,1)S(1)}) custom-call(s32[3]{0:T(128)S(1)} %pad_add_fusion.where_ref, bf16[128,16,128]{2,1,0:T(8,128)(2,1)S(1)} %all-to-all-done.1.m_ref, f32[1,512]{1,0:T(1,128)S(1)} %broadcast_in_dim.12.gain_ref, ...), custom_call_target="tpu_custom_call" | custom-call | flops 2952790016 | bytes 8388608 | tf_op jit(solution)/shard_map/pallas_call | solution.py:607
  68.1 3.5 %shard_map.87 = (bf16[2,512,512]{2,1,0:T(8,128)(2,1)S(1)}, bf16[2,512,512]{2,1,0:T(8,128)(2,1)}, bf16[2,32,512]{2,1,0:T(8,128)(2,1)S(1)}, bf16[2,32,512]{2,1,0:T...) custom-call(s32[3]{0:T(128)S(1)} %pad_add_fusion.where_ref, ...), custom_call_target="tpu_custom_call" | custom-call | flops 1342177280 | bytes 7340032 | tf_op jit(solution)/shard_map/pallas_call | solution.py:609
  73.8 2.0 collective-permute-start.22
  75.8 8.9 %all-to-all-start.2 = ((bf16[128,16,128]{2,1,0:T(8,128)(2,1)}), bf16[128,16,128]{2,1,0:T(8,128)(2,1)S(1)}, u32[]{:S(2)}, u32[]{:S(2)}) async-start(bf16[128,16,128]{2,1,0:T(8,128)(2,1)} %get-tuple-element.64), calls=%async_computation.2 | async-start | bytes 1048576 | tf_op jit(solution)/shard_map/all_to_all | solution.py:581
  84.7 1.4 copy-done.6
  86.1 1.2 copy-done.18
  87.4 2.4 shard_map.89
  89.8 2.0 copy-done.8
  92.8 5.0 %all-to-all-done.2.g_ref = bf16[128,16,128]{2,1,0:T(8,128)(2,1)S(1)} async-done(((bf16[128,16,128]{2,1,0:T(8,128)(2,1)}), bf16[128,16,128]{2,1,0:T(8,128)(2,1)S(1)}, u32[]{:S(2)}, u32[]{:S(2)}) %all-to-all-start.2) | async-done | bytes 524320 | tf_op jit(solution)/shard_map/all_to_all | solution.py:581
  97.8 1.4 copy-done.7
  99.2 2.2 copy-done.9
  101.4 1.2 copy-done.24
  102.6 8.6 %shard_map.90 = (bf16[2,512,512]{2,1,0:T(8,128)(2,1)S(1)}, bf16[2,512,512]{2,1,0:T(8,128)(2,1)}, bf16[4,512,512]{2,1,0:T(8,128)(2,1)S(1)}) custom-call(s32[3]{0:T(128)S(1)} %pad_add_fusion.where_ref, bf16[128,16,128]{2,1,0:T(8,128)(2,1)S(1)} %all-to-all-done.2.g_ref, f32[1,512]{1,0:T(1,128)S(1)} %broadcast_in_dim.10.gain_ref, ...), custom_call_target="tpu_custom_call" | custom-call | flops 2013265920 | bytes 12582912 | tf_op jit(solution)/shard_map/pallas_call | solution.py:613
  111.3 1.3 copy-done.11
  113.5 1.4 collective-permute-start.23
  115.0 2.5 shard_map.94
  117.4 5.2 %all-to-all-start.3 = ((bf16[64,16,512]{2,1,0:T(8,128)(2,1)}), bf16[64,16,512]{2,1,0:T(8,128)(2,1)S(1)}, u32[]{:S(2)}, u32[]{:S(2)}) async-start(bf16[64,16,512]{2,1,0:T(8,128)(2,1)} %shard_map.94), calls=%async_computation.3 | async-start | bytes 2097152 | tf_op jit(solution)/shard_map/all_to_all | solution.py:581
  123.6 1.2 copy-done.20
  124.9 1.2 copy-done.22
  126.5 14.2 %all-to-all-done.3.parts_ref = bf16[64,16,512]{2,1,0:T(8,128)(2,1)S(1)} async-done(((bf16[64,16,512]{2,1,0:T(8,128)(2,1)}), bf16[64,16,512]{2,1,0:T(8,128)(2,1)S(1)}, u32[]{:S(2)}, u32[]{:S(2)}) %all-to-all-start.3) | async-done | bytes 1048608 | tf_op jit(solution)/shard_map/all_to_all | solution.py:581
  141.2 32.0 %all_to_all.30.both_ref = bf16[64,32,512]{2,1,0:T(8,128)(2,1)S(1)} all-to-all(bf16[64,32,512]{2,1,0:T(8,128)(2,1)S(1)} %shard_map.96), channel_id=1, replica_groups=mesh['y'=4,'zl'=2,'zh'=2,'x'=4,'c'=2] {'y','zl','zh','x'}, dimensions={0} | all-to-all | bytes 4194304 | tf_op jit(solution)/shard_map/all_to_all | solution.py:581
  173.3 1.3 shard_map.97
  174.5 1.3 copy-done
  175.8 5.9 %all-to-all-start.5 = ((bf16[64,16,512]{2,1,0:T(8,128)(2,1)}), bf16[64,16,512]{2,1,0:T(8,128)(2,1)}, u32[]{:S(2)}, u32[]{:S(2)}) async-start(bf16[64,16,512]{2,1,0:T(8,128)(2,1)} %shard_map.97), calls=%async_computation.5 | async-start | bytes 2097152 | tf_op jit(solution)/shard_map/all_to_all | solution.py:581
  181.8 1.6 copy-done.1
  183.4 3.1 %collective-permute-start.25 = (bf16[64,16,512]{2,1,0:T(8,128)(2,1)S(1)}, bf16[64,16,512]{2,1,0:T(8,128)(2,1)}, u32[]{:S(2)}, u32[]{:S(2)}) collective-permute-start(bf16[64,16,512]{2,1,0:T(8,128)(2,1)S(1)} %shard_map.98.own_ref), channel_id=1, source_target_pairs={{0,1},{1,0},{2,3},{3,2},{4,5},{5,4},{6,7},{7,6},{8,9},{9,8},{10,11... | collective-permute-start | bytes 3145736 | tf_op jit(solution)/shard_map/ppermute | solution.py:592
  186.5 10.3 %all-to-all-done.5.own_ref = bf16[64,16,512]{2,1,0:T(8,128)(2,1)} async-done(((bf16[64,16,512]{2,1,0:T(8,128)(2,1)}), bf16[64,16,512]{2,1,0:T(8,128)(2,1)}, u32[]{:S(2)}, u32[]{:S(2)}) %all-to-all-start.5) | async-done | bytes 1048608 | tf_op jit(solution)/shard_map/all_to_all | solution.py:581
  196.8 4.6 %collective-permute-start.24 = (bf16[64,16,512]{2,1,0:T(8,128)(2,1)}, bf16[64,16,512]{2,1,0:T(8,128)(2,1)S(1)}, u32[]{:S(2)}, u32[]{:S(2)}) collective-permute-start(bf16[64,16,512]{2,1,0:T(8,128)(2,1)} %all-to-all-done.5.own_ref), channel_id=1, source_target_pairs={{0,1},{1,0},{2,3},{3,2},{4,5},{5,4},{6,7},{7,6},{8,9},{9,8},{10,11... | collective-permute-start | bytes 3145736 | tf_op jit(solution)/shard_map/ppermute | solution.py:592
  201.4 1.6 copy-done.12
  203.0 1.0 copy-done.14
  204.0 1.9 shard_map.91
  206.0 1.9 collective-permute-start.15
  207.8 1.7 collective-permute-start.16
  209.5 5.4 %collective-permute-done.14.refs_1_ = bf16[2,2,16,512]{3,2,1,0:T(8,128)(2,1)S(1)} collective-permute-done((bf16[2,2,16,512]{3,2,1,0:T(8,128)(2,1)S(1)}, bf16[2,2,16,512]{3,2,1,0:T(8,128)(2,1)S(1)}, u32[]{:S(2)}, u32[]{:S(2)}) %collective-permute-start.14) | collective-permute-done | bytes 65568 | tf_op jit(solution)/shard_map/ppermute | solution.py:587
  214.9 1.2 collective-permute-start.17
  216.1 1.8 collective-permute-start.19
  217.8 1.7 collective-permute-done.17.refs_4_
  221.5 2.0 collective-permute-done.20.refs_7_
  224.1 2.9 %collective-permute-start.21 = (bf16[8,2,16,512]{3,2,1,0:T(8,128)(2,1)S(1)}, bf16[8,2,16,512]{3,2,1,0:T(8,128)(2,1)S(1)}, u32[]{:S(2)}, u32[]{:S(2)}) collective-permute-start(bf16[8,2,16,512]{3,2,1,0:T(8,128)(2,1)S(1)} %get-tuple-element.79), channel_id=1, source_target_pairs={{0,1},{1,0},{2,3},{3,2},{4,5},{5,4},{6,7},{7,6},{8,9},{9,8},{10,11... | collective-permute-start | bytes 786440 | tf_op jit(solution)/shard_map/ppermute | solution.py:592
  227.3 4.5 %collective-permute-done.8.refs_2_ = bf16[2,32,512]{2,1,0:T(8,128)(2,1)S(1)} collective-permute-done((bf16[2,32,512]{2,1,0:T(8,128)(2,1)S(1)}, bf16[2,32,512]{2,1,0:T(8,128)(2,1)S(1)}, u32[]{:S(2)}, u32[]{:S(2)}) %collective-permute-start.8) | collective-permute-done | bytes 65568 | tf_op jit(solution)/shard_map/ppermute | solution.py:587
  232.8 1.3 collective-permute-start.11
  234.1 2.6 %collective-permute-done.10.refs_4_ = bf16[2,32,512]{2,1,0:T(8,128)(2,1)S(1)} collective-permute-done((bf16[2,32,512]{2,1,0:T(8,128)(2,1)S(1)}, bf16[2,32,512]{2,1,0:T(8,128)(2,1)S(1)}, u32[]{:S(2)}, u32[]{:S(2)}) %collective-permute-start.10) | collective-permute-done | bytes 65568 | tf_op jit(solution)/shard_map/ppermute | solution.py:587
  237.1 2.1 collective-permute-start.13
  239.8 3.1 %collective-permute-done.13.refs_7_ = bf16[2,32,512]{2,1,0:T(8,128)(2,1)S(1)} collective-permute-done((bf16[2,32,512]{2,1,0:T(8,128)(2,1)S(1)}, bf16[2,32,512]{2,1,0:T(8,128)(2,1)S(1)}, u32[]{:S(2)}, u32[]{:S(2)}) %collective-permute-start.13) | collective-permute-done | bytes 65568 | tf_op jit(solution)/shard_map/ppermute | solution.py:587
  242.9 2.3 shard_map.88
  245.2 1.4 shard_map.93
  246.6 4.0 %widen.3 = f32[2,1024,512]{2,1,0:T(8,128)} custom-call(s32[3]{0:T(128)S(1)} %pad_add_fusion.where_ref, bf16[64,16,512]{2,1,0:T(8,128)(2,1)S(1)} %shard_map.98.own_ref, bf16[64,16,512]{2,1,0:T(8,128)(2,1)} %collective-permute-done.25.got_ref), custom_call_target="tpu_custom_call" | custom-call | bytes 6291456 | tf_op jit(solution)/shard_map/widen/pallas_call | solution.py:568
  250.6 4.0 %widen.2 = f32[2,1024,512]{2,1,0:T(8,128)} custom-call(s32[3]{0:T(128)S(1)} %pad_add_fusion.where_ref, bf16[64,16,512]{2,1,0:T(8,128)(2,1)} %all-to-all-done.5.own_ref, bf16[64,16,512]{2,1,0:T(8,128)(2,1)S(1)} %collective-permute-done.24.got_ref), custom_call_target="tpu_custom_call" | custom-call | bytes 6291456 | tf_op jit(solution)/shard_map/widen/pallas_call | solution.py:568
  (85 shorter events, 13.9 us)
Async XLA Ops:
  0.6 20.1 %all-to-all-start = ((bf16[16,2,16,512]{3,2,1,0:T(8,128)(2,1)}), bf16[16,2,16,512]{3,2,1,0:T(8,128)(2,1)S(1)}, u32[]{:S(2)}, u32[]{:S(2)}) async-start(bf16[16,2,16,512]{3,2,1,0:T(8,128)(2,1)} %bitcast.13), calls=%async_computation | async-start | bytes 1048576 | tf_op jit(solution)/shard_map/all_to_all | solution.py:581
  20.8 1.6 copy-start.2
  22.3 7.1 %copy-start.13 = (bf16[16,2,16,512]{3,2,1,0:T(8,128)(2,1)}, bf16[16,2,16,512]{3,2,1,0:T(8,128)(2,1)S(1)}, u32[]{:S(2)}) copy-start(bf16[16,2,16,512]{3,2,1,0:T(8,128)(2,1)S(1)} %all-to-all-done.x_ref) | copy-start | bytes 1572868
  22.4 16.1 %copy-start.25 = (bf16[32,16,512]{2,1,0:T(8,128)(2,1)S(1)}, bf16[32,16,512]{2,1,0:T(8,128)(2,1)}, u32[]{:S(2)}) copy-start(bf16[32,16,512]{2,1,0:T(8,128)(2,1)} %tile_ref.1) | copy-start | bytes 1572868
  22.4 32.2 %copy-start.10 = (bf16[4,512,512]{2,1,0:T(8,128)(2,1)S(1)}, bf16[4,512,512]{2,1,0:T(8,128)(2,1)}, u32[]{:S(2)}) copy-start(bf16[4,512,512]{2,1,0:T(8,128)(2,1)} %w_ref.7) | copy-start | bytes 6291460
  29.4 1.1 copy-start.5
  30.6 1.0 copy-start.17
  31.5 0.8 copy-start.26
  32.3 22.2 %all-to-all-start.1 = ((bf16[128,16,128]{2,1,0:T(8,128)(2,1)}), bf16[128,16,128]{2,1,0:T(8,128)(2,1)S(1)}, u32[]{:S(2)}, u32[]{:S(2)}) async-start(bf16[128,16,128]{2,1,0:T(8,128)(2,1)} %copy-done.26), calls=%async_computation.1 | async-start | bytes 1048576 | tf_op jit(solution)/shard_map/all_to_all | solution.py:581
  39.7 9.2 %collective-permute-start = (bf16[2,32,512]{2,1,0:T(8,128)(2,1)S(1)}, bf16[2,32,512]{2,1,0:T(8,128)(2,1)S(1)}, u32[]{:S(2)}, u32[]{:S(2)}) collective-permute-start(bf16[2,32,512]{2,1,0:T(8,128)(2,1)S(1)} %get-tuple-element.46), channel_id=1, source_target_pairs={{0,16},{16,32},{32,48},{48,64},{64,80},{80,96},{96,112},{112,0},{1... | collective-permute-start | bytes 196616 | tf_op jit(solution)/shard_map/ppermute | solution.py:587
  41.2 9.7 %collective-permute-start.1 = (bf16[2,32,512]{2,1,0:T(8,128)(2,1)S(1)}, bf16[2,32,512]{2,1,0:T(8,128)(2,1)S(1)}, u32[]{:S(2)}, u32[]{:S(2)}) collective-permute-start(bf16[2,32,512]{2,1,0:T(8,128)(2,1)S(1)} %get-tuple-element.47), channel_id=1, source_target_pairs={{0,32},{16,48},{32,64},{48,80},{64,96},{80,112},{96,0},{112,16},{1... | collective-permute-start | bytes 196616 | tf_op jit(solution)/shard_map/ppermute | solution.py:587
  42.5 10.9 %collective-permute-start.2 = (bf16[2,32,512]{2,1,0:T(8,128)(2,1)S(1)}, bf16[2,32,512]{2,1,0:T(8,128)(2,1)S(1)}, u32[]{:S(2)}, u32[]{:S(2)}) collective-permute-start(bf16[2,32,512]{2,1,0:T(8,128)(2,1)S(1)} %get-tuple-element.48), channel_id=1, source_target_pairs={{0,48},{16,64},{32,80},{48,96},{64,112},{80,0},{96,16},{112,32},{1... | collective-permute-start | bytes 196616 | tf_op jit(solution)/shard_map/ppermute | solution.py:587
  44.1 9.3 %collective-permute-start.3 = (bf16[2,32,512]{2,1,0:T(8,128)(2,1)S(1)}, bf16[2,32,512]{2,1,0:T(8,128)(2,1)S(1)}, u32[]{:S(2)}, u32[]{:S(2)}) collective-permute-start(bf16[2,32,512]{2,1,0:T(8,128)(2,1)S(1)} %get-tuple-element.49), channel_id=1, source_target_pairs={{0,64},{16,80},{32,96},{48,112},{64,0},{80,16},{96,32},{112,48},{1... | collective-permute-start | bytes 196616 | tf_op jit(solution)/shard_map/ppermute | solution.py:587
  45.9 7.5 %collective-permute-start.4 = (bf16[2,32,512]{2,1,0:T(8,128)(2,1)S(1)}, bf16[2,32,512]{2,1,0:T(8,128)(2,1)S(1)}, u32[]{:S(2)}, u32[]{:S(2)}) collective-permute-start(bf16[2,32,512]{2,1,0:T(8,128)(2,1)S(1)} %get-tuple-element.50), channel_id=1, source_target_pairs={{0,80},{16,96},{32,112},{48,0},{64,16},{80,32},{96,48},{112,64},{1... | collective-permute-start | bytes 196616 | tf_op jit(solution)/shard_map/ppermute | solution.py:587
  48.9 4.5 %collective-permute-start.5 = (bf16[2,32,512]{2,1,0:T(8,128)(2,1)S(1)}, bf16[2,32,512]{2,1,0:T(8,128)(2,1)S(1)}, u32[]{:S(2)}, u32[]{:S(2)}) collective-permute-start(bf16[2,32,512]{2,1,0:T(8,128)(2,1)S(1)} %get-tuple-element.51), channel_id=1, source_target_pairs={{0,96},{16,112},{32,0},{48,16},{64,32},{80,48},{96,64},{112,80},{1... | collective-permute-start | bytes 196616 | tf_op jit(solution)/shard_map/ppermute | solution.py:587
  51.0 3.6 %collective-permute-start.6 = (bf16[2,32,512]{2,1,0:T(8,128)(2,1)S(1)}, bf16[2,32,512]{2,1,0:T(8,128)(2,1)S(1)}, u32[]{:S(2)}, u32[]{:S(2)}) collective-permute-start(bf16[2,32,512]{2,1,0:T(8,128)(2,1)S(1)} %get-tuple-element.52), channel_id=1, source_target_pairs={{0,112},{16,0},{32,16},{48,32},{64,48},{80,64},{96,80},{112,96},{1... | collective-permute-start | bytes 196616 | tf_op jit(solution)/shard_map/ppermute | solution.py:587
  71.5 1.0 copy-start.15
  72.5 0.6 copy-start.27
  73.1 0.6 copy-start.29
  73.8 24.0 %copy-start.3 = (bf16[4,512,512]{2,1,0:T(8,128)(2,1)S(1)}, bf16[4,512,512]{2,1,0:T(8,128)(2,1)}, u32[]{:S(2)}) copy-start(bf16[4,512,512]{2,1,0:T(8,128)(2,1)} %w_ref.9) | copy-start | bytes 6291460
  73.8 41.2 %collective-permute-start.22 = (bf16[2,512,512]{2,1,0:T(8,128)(2,1)}, bf16[2,512,512]{2,1,0:T(8,128)(2,1)}, u32[]{:S(2)}, u32[]{:S(2)}) collective-permute-start(bf16[2,512,512]{2,1,0:T(8,128)(2,1)} %get-tuple-element.81), channel_id=1, source_target_pairs={{0,1},{1,0},{2,3},{3,2},{4,5},{5,4},{6,7},{7,6},{8,9},{9,8},{10,11... | collective-permute-start | bytes 3145736 | tf_op jit(solution)/shard_map/ppermute | solution.py:592
  75.8 22.0 %all-to-all-start.2 = ((bf16[128,16,128]{2,1,0:T(8,128)(2,1)}), bf16[128,16,128]{2,1,0:T(8,128)(2,1)S(1)}, u32[]{:S(2)}, u32[]{:S(2)}) async-start(bf16[128,16,128]{2,1,0:T(8,128)(2,1)} %get-tuple-element.64), calls=%async_computation.2 | async-start | bytes 1048576 | tf_op jit(solution)/shard_map/all_to_all | solution.py:581
  84.7 1.4 copy-start.6
  86.1 1.2 copy-start.18
  89.8 2.0 copy-start.8
  91.8 1.0 copy-start.23
  97.8 1.4 copy-start.7
  99.2 2.2 copy-start.9
  101.4 1.2 copy-start.24
  102.6 12.4 %copy-start.16 = (bf16[2,512,512]{2,1,0:T(8,128)(2,1)S(1)}, bf16[2,512,512]{2,1,0:T(8,128)(2,1)}, u32[]{:S(2)}) copy-start(bf16[2,512,512]{2,1,0:T(8,128)(2,1)} %copy-done.15) | copy-start | bytes 3145732
  111.3 1.3 copy-start.11
  112.6 1.0 copy-start.19
  113.5 9.1 %collective-permute-start.23 = (bf16[2,512,512]{2,1,0:T(8,128)(2,1)}, bf16[2,512,512]{2,1,0:T(8,128)(2,1)S(1)}, u32[]{:S(2)}, u32[]{:S(2)}) collective-permute-start(bf16[2,512,512]{2,1,0:T(8,128)(2,1)} %get-tuple-element.83), channel_id=1, source_target_pairs={{0,1},{1,0},{2,3},{3,2},{4,5},{5,4},{6,7},{7,6},{8,9},{9,8},{10,11... | collective-permute-start | bytes 3145736 | tf_op jit(solution)/shard_map/ppermute | solution.py:592
  117.4 23.3 %all-to-all-start.3 = ((bf16[64,16,512]{2,1,0:T(8,128)(2,1)}), bf16[64,16,512]{2,1,0:T(8,128)(2,1)S(1)}, u32[]{:S(2)}, u32[]{:S(2)}) async-start(bf16[64,16,512]{2,1,0:T(8,128)(2,1)} %shard_map.94), calls=%async_computation.3 | async-start | bytes 2097152 | tf_op jit(solution)/shard_map/all_to_all | solution.py:581
  122.7 1.0 copy-start.21
  123.6 1.2 copy-start.20
  124.9 1.2 copy-start.22
  174.5 1.3 copy-start
  175.8 21.0 %all-to-all-start.5 = ((bf16[64,16,512]{2,1,0:T(8,128)(2,1)}), bf16[64,16,512]{2,1,0:T(8,128)(2,1)}, u32[]{:S(2)}, u32[]{:S(2)}) async-start(bf16[64,16,512]{2,1,0:T(8,128)(2,1)} %shard_map.97), calls=%async_computation.5 | async-start | bytes 2097152 | tf_op jit(solution)/shard_map/all_to_all | solution.py:581
  181.8 1.6 copy-start.1
  183.4 18.0 %copy-start.4 = (bf16[4,512,512]{2,1,0:T(8,128)(2,1)S(1)}, bf16[4,512,512]{2,1,0:T(8,128)(2,1)}, u32[]{:S(2)}) copy-start(bf16[4,512,512]{2,1,0:T(8,128)(2,1)} %w_ref.9) | copy-start | bytes 6291460
  183.4 63.1 %collective-permute-start.25 = (bf16[64,16,512]{2,1,0:T(8,128)(2,1)S(1)}, bf16[64,16,512]{2,1,0:T(8,128)(2,1)}, u32[]{:S(2)}, u32[]{:S(2)}) collective-permute-start(bf16[64,16,512]{2,1,0:T(8,128)(2,1)S(1)} %shard_map.98.own_ref), channel_id=1, source_target_pairs={{0,1},{1,0},{2,3},{3,2},{4,5},{5,4},{6,7},{7,6},{8,9},{9,8},{10,11... | collective-permute-start | bytes 3145736 | tf_op jit(solution)/shard_map/ppermute | solution.py:592
  196.8 53.8 %collective-permute-start.24 = (bf16[64,16,512]{2,1,0:T(8,128)(2,1)}, bf16[64,16,512]{2,1,0:T(8,128)(2,1)S(1)}, u32[]{:S(2)}, u32[]{:S(2)}) collective-permute-start(bf16[64,16,512]{2,1,0:T(8,128)(2,1)} %all-to-all-done.5.own_ref), channel_id=1, source_target_pairs={{0,1},{1,0},{2,3},{3,2},{4,5},{5,4},{6,7},{7,6},{8,9},{9,8},{10,11... | collective-permute-start | bytes 3145736 | tf_op jit(solution)/shard_map/ppermute | solution.py:592
  201.4 1.6 copy-start.12
  203.0 1.0 copy-start.14
  204.0 17.3 %copy-start.30 = (bf16[2,32,512]{2,1,0:T(8,128)(2,1)S(1)}, bf16[2,32,512]{2,1,0:T(8,128)(2,1)}, u32[]{:S(2)}) copy-start(bf16[2,32,512]{2,1,0:T(8,128)(2,1)} %copy-done.29) | copy-start | bytes 196612
  204.0 23.0 %copy-start.28 = (bf16[2,32,512]{2,1,0:T(8,128)(2,1)S(1)}, bf16[2,32,512]{2,1,0:T(8,128)(2,1)}, u32[]{:S(2)}) copy-start(bf16[2,32,512]{2,1,0:T(8,128)(2,1)} %copy-done.27) | copy-start | bytes 196612
  205.9 9.0 %collective-permute-start.14 = (bf16[2,2,16,512]{3,2,1,0:T(8,128)(2,1)S(1)}, bf16[2,2,16,512]{3,2,1,0:T(8,128)(2,1)S(1)}, u32[]{:S(2)}, u32[]{:S(2)}) collective-permute-start(bf16[2,2,16,512]{3,2,1,0:T(8,128)(2,1)S(1)} %get-tuple-element.71), channel_id=1, source_target_pairs={{0,2},{2,4},{4,6},{6,8},{8,10},{10,12},{12,14},{14,0},{1,3},{3,5},... | collective-permute-start | bytes 196616 | tf_op jit(solution)/shard_map/ppermute | solution.py:587
  206.0 10.1 %collective-permute-start.15 = (bf16[2,2,16,512]{3,2,1,0:T(8,128)(2,1)S(1)}, bf16[2,2,16,512]{3,2,1,0:T(8,128)(2,1)S(1)}, u32[]{:S(2)}, u32[]{:S(2)}) collective-permute-start(bf16[2,2,16,512]{3,2,1,0:T(8,128)(2,1)S(1)} %get-tuple-element.72), channel_id=1, source_target_pairs={{0,4},{2,6},{4,8},{6,10},{8,12},{10,14},{12,0},{14,2},{1,5},{3,7},... | collective-permute-start | bytes 196616 | tf_op jit(solution)/shard_map/ppermute | solution.py:587
  207.8 8.2 %collective-permute-start.16 = (bf16[2,2,16,512]{3,2,1,0:T(8,128)(2,1)S(1)}, bf16[2,2,16,512]{3,2,1,0:T(8,128)(2,1)S(1)}, u32[]{:S(2)}, u32[]{:S(2)}) collective-permute-start(bf16[2,2,16,512]{3,2,1,0:T(8,128)(2,1)S(1)} %get-tuple-element.73), channel_id=1, source_target_pairs={{0,6},{2,8},{4,10},{6,12},{8,14},{10,0},{12,2},{14,4},{1,7},{3,9},... | collective-permute-start | bytes 196616 | tf_op jit(solution)/shard_map/ppermute | solution.py:587
  214.9 4.6 %collective-permute-start.17 = (bf16[2,2,16,512]{3,2,1,0:T(8,128)(2,1)S(1)}, bf16[2,2,16,512]{3,2,1,0:T(8,128)(2,1)S(1)}, u32[]{:S(2)}, u32[]{:S(2)}) collective-permute-start(bf16[2,2,16,512]{3,2,1,0:T(8,128)(2,1)S(1)} %get-tuple-element.74), channel_id=1, source_target_pairs={{0,8},{2,10},{4,12},{6,14},{8,0},{10,2},{12,4},{14,6},{1,9},{3,11}... | collective-permute-start | bytes 196616 | tf_op jit(solution)/shard_map/ppermute | solution.py:587
  216.1 5.2 %collective-permute-start.18 = (bf16[2,2,16,512]{3,2,1,0:T(8,128)(2,1)S(1)}, bf16[2,2,16,512]{3,2,1,0:T(8,128)(2,1)S(1)}, u32[]{:S(2)}, u32[]{:S(2)}) collective-permute-start(bf16[2,2,16,512]{3,2,1,0:T(8,128)(2,1)S(1)} %get-tuple-element.75), channel_id=1, source_target_pairs={{0,10},{2,12},{4,14},{6,0},{8,2},{10,4},{12,6},{14,8},{1,11},{3,13... | collective-permute-start | bytes 196616 | tf_op jit(solution)/shard_map/ppermute | solution.py:587
  216.1 5.4 %collective-permute-start.19 = (bf16[2,2,16,512]{3,2,1,0:T(8,128)(2,1)S(1)}, bf16[2,2,16,512]{3,2,1,0:T(8,128)(2,1)S(1)}, u32[]{:S(2)}, u32[]{:S(2)}) collective-permute-start(bf16[2,2,16,512]{3,2,1,0:T(8,128)(2,1)S(1)} %get-tuple-element.76), channel_id=1, source_target_pairs={{0,12},{2,14},{4,0},{6,2},{8,4},{10,6},{12,8},{14,10},{1,13},{3,15... | collective-permute-start | bytes 196616 | tf_op jit(solution)/shard_map/ppermute | solution.py:587
  219.5 4.0 %collective-permute-start.20 = (bf16[2,2,16,512]{3,2,1,0:T(8,128)(2,1)S(1)}, bf16[2,2,16,512]{3,2,1,0:T(8,128)(2,1)S(1)}, u32[]{:S(2)}, u32[]{:S(2)}) collective-permute-start(bf16[2,2,16,512]{3,2,1,0:T(8,128)(2,1)S(1)} %get-tuple-element.77), channel_id=1, source_target_pairs={{0,14},{2,0},{4,2},{6,4},{8,6},{10,8},{12,10},{14,12},{1,15},{3,1}... | collective-permute-start | bytes 196616 | tf_op jit(solution)/shard_map/ppermute | solution.py:587
  221.3 6.0 %collective-permute-start.7 = (bf16[2,32,512]{2,1,0:T(8,128)(2,1)S(1)}, bf16[2,32,512]{2,1,0:T(8,128)(2,1)S(1)}, u32[]{:S(2)}, u32[]{:S(2)}) collective-permute-start(bf16[2,32,512]{2,1,0:T(8,128)(2,1)S(1)} %copy-done.30), channel_id=1, source_target_pairs={{0,16},{16,32},{32,48},{48,64},{64,80},{80,96},{96,112},{112,0},{1... | collective-permute-start | bytes 196616 | tf_op jit(solution)/shard_map/ppermute | solution.py:587
  224.1 21.1 %collective-permute-start.21 = (bf16[8,2,16,512]{3,2,1,0:T(8,128)(2,1)S(1)}, bf16[8,2,16,512]{3,2,1,0:T(8,128)(2,1)S(1)}, u32[]{:S(2)}, u32[]{:S(2)}) collective-permute-start(bf16[8,2,16,512]{3,2,1,0:T(8,128)(2,1)S(1)} %get-tuple-element.79), channel_id=1, source_target_pairs={{0,1},{1,0},{2,3},{3,2},{4,5},{5,4},{6,7},{7,6},{8,9},{9,8},{10,11... | collective-permute-start | bytes 786440 | tf_op jit(solution)/shard_map/ppermute | solution.py:592
  227.0 4.8 %collective-permute-start.8 = (bf16[2,32,512]{2,1,0:T(8,128)(2,1)S(1)}, bf16[2,32,512]{2,1,0:T(8,128)(2,1)S(1)}, u32[]{:S(2)}, u32[]{:S(2)}) collective-permute-start(bf16[2,32,512]{2,1,0:T(8,128)(2,1)S(1)} %copy-done.28), channel_id=1, source_target_pairs={{0,32},{16,48},{32,64},{48,80},{64,96},{80,112},{96,0},{112,16},{1... | collective-permute-start | bytes 196616 | tf_op jit(solution)/shard_map/ppermute | solution.py:587
  227.3 5.5 %collective-permute-start.9 = (bf16[2,32,512]{2,1,0:T(8,128)(2,1)S(1)}, bf16[2,32,512]{2,1,0:T(8,128)(2,1)S(1)}, u32[]{:S(2)}, u32[]{:S(2)}) collective-permute-start(bf16[2,32,512]{2,1,0:T(8,128)(2,1)S(1)} %get-tuple-element.59), channel_id=1, source_target_pairs={{0,48},{16,64},{32,80},{48,96},{64,112},{80,0},{96,16},{112,32},{1... | collective-permute-start | bytes 196616 | tf_op jit(solution)/shard_map/ppermute | solution.py:587
  231.8 4.9 %collective-permute-start.10 = (bf16[2,32,512]{2,1,0:T(8,128)(2,1)S(1)}, bf16[2,32,512]{2,1,0:T(8,128)(2,1)S(1)}, u32[]{:S(2)}, u32[]{:S(2)}) collective-permute-start(bf16[2,32,512]{2,1,0:T(8,128)(2,1)S(1)} %get-tuple-element.60), channel_id=1, source_target_pairs={{0,64},{16,80},{32,96},{48,112},{64,0},{80,16},{96,32},{112,48},{1... | collective-permute-start | bytes 196616 | tf_op jit(solution)/shard_map/ppermute | solution.py:587
  232.8 4.3 %collective-permute-start.11 = (bf16[2,32,512]{2,1,0:T(8,128)(2,1)S(1)}, bf16[2,32,512]{2,1,0:T(8,128)(2,1)S(1)}, u32[]{:S(2)}, u32[]{:S(2)}) collective-permute-start(bf16[2,32,512]{2,1,0:T(8,128)(2,1)S(1)} %get-tuple-element.61), channel_id=1, source_target_pairs={{0,80},{16,96},{32,112},{48,0},{64,16},{80,32},{96,48},{112,64},{1... | collective-permute-start | bytes 196616 | tf_op jit(solution)/shard_map/ppermute | solution.py:587
  236.7 3.1 %collective-permute-start.12 = (bf16[2,32,512]{2,1,0:T(8,128)(2,1)S(1)}, bf16[2,32,512]{2,1,0:T(8,128)(2,1)S(1)}, u32[]{:S(2)}, u32[]{:S(2)}) collective-permute-start(bf16[2,32,512]{2,1,0:T(8,128)(2,1)S(1)} %get-tuple-element.62), channel_id=1, source_target_pairs={{0,96},{16,112},{32,0},{48,16},{64,32},{80,48},{96,64},{112,80},{1... | collective-permute-start | bytes 196616 | tf_op jit(solution)/shard_map/ppermute | solution.py:587
  237.1 5.8 %collective-permute-start.13 = (bf16[2,32,512]{2,1,0:T(8,128)(2,1)S(1)}, bf16[2,32,512]{2,1,0:T(8,128)(2,1)S(1)}, u32[]{:S(2)}, u32[]{:S(2)}) collective-permute-start(bf16[2,32,512]{2,1,0:T(8,128)(2,1)S(1)} %get-tuple-element.63), channel_id=1, source_target_pairs={{0,112},{16,0},{32,16},{48,32},{64,48},{80,64},{96,80},{112,96},{1... | collective-permute-start | bytes 196616 | tf_op jit(solution)/shard_map/ppermute | solution.py:587
where the time goes:
time: 258 us; the launch traced here: 255 us
  starting transfers between devices  72.8 us (28%)
  waiting for transfers between devices  64.2 us (25%)
  Pallas kernels  55.3 us (21%)
  blocking collectives  32 us (12%)
  local copies, waits for them, and re-layouts  28.7 us (11%)
    all_to_all x5, waiting for transfers between devices, exchange(): return lax.all_to_all(values, axes, split_axis=0, concat_axis=0, tiled=True)  39.7 us
    all_to_all x5, starting transfers between devices, exchange(): return lax.all_to_all(values, axes, split_axis=0, concat_axis=0, tiled=True)  35.1 us
    all_to_all x1, blocking collectives, exchange(): return lax.all_to_all(values, axes, split_axis=0, concat_axis=0, tiled=True)  32 us
    unnamed x62, local copies, waits for them, and re-layouts  28.4 us
    ppermute x21, waiting for transfers between devices, shifted(): lax.ppermute(pieces[k], axes, [(i, (i + k) % n) for i in range(n)])  24.6 us
    ppermute x21, starting transfers between devices, shifted(): lax.ppermute(pieces[k], axes, [(i, (i + k) % n) for i in range(n)])  23.6 us
    ppermute x5, starting transfers between devices, swap(): return lax.ppermute(value, 'c', [(0, 1), (1, 0)])  14 us
    pallas_call x1, Pallas kernels, layer(): col_grad(where, mid_lines, gain_col, w_col, *grad_parts)  13.5 us
  transfers between devices with their start and end apart: 31, of which 17 were waited for; matrix products, arithmetic and copies ran while one was open for 0% of the time, Pallas kernels for 10%

commit v1 on v0

v1 whole, which is shorter than its diff:
```python
import jax
import jax.numpy as jnp
from jax import lax
from jax.experimental import pallas as pl
from jax.experimental.pallas import tpu as pltpu
from jax.sharding import Mesh, PartitionSpec as P


HEADS = 8
HEAD = 64
D = 512
PAIR = 128
N_PAIR = D // PAIR
LINE = 256
TOK = 512
N_ROW = 8
N_COL = 16
N_DEV = N_ROW * N_COL
EPSILON = 1e-06
SCALE = HEAD ** (-0.5)

F32 = jnp.float32
BF16 = jnp.bfloat16

AXES = ("y", "zl", "zh", "x", "c")
ROW = ("y", "zl")
COL = ("zh", "x", "c")
BOTH = COL + ROW
CHIPS = ("y", "zl", "zh", "x")


def dot(left, right):
    return lax.dot_general(left, right, (((1,), (0,)), ((), ())), preferred_element_type=F32)


def dot_nt(left, right):
    return lax.dot_general(left, right, (((1,), (1,)), ((), ())), preferred_element_type=F32)


def stack_halves(value):
    lane = lax.broadcasted_iota(jnp.int32, value.shape, 1)
    zero = jnp.zeros_like(value)
    low, high = jnp.where(lane < HEAD, value, zero), jnp.where(lane >= HEAD, value, zero)
    return jnp.concatenate([low, high], axis=0)


def pick_halves(value):
    low, high = value[:LINE], value[LINE:]
    lane = lax.broadcasted_iota(jnp.int32, low.shape, 1)
    return jnp.where(lane < HEAD, low, high)


def turn_halves(value):
    return jnp.concatenate([value[:LINE].T, value[LINE:].T], axis=0)


def gain_row(keep_ref, block, first, count):
    head = lax.broadcasted_iota(jnp.int32, (1, count * HEAD), 1) // HEAD
    gain = jnp.zeros((1, count * HEAD), F32)
    for i in range(count):
        gain = jnp.where(head == i, keep_ref[block, first + i].astype(F32), gain)
    return gain


def inverse_rms(values_f):
    return lax.rsqrt(jnp.mean(values_f * values_f, axis=-1, keepdims=True) + EPSILON)


def softmax(q_pair, k_pair):
    scores = dot_nt(stack_halves(q_pair), k_pair)
    peak = jnp.max(scores, axis=-1, keepdims=True)
    grown = jnp.exp(scores - peak)
    return grown * (1.0 / jnp.sum(grown, axis=-1, keepdims=True))


def slot(col_local, group, row_local):
    return col_local * 8 + group * 2 + row_local


def copies_of(source, target, sems, count):
    return [pltpu.make_async_copy(source.at[i], target.at[i], sems.at[i]) for i in range(count)]


def start_all(copies):
    for copy in copies:
        copy.start()


def wait_all(copies):
    for copy in copies:
        copy.wait()


def project(normed, qkv_ref, w_s, copies):
    copies[0].wait()
    qkv_ref[0] = (dot(normed, w_s[0]).astype(BF16).astype(F32) * SCALE).astype(BF16)
    copies[1].wait()
    qkv_ref[1] = dot(normed, w_s[1]).astype(BF16)
    copies[2].wait()
    qkv_ref[2] = dot(normed, w_s[2]).astype(BF16)


PER_STEP = 2


def each_pair(visit):
    def step(index, carry):
        line = index // (N_PAIR // PER_STEP)
        first = lax.rem(index, N_PAIR // PER_STEP) * PER_STEP
        rows = pl.ds(pl.multiple_of(line * LINE, LINE), LINE)
        for offset in range(PER_STEP):
            pair = first + offset
            lanes = pl.ds(pl.multiple_of(pair * PAIR, PAIR), PAIR)
            visit(rows, lanes, line * N_PAIR + pair, pair)
        return carry

    lax.fori_loop(0, 2 * N_PAIR // PER_STEP, step, 0)


def row_forward_kernel(
    keep_ref, x_ref, w_ref, mid_ref, qkv_ref, left_ref,
    mix_s, mid_s, qkv_s, left_s, w_s, w_sem, mid_sem, qkv_sem, left_sem,
):
    weights = copies_of(w_ref, w_s, w_sem, 4)
    start_all(weights)
    saved = copies_of(qkv_s, qkv_ref, qkv_sem, 3)
    lefts = copies_of(left_s, left_ref, left_sem, 2)
    for rr in range(2):
        u = x_ref[:, rr].astype(F32).reshape(LINE, D)
        left_s[0, rr * LINE : (rr + 1) * LINE, :] = (u * inverse_rms(u)).astype(BF16)
    project(left_s[0], qkv_s, w_s, weights)
    lefts[0].start()
    start_all(saved)

    def visit(rows, lanes, at, pair):
        probs = softmax(qkv_s[0, rows, lanes], qkv_s[1, rows, lanes]).astype(BF16)
        mixed = pick_halves(dot(probs, qkv_s[2, rows, lanes]))
        left_s[1, rows, lanes] = (mixed * gain_row(keep_ref, 0, pair * 2, 2)).astype(BF16)

    each_pair(visit)
    lefts[1].start()
    weights[3].wait()
    added = dot(left_s[1], w_s[3])
    for rr in range(2):
        u = x_ref[:, rr].astype(F32).reshape(LINE, D)
        mid = (u + added[rr * LINE : (rr + 1) * LINE]).reshape(16, 2, 8, D)
        for cc in range(2):
            for group in range(4):
                piece = mid[:, cc, :, group * 128 : (group + 1) * 128].reshape(128, 128)
                mix_s[pl.ds(slot(cc, group, rr), 128, stride=16), :] = piece
    sends = []
    for part in range(4):
        rows = slice(part * 32, (part + 1) * 32)
        mid_s[rows] = mix_s[part * 512 : (part + 1) * 512, :].reshape(32, 16, 128).astype(BF16)
        sends.append(pltpu.make_async_copy(mid_s.at[rows], mid_ref.at[rows], mid_sem.at[part]))
        sends[-1].start()
    wait_all(saved + lefts + sends)


def row_prepare_kernel(qkv_ref, left_ref, probs_ref, turned_ref):
    def visit(rows, lanes, at, pair):
        probs_ref[at] = softmax(qkv_ref[0, rows, lanes], qkv_ref[1, rows, lanes])

    each_pair(visit)
    for which in range(2):
        turned_ref[which] = left_ref[which].T


def attention_backward(rows, lanes, qkv, da_ref, probs, right_ref):
    q_pair, k_pair, v_pair = (qkv[i, rows, lanes] for i in range(3))
    da_pair = da_ref[rows, lanes]
    low = probs.astype(BF16)
    grad_probs = dot_nt(stack_halves(da_pair), v_pair)
    total = jnp.sum(probs * grad_probs, axis=-1, keepdims=True)
    grads = (probs * (grad_probs - total)).astype(BF16)
    right_ref[0, rows, lanes] = (pick_halves(dot(grads, k_pair)) * SCALE).astype(BF16)
    right_ref[1, rows, lanes] = pick_halves(dot(turn_halves(grads), q_pair)).astype(BF16)
    right_ref[2, rows, lanes] = pick_halves(dot(turn_halves(low), da_pair)).astype(BF16)
    return low


def input_gradient(u, right_ref, w_s, rows):
    inv = inverse_rms(u)
    dn = (
        dot_nt(right_ref[0, rows, :], w_s[0])
        + dot_nt(right_ref[1, rows, :], w_s[1])
        + dot_nt(right_ref[2, rows, :], w_s[2])
    )
    mean = jnp.mean(dn * u, axis=-1, keepdims=True)
    return right_ref[3, rows, :].astype(F32) + inv * dn - u * (inv * inv * inv * mean)


def weight_gradients(side, turned, right_ref, target):
    for j in range(2):
        which = side * 2 + j
        target[j] = dot(turned[which // 3], right_ref[which]).astype(BF16)


def row_backward_kernel(
    where_ref, keep_heads_ref, g_ref, qkv_ref, turned_ref, probs_ref, w_ref,
    keep_ref, send_ref, right_ref,
    mix_s, da_s, wo_s, qkv_s, turned_s, probs_s, keep_s, send_s, right_s,
    wo_sem, qkv_sem, turned_sem, probs_sem, half_sem, right_sem,
):
    weight = pltpu.make_async_copy(w_ref.at[3], wo_s, wo_sem)
    weight.start()
    saved = copies_of(qkv_ref, qkv_s, qkv_sem, 3)
    start_all(saved)
    probs = [
        pltpu.make_async_copy(
            probs_ref.at[i * 2 : (i + 1) * 2], probs_s.at[i * 2 : (i + 1) * 2], probs_sem.at[i]
        )
        for i in range(4)
    ]
    start_all(probs)
    turned = copies_of(turned_ref, turned_s, turned_sem, 2)
    start_all(turned)
    mix_s[...] = g_ref[...].astype(F32).reshape(N_DEV * 16, 128)
    for rr in range(2):
        for group in range(4):
            sides = [
                mix_s[pl.ds(slot(cc, group, rr), 128, stride=16), :].reshape(16, 8, 128)
                for cc in range(2)
            ]
            right_s[3, rr * LINE : (rr + 1) * LINE, group * 128 : (group + 1) * 128] = (
                jnp.stack(sides, axis=1).reshape(LINE, 128).astype(BF16)
            )
    weight.wait()
    gain = gain_row(keep_heads_ref, 0, 0, HEADS)
    da_s[...] = (dot_nt(right_s[3], wo_s[...]) * gain).astype(BF16)
    wait_all(saved + probs)

    def visit(rows, lanes, at, pair):
        attention_backward(rows, lanes, qkv_s, da_s, probs_s[at], right_s)

    each_pair(visit)
    rights = copies_of(right_s, right_ref, right_sem, 4)
    start_all(rights)
    wait_all(turned)
    core = where_ref[4]
    weight_gradients(1 - core, turned_s, right_s, send_s)
    sent = pltpu.make_async_copy(send_s, send_ref, half_sem.at[0])
    sent.start()
    weight_gradients(core, turned_s, right_s, keep_s)
    kept = pltpu.make_async_copy(keep_s, keep_ref, half_sem.at[1])
    kept.start()
    wait_all(rights + [sent, kept])


def row_input_gradient_kernel(where_ref, x_ref, right_ref, w_ref, *refs):
    outs, w_s, sems, gin_s = refs[:4], refs[4], refs[5], refs[6]
    copies = copies_of(w_ref, w_s, sems, 3)
    start_all(copies)
    wait_all(copies)
    for rr in range(2):
        rows = slice(rr * LINE, (rr + 1) * LINE)
        u = x_ref[:, rr].astype(F32).reshape(LINE, D)
        grad_in = input_gradient(u, right_ref, w_s, rows)
        gin_s[:, :, :, rr] = grad_in.astype(BF16).reshape(2, 4, 2, 16, D)
    for shift in range(4):
        outs[shift][...] = gin_s[:, lax.rem(where_ref[3] + shift, 4)]


def col_kernel(where_ref, keep_heads_ref, m_ref, w_ref, *refs):
    parts, got_ref, refs = refs[:4], refs[4], refs[5:]
    gmid_ref, left_ref, right_ref, u_ref = refs[:4]
    mix_s, u_s, ulow_s, left_s, right_s, qkv_s, da_s, w_s = refs[4:12]
    w_sem, left_sem, right_sem, u_sem = refs[12:]
    mine = where_ref[1]
    weights = copies_of(w_ref, w_s, w_sem, 4)
    for i in (3, 0, 1, 2):
        weights[i].start()
    lefts = copies_of(left_s, left_ref, left_sem, 2)
    rights = copies_of(right_s, right_ref, right_sem, 4)
    for shift in range(4):
        source = lax.rem(where_ref[0] + (4 - shift), 4) * 2
        for grid_row, piece in ((source + mine, parts[shift].at[mine]), (source + (1 - mine), got_ref.at[shift])):
            for cc in range(2):
                for rr in range(2):
                    at = pl.multiple_of(grid_row * 16 + (cc * LINE + rr * 128), 16)
                    right_s[3, pl.ds(at, 16), :] = piece[cc, rr * 16 : (rr + 1) * 16, :]
    rights[3].start()
    weights[3].wait()
    gain = gain_row(keep_heads_ref, 1, 0, HEADS)
    da_s[...] = (dot_nt(right_s[3], w_s[3]) * gain).astype(BF16)
    mix_s[...] = m_ref[...].astype(F32).reshape(N_DEV * 16, 128)
    for cc in range(2):
        for rr in range(2):
            base = cc * LINE + rr * 128
            for group in range(4):
                for grid_row in range(N_ROW):
                    start = base + grid_row * 16
                    u_s[start : start + 16, group * 128 : (group + 1) * 128] = mix_s[
                        pl.ds(grid_row * 16 + slot(cc, group, rr), 16, stride=128), :
                    ]
    u = u_s[...]
    ulow_s[...] = u.astype(BF16)
    kept_u = pltpu.make_async_copy(ulow_s, u_ref, u_sem)
    kept_u.start()
    left_s[0] = (u * inverse_rms(u)).astype(BF16)
    lefts[0].start()
    project(left_s[0], qkv_s, w_s, weights)

    def visit(rows, lanes, at, pair):
        probs = softmax(qkv_s[0, rows, lanes], qkv_s[1, rows, lanes])
        low = attention_backward(rows, lanes, qkv_s, da_s, probs, right_s)
        mixed = pick_halves(dot(low, qkv_s[2, rows, lanes]))
        left_s[1, rows, lanes] = (mixed * gain_row(keep_heads_ref, 1, pair * 2, 2)).astype(BF16)

    each_pair(visit)
    lefts[1].start()
    start_all(rights[:3])
    for cc in range(2):
        rows = slice(cc * LINE, (cc + 1) * LINE)
        grad_in = input_gradient(u_s[rows, :], right_s, w_s, rows)
        for rr in range(2):
            for group in range(4):
                for grid_row in range(N_ROW):
                    start = rr * 128 + grid_row * 16
                    mix_s[pl.ds(grid_row * 16 + slot(cc, group, rr), 16, stride=128), :] = grad_in[
                        start : start + 16, group * 128 : (group + 1) * 128
                    ]
    gmid_ref[...] = mix_s[...].reshape(N_DEV, 16, 128).astype(BF16)
    wait_all(lefts + rights + [kept_u])


def col_output_kernel(where_ref, left_ref, right_ref, u_ref, w_ref, *refs):
    keep_ref, send_ref, outs = refs[0], refs[1], refs[2:6]
    turned_s, out_s, wo_s, sem = refs[6:]
    core = where_ref[4]
    copy = pltpu.make_async_copy(w_ref.at[3], wo_s, sem)
    copy.start()
    for which in range(2):
        turned_s[which] = left_ref[which].T
    weight_gradients(1 - core, turned_s, right_ref, send_ref)
    weight_gradients(core, turned_s, right_ref, keep_ref)
    copy.wait()
    out_s[...] = (u_ref[...].astype(F32) + dot(left_ref[1], wo_s[...])).astype(BF16)
    for shift in range(4):
        for low in range(2):
            start = lax.rem(where_ref[0] + shift, 4) * 32 + low * 16
            for cc in range(2):
                for rr in range(2):
                    at = pl.multiple_of(start + (cc * LINE + rr * 128), 16)
                    outs[shift][low, cc, rr * 16 : (rr + 1) * 16, :] = out_s[pl.ds(at, 16), :]


def tile_to_lines_kernel(where_ref, tile_ref, *refs):
    outs, mix_s = refs[:4], refs[4]
    tile = tile_ref[...].astype(F32).reshape(TOK, D)
    for group in range(4):
        lanes = slice(group * 128, (group + 1) * 128)
        mix_s[group] = tile[:, lanes]
        for shift in range(4):
            for low in range(2):
                peer = lax.rem(where_ref[0] + shift, 4) * 2 + low
                for cc in range(2):
                    for rr in range(2):
                        piece = mix_s[group, pl.ds(peer + (rr * 16 + cc * 8), 16, stride=32), :]
                        outs[shift][low, cc, rr * 16 : (rr + 1) * 16, lanes] = piece.astype(BF16)


def pass_low_kernel(where_ref, *refs):
    parts, pass_ref = refs[:4], refs[4]
    for shift in range(4):
        pass_ref[shift] = parts[shift][1 - where_ref[1]]


def lines_to_tile_kernel(where_ref, *refs):
    parts, got_ref, tile_ref, mix_s = refs[:4], refs[4], refs[5], refs[6]
    mine = where_ref[1]
    for group in range(4):
        lanes = slice(group * 128, (group + 1) * 128)
        for shift in range(4):
            source = lax.rem(where_ref[0] + (4 - shift), 4) * 2
            for peer, piece in ((source + mine, parts[shift].at[mine]), (source + (1 - mine), got_ref.at[shift])):
                for cc in range(2):
                    for rr in range(2):
                        value = piece[cc, rr * 16 : (rr + 1) * 16, lanes].astype(F32)
                        mix_s[group, pl.ds(peer + (rr * 16 + cc * 8), 16, stride=32), :] = value
        tile_ref[:, :, lanes] = mix_s[group].astype(BF16).reshape(32, 16, 128)


def pass_high_kernel(where_ref, *refs):
    parts, pass_ref = refs[:4], refs[4]
    for shift in range(4):
        pass_ref[shift] = parts[shift][1 - where_ref[2]]


def pass_core_kernel(where_ref, *refs):
    parts, got_ref, pass_ref = refs[:4], refs[4], refs[5]
    high, other = where_ref[2], 1 - where_ref[4]
    for shift in range(4):
        pass_ref[0, shift] = parts[shift][high, other]
        pass_ref[1, shift] = got_ref[shift, other]


def join_kernel(where_ref, *refs):
    parts, got_ref, passed_ref, tile_ref = refs[:4], refs[4], refs[5], refs[6]
    high, core = where_ref[2], where_ref[4]
    for shift in range(4):
        source = lax.rem(where_ref[3] + (4 - shift), 4)
        tile_ref[high, source, core] = parts[shift][high, core]
        tile_ref[1 - high, source, core] = got_ref[shift, core]
        tile_ref[high, source, 1 - core] = passed_ref[0, shift]
        tile_ref[1 - high, source, 1 - core] = passed_ref[1, shift]


def pair_sum_kernel(where_ref, keep_ref, got_ref, *refs):
    outs, sum_s = refs[:4], refs[4]
    total = keep_ref[...].astype(F32) + got_ref[...].astype(F32)
    sum_s[...] = total.astype(BF16).reshape(4, 256, D)
    for shift in range(4):
        outs[shift][...] = sum_s[lax.rem(where_ref[3] + shift, 4)]


def merge_kernel(keep_ref, got_ref, *refs):
    quarters, both_ref = refs[:4], refs[4]
    total = keep_ref[...].astype(F32) + got_ref[...].astype(F32)
    rows = total.astype(BF16).reshape(64, 16, D)
    quarter = quarters[0][...].astype(F32)
    for i in range(1, 4):
        quarter = quarter + quarters[i][...].astype(F32)
    quarter = quarter.astype(BF16).reshape(16, 16, D)
    for group in range(4):
        lanes = slice(group * 128, (group + 1) * 128)
        both_ref[:, group * 16 : (group + 1) * 16, :] = rows[:, :, lanes]
        for block in range(16):
            both_ref[block * 4 + group, 64:80, :] = quarter[block, :, lanes]


def chip_sum(parts_ref, rows, first, step):
    total = parts_ref[first, rows, :].astype(F32)
    for chip in range(first + step, 64, step):
        total = total + parts_ref[chip, rows, :].astype(F32)
    return total.astype(BF16)


def spread_kernel(both_ref, spread_ref):
    row_sum = chip_sum(both_ref, slice(0, 64), 0, 1)
    spread_ref[:, 0:64, :] = jnp.broadcast_to(row_sum[None], (64, 64, 128))
    for quarter in range(4):
        part = chip_sum(both_ref, slice(64, 80), quarter, 4)
        first = 64 + quarter * 16
        spread_ref[:, first : first + 16, :] = jnp.broadcast_to(part[None], (64, 16, 128))


def widen_kernel(where_ref, chunks_ref, *refs):
    row_ref, col_ref = refs[-2:]
    for group in range(4):
        lanes = slice(group * 128, (group + 1) * 128)
        piece = chunks_ref[:, group * 16 : (group + 1) * 16, :].astype(F32)
        row_ref[0, :, lanes] = piece.reshape(256, 128)
        for quarter in range(4):
            for block in range(4):
                first = 64 + quarter * 16
                col_ref[0, quarter, block * 16 : (block + 1) * 16, lanes] = chunks_ref[
                    block * 4 + group, first : first + 16, :
                ].astype(F32)


MIB = 1 << 20
SMEM = pl.BlockSpec(memory_space=pltpu.SMEM)
VMEM = pl.BlockSpec(memory_space=pltpu.VMEM)
HBM = pl.BlockSpec(memory_space=pltpu.HBM)


GRANT = 60 * 1024 * 1024
SPACE = {"s": SMEM, "v": VMEM, "h": HBM}


def call(kernel, ins, out_kinds, outs, scratch, flops, moved):
    spaces = tuple(SPACE[kind] for kind in out_kinds)
    return pl.pallas_call(
        kernel,
        in_specs=[SPACE[kind] for kind in ins],
        out_specs=spaces if isinstance(outs, tuple) else spaces[0],
        out_shape=outs,
        scratch_shapes=scratch,
        compiler_params=pltpu.CompilerParams(vmem_limit_bytes=GRANT),
        cost_estimate=pl.CostEstimate(flops=flops, bytes_accessed=moved, transcendentals=0),
    )


def shape(*dims, dtype=BF16):
    return jax.ShapeDtypeStruct(dims, dtype)


MATMUL = 2 * TOK * D * D
ATTEND = 2 * 16 * LINE * LINE * HEAD
MIX = pltpu.VMEM((N_DEV * 16, 128), F32)
MIX_TILE = pltpu.VMEM((4, TOK, 128), F32)
DMA = pltpu.SemaphoreType.DMA
WEIGHTS = [pltpu.VMEM((4, D, D), BF16), DMA((4,))]
WEIGHT = [pltpu.VMEM((D, D), BF16), DMA]
PIECE = shape(2, 2, 32, D)
PASS = shape(4, 2, 32, D)
QUARTER = shape(256, D)
HALF = shape(2, D, D)
HALF_S = pltpu.VMEM((2, D, D), BF16)


def token_scratch(*lead, dtype=BF16):
    return pltpu.VMEM((*lead, TOK, D), dtype)


row_forward = call(
    row_forward_kernel,
    "svh",
    "hhh",
    (shape(N_DEV, 16, 128), shape(3, TOK, D), shape(2, TOK, D)),
    [
        MIX, pltpu.VMEM((N_DEV, 16, 128), BF16), token_scratch(3), token_scratch(2), *WEIGHTS,
        DMA((4,)), DMA((3,)), DMA((2,)),
    ],
    4 * MATMUL + 2 * ATTEND,
    6 * MIB,
)
row_prepare = call(
    row_prepare_kernel,
    "vv",
    "vv",
    (shape(8, TOK, LINE, dtype=F32), shape(2, D, TOK)),
    [],
    ATTEND,
    8 * MIB,
)
row_backward = call(
    row_backward_kernel,
    "ssvhhhh",
    "hhh",
    (HALF, HALF, shape(4, TOK, D)),
    [
        MIX, token_scratch(), pltpu.VMEM((D, D), BF16), token_scratch(3),
        pltpu.VMEM((2, D, TOK), BF16), pltpu.VMEM((8, TOK, LINE), F32), HALF_S, HALF_S,
        token_scratch(4), DMA, DMA((3,)), DMA((2,)), DMA((4,)), DMA((2,)), DMA((4,)),
    ],
    5 * MATMUL + 5 * ATTEND,
    12 * MIB,
)
row_input_gradient = call(
    row_input_gradient_kernel,
    "svvh",
    "v" * 4,
    (shape(2, 2, 2, 16, D),) * 4,
    [*WEIGHTS, pltpu.VMEM((2, 4, 2, 2, 16, D), BF16)],
    3 * MATMUL,
    5 * MIB,
)
col_grad = call(
    col_kernel,
    "ssvh" + "v" * 5,
    "vhhh",
    (shape(N_DEV, 16, 128), shape(2, TOK, D), shape(4, TOK, D), shape(TOK, D)),
    [
        MIX, token_scratch(dtype=F32), token_scratch(), token_scratch(2), token_scratch(4),
        token_scratch(3), token_scratch(), *WEIGHTS, DMA((2,)), DMA((4,)), DMA,
    ],
    8 * MATMUL + 6 * ATTEND,
    8 * MIB,
)
col_output = call(
    col_output_kernel,
    "svvvh",
    "v" * 6,
    (HALF, HALF) + (PIECE,) * 4,
    [pltpu.VMEM((2, D, TOK), BF16), token_scratch(), *WEIGHT],
    5 * MATMUL,
    7 * MIB,
)
tile_to_lines = call(tile_to_lines_kernel, "sv", "v" * 4, (PIECE,) * 4, [MIX_TILE], 0, MIB)
pass_low = call(pass_low_kernel, "s" + "v" * 4, "v", PASS, [], 0, MIB)
lines_to_tile = call(lines_to_tile_kernel, "s" + "v" * 5, "v", shape(32, 16, D), [MIX_TILE], 0, MIB)
CHIP_PASS = shape(4, 2, 2, 16, D)
CORE_PASS = shape(2, 4, 2, 16, D)
pass_high = call(pass_high_kernel, "s" + "v" * 4, "v", CHIP_PASS, [], 0, MIB)
pass_core = call(pass_core_kernel, "s" + "v" * 5, "v", CORE_PASS, [], 0, MIB)
join = call(join_kernel, "s" + "v" * 6, "v", shape(2, 4, 2, 2, 16, D), [], 0, MIB)
pair_sum = call(
    pair_sum_kernel, "svv", "v" * 4, (QUARTER,) * 4, [pltpu.VMEM((4, 256, D), BF16)], 0, 3 * MIB,
)
merge = call(merge_kernel, "v" * 6, "v", shape(64, 80, 128), [], 0, 4 * MIB)
spread = call(spread_kernel, "v", "v", shape(64, 128, 128), [], 0, 3 * MIB)


def widen(where, chunks, side, *before):
    half = lambda ref: ref[4] if side == 0 else 1 - ref[4]
    outs = (
        pl.BlockSpec((1, 256, D), lambda i, ref: (half(ref), i, 0)),
        pl.BlockSpec((1, 4, 64, D), lambda i, ref: (half(ref), 0, i, 0)),
    )
    return pl.pallas_call(
        widen_kernel,
        grid_spec=pltpu.PrefetchScalarGridSpec(
            num_scalar_prefetch=1,
            grid=(4,),
            in_specs=[pl.BlockSpec((16, 128, 128), lambda i, ref: (i, 0, 0))]
            + [pl.BlockSpec(memory_space=pl.ANY)] * len(before),
            out_specs=outs,
        ),
        out_shape=(shape(2, 1024, D, dtype=F32), shape(2, 4, 256, D, dtype=F32)),
        input_output_aliases={2: 0, 3: 1} if before else {},
        name="widen",
        compiler_params=pltpu.CompilerParams(vmem_limit_bytes=GRANT),
        cost_estimate=pl.CostEstimate(flops=0, bytes_accessed=6 * MIB, transcendentals=0),
    )(where, chunks, *before)


def exchange(values, axes):
    return lax.all_to_all(values, axes, split_axis=0, concat_axis=0, tiled=True)


def shifted(pieces, axes):
    n = len(pieces)
    return [pieces[0]] + [
        lax.ppermute(pieces[k], axes, [(i, (i + k) % n) for i in range(n)]) for k in range(1, n)
    ]


def swap(value, axis):
    return lax.ppermute(value, axis, [(0, 1), (1, 0)])


def layer(latents, cotangent, w_row, w_col, keep_heads):
    where = jnp.stack([lax.axis_index(name) for name in AXES]).astype(jnp.int32)
    rows_in = exchange(latents.reshape(16, 2, 16, D), COL)
    grad_pieces = tile_to_lines(where, cotangent)
    grad_parts = shifted(grad_pieces, "y")
    grad_pass = pass_low(where, *grad_parts)
    grad_pass = swap(grad_pass, "zl")
    mid_send, qkv_row, left_row = row_forward(keep_heads, rows_in, w_row)
    mid_lines = exchange(mid_send, BOTH)
    probs_row, turned_row = row_prepare(qkv_row, left_row)
    grad_send, left_col, right_col, u_col = col_grad(
        where, keep_heads, mid_lines, w_col, *grad_parts, grad_pass
    )
    grad_rows = exchange(grad_send, BOTH)
    keep_col, send_col, *out_pieces = col_output(where, left_col, right_col, u_col, w_col)
    got_col = swap(send_col, "c")
    quarters = pair_sum(where, keep_col, got_col)
    quarters = shifted(quarters, "x")
    keep_row, send_row, right_row = row_backward(
        where, keep_heads, grad_rows, qkv_row, turned_row, probs_row, w_row
    )
    got_row = swap(send_row, "c")
    merged = merge(keep_row, got_row, *quarters)
    both = exchange(merged, CHIPS)
    totals = spread(both)
    chunks = exchange(totals, CHIPS)
    gin_pieces = row_input_gradient(where, rows_in, right_row, w_row)
    gin_parts = shifted(gin_pieces, "x")
    gin_pass = pass_high(where, *gin_parts)
    gin_got = swap(gin_pass, "zh")
    gin_core = pass_core(where, *gin_parts, gin_got)
    gin_core = swap(gin_core, "c")
    grad_latents = join(where, *gin_parts, gin_got, gin_core).reshape(32, 16, D)
    out_parts = shifted(out_pieces, "y")
    out_pass = pass_low(where, *out_parts)
    out_pass = swap(out_pass, "zl")
    output = lines_to_tile(where, *out_parts, out_pass)
    other = swap(chunks, "c")
    halves_done = widen(where, chunks, 0)
    grad_row, grad_col = widen(where, other, 1, *halves_done)
    return (output, grad_latents, grad_row.reshape(4, D, D), grad_col.reshape(4, D, D))


def solution(mesh):
    fine = Mesh(mesh.devices.reshape(4, 2, 2, 4, 2), AXES)
    tile = P(ROW, COL, None)
    return jax.shard_map(
        layer,
        mesh=fine,
        in_specs=(tile, tile, P(), P(), P()),
        out_specs=(tile, tile, P(), P()),
        check_vma=False,
    )
```

time: 258 us -> 257 us (level)
  blocking collectives: 32 us -> 81.4 us
  starting transfers between devices: 72.8 us -> 40.4 us
  Pallas kernels: 55.3 us -> 85.1 us
  waiting for transfers between devices: 64.2 us -> 35.8 us
  local copies, waits for them, and re-layouts: 28.7 us -> 9.11 us
    all_to_all x1 -> x3, blocking collectives: 32 us -> 81.4 us  [exchange(): return lax.all_to_all(values, axes, split_axis=0, concat_axis=0, tiled=True)]
    all_to_all x5 -> x2, waiting for transfers between devices: 39.7 us -> 0.01 us  [exchange(): return lax.all_to_all(values, axes, split_axis=0, concat_axis=0, tiled=True)]
    all_to_all x5 -> x2, starting transfers between devices: 35.1 us -> 13.8 us  [exchange(): return lax.all_to_all(values, axes, split_axis=0, concat_axis=0, tiled=True)]
    unnamed x62 -> x48, local copies, waits for them, and re-layouts: 28.4 us -> 8.51 us
    pallas_call x13 -> x14, Pallas kernels: 46.2 us -> 65.7 us  [the longest x1 14.4 us: layer(): col_grad(where, keep_heads, mid_lines, w_col, *grad_parts, grad_pass)]
    ppermute x21 -> x12, starting transfers between devices: 23.6 us -> 14.2 us  [shifted(): lax.ppermute(pieces[k], axes, [(i, (i + k) % n) for i in range(n)])]
    ppermute x5 -> x7, waiting for transfers between devices: 0.01 us -> 6.09 us  [swap(): return lax.ppermute(value, axis, [(0, 1), (1, 0)])]
    ppermute x21 -> x12, waiting for transfers between devices: 24.6 us -> 29.7 us  [shifted(): lax.ppermute(pieces[k], axes, [(i, (i + k) % n) for i in range(n)])]
  transfers between devices with their start and end apart: 31 -> 21, of which waited for: 17 -> 11; matrix products, arithmetic and copies ran while one was open for 0% -> 0% of each run, Pallas kernels for 10% -> 20%
where the time goes in v1:
time: 257 us; the launch traced here: 253 us
  Pallas kernels  85.1 us (33%)
  blocking collectives  81.4 us (32%)
  starting transfers between devices  40.4 us (16%)
  waiting for transfers between devices  35.8 us (14%)
  local copies, waits for them, and re-layouts  9.11 us (4%)
    all_to_all x3, blocking collectives, exchange(): return lax.all_to_all(values, axes, split_axis=0, concat_axis=0, tiled=True)  81.4 us
    ppermute x12, waiting for transfers between devices, shifted(): lax.ppermute(pieces[k], axes, [(i, (i + k) % n) for i in range(n)])  29.7 us
    pallas_call x1, Pallas kernels, layer(): col_grad(where, keep_heads, mid_lines, w_col, *grad_parts, grad_pass)  14.4 us
    ppermute x12, starting transfers between devices, shifted(): lax.ppermute(pieces[k], axes, [(i, (i + k) % n) for i in range(n)])  14.2 us
    all_to_all x2, starting transfers between devices, exchange(): return lax.all_to_all(values, axes, split_axis=0, concat_axis=0, tiled=True)  13.8 us
    ppermute x7, starting transfers between devices, swap(): return lax.ppermute(value, axis, [(0, 1), (1, 0)])  12.4 us
    pallas_call x1, Pallas kernels, layer(): row_backward(where, keep_heads, grad_rows, qkv_row, turned_row, probs_row...  11.2 us
    pallas_call x2, Pallas kernels, widen(): pl.pallas_call(widen_kernel, grid_spec=pltpu.PrefetchScalarGridSpec(num_s...  9.76 us
  transfers between devices with their start and end apart: 21, of which 11 were waited for; matrix products, arithmetic and copies ran while one was open for 0% of the time, Pallas kernels for 20%

profile of v1, /device:TPU:1, one launch (start us, length us, event | category | flops | bytes accessed | tf_op | source)
XLA Modules:
  0.0 252.6 jit_solution(10165699696279058066)
XLA Ops:
  0.6 20.2 %all_to_all.25.x_ref = bf16[16,2,16,512]{3,2,1,0:T(8,128)(2,1)} all-to-all(bf16[16,2,16,512]{3,2,1,0:T(8,128)(2,1)} %bitcast.11), channel_id=1, replica_groups=mesh['y'=4,'zl'=2,'zh'=2,'x'=4,'c'=2] {'zh','x','c'}, dimensions={0} | all-to-all | bytes 1048576 | tf_op jit(solution)/shard_map/all_to_all | solution.py:610
  20.9 8.5 %shard_map.84 = (bf16[128,16,128]{2,1,0:T(8,128)(2,1)}, bf16[3,512,512]{2,1,0:T(8,128)(2,1)}, bf16[2,512,512]{2,1,0:T(8,128)(2,1)}) custom-call(s32[2,8]{1,0:T(2,128)} %keep_heads_ref.3, bf16[16,2,16,512]{3,2,1,0:T(8,128)(2,1)} %all_to_all.25.x_ref, bf16[4,512,512]{2,1,0:T(8,128)(2,1)} %w_ref.9), custom_call_target="tpu_custom_call" | custom-call | flops 1342177280 | bytes 6291456 | tf_op jit(solution)/shard_map/pallas_call | solution.py:631
  29.4 6.0 %all-to-all-start.1 = ((bf16[128,16,128]{2,1,0:T(8,128)(2,1)}), bf16[128,16,128]{2,1,0:T(8,128)(2,1)S(1)}, u32[]{:S(2)}, u32[]{:S(2)}) async-start(bf16[128,16,128]{2,1,0:T(8,128)(2,1)} %get-tuple-element.38), calls=%async_computation.1 | async-start | bytes 1048576 | tf_op jit(solution)/shard_map/all_to_all | solution.py:610
  35.3 0.6 stack.23.where_ref
  35.9 2.5 shard_map.85
  38.4 1.4 collective-permute-start
  39.8 2.5 collective-permute-start.1
  42.2 1.1 collective-permute-start.2
  43.4 4.1 %collective-permute-done.refs_1_ = bf16[2,2,32,512]{3,2,1,0:T(8,128)(2,1)S(1)} collective-permute-done((bf16[2,2,32,512]{3,2,1,0:T(8,128)(2,1)}, bf16[2,2,32,512]{3,2,1,0:T(8,128)(2,1)S(1)}, u32[]{:S(2)}, u32[]{:S(2)}) %collective-permute-start) | collective-permute-done | bytes 131104 | tf_op jit(solution)/shard_map/ppermute | solution.py:616
  47.4 3.4 %collective-permute-done.1.refs_2_ = bf16[2,2,32,512]{3,2,1,0:T(8,128)(2,1)S(1)} collective-permute-done((bf16[2,2,32,512]{3,2,1,0:T(8,128)(2,1)}, bf16[2,2,32,512]{3,2,1,0:T(8,128)(2,1)S(1)}, u32[]{:S(2)}, u32[]{:S(2)}) %collective-permute-start.1) | collective-permute-done | bytes 131104 | tf_op jit(solution)/shard_map/ppermute | solution.py:616
  50.8 0.7 copy-done.18
  51.5 1.8 shard_map.86
  53.4 1.3 collective-permute-start.3
  54.7 6.1 %collective-permute-done.3.refs_4_ = bf16[4,2,32,512]{3,2,1,0:T(8,128)(2,1)S(1)} collective-permute-done((bf16[4,2,32,512]{3,2,1,0:T(8,128)(2,1)}, bf16[4,2,32,512]{3,2,1,0:T(8,128)(2,1)S(1)}, u32[]{:S(2)}, u32[]{:S(2)}) %collective-permute-start.3) | collective-permute-done | bytes 262176 | tf_op jit(solution)/shard_map/ppermute | solution.py:621
  60.8 0.7 copy-done.20
  61.5 0.8 copy-done.8
  62.3 14.4 %shard_map.87 = (bf16[128,16,128]{2,1,0:T(8,128)(2,1)}, bf16[2,512,512]{2,1,0:T(8,128)(2,1)}, bf16[4,512,512]{2,1,0:T(8,128)(2,1)}, bf16[512,512]{1,0:T(8,128)(2,1)}) custom-call(s32[5]{0:T(128)} %stack.23.where_ref, s32[2,8]{1,0:T(2,128)} %keep_heads_ref.3, bf16[128,16,128]{2,1,0:T(8,128)(2,1)} %copy-done.8, bf16[4,512,512]{2,1,0:T(8,128)(2,1)} %w_ref.7, ...), custom_call_target="tpu_custom_call" | custom-call | flops 2952790016 | bytes 8388608 | tf_op jit(solution)/shard_map/pallas_call | solution.py:634
  76.7 7.8 %all-to-all-start.2 = ((bf16[128,16,128]{2,1,0:T(8,128)(2,1)}), bf16[128,16,128]{2,1,0:T(8,128)(2,1)S(1)}, u32[]{:S(2)}, u32[]{:S(2)}) async-start(bf16[128,16,128]{2,1,0:T(8,128)(2,1)} %get-tuple-element.50), calls=%async_computation.2 | async-start | bytes 1048576 | tf_op jit(solution)/shard_map/all_to_all | solution.py:610
  84.5 5.5 %shard_map.88 = (bf16[2,512,512]{2,1,0:T(8,128)(2,1)}, bf16[2,512,512]{2,1,0:T(8,128)(2,1)}, bf16[2,2,32,512]{3,2,1,0:T(8,128)(2,1)}, bf16[2,2,32,512]{3,2,1,0:T...) custom-call(s32[5]{0:T(128)} %stack.23.where_ref, ...), custom_call_target="tpu_custom_call" | custom-call | flops 1342177280 | bytes 7340032 | tf_op jit(solution)/shard_map/pallas_call | solution.py:638
  90.0 1.3 collective-permute-start.14
  91.3 6.2 %shard_map.91 = (f32[8,512,256]{2,1,0:T(8,128)}, bf16[2,512,512]{2,1,0:T(8,128)(2,1)}) custom-call(bf16[3,512,512]{2,1,0:T(8,128)(2,1)} %get-tuple-element.51.qkv_ref, bf16[2,512,512]{2,1,0:T(8,128)(2,1)} %get-tuple-element.52.left_ref), custom_call_target="tpu_custom_call" | custom-call | flops 134217728 | bytes 8388608 | tf_op jit(solution)/shard_map/pallas_call | solution.py:633
  97.5 0.8 copy-done.1
  98.3 11.2 %shard_map.92 = (bf16[2,512,512]{2,1,0:T(8,128)(2,1)}, bf16[2,512,512]{2,1,0:T(8,128)(2,1)}, bf16[4,512,512]{2,1,0:T(8,128)(2,1)}) custom-call(s32[5]{0:T(128)} %stack.23.where_ref, s32[2,8]{1,0:T(2,128)} %keep_heads_ref.3, bf16[128,16,128]{2,1,0:T(8,128)(2,1)} %copy-done.1, bf16[3,512,512]{2,1,0:T(8,128)(2,1)} %get-tuple-element.51.qkv_ref, ...), custom_call_target="tpu_custom_call" | custom-call | flops 2013265920 | bytes 12582912 | tf_op jit(solution)/shard_map/pallas_call | solution.py:642
  109.5 1.5 collective-permute-start.13
  111.0 1.0 copy-done.6
  112.0 3.1 %shard_map.97 = (bf16[256,512]{1,0:T(8,128)(2,1)}, bf16[256,512]{1,0:T(8,128)(2,1)}, bf16[256,512]{1,0:T(8,128)(2,1)}, bf16[256,512]{1,0:T(8,128)(2,1)}) custom-call(s32[5]{0:T(128)} %stack.23.where_ref, bf16[2,512,512]{2,1,0:T(8,128)(2,1)} %get-tuple-element.62.keep_ref, bf16[2,512,512]{2,1,0:T(8,128)(2,1)} %copy-done.6), custom_call_target="tpu_custom_call" | custom-call | bytes 3145728 | tf_op jit(solution)/shard_map/pallas_call | solution.py:640
  115.1 0.3 collective-permute-start.15
  115.4 1.9 collective-permute-start.16
  117.3 0.9 collective-permute-start.17
  118.2 6.6 %collective-permute-done.15.refs_1_ = bf16[256,512]{1,0:T(8,128)(2,1)S(1)} collective-permute-done((bf16[256,512]{1,0:T(8,128)(2,1)}, bf16[256,512]{1,0:T(8,128)(2,1)S(1)}, u32[]{:S(2)}, u32[]{:S(2)}) %collective-permute-start.15) | collective-permute-done | bytes 262176 | tf_op jit(solution)/shard_map/ppermute | solution.py:616
  124.8 4.7 %collective-permute-done.16.refs_2_ = bf16[256,512]{1,0:T(8,128)(2,1)S(1)} collective-permute-done((bf16[256,512]{1,0:T(8,128)(2,1)}, bf16[256,512]{1,0:T(8,128)(2,1)S(1)}, u32[]{:S(2)}, u32[]{:S(2)}) %collective-permute-start.16) | collective-permute-done | bytes 262176 | tf_op jit(solution)/shard_map/ppermute | solution.py:616
  129.5 0.8 collective-permute-done.17.refs_3_
  130.3 0.7 copy-done.14
  131.0 0.4 copy-done.5
  131.4 3.3 %shard_map.98 = bf16[64,80,128]{2,1,0:T(8,128)(2,1)} custom-call(bf16[2,512,512]{2,1,0:T(8,128)(2,1)} %get-tuple-element.60.keep_ref, bf16[2,512,512]{2,1,0:T(8,128)(2,1)} %copy-done.5, bf16[256,512]{1,0:T(8,128)(2,1)} %get-tuple-element.64.refs_0_, bf16[256,512]{1,0:T(8,128)(2,1)} %copy-done.12, bf16[256,512]{1,0:T(8,128)(2,1)} %copy-done.13, ...), custom_call_target="tpu_custom_call" | custom-call | bytes 4194304 | tf_op jit(solution)/shard_map/pallas_call | solution.py:646
  134.7 28.7 %all_to_all.26.both_ref = bf16[64,80,128]{2,1,0:T(8,128)(2,1)} all-to-all(bf16[64,80,128]{2,1,0:T(8,128)(2,1)} %shard_map.98), channel_id=1, replica_groups=mesh['y'=4,'zl'=2,'zh'=2,'x'=4,'c'=2] {'y','zl','zh','x'}, dimensions={0} | all-to-all | bytes 2621440 | tf_op jit(solution)/shard_map/all_to_all | solution.py:610
  163.4 3.0 %shard_map.99 = bf16[64,128,128]{2,1,0:T(8,128)(2,1)} custom-call(bf16[64,80,128]{2,1,0:T(8,128)(2,1)} %all_to_all.26.both_ref), custom_call_target="tpu_custom_call" | custom-call | bytes 3145728 | tf_op jit(solution)/shard_map/pallas_call | solution.py:648
  166.4 32.4 %all_to_all.27.chunks_ref = bf16[64,128,128]{2,1,0:T(8,128)(2,1)S(1)} all-to-all(bf16[64,128,128]{2,1,0:T(8,128)(2,1)} %shard_map.99), channel_id=1, replica_groups=mesh['y'=4,'zl'=2,'zh'=2,'x'=4,'c'=2] {'y','zl','zh','x'}, dimensions={0} | all-to-all | bytes 4194304 | tf_op jit(solution)/shard_map/all_to_all | solution.py:610
  198.9 3.2 %collective-permute-start.18 = (bf16[64,128,128]{2,1,0:T(8,128)(2,1)S(1)}, bf16[64,128,128]{2,1,0:T(8,128)(2,1)}, u32[]{:S(2)}, u32[]{:S(2)}) collective-permute-start(bf16[64,128,128]{2,1,0:T(8,128)(2,1)S(1)} %all_to_all.27.chunks_ref), channel_id=1, source_target_pairs={{0,1},{1,0},{2,3},{3,2},{4,5},{5,4},{6,7},{7,6},{8,9},{9,8},{10,11... | collective-permute-start | bytes 6291464 | tf_op jit(solution)/shard_map/ppermute | solution.py:621
  202.1 5.2 %shard_map.93 = (bf16[2,2,2,16,512]{4,3,2,1,0:T(8,128)(2,1)}, bf16[2,2,2,16,512]{4,3,2,1,0:T(8,128)(2,1)}, bf16[2,2,2,16,512]{4,3,2,1,0:T(8,128)(2,1)}, bf16[2,2,2,16,512]{4,3,2,1,0:T(8,128)(2,1)}) custom-call(s32[5]{0:T(128)} %stack.23.where_ref, bf16[16,2,16,512]{3,2,1,0:T(8,128)(2,1)} %all_to_all.25.x_ref, ...), custom_call_target="tpu_custom_call" | custom-call | flops 805306368 | bytes 5242880 | tf_op jit(solution)/shard_map/pallas_call | solution.py:650
  207.3 2.2 collective-permute-start.9
  209.5 1.2 collective-permute-start.10
  210.7 2.9 %collective-permute-done.8.refs_1_ = bf16[2,2,2,16,512]{4,3,2,1,0:T(8,128)(2,1)S(1)} collective-permute-done((bf16[2,2,2,16,512]{4,3,2,1,0:T(8,128)(2,1)}, bf16[2,2,2,16,512]{4,3,2,1,0:T(8,128)(2,1)S(1)}, u32[]{:S(2)}, u32[]{:S(2)}) %collective-permute-start.8) | collective-permute-done | bytes 131104 | tf_op jit(solution)/shard_map/ppermute | solution.py:616
  213.6 1.7 collective-permute-done.9.refs_2_
  215.4 0.8 collective-permute-done.10.refs_3_
  216.2 0.7 copy-done.4
  216.9 1.8 shard_map.94
  218.7 1.5 collective-permute-start.11
  220.2 1.4 collective-permute-start.5
  221.6 1.3 collective-permute-start.6
  223.0 4.3 %collective-permute-done.4.refs_1_ = bf16[2,2,32,512]{3,2,1,0:T(8,128)(2,1)S(1)} collective-permute-done((bf16[2,2,32,512]{3,2,1,0:T(8,128)(2,1)S(1)}, bf16[2,2,32,512]{3,2,1,0:T(8,128)(2,1)S(1)}, u32[]{:S(2)}, u32[]{:S(2)}) %collective-permute-start.4) | collective-permute-done | bytes 131104 | tf_op jit(solution)/shard_map/ppermute | solution.py:616
  227.3 0.4 collective-permute-done.6.refs_3_
  227.6 0.3 copy-done.9
  228.0 0.3 copy-done.11
  228.3 1.8 shard_map.89
  230.2 0.7 copy-done.7
  230.9 1.9 shard_map.95
  232.9 3.5 %collective-permute-start.12 = (bf16[2,4,2,16,512]{4,3,2,1,0:T(8,128)(2,1)}, bf16[2,4,2,16,512]{4,3,2,1,0:T(8,128)(2,1)S(1)}, u32[]{:S(2)}, u32[]{:S(2)}) collective-permute-start(bf16[2,4,2,16,512]{4,3,2,1,0:T(8,128)(2,1)} %shard_map.95), channel_id=1, source_target_pairs={{0,1},{1,0},{2,3},{3,2},{4,5},{5,4},{6,7},{7,6},{8,9},{9,8},{10,11... | collective-permute-start | bytes 786440 | tf_op jit(solution)/shard_map/ppermute | solution.py:621
  236.3 0.7 copy-done.15
  237.0 2.9 %shard_map.90 = bf16[32,16,512]{2,1,0:T(8,128)(2,1)} custom-call(s32[5]{0:T(128)} %stack.23.where_ref, bf16[2,2,32,512]{3,2,1,0:T(8,128)(2,1)} %get-tuple-element.46.refs_0_, bf16[2,2,32,512]{3,2,1,0:T(8,128)(2,1)} %copy-done.9, bf16[2,2,32,512]{3,2,1,0:T(8,128)(2,1)} %copy-done.10, bf16[2,2,32,512]{3,2,1,0:T(8,128)(2,1)} %copy-done.11, ...), custom_call_target="tpu_custom_call" | custom-call | bytes 1048576 | tf_op jit(solution)/shard_map/pallas_call | solution.py:660
  240.0 0.7 copy-done.16
  240.7 2.1 shard_map.96
  242.8 4.9 %widen.2 = (f32[2,1024,512]{2,1,0:T(8,128)}, f32[2,4,256,512]{3,2,1,0:T(8,128)}) custom-call(s32[5]{0:T(128)} %stack.23.where_ref, bf16[64,128,128]{2,1,0:T(8,128)(2,1)} %copy-done), custom_call_target="tpu_custom_call" | custom-call | bytes 6291456 | tf_op jit(solution)/shard_map/widen/pallas_call | solution.py:592
  247.7 4.9 %widen.3 = (f32[2,1024,512]{2,1,0:T(8,128)}, f32[2,4,256,512]{3,2,1,0:T(8,128)}) custom-call(s32[5]{0:T(128)} %stack.23.where_ref, bf16[64,128,128]{2,1,0:T(8,128)(2,1)} %collective-permute-done.18.chunks_ref, f32[2,1024,512]{2,1,0:T(8,128)} %get-tuple-element.68.refs_0_, ...), custom_call_target="tpu_custom_call", output_to_operand_aliasing={{0}: (2, {}), {1}: (3, {})} | custom-call | bytes 6291456 | tf_op jit(solution)/shard_map/widen/pallas_call | solution.py:592
  (48 shorter events, 0.3 us)
Async XLA Ops:
  29.4 31.4 %all-to-all-start.1 = ((bf16[128,16,128]{2,1,0:T(8,128)(2,1)}), bf16[128,16,128]{2,1,0:T(8,128)(2,1)S(1)}, u32[]{:S(2)}, u32[]{:S(2)}) async-start(bf16[128,16,128]{2,1,0:T(8,128)(2,1)} %get-tuple-element.38), calls=%async_computation.1 | async-start | bytes 1048576 | tf_op jit(solution)/shard_map/all_to_all | solution.py:610
  38.4 9.0 %collective-permute-start = (bf16[2,2,32,512]{3,2,1,0:T(8,128)(2,1)}, bf16[2,2,32,512]{3,2,1,0:T(8,128)(2,1)S(1)}, u32[]{:S(2)}, u32[]{:S(2)}) collective-permute-start(bf16[2,2,32,512]{3,2,1,0:T(8,128)(2,1)} %get-tuple-element.40), channel_id=1, source_target_pairs={{0,32},{32,64},{64,96},{96,0},{1,33},{33,65},{65,97},{97,1},{2,34}... | collective-permute-start | bytes 393224 | tf_op jit(solution)/shard_map/ppermute | solution.py:616
  39.8 11.1 %collective-permute-start.1 = (bf16[2,2,32,512]{3,2,1,0:T(8,128)(2,1)}, bf16[2,2,32,512]{3,2,1,0:T(8,128)(2,1)S(1)}, u32[]{:S(2)}, u32[]{:S(2)}) collective-permute-start(bf16[2,2,32,512]{3,2,1,0:T(8,128)(2,1)} %get-tuple-element.41), channel_id=1, source_target_pairs={{0,64},{32,96},{64,0},{96,32},{1,65},{33,97},{65,1},{97,33},{2,66}... | collective-permute-start | bytes 393224 | tf_op jit(solution)/shard_map/ppermute | solution.py:616
  42.2 8.6 %collective-permute-start.2 = (bf16[2,2,32,512]{3,2,1,0:T(8,128)(2,1)}, bf16[2,2,32,512]{3,2,1,0:T(8,128)(2,1)S(1)}, u32[]{:S(2)}, u32[]{:S(2)}) collective-permute-start(bf16[2,2,32,512]{3,2,1,0:T(8,128)(2,1)} %get-tuple-element.42), channel_id=1, source_target_pairs={{0,96},{32,0},{64,32},{96,64},{1,97},{33,1},{65,33},{97,65},{2,98}... | collective-permute-start | bytes 393224 | tf_op jit(solution)/shard_map/ppermute | solution.py:616
  47.4 3.4 %copy-start.17 = (bf16[2,2,32,512]{3,2,1,0:T(8,128)(2,1)}, bf16[2,2,32,512]{3,2,1,0:T(8,128)(2,1)S(1)}, u32[]{:S(2)}) copy-start(bf16[2,2,32,512]{3,2,1,0:T(8,128)(2,1)S(1)} %collective-permute-done.refs_1_) | copy-start | bytes 393220
  50.8 0.7 copy-start.18
  50.8 0.7 copy-start.19
  53.4 7.4 %collective-permute-start.3 = (bf16[4,2,32,512]{3,2,1,0:T(8,128)(2,1)}, bf16[4,2,32,512]{3,2,1,0:T(8,128)(2,1)S(1)}, u32[]{:S(2)}, u32[]{:S(2)}) collective-permute-start(bf16[4,2,32,512]{3,2,1,0:T(8,128)(2,1)} %shard_map.86), channel_id=1, source_target_pairs={{0,16},{16,0},{1,17},{17,1},{2,18},{18,2},{3,19},{19,3},{4,20},{20... | collective-permute-start | bytes 786440 | tf_op jit(solution)/shard_map/ppermute | solution.py:621
  60.8 0.7 copy-start.20
  61.5 0.8 copy-start.8
  76.7 20.8 %all-to-all-start.2 = ((bf16[128,16,128]{2,1,0:T(8,128)(2,1)}), bf16[128,16,128]{2,1,0:T(8,128)(2,1)S(1)}, u32[]{:S(2)}, u32[]{:S(2)}) async-start(bf16[128,16,128]{2,1,0:T(8,128)(2,1)} %get-tuple-element.50), calls=%async_computation.2 | async-start | bytes 1048576 | tf_op jit(solution)/shard_map/all_to_all | solution.py:610
  90.0 21.0 %collective-permute-start.14 = (bf16[2,512,512]{2,1,0:T(8,128)(2,1)}, bf16[2,512,512]{2,1,0:T(8,128)(2,1)S(1)}, u32[]{:S(2)}, u32[]{:S(2)}) collective-permute-start(bf16[2,512,512]{2,1,0:T(8,128)(2,1)} %get-tuple-element.63), channel_id=1, source_target_pairs={{0,1},{1,0},{2,3},{3,2},{4,5},{5,4},{6,7},{7,6},{8,9},{9,8},{10,11... | collective-permute-start | bytes 3145736 | tf_op jit(solution)/shard_map/ppermute | solution.py:621
  97.5 0.8 copy-start.1
  109.5 20.8 %collective-permute-start.13 = (bf16[2,512,512]{2,1,0:T(8,128)(2,1)}, bf16[2,512,512]{2,1,0:T(8,128)(2,1)S(1)}, u32[]{:S(2)}, u32[]{:S(2)}) collective-permute-start(bf16[2,512,512]{2,1,0:T(8,128)(2,1)} %get-tuple-element.61), channel_id=1, source_target_pairs={{0,1},{1,0},{2,3},{3,2},{4,5},{5,4},{6,7},{7,6},{8,9},{9,8},{10,11... | collective-permute-start | bytes 3145736 | tf_op jit(solution)/shard_map/ppermute | solution.py:621
  111.0 1.0 copy-start.6
  115.1 9.7 %collective-permute-start.15 = (bf16[256,512]{1,0:T(8,128)(2,1)}, bf16[256,512]{1,0:T(8,128)(2,1)S(1)}, u32[]{:S(2)}, u32[]{:S(2)}) collective-permute-start(bf16[256,512]{1,0:T(8,128)(2,1)} %get-tuple-element.65), channel_id=1, source_target_pairs={{0,2},{2,4},{4,6},{6,0},{1,3},{3,5},{5,7},{7,1},{8,10},{10,12},{12... | collective-permute-start | bytes 786440 | tf_op jit(solution)/shard_map/ppermute | solution.py:616
  115.4 14.1 %collective-permute-start.16 = (bf16[256,512]{1,0:T(8,128)(2,1)}, bf16[256,512]{1,0:T(8,128)(2,1)S(1)}, u32[]{:S(2)}, u32[]{:S(2)}) collective-permute-start(bf16[256,512]{1,0:T(8,128)(2,1)} %get-tuple-element.66), channel_id=1, source_target_pairs={{0,4},{2,6},{4,0},{6,2},{1,5},{3,7},{5,1},{7,3},{8,12},{10,14},{12... | collective-permute-start | bytes 786440 | tf_op jit(solution)/shard_map/ppermute | solution.py:616
  117.3 13.0 %collective-permute-start.17 = (bf16[256,512]{1,0:T(8,128)(2,1)}, bf16[256,512]{1,0:T(8,128)(2,1)S(1)}, u32[]{:S(2)}, u32[]{:S(2)}) collective-permute-start(bf16[256,512]{1,0:T(8,128)(2,1)} %get-tuple-element.67), channel_id=1, source_target_pairs={{0,6},{2,0},{4,2},{6,4},{1,7},{3,1},{5,3},{7,5},{8,14},{10,8},{12,... | collective-permute-start | bytes 786440 | tf_op jit(solution)/shard_map/ppermute | solution.py:616
  124.8 5.5 %copy-start.12 = (bf16[256,512]{1,0:T(8,128)(2,1)}, bf16[256,512]{1,0:T(8,128)(2,1)S(1)}, u32[]{:S(2)}) copy-start(bf16[256,512]{1,0:T(8,128)(2,1)S(1)} %collective-permute-done.15.refs_1_) | copy-start | bytes 786436
  129.5 0.8 copy-start.13
  130.3 0.7 copy-start.14
  130.3 1.1 copy-start.5
  198.9 8.4 %copy-start = (bf16[64,128,128]{2,1,0:T(8,128)(2,1)}, bf16[64,128,128]{2,1,0:T(8,128)(2,1)S(1)}, u32[]{:S(2)}) copy-start(bf16[64,128,128]{2,1,0:T(8,128)(2,1)S(1)} %all_to_all.27.chunks_ref) | copy-start | bytes 6291460
  198.9 48.9 %collective-permute-start.18 = (bf16[64,128,128]{2,1,0:T(8,128)(2,1)S(1)}, bf16[64,128,128]{2,1,0:T(8,128)(2,1)}, u32[]{:S(2)}, u32[]{:S(2)}) collective-permute-start(bf16[64,128,128]{2,1,0:T(8,128)(2,1)S(1)} %all_to_all.27.chunks_ref), channel_id=1, source_target_pairs={{0,1},{1,0},{2,3},{3,2},{4,5},{5,4},{6,7},{7,6},{8,9},{9,8},{10,11... | collective-permute-start | bytes 6291464 | tf_op jit(solution)/shard_map/ppermute | solution.py:621
  202.1 18.1 %copy-start.23 = (bf16[2,2,32,512]{3,2,1,0:T(8,128)(2,1)S(1)}, bf16[2,2,32,512]{3,2,1,0:T(8,128)(2,1)}, u32[]{:S(2)}) copy-start(bf16[2,2,32,512]{3,2,1,0:T(8,128)(2,1)} %get-tuple-element.47) | copy-start | bytes 393220
  202.1 18.1 %copy-start.22 = (bf16[2,2,32,512]{3,2,1,0:T(8,128)(2,1)S(1)}, bf16[2,2,32,512]{3,2,1,0:T(8,128)(2,1)}, u32[]{:S(2)}) copy-start(bf16[2,2,32,512]{3,2,1,0:T(8,128)(2,1)} %get-tuple-element.48) | copy-start | bytes 393220
  202.1 19.6 %copy-start.21 = (bf16[2,2,32,512]{3,2,1,0:T(8,128)(2,1)S(1)}, bf16[2,2,32,512]{3,2,1,0:T(8,128)(2,1)}, u32[]{:S(2)}) copy-start(bf16[2,2,32,512]{3,2,1,0:T(8,128)(2,1)} %get-tuple-element.49) | copy-start | bytes 393220
  207.3 6.4 %collective-permute-start.8 = (bf16[2,2,2,16,512]{4,3,2,1,0:T(8,128)(2,1)}, bf16[2,2,2,16,512]{4,3,2,1,0:T(8,128)(2,1)S(1)}, u32[]{:S(2)}, u32[]{:S(2)}) collective-permute-start(bf16[2,2,2,16,512]{4,3,2,1,0:T(8,128)(2,1)} %get-tuple-element.57), channel_id=1, source_target_pairs={{0,2},{2,4},{4,6},{6,0},{1,3},{3,5},{5,7},{7,1},{8,10},{10,12},{12... | collective-permute-start | bytes 393224 | tf_op jit(solution)/shard_map/ppermute | solution.py:616
  207.3 8.0 %collective-permute-start.9 = (bf16[2,2,2,16,512]{4,3,2,1,0:T(8,128)(2,1)}, bf16[2,2,2,16,512]{4,3,2,1,0:T(8,128)(2,1)S(1)}, u32[]{:S(2)}, u32[]{:S(2)}) collective-permute-start(bf16[2,2,2,16,512]{4,3,2,1,0:T(8,128)(2,1)} %get-tuple-element.58), channel_id=1, source_target_pairs={{0,4},{2,6},{4,0},{6,2},{1,5},{3,7},{5,1},{7,3},{8,12},{10,14},{12... | collective-permute-start | bytes 393224 | tf_op jit(solution)/shard_map/ppermute | solution.py:616
  209.5 6.6 %collective-permute-start.10 = (bf16[2,2,2,16,512]{4,3,2,1,0:T(8,128)(2,1)}, bf16[2,2,2,16,512]{4,3,2,1,0:T(8,128)(2,1)S(1)}, u32[]{:S(2)}, u32[]{:S(2)}) collective-permute-start(bf16[2,2,2,16,512]{4,3,2,1,0:T(8,128)(2,1)} %get-tuple-element.59), channel_id=1, source_target_pairs={{0,6},{2,0},{4,2},{6,4},{1,7},{3,1},{5,3},{7,5},{8,14},{10,8},{12,... | collective-permute-start | bytes 393224 | tf_op jit(solution)/shard_map/ppermute | solution.py:616
  213.6 2.5 %copy-start.2 = (bf16[2,2,2,16,512]{4,3,2,1,0:T(8,128)(2,1)}, bf16[2,2,2,16,512]{4,3,2,1,0:T(8,128)(2,1)S(1)}, u32[]{:S(2)}) copy-start(bf16[2,2,2,16,512]{4,3,2,1,0:T(8,128)(2,1)S(1)} %collective-permute-done.8.refs_1_) | copy-start | bytes 393220
  215.4 0.8 copy-start.3
  216.2 0.7 copy-start.4
  218.7 11.5 %collective-permute-start.11 = (bf16[4,2,2,16,512]{4,3,2,1,0:T(8,128)(2,1)}, bf16[4,2,2,16,512]{4,3,2,1,0:T(8,128)(2,1)S(1)}, u32[]{:S(2)}, u32[]{:S(2)}) collective-permute-start(bf16[4,2,2,16,512]{4,3,2,1,0:T(8,128)(2,1)} %shard_map.94), channel_id=1, source_target_pairs={{0,8},{8,0},{1,9},{9,1},{2,10},{10,2},{3,11},{11,3},{4,12},{12,4},... | collective-permute-start | bytes 786440 | tf_op jit(solution)/shard_map/ppermute | solution.py:621
  220.2 7.1 %collective-permute-start.4 = (bf16[2,2,32,512]{3,2,1,0:T(8,128)(2,1)S(1)}, bf16[2,2,32,512]{3,2,1,0:T(8,128)(2,1)S(1)}, u32[]{:S(2)}, u32[]{:S(2)}) collective-permute-start(bf16[2,2,32,512]{3,2,1,0:T(8,128)(2,1)S(1)} %copy-done.23), channel_id=1, source_target_pairs={{0,32},{32,64},{64,96},{96,0},{1,33},{33,65},{65,97},{97,1},{2,34}... | collective-permute-start | bytes 393224 | tf_op jit(solution)/shard_map/ppermute | solution.py:616
  220.2 7.1 %collective-permute-start.5 = (bf16[2,2,32,512]{3,2,1,0:T(8,128)(2,1)S(1)}, bf16[2,2,32,512]{3,2,1,0:T(8,128)(2,1)S(1)}, u32[]{:S(2)}, u32[]{:S(2)}) collective-permute-start(bf16[2,2,32,512]{3,2,1,0:T(8,128)(2,1)S(1)} %copy-done.22), channel_id=1, source_target_pairs={{0,64},{32,96},{64,0},{96,32},{1,65},{33,97},{65,1},{97,33},{2,66}... | collective-permute-start | bytes 393224 | tf_op jit(solution)/shard_map/ppermute | solution.py:616
  221.6 6.0 %collective-permute-start.6 = (bf16[2,2,32,512]{3,2,1,0:T(8,128)(2,1)S(1)}, bf16[2,2,32,512]{3,2,1,0:T(8,128)(2,1)S(1)}, u32[]{:S(2)}, u32[]{:S(2)}) collective-permute-start(bf16[2,2,32,512]{3,2,1,0:T(8,128)(2,1)S(1)} %copy-done.21), channel_id=1, source_target_pairs={{0,96},{32,0},{64,32},{96,64},{1,97},{33,1},{65,33},{97,65},{2,98}... | collective-permute-start | bytes 393224 | tf_op jit(solution)/shard_map/ppermute | solution.py:616
  227.3 0.7 copy-start.9
  227.3 0.7 copy-start.10
  227.6 0.7 copy-start.11
  230.1 6.2 %collective-permute-start.7 = (bf16[4,2,32,512]{3,2,1,0:T(8,128)(2,1)}, bf16[4,2,32,512]{3,2,1,0:T(8,128)(2,1)S(1)}, u32[]{:S(2)}, u32[]{:S(2)}) collective-permute-start(bf16[4,2,32,512]{3,2,1,0:T(8,128)(2,1)} %shard_map.89), channel_id=1, source_target_pairs={{0,16},{16,0},{1,17},{17,1},{2,18},{18,2},{3,19},{19,3},{4,20},{20... | collective-permute-start | bytes 786440 | tf_op jit(solution)/shard_map/ppermute | solution.py:621
  230.2 0.7 copy-start.7
  232.9 7.1 %collective-permute-start.12 = (bf16[2,4,2,16,512]{4,3,2,1,0:T(8,128)(2,1)}, bf16[2,4,2,16,512]{4,3,2,1,0:T(8,128)(2,1)S(1)}, u32[]{:S(2)}, u32[]{:S(2)}) collective-permute-start(bf16[2,4,2,16,512]{4,3,2,1,0:T(8,128)(2,1)} %shard_map.95), channel_id=1, source_target_pairs={{0,1},{1,0},{2,3},{3,2},{4,5},{5,4},{6,7},{7,6},{8,9},{9,8},{10,11... | collective-permute-start | bytes 786440 | tf_op jit(solution)/shard_map/ppermute | solution.py:621
  236.3 0.7 copy-start.15
  240.0 0.7 copy-start.16

commit v2 on v1

--- a/solution.py
+++ b/solution.py
@@ -1,3 +1,5 @@
+import functools
+
 import jax
 import jax.numpy as jnp
 from jax import lax
@@ -159,7 +161,8 @@
 
 def row_prepare_kernel(qkv_ref, left_ref, probs_ref, turned_ref):
     def visit(rows, lanes, at, pair):
-        probs_ref[at] = softmax(qkv_ref[0, rows, lanes], qkv_ref[1, rows, lanes])
+        probs = softmax(qkv_ref[0, rows, lanes], qkv_ref[1, rows, lanes])
+        probs_ref[at] = probs.astype(BF16)
 
     each_pair(visit)
     for which in range(2):
@@ -170,6 +173,7 @@
     q_pair, k_pair, v_pair = (qkv[i, rows, lanes] for i in range(3))
     da_pair = da_ref[rows, lanes]
     low = probs.astype(BF16)
+    probs = probs.astype(F32)
     grad_probs = dot_nt(stack_halves(da_pair), v_pair)
     total = jnp.sum(probs * grad_probs, axis=-1, keepdims=True)
     grads = (probs * (grad_probs - total)).astype(BF16)
@@ -248,7 +252,7 @@
 
 
 def row_input_gradient_kernel(where_ref, x_ref, right_ref, w_ref, *refs):
-    outs, w_s, sems, gin_s = refs[:4], refs[4], refs[5], refs[6]
+    outs, w_s, sems, gin_s = refs[:8], refs[8], refs[9], refs[10]
     copies = copies_of(w_ref, w_s, sems, 3)
     start_all(copies)
     wait_all(copies)
@@ -256,9 +260,10 @@
         rows = slice(rr * LINE, (rr + 1) * LINE)
         u = x_ref[:, rr].astype(F32).reshape(LINE, D)
         grad_in = input_gradient(u, right_ref, w_s, rows)
-        gin_s[:, :, :, rr] = grad_in.astype(BF16).reshape(2, 4, 2, 16, D)
-    for shift in range(4):
-        outs[shift][...] = gin_s[:, lax.rem(where_ref[3] + shift, 4)]
+        gin_s[:, :, rr] = grad_in.astype(BF16).reshape(8, 2, 16, D)
+    chip = where_ref[2] * 4 + where_ref[3]
+    for shift in range(8):
+        outs[shift][...] = gin_s[lax.rem(chip + shift, 8)]
 
 
 def col_kernel(where_ref, keep_heads_ref, m_ref, w_ref, *refs):
@@ -272,17 +277,6 @@
         weights[i].start()
     lefts = copies_of(left_s, left_ref, left_sem, 2)
     rights = copies_of(right_s, right_ref, right_sem, 4)
-    for shift in range(4):
-        source = lax.rem(where_ref[0] + (4 - shift), 4) * 2
-        for grid_row, piece in ((source + mine, parts[shift].at[mine]), (source + (1 - mine), got_ref.at[shift])):
-            for cc in range(2):
-                for rr in range(2):
-                    at = pl.multiple_of(grid_row * 16 + (cc * LINE + rr * 128), 16)
-                    right_s[3, pl.ds(at, 16), :] = piece[cc, rr * 16 : (rr + 1) * 16, :]
-    rights[3].start()
-    weights[3].wait()
-    gain = gain_row(keep_heads_ref, 1, 0, HEADS)
-    da_s[...] = (dot_nt(right_s[3], w_s[3]) * gain).astype(BF16)
     mix_s[...] = m_ref[...].astype(F32).reshape(N_DEV * 16, 128)
     for cc in range(2):
         for rr in range(2):
@@ -299,6 +293,17 @@
     kept_u.start()
     left_s[0] = (u * inverse_rms(u)).astype(BF16)
     lefts[0].start()
+    for shift in range(4):
+        source = lax.rem(where_ref[0] + (4 - shift), 4) * 2
+        for grid_row, piece in ((source + mine, parts[shift].at[mine]), (source + (1 - mine), got_ref.at[shift])):
+            for cc in range(2):
+                for rr in range(2):
+                    at = pl.multiple_of(grid_row * 16 + (cc * LINE + rr * 128), 16)
+                    right_s[3, pl.ds(at, 16), :] = piece[cc, rr * 16 : (rr + 1) * 16, :]
+    rights[3].start()
+    weights[3].wait()
+    gain = gain_row(keep_heads_ref, 1, 0, HEADS)
+    da_s[...] = (dot_nt(right_s[3], w_s[3]) * gain).astype(BF16)
     project(left_s[0], qkv_s, w_s, weights)
 
     def visit(rows, lanes, at, pair):
@@ -325,24 +330,37 @@
 
 
 def col_output_kernel(where_ref, left_ref, right_ref, u_ref, w_ref, *refs):
-    keep_ref, send_ref, outs = refs[0], refs[1], refs[2:6]
-    turned_s, out_s, wo_s, sem = refs[6:]
+    keep_ref, send_ref, outs = refs[0], refs[1], refs[2:10]
+    left_s, right_s, ulow_s, wo_s, turned_s, out_s, keep_s, send_s = refs[10:18]
+    left_sem, right_sem, one_sem, half_sem = refs[18:]
+    lefts = copies_of(left_ref, left_s, left_sem, 2)
+    rights = copies_of(right_ref, right_s, right_sem, 4)
+    others = [
+        pltpu.make_async_copy(w_ref.at[3], wo_s, one_sem.at[0]),
+        pltpu.make_async_copy(u_ref, ulow_s, one_sem.at[1]),
+    ]
+    start_all(lefts + rights + others)
     core = where_ref[4]
-    copy = pltpu.make_async_copy(w_ref.at[3], wo_s, sem)
-    copy.start()
     for which in range(2):
-        turned_s[which] = left_ref[which].T
-    weight_gradients(1 - core, turned_s, right_ref, send_ref)
-    weight_gradients(core, turned_s, right_ref, keep_ref)
-    copy.wait()
-    out_s[...] = (u_ref[...].astype(F32) + dot(left_ref[1], wo_s[...])).astype(BF16)
-    for shift in range(4):
-        for low in range(2):
-            start = lax.rem(where_ref[0] + shift, 4) * 32 + low * 16
-            for cc in range(2):
-                for rr in range(2):
-                    at = pl.multiple_of(start + (cc * LINE + rr * 128), 16)
-                    outs[shift][low, cc, rr * 16 : (rr + 1) * 16, :] = out_s[pl.ds(at, 16), :]
+        lefts[which].wait()
+        turned_s[which] = left_s[which].T
+    wait_all(rights)
+    weight_gradients(1 - core, turned_s, right_s, send_s)
+    sent = pltpu.make_async_copy(send_s, send_ref, half_sem.at[0])
+    sent.start()
+    weight_gradients(core, turned_s, right_s, keep_s)
+    kept = pltpu.make_async_copy(keep_s, keep_ref, half_sem.at[1])
+    kept.start()
+    wait_all(others)
+    out_s[...] = (ulow_s[...].astype(F32) + dot(left_s[1], wo_s[...])).astype(BF16)
+    me = where_ref[0] * 2 + where_ref[1]
+    for shift in range(8):
+        start = lax.rem(me + shift, 8) * 16
+        for cc in range(2):
+            for rr in range(2):
+                at = pl.multiple_of(start + (cc * LINE + rr * 128), 16)
+                outs[shift][cc, rr * 16 : (rr + 1) * 16, :] = out_s[pl.ds(at, 16), :]
+    wait_all([sent, kept])
 
 
 def tile_to_lines_kernel(where_ref, tile_ref, *refs):
@@ -367,43 +385,32 @@
 
 
 def lines_to_tile_kernel(where_ref, *refs):
-    parts, got_ref, tile_ref, mix_s = refs[:4], refs[4], refs[5], refs[6]
-    mine = where_ref[1]
+    parts, tile_ref, mix_s = refs[:8], refs[8], refs[9]
+    me = where_ref[0] * 2 + where_ref[1]
     for group in range(4):
         lanes = slice(group * 128, (group + 1) * 128)
-        for shift in range(4):
-            source = lax.rem(where_ref[0] + (4 - shift), 4) * 2
-            for peer, piece in ((source + mine, parts[shift].at[mine]), (source + (1 - mine), got_ref.at[shift])):
-                for cc in range(2):
-                    for rr in range(2):
-                        value = piece[cc, rr * 16 : (rr + 1) * 16, lanes].astype(F32)
-                        mix_s[group, pl.ds(peer + (rr * 16 + cc * 8), 16, stride=32), :] = value
+        for shift in range(8):
+            peer = lax.rem(me + (8 - shift), 8)
+            for cc in range(2):
+                for rr in range(2):
+                    piece = parts[shift][cc, rr * 16 : (rr + 1) * 16, lanes].astype(F32)
+                    mix_s[group, pl.ds(peer + (rr * 16 + cc * 8), 16, stride=32), :] = piece
         tile_ref[:, :, lanes] = mix_s[group].astype(BF16).reshape(32, 16, 128)
 
 
-def pass_high_kernel(where_ref, *refs):
-    parts, pass_ref = refs[:4], refs[4]
-    for shift in range(4):
-        pass_ref[shift] = parts[shift][1 - where_ref[2]]
-
-
 def pass_core_kernel(where_ref, *refs):
-    parts, got_ref, pass_ref = refs[:4], refs[4], refs[5]
-    high, other = where_ref[2], 1 - where_ref[4]
-    for shift in range(4):
-        pass_ref[0, shift] = parts[shift][high, other]
-        pass_ref[1, shift] = got_ref[shift, other]
+    parts, pass_ref = refs[:8], refs[8]
+    for shift in range(8):
+        pass_ref[shift] = parts[shift][1 - where_ref[4]]
 
 
 def join_kernel(where_ref, *refs):
-    parts, got_ref, passed_ref, tile_ref = refs[:4], refs[4], refs[5], refs[6]
-    high, core = where_ref[2], where_ref[4]
-    for shift in range(4):
-        source = lax.rem(where_ref[3] + (4 - shift), 4)
-        tile_ref[high, source, core] = parts[shift][high, core]
-        tile_ref[1 - high, source, core] = got_ref[shift, core]
-        tile_ref[high, source, 1 - core] = passed_ref[0, shift]
-        tile_ref[1 - high, source, 1 - core] = passed_ref[1, shift]
+    parts, passed_ref, tile_ref = refs[:8], refs[8], refs[9]
+    chip, core = where_ref[2] * 4 + where_ref[3], where_ref[4]
+    for shift in range(8):
+        source = lax.rem(chip + (8 - shift), 8)
+        tile_ref[source, core] = parts[shift][core]
+        tile_ref[source, 1 - core] = passed_ref[shift]
 
 
 def pair_sum_kernel(where_ref, keep_ref, got_ref, *refs):
@@ -445,18 +452,33 @@
         spread_ref[:, first : first + 16, :] = jnp.broadcast_to(part[None], (64, 16, 128))
 
 
-def widen_kernel(where_ref, chunks_ref, *refs):
-    row_ref, col_ref = refs[-2:]
-    for group in range(4):
-        lanes = slice(group * 128, (group + 1) * 128)
-        piece = chunks_ref[:, group * 16 : (group + 1) * 16, :].astype(F32)
-        row_ref[0, :, lanes] = piece.reshape(256, 128)
-        for quarter in range(4):
-            for block in range(4):
-                first = 64 + quarter * 16
-                col_ref[0, quarter, block * 16 : (block + 1) * 16, lanes] = chunks_ref[
-                    block * 4 + group, first : first + 16, :
-                ].astype(F32)
+def widen_kernel(side, where_ref, chunks_ref, *refs):
+    row_ref, col_ref, row_s, col_s, row_sem, col_sem = refs[-6:]
+    half = where_ref[4] if side == 0 else 1 - where_ref[4]
+    copies = []
+    for part in range(4):
+        chunks = slice(part * 16, (part + 1) * 16)
+        for group in range(4):
+            lanes = slice(group * 128, (group + 1) * 128)
+            piece = chunks_ref[chunks, group * 16 : (group + 1) * 16, :].astype(F32)
+            row_s[part, :, lanes] = piece.reshape(256, 128)
+        rows = pl.ds(part * 256, 256)
+        copies.append(
+            pltpu.make_async_copy(row_s.at[part], row_ref.at[half, rows], row_sem.at[part])
+        )
+        copies[-1].start()
+    for quarter in range(4):
+        first = 64 + quarter * 16
+        for block in range(16):
+            for group in range(4):
+                col_s[quarter, block * 16 : (block + 1) * 16, group * 128 : (group + 1) * 128] = (
+                    chunks_ref[block * 4 + group, first : first + 16, :].astype(F32)
+                )
+        copies.append(
+            pltpu.make_async_copy(col_s.at[quarter], col_ref.at[half, quarter], col_sem.at[quarter])
+        )
+        copies[-1].start()
+    wait_all(copies)
 
 
 MIB = 1 << 20
@@ -465,11 +487,10 @@
 HBM = pl.BlockSpec(memory_space=pltpu.HBM)
 
 
-GRANT = 60 * 1024 * 1024
 SPACE = {"s": SMEM, "v": VMEM, "h": HBM}
 
 
-def call(kernel, ins, out_kinds, outs, scratch, flops, moved):
+def call(kernel, ins, out_kinds, outs, scratch, flops, moved, grant=16):
     spaces = tuple(SPACE[kind] for kind in out_kinds)
     return pl.pallas_call(
         kernel,
@@ -477,7 +498,7 @@
         out_specs=spaces if isinstance(outs, tuple) else spaces[0],
         out_shape=outs,
         scratch_shapes=scratch,
-        compiler_params=pltpu.CompilerParams(vmem_limit_bytes=GRANT),
+        compiler_params=pltpu.CompilerParams(vmem_limit_bytes=grant * MIB),
         cost_estimate=pl.CostEstimate(flops=flops, bytes_accessed=moved, transcendentals=0),
     )
 
@@ -493,6 +514,7 @@
 DMA = pltpu.SemaphoreType.DMA
 WEIGHTS = [pltpu.VMEM((4, D, D), BF16), DMA((4,))]
 WEIGHT = [pltpu.VMEM((D, D), BF16), DMA]
+LINES = shape(2, 32, D)
 PIECE = shape(2, 2, 32, D)
 PASS = shape(4, 2, 32, D)
 QUARTER = shape(256, D)
@@ -515,15 +537,10 @@
     ],
     4 * MATMUL + 2 * ATTEND,
     6 * MIB,
+    grant=50,
 )
 row_prepare = call(
-    row_prepare_kernel,
-    "vv",
-    "vv",
-    (shape(8, TOK, LINE, dtype=F32), shape(2, D, TOK)),
-    [],
-    ATTEND,
-    8 * MIB,
+    row_prepare_kernel, "vv", "vv", (shape(8, TOK, LINE), shape(2, D, TOK)), [], ATTEND, 8 * MIB
 )
 row_backward = call(
     row_backward_kernel,
@@ -532,18 +549,19 @@
     (HALF, HALF, shape(4, TOK, D)),
     [
         MIX, token_scratch(), pltpu.VMEM((D, D), BF16), token_scratch(3),
-        pltpu.VMEM((2, D, TOK), BF16), pltpu.VMEM((8, TOK, LINE), F32), HALF_S, HALF_S,
+        pltpu.VMEM((2, D, TOK), BF16), pltpu.VMEM((8, TOK, LINE), BF16), HALF_S, HALF_S,
         token_scratch(4), DMA, DMA((3,)), DMA((2,)), DMA((4,)), DMA((2,)), DMA((4,)),
     ],
     5 * MATMUL + 5 * ATTEND,
     12 * MIB,
+    grant=50,
 )
 row_input_gradient = call(
     row_input_gradient_kernel,
     "svvh",
-    "v" * 4,
-    (shape(2, 2, 2, 16, D),) * 4,
-    [*WEIGHTS, pltpu.VMEM((2, 4, 2, 2, 16, D), BF16)],
+    "v" * 8,
+    (shape(2, 2, 16, D),) * 8,
+    [*WEIGHTS, pltpu.VMEM((8, 2, 2, 16, D), BF16)],
     3 * MATMUL,
     5 * MIB,
 )
@@ -558,24 +576,28 @@
     ],
     8 * MATMUL + 6 * ATTEND,
     8 * MIB,
+    grant=48,
 )
 col_output = call(
     col_output_kernel,
-    "svvvh",
-    "v" * 6,
-    (HALF, HALF) + (PIECE,) * 4,
-    [pltpu.VMEM((2, D, TOK), BF16), token_scratch(), *WEIGHT],
+    "shhhh",
+    "hh" + "v" * 8,
+    (HALF, HALF) + (LINES,) * 8,
+    [
+        token_scratch(2), token_scratch(4), token_scratch(), pltpu.VMEM((D, D), BF16),
+        pltpu.VMEM((2, D, TOK), BF16), token_scratch(), HALF_S, HALF_S,
+        DMA((2,)), DMA((4,)), DMA((2,)), DMA((2,)),
+    ],
     5 * MATMUL,
     7 * MIB,
+    grant=52,
 )
 tile_to_lines = call(tile_to_lines_kernel, "sv", "v" * 4, (PIECE,) * 4, [MIX_TILE], 0, MIB)
 pass_low = call(pass_low_kernel, "s" + "v" * 4, "v", PASS, [], 0, MIB)
-lines_to_tile = call(lines_to_tile_kernel, "s" + "v" * 5, "v", shape(32, 16, D), [MIX_TILE], 0, MIB)
-CHIP_PASS = shape(4, 2, 2, 16, D)
-CORE_PASS = shape(2, 4, 2, 16, D)
-pass_high = call(pass_high_kernel, "s" + "v" * 4, "v", CHIP_PASS, [], 0, MIB)
-pass_core = call(pass_core_kernel, "s" + "v" * 5, "v", CORE_PASS, [], 0, MIB)
-join = call(join_kernel, "s" + "v" * 6, "v", shape(2, 4, 2, 2, 16, D), [], 0, MIB)
+lines_to_tile = call(lines_to_tile_kernel, "s" + "v" * 8, "v", shape(32, 16, D), [MIX_TILE], 0, MIB)
+CORE_PASS = shape(8, 2, 16, D)
+pass_core = call(pass_core_kernel, "s" + "v" * 8, "v", CORE_PASS, [], 0, MIB)
+join = call(join_kernel, "s" + "v" * 9, "v", shape(8, 2, 2, 16, D), [], 0, MIB)
 pair_sum = call(
     pair_sum_kernel, "svv", "v" * 4, (QUARTER,) * 4, [pltpu.VMEM((4, 256, D), BF16)], 0, 3 * MIB,
 )
@@ -584,24 +606,17 @@
 
 
 def widen(where, chunks, side, *before):
-    half = lambda ref: ref[4] if side == 0 else 1 - ref[4]
-    outs = (
-        pl.BlockSpec((1, 256, D), lambda i, ref: (half(ref), i, 0)),
-        pl.BlockSpec((1, 4, 64, D), lambda i, ref: (half(ref), 0, i, 0)),
-    )
     return pl.pallas_call(
-        widen_kernel,
-        grid_spec=pltpu.PrefetchScalarGridSpec(
-            num_scalar_prefetch=1,
-            grid=(4,),
-            in_specs=[pl.BlockSpec((16, 128, 128), lambda i, ref: (i, 0, 0))]
-            + [pl.BlockSpec(memory_space=pl.ANY)] * len(before),
-            out_specs=outs,
-        ),
+        functools.partial(widen_kernel, side),
+        in_specs=[SMEM, VMEM] + [HBM] * len(before),
+        out_specs=(HBM, HBM),
         out_shape=(shape(2, 1024, D, dtype=F32), shape(2, 4, 256, D, dtype=F32)),
+        scratch_shapes=[
+            pltpu.VMEM((4, 256, D), F32), pltpu.VMEM((4, 256, D), F32), DMA((4,)), DMA((4,)),
+        ],
         input_output_aliases={2: 0, 3: 1} if before else {},
         name="widen",
-        compiler_params=pltpu.CompilerParams(vmem_limit_bytes=GRANT),
+        compiler_params=pltpu.CompilerParams(vmem_limit_bytes=16 * MIB),
         cost_estimate=pl.CostEstimate(flops=0, bytes_accessed=6 * MIB, transcendentals=0),
     )(where, chunks, *before)
 
@@ -648,16 +663,12 @@
     totals = spread(both)
     chunks = exchange(totals, CHIPS)
     gin_pieces = row_input_gradient(where, rows_in, right_row, w_row)
-    gin_parts = shifted(gin_pieces, "x")
-    gin_pass = pass_high(where, *gin_parts)
-    gin_got = swap(gin_pass, "zh")
-    gin_core = pass_core(where, *gin_parts, gin_got)
+    gin_parts = shifted(gin_pieces, ("zh", "x"))
+    gin_core = pass_core(where, *gin_parts)
     gin_core = swap(gin_core, "c")
-    grad_latents = join(where, *gin_parts, gin_got, gin_core).reshape(32, 16, D)
-    out_parts = shifted(out_pieces, "y")
-    out_pass = pass_low(where, *out_parts)
-    out_pass = swap(out_pass, "zl")
-    output = lines_to_tile(where, *out_parts, out_pass)
+    grad_latents = join(where, *gin_parts, gin_core).reshape(32, 16, D)
+    out_parts = shifted(out_pieces, ROW)
+    output = lines_to_tile(where, *out_parts)
     other = swap(chunks, "c")
     halves_done = widen(where, chunks, 0)
     grad_row, grad_col = widen(where, other, 1, *halves_done)

time: 257 us -> 244 us (0.949)
  Pallas kernels: 85.1 us -> 52.9 us
  local copies, waits for them, and re-layouts: 9.11 us -> 15.5 us
  starting transfers between devices: 40.4 us -> 46.3 us
  waiting for transfers between devices: 35.8 us -> 41.3 us
    pallas_call x7 -> x5, Pallas kernels: 20.4 us -> 9.56 us  [the longest x2 5.34 us: widen(): pl.pallas_call(functools.partial(widen_kernel, side), in_specs=[SMEM, VME...]
    ppermute x12 -> x20, starting transfers between devices: 14.2 us -> 23.1 us  [shifted(): lax.ppermute(pieces[k], axes, [(i, (i + k) % n) for i in range(n)])]
    unnamed x48 -> x64, local copies, waits for them, and re-layouts: 8.51 us -> 15.4 us
    ppermute x12 -> x20, waiting for transfers between devices: 29.7 us -> 35.3 us  [shifted(): lax.ppermute(pieces[k], axes, [(i, (i + k) % n) for i in range(n)])]
    pallas_call x1, Pallas kernels: 6.17 us -> 2.45 us  [layer(): probs_row, turned_row = row_prepare(qkv_row, left_row)]
    ppermute x7 -> x5, starting transfers between devices: 12.4 us -> 8.85 us  [swap(): return lax.ppermute(value, axis, [(0, 1), (1, 0)])]
    pallas_call x1, Pallas kernels: 5.18 us -> 1.94 us  [layer(): gin_pieces = row_input_gradient(where, rows_in, right_row, w_row)]
    pallas_call x1, Pallas kernels: 3.28 us -> 0.41 us  [layer(): merged = merge(keep_row, got_row, *quarters)]
  transfers between devices with their start and end apart: 21 -> 27, of which waited for: 11 -> 14; matrix products, arithmetic and copies ran while one was open for 0% -> 0% of each run, Pallas kernels for 20% -> 12%
where the time goes in v2:
time: 244 us; the launch traced here: 240 us
  blocking collectives  82.7 us (34%)
  Pallas kernels  52.9 us (22%)
  starting transfers between devices  46.3 us (19%)
  waiting for transfers between devices  41.3 us (17%)
  local copies, waits for them, and re-layouts  15.5 us (6%)
    all_to_all x3, blocking collectives, exchange(): return lax.all_to_all(values, axes, split_axis=0, concat_axis=0, tiled=True)  82.7 us
    ppermute x20, waiting for transfers between devices, shifted(): lax.ppermute(pieces[k], axes, [(i, (i + k) % n) for i in range(n)])  35.3 us
    ppermute x20, starting transfers between devices, shifted(): lax.ppermute(pieces[k], axes, [(i, (i + k) % n) for i in range(n)])  23.1 us
    unnamed x64, local copies, waits for them, and re-layouts  15.4 us
    all_to_all x2, starting transfers between devices, exchange(): return lax.all_to_all(values, axes, split_axis=0, concat_axis=0, tiled=True)  14.4 us
    pallas_call x1, Pallas kernels, layer(): col_grad(where, keep_heads, mid_lines, w_col, *grad_parts, grad_pass)  12.2 us
    pallas_call x1, Pallas kernels, layer(): row_backward(where, keep_heads, grad_rows, qkv_row, turned_row, probs_row...  10 us
    ppermute x5, starting transfers between devices, swap(): return lax.ppermute(value, axis, [(0, 1), (1, 0)])  8.85 us
  transfers between devices with their start and end apart: 27, of which 14 were waited for; matrix products, arithmetic and copies ran while one was open for 0% of the time, Pallas kernels for 12%

profile of v2, /device:TPU:1, one launch (start us, length us, event | category | flops | bytes accessed | tf_op | source)
XLA Modules:
  0.0 239.8 jit_solution(13033602473835119134)
XLA Ops:
  0.6 20.1 %all_to_all.25.x_ref = bf16[16,2,16,512]{3,2,1,0:T(8,128)(2,1)S(1)} all-to-all(bf16[16,2,16,512]{3,2,1,0:T(8,128)(2,1)} %bitcast.12), channel_id=1, replica_groups=mesh['y'=4,'zl'=2,'zh'=2,'x'=4,'c'=2] {'zh','x','c'}, dimensions={0} | all-to-all | bytes 1048576 | tf_op jit(solution)/shard_map/all_to_all | solution.py:625
  20.8 0.7 copy-done.30
  21.4 8.2 %shard_map.84 = (bf16[128,16,128]{2,1,0:T(8,128)(2,1)S(1)}, bf16[3,512,512]{2,1,0:T(8,128)(2,1)S(1)}, bf16[2,512,512]{2,1,0:T(8,128)(2,1)S(1)}) custom-call(s32[2,8]{1,0:T(2,128)S(1)} %copy-done.30, bf16[16,2,16,512]{3,2,1,0:T(8,128)(2,1)S(1)} %all_to_all.25.x_ref, bf16[4,512,512]{2,1,0:T(8,128)(2,1)} %w_ref.9), custom_call_target="tpu_custom_call" | custom-call | flops 1342177280 | bytes 6291456 | tf_op jit(solution)/shard_map/pallas_call | solution.py:646
  29.6 1.0 copy-done.5
  30.6 0.8 copy-done.9
  31.4 6.0 %all-to-all-start.1 = ((bf16[128,16,128]{2,1,0:T(8,128)(2,1)}), bf16[128,16,128]{2,1,0:T(8,128)(2,1)S(1)}, u32[]{:S(2)}, u32[]{:S(2)}) async-start(bf16[128,16,128]{2,1,0:T(8,128)(2,1)} %copy-done.9), calls=%async_computation.1 | async-start | bytes 1048576 | tf_op jit(solution)/shard_map/all_to_all | solution.py:625
  37.5 1.2 shard_map.85
  38.7 1.4 collective-permute-start
  40.2 2.5 %collective-permute-start.1 = (bf16[2,2,32,512]{3,2,1,0:T(8,128)(2,1)S(1)}, bf16[2,2,32,512]{3,2,1,0:T(8,128)(2,1)S(1)}, u32[]{:S(2)}, u32[]{:S(2)}) collective-permute-start(bf16[2,2,32,512]{3,2,1,0:T(8,128)(2,1)S(1)} %get-tuple-element.49), channel_id=1, source_target_pairs={{0,64},{32,96},{64,0},{96,32},{1,65},{33,97},{65,1},{97,33},{2,66}... | collective-permute-start | bytes 393224 | tf_op jit(solution)/shard_map/ppermute | solution.py:631
  42.6 1.1 collective-permute-start.2
  43.7 5.1 %collective-permute-done.refs_1_ = bf16[2,2,32,512]{3,2,1,0:T(8,128)(2,1)S(1)} collective-permute-done((bf16[2,2,32,512]{3,2,1,0:T(8,128)(2,1)S(1)}, bf16[2,2,32,512]{3,2,1,0:T(8,128)(2,1)S(1)}, u32[]{:S(2)}, u32[]{:S(2)}) %collective-permute-start) | collective-permute-done | bytes 131104 | tf_op jit(solution)/shard_map/ppermute | solution.py:631
  48.9 4.0 %collective-permute-done.1.refs_2_ = bf16[2,2,32,512]{3,2,1,0:T(8,128)(2,1)S(1)} collective-permute-done((bf16[2,2,32,512]{3,2,1,0:T(8,128)(2,1)S(1)}, bf16[2,2,32,512]{3,2,1,0:T(8,128)(2,1)S(1)}, u32[]{:S(2)}, u32[]{:S(2)}) %collective-permute-start.1) | collective-permute-done | bytes 131104 | tf_op jit(solution)/shard_map/ppermute | solution.py:631
  53.4 1.4 collective-permute-start.3
  54.8 6.0 %collective-permute-done.3.refs_4_ = bf16[4,2,32,512]{3,2,1,0:T(8,128)(2,1)S(1)} collective-permute-done((bf16[4,2,32,512]{3,2,1,0:T(8,128)(2,1)S(1)}, bf16[4,2,32,512]{3,2,1,0:T(8,128)(2,1)S(1)}, u32[]{:S(2)}, u32[]{:S(2)}) %collective-permute-start.3) | collective-permute-done | bytes 262176 | tf_op jit(solution)/shard_map/ppermute | solution.py:636
  60.9 0.7 copy-done.16
  61.6 0.9 copy-done.12
  62.5 0.9 copy-done.17
  63.4 12.2 %shard_map.87 = (bf16[128,16,128]{2,1,0:T(8,128)(2,1)S(1)}, bf16[2,512,512]{2,1,0:T(8,128)(2,1)S(1)}, bf16[4,512,512]{2,1,0:T(8,128)(2,1)S(1)}, bf16[512,512]{1,0:T(8,128)(2,1)S(1)}) custom-call(s32[5]{0:T(128)S(1)} %stack.23.where_ref, s32[2,8]{1,0:T(2,128)S(1)} %copy-done.31, bf16[128,16,128]{2,1,0:T(8,128)(2,1)S(1)} %all-to-all-done.1.m_ref, ...), custom_call_target="tpu_custom_call" | custom-call | flops 2952790016 | bytes 8388608 | tf_op jit(solution)/shard_map/pallas_call | solution.py:649
  75.7 1.3 copy-done
  77.0 1.0 copy-done.7
  78.0 0.8 copy-done.10
  78.7 8.4 %all-to-all-start.2 = ((bf16[128,16,128]{2,1,0:T(8,128)(2,1)}), bf16[128,16,128]{2,1,0:T(8,128)(2,1)}, u32[]{:S(2)}, u32[]{:S(2)}) async-start(bf16[128,16,128]{2,1,0:T(8,128)(2,1)} %copy-done.10), calls=%async_computation.2 | async-start | bytes 1048576 | tf_op jit(solution)/shard_map/all_to_all | solution.py:625
  87.2 4.8 %shard_map.88 = (bf16[2,512,512]{2,1,0:T(8,128)(2,1)}, bf16[2,512,512]{2,1,0:T(8,128)(2,1)}, bf16[2,32,512]{2,1,0:T(8,128)(2,1)S(1)}, bf16[2,32,512]{2,1,0:T(8,1...) custom-call(s32[5]{0:T(128)S(1)} %stack.23.where_ref, ...), custom_call_target="tpu_custom_call" | custom-call | flops 1342177280 | bytes 7340032 | tf_op jit(solution)/shard_map/pallas_call | solution.py:653
  91.9 0.6 copy-done.18
  92.6 0.6 copy-done.20
  93.2 0.6 copy-done.22
  93.8 0.6 copy-done.24
  94.4 0.6 copy-done.26
  95.1 0.6 copy-done.28
  95.7 1.3 collective-permute-start.20
  97.0 2.4 %shard_map.90 = (bf16[8,512,256]{2,1,0:T(8,128)(2,1)S(1)}, bf16[2,512,512]{2,1,0:T(8,128)(2,1)S(1)}) custom-call(bf16[3,512,512]{2,1,0:T(8,128)(2,1)S(1)} %get-tuple-element.63.qkv_ref, bf16[2,512,512]{2,1,0:T(8,128)(2,1)S(1)} %copy-done.6), custom_call_target="tpu_custom_call" | custom-call | flops 134217728 | bytes 8388608 | tf_op jit(solution)/shard_map/pallas_call | solution.py:648
  99.5 1.3 copy-done.13
  100.8 1.0 copy-done.14
  101.8 1.2 copy-done.15
  103.0 10.0 %shard_map.91 = (bf16[2,512,512]{2,1,0:T(8,128)(2,1)S(1)}, bf16[2,512,512]{2,1,0:T(8,128)(2,1)S(1)}, bf16[4,512,512]{2,1,0:T(8,128)(2,1)}) custom-call(s32[5]{0:T(128)S(1)} %stack.23.where_ref, s32[2,8]{1,0:T(2,128)S(1)} %copy-done.31, bf16[128,16,128]{2,1,0:T(8,128)(2,1)} %all-to-all-done.2.g_ref, bf16[3,512,512]{2,1,0:T(8,128)(2,1)} %copy-done.3, ...), custom_call_target="tpu_custom_call" | custom-call | flops 2013265920 | bytes 12582912 | tf_op jit(solution)/shard_map/pallas_call | solution.py:657
  113.1 1.2 shard_map.95
  114.9 2.4 collective-permute-start.22
  117.3 1.2 collective-permute-start.23
  118.4 4.5 %collective-permute-done.21.refs_1_ = bf16[256,512]{1,0:T(8,128)(2,1)S(1)} collective-permute-done((bf16[256,512]{1,0:T(8,128)(2,1)S(1)}, bf16[256,512]{1,0:T(8,128)(2,1)S(1)}, u32[]{:S(2)}, u32[]{:S(2)}) %collective-permute-start.21) | collective-permute-done | bytes 262176 | tf_op jit(solution)/shard_map/ppermute | solution.py:631
  122.9 5.9 %collective-permute-done.22.refs_2_ = bf16[256,512]{1,0:T(8,128)(2,1)S(1)} collective-permute-done((bf16[256,512]{1,0:T(8,128)(2,1)S(1)}, bf16[256,512]{1,0:T(8,128)(2,1)S(1)}, u32[]{:S(2)}, u32[]{:S(2)}) %collective-permute-start.22) | collective-permute-done | bytes 262176 | tf_op jit(solution)/shard_map/ppermute | solution.py:631
  129.4 30.1 %all_to_all.26.both_ref = bf16[64,80,128]{2,1,0:T(8,128)(2,1)S(1)} all-to-all(bf16[64,80,128]{2,1,0:T(8,128)(2,1)S(1)} %shard_map.96), channel_id=1, replica_groups=mesh['y'=4,'zl'=2,'zh'=2,'x'=4,'c'=2] {'y','zl','zh','x'}, dimensions={0} | all-to-all | bytes 2621440 | tf_op jit(solution)/shard_map/all_to_all | solution.py:625
  159.9 32.4 %all_to_all.27.chunks_ref = bf16[64,128,128]{2,1,0:T(8,128)(2,1)S(1)} all-to-all(bf16[64,128,128]{2,1,0:T(8,128)(2,1)S(1)} %shard_map.97), channel_id=1, replica_groups=mesh['y'=4,'zl'=2,'zh'=2,'x'=4,'c'=2] {'y','zl','zh','x'}, dimensions={0} | all-to-all | bytes 4194304 | tf_op jit(solution)/shard_map/all_to_all | solution.py:625
  192.4 3.3 %collective-permute-start.24 = (bf16[64,128,128]{2,1,0:T(8,128)(2,1)S(1)}, bf16[64,128,128]{2,1,0:T(8,128)(2,1)S(1)}, u32[]{:S(2)}, u32[]{:S(2)}) collective-permute-start(bf16[64,128,128]{2,1,0:T(8,128)(2,1)S(1)} %all_to_all.27.chunks_ref), channel_id=1, source_target_pairs={{0,1},{1,0},{2,3},{3,2},{4,5},{5,4},{6,7},{7,6},{8,9},{9,8},{10,11... | collective-permute-start | bytes 6291464 | tf_op jit(solution)/shard_map/ppermute | solution.py:636
  195.7 1.9 shard_map.92
  197.8 2.2 collective-permute-start.12
  199.9 1.5 collective-permute-start.13
  201.5 2.4 collective-permute-start.14
  203.8 2.9 %collective-permute-done.11.refs_1_ = bf16[2,2,16,512]{3,2,1,0:T(8,128)(2,1)S(1)} collective-permute-done((bf16[2,2,16,512]{3,2,1,0:T(8,128)(2,1)S(1)}, bf16[2,2,16,512]{3,2,1,0:T(8,128)(2,1)S(1)}, u32[]{:S(2)}, u32[]{:S(2)}) %collective-permute-start.11) | collective-permute-done | bytes 65568 | tf_op jit(solution)/shard_map/ppermute | solution.py:631
  206.8 1.6 collective-permute-start.16
  208.4 2.6 %collective-permute-start.17 = (bf16[2,2,16,512]{3,2,1,0:T(8,128)(2,1)S(1)}, bf16[2,2,16,512]{3,2,1,0:T(8,128)(2,1)S(1)}, u32[]{:S(2)}, u32[]{:S(2)}) collective-permute-start(bf16[2,2,16,512]{3,2,1,0:T(8,128)(2,1)S(1)} %get-tuple-element.75), channel_id=1, source_target_pairs={{0,14},{2,0},{4,2},{6,4},{8,6},{10,8},{12,10},{14,12},{1,15},{3,1}... | collective-permute-start | bytes 196616 | tf_op jit(solution)/shard_map/ppermute | solution.py:631
  211.0 0.8 collective-permute-done.15.refs_5_
  211.8 1.8 collective-permute-done.17.refs_7_
  214.2 2.7 %collective-permute-start.18 = (bf16[8,2,16,512]{3,2,1,0:T(8,128)(2,1)S(1)}, bf16[8,2,16,512]{3,2,1,0:T(8,128)(2,1)S(1)}, u32[]{:S(2)}, u32[]{:S(2)}) collective-permute-start(bf16[8,2,16,512]{3,2,1,0:T(8,128)(2,1)S(1)} %shard_map.93), channel_id=1, source_target_pairs={{0,1},{1,0},{2,3},{3,2},{4,5},{5,4},{6,7},{7,6},{8,9},{9,8},{10,11... | collective-permute-start | bytes 786440 | tf_op jit(solution)/shard_map/ppermute | solution.py:636
  217.1 1.9 collective-permute-start.6
  219.0 3.6 %collective-permute-done.4.refs_1_ = bf16[2,32,512]{2,1,0:T(8,128)(2,1)S(1)} collective-permute-done((bf16[2,32,512]{2,1,0:T(8,128)(2,1)S(1)}, bf16[2,32,512]{2,1,0:T(8,128)(2,1)S(1)}, u32[]{:S(2)}, u32[]{:S(2)}) %collective-permute-start.4) | collective-permute-done | bytes 65568 | tf_op jit(solution)/shard_map/ppermute | solution.py:631
  222.6 0.8 collective-permute-start.8
  223.4 1.2 collective-permute-done.6.refs_3_
  224.6 0.7 collective-permute-start.9
  225.3 1.9 collective-permute-done.7.refs_4_
  227.7 2.9 %collective-permute-done.10.refs_7_ = bf16[2,32,512]{2,1,0:T(8,128)(2,1)S(1)} collective-permute-done((bf16[2,32,512]{2,1,0:T(8,128)(2,1)S(1)}, bf16[2,32,512]{2,1,0:T(8,128)(2,1)S(1)}, u32[]{:S(2)}, u32[]{:S(2)}) %collective-permute-start.10) | collective-permute-done | bytes 65568 | tf_op jit(solution)/shard_map/ppermute | solution.py:631
  230.6 2.3 shard_map.89
  232.9 1.4 shard_map.94
  234.3 2.7 %widen.2 = (f32[2,1024,512]{2,1,0:T(8,128)}, f32[2,4,256,512]{3,2,1,0:T(8,128)}) custom-call(s32[5]{0:T(128)S(1)} %stack.23.where_ref, bf16[64,128,128]{2,1,0:T(8,128)(2,1)S(1)} %all_to_all.27.chunks_ref), custom_call_target="tpu_custom_call" | custom-call | bytes 6291456 | tf_op jit(solution)/shard_map/widen/pallas_call | solution.py:609
  237.0 2.7 %widen.3 = (f32[2,1024,512]{2,1,0:T(8,128)}, f32[2,4,256,512]{3,2,1,0:T(8,128)}) custom-call(s32[5]{0:T(128)S(1)} %stack.23.where_ref, bf16[64,128,128]{2,1,0:T(8,128)(2,1)S(1)} %collective-permute-done.24.chunks_ref, f32[2,1024,512]{2,1,0:T(8,128)} %get-tuple-element.84.refs_0_, ...), custom_call_target="tpu_custom_call", output_to_operand_aliasing={{0}: (2, {}), {1}: (3, {})} | custom-call | bytes 6291456 | tf_op jit(solution)/shard_map/widen/pallas_call | solution.py:609
  (74 shorter events, 3.7 us)
Async XLA Ops:
  20.7 0.7 copy-start.30
  21.4 16.1 %copy-start.8 = (bf16[32,16,512]{2,1,0:T(8,128)(2,1)S(1)}, bf16[32,16,512]{2,1,0:T(8,128)(2,1)}, u32[]{:S(2)}) copy-start(bf16[32,16,512]{2,1,0:T(8,128)(2,1)} %tile_ref.1) | copy-start | bytes 1572868
  29.6 1.0 copy-start.5
  30.6 0.8 copy-start.9
  31.4 65.6 %copy-start.3 = (bf16[3,512,512]{2,1,0:T(8,128)(2,1)}, bf16[3,512,512]{2,1,0:T(8,128)(2,1)S(1)}, u32[]{:S(2)}) copy-start(bf16[3,512,512]{2,1,0:T(8,128)(2,1)S(1)} %get-tuple-element.63.qkv_ref) | copy-start | bytes 4718596
  31.4 30.1 %copy-start.31 = (s32[2,8]{1,0:T(2,128)S(1)}, s32[2,8]{1,0:T(2,128)}, u32[]{:S(2)}) copy-start(s32[2,8]{1,0:T(2,128)} %keep_heads_ref.3) | copy-start | bytes 196
  31.4 30.1 %all-to-all-start.1 = ((bf16[128,16,128]{2,1,0:T(8,128)(2,1)}), bf16[128,16,128]{2,1,0:T(8,128)(2,1)S(1)}, u32[]{:S(2)}, u32[]{:S(2)}) async-start(bf16[128,16,128]{2,1,0:T(8,128)(2,1)} %copy-done.9), calls=%async_computation.1 | async-start | bytes 1048576 | tf_op jit(solution)/shard_map/all_to_all | solution.py:625
  38.7 10.1 %collective-permute-start = (bf16[2,2,32,512]{3,2,1,0:T(8,128)(2,1)S(1)}, bf16[2,2,32,512]{3,2,1,0:T(8,128)(2,1)S(1)}, u32[]{:S(2)}, u32[]{:S(2)}) collective-permute-start(bf16[2,2,32,512]{3,2,1,0:T(8,128)(2,1)S(1)} %get-tuple-element.48), channel_id=1, source_target_pairs={{0,32},{32,64},{64,96},{96,0},{1,33},{33,65},{65,97},{97,1},{2,34}... | collective-permute-start | bytes 393224 | tf_op jit(solution)/shard_map/ppermute | solution.py:631
  40.2 12.7 %collective-permute-start.1 = (bf16[2,2,32,512]{3,2,1,0:T(8,128)(2,1)S(1)}, bf16[2,2,32,512]{3,2,1,0:T(8,128)(2,1)S(1)}, u32[]{:S(2)}, u32[]{:S(2)}) collective-permute-start(bf16[2,2,32,512]{3,2,1,0:T(8,128)(2,1)S(1)} %get-tuple-element.49), channel_id=1, source_target_pairs={{0,64},{32,96},{64,0},{96,32},{1,65},{33,97},{65,1},{97,33},{2,66}... | collective-permute-start | bytes 393224 | tf_op jit(solution)/shard_map/ppermute | solution.py:631
  42.6 10.2 %collective-permute-start.2 = (bf16[2,2,32,512]{3,2,1,0:T(8,128)(2,1)S(1)}, bf16[2,2,32,512]{3,2,1,0:T(8,128)(2,1)S(1)}, u32[]{:S(2)}, u32[]{:S(2)}) collective-permute-start(bf16[2,2,32,512]{3,2,1,0:T(8,128)(2,1)S(1)} %get-tuple-element.50), channel_id=1, source_target_pairs={{0,96},{32,0},{64,32},{96,64},{1,97},{33,1},{65,33},{97,65},{2,98}... | collective-permute-start | bytes 393224 | tf_op jit(solution)/shard_map/ppermute | solution.py:631
  52.8 8.0 %copy-start.11 = (bf16[2,2,32,512]{3,2,1,0:T(8,128)(2,1)}, bf16[2,2,32,512]{3,2,1,0:T(8,128)(2,1)S(1)}, u32[]{:S(2)}) copy-start(bf16[2,2,32,512]{3,2,1,0:T(8,128)(2,1)S(1)} %collective-permute-done.2.refs_3_) | copy-start | bytes 393220
  53.4 7.5 %collective-permute-start.3 = (bf16[4,2,32,512]{3,2,1,0:T(8,128)(2,1)S(1)}, bf16[4,2,32,512]{3,2,1,0:T(8,128)(2,1)S(1)}, u32[]{:S(2)}, u32[]{:S(2)}) collective-permute-start(bf16[4,2,32,512]{3,2,1,0:T(8,128)(2,1)S(1)} %shard_map.86), channel_id=1, source_target_pairs={{0,16},{16,0},{1,17},{17,1},{2,18},{18,2},{3,19},{19,3},{4,20},{20... | collective-permute-start | bytes 786440 | tf_op jit(solution)/shard_map/ppermute | solution.py:636
  60.9 0.7 copy-start.16
  61.6 0.9 copy-start.12
  62.5 0.9 copy-start.17
  75.7 1.3 copy-start
  77.0 1.0 copy-start.7
  78.0 0.8 copy-start.10
  78.7 23.0 %all-to-all-start.2 = ((bf16[128,16,128]{2,1,0:T(8,128)(2,1)}), bf16[128,16,128]{2,1,0:T(8,128)(2,1)}, u32[]{:S(2)}, u32[]{:S(2)}) async-start(bf16[128,16,128]{2,1,0:T(8,128)(2,1)} %copy-done.10), calls=%async_computation.2 | async-start | bytes 1048576 | tf_op jit(solution)/shard_map/all_to_all | solution.py:625
  87.2 9.8 %copy-start.6 = (bf16[2,512,512]{2,1,0:T(8,128)(2,1)S(1)}, bf16[2,512,512]{2,1,0:T(8,128)(2,1)}, u32[]{:S(2)}) copy-start(bf16[2,512,512]{2,1,0:T(8,128)(2,1)} %copy-done.5) | copy-start | bytes 3145732
  91.9 0.6 copy-start.18
  92.6 0.6 copy-start.20
  93.2 0.6 copy-start.22
  93.8 0.6 copy-start.24
  94.4 0.6 copy-start.26
  95.1 0.6 copy-start.28
  95.7 17.4 %collective-permute-start.20 = (bf16[2,512,512]{2,1,0:T(8,128)(2,1)}, bf16[2,512,512]{2,1,0:T(8,128)(2,1)S(1)}, u32[]{:S(2)}, u32[]{:S(2)}) collective-permute-start(bf16[2,512,512]{2,1,0:T(8,128)(2,1)} %get-tuple-element.79), channel_id=1, source_target_pairs={{0,1},{1,0},{2,3},{3,2},{4,5},{5,4},{6,7},{7,6},{8,9},{9,8},{10,11... | collective-permute-start | bytes 3145736 | tf_op jit(solution)/shard_map/ppermute | solution.py:636
  99.5 1.3 copy-start.13
  100.8 1.0 copy-start.14
  101.8 1.2 copy-start.15
  103.0 10.1 %copy-start.4 = (bf16[2,512,512]{2,1,0:T(8,128)(2,1)S(1)}, bf16[2,512,512]{2,1,0:T(8,128)(2,1)}, u32[]{:S(2)}) copy-start(bf16[2,512,512]{2,1,0:T(8,128)(2,1)} %get-tuple-element.78.keep_ref) | copy-start | bytes 3145732
  113.0 16.0 %collective-permute-start.19 = (bf16[2,512,512]{2,1,0:T(8,128)(2,1)S(1)}, bf16[2,512,512]{2,1,0:T(8,128)(2,1)S(1)}, u32[]{:S(2)}, u32[]{:S(2)}) collective-permute-start(bf16[2,512,512]{2,1,0:T(8,128)(2,1)S(1)} %get-tuple-element.77), channel_id=1, source_target_pairs={{0,1},{1,0},{2,3},{3,2},{4,5},{5,4},{6,7},{7,6},{8,9},{9,8},{10,11... | collective-permute-start | bytes 3145736 | tf_op jit(solution)/shard_map/ppermute | solution.py:636
  114.3 8.7 %collective-permute-start.21 = (bf16[256,512]{1,0:T(8,128)(2,1)S(1)}, bf16[256,512]{1,0:T(8,128)(2,1)S(1)}, u32[]{:S(2)}, u32[]{:S(2)}) collective-permute-start(bf16[256,512]{1,0:T(8,128)(2,1)S(1)} %get-tuple-element.81), channel_id=1, source_target_pairs={{0,2},{2,4},{4,6},{6,0},{1,3},{3,5},{5,7},{7,1},{8,10},{10,12},{12... | collective-permute-start | bytes 786440 | tf_op jit(solution)/shard_map/ppermute | solution.py:631
  114.9 14.0 %collective-permute-start.22 = (bf16[256,512]{1,0:T(8,128)(2,1)S(1)}, bf16[256,512]{1,0:T(8,128)(2,1)S(1)}, u32[]{:S(2)}, u32[]{:S(2)}) collective-permute-start(bf16[256,512]{1,0:T(8,128)(2,1)S(1)} %get-tuple-element.82), channel_id=1, source_target_pairs={{0,4},{2,6},{4,0},{6,2},{1,5},{3,7},{5,1},{7,3},{8,12},{10,14},{12... | collective-permute-start | bytes 786440 | tf_op jit(solution)/shard_map/ppermute | solution.py:631
  117.3 11.7 %collective-permute-start.23 = (bf16[256,512]{1,0:T(8,128)(2,1)S(1)}, bf16[256,512]{1,0:T(8,128)(2,1)S(1)}, u32[]{:S(2)}, u32[]{:S(2)}) collective-permute-start(bf16[256,512]{1,0:T(8,128)(2,1)S(1)} %get-tuple-element.83), channel_id=1, source_target_pairs={{0,6},{2,0},{4,2},{6,4},{1,7},{3,1},{5,3},{7,5},{8,14},{10,8},{12,... | collective-permute-start | bytes 786440 | tf_op jit(solution)/shard_map/ppermute | solution.py:631
  159.9 35.8 %copy-start.1 = (bf16[4,512,512]{2,1,0:T(8,128)(2,1)S(1)}, bf16[4,512,512]{2,1,0:T(8,128)(2,1)}, u32[]{:S(2)}) copy-start(bf16[4,512,512]{2,1,0:T(8,128)(2,1)} %w_ref.9) | copy-start | bytes 6291460
  159.9 35.8 %copy-start.2 = (bf16[4,512,512]{2,1,0:T(8,128)(2,1)S(1)}, bf16[4,512,512]{2,1,0:T(8,128)(2,1)}, u32[]{:S(2)}) copy-start(bf16[4,512,512]{2,1,0:T(8,128)(2,1)} %get-tuple-element.67.right_ref) | copy-start | bytes 6291460
  192.4 44.6 %collective-permute-start.24 = (bf16[64,128,128]{2,1,0:T(8,128)(2,1)S(1)}, bf16[64,128,128]{2,1,0:T(8,128)(2,1)S(1)}, u32[]{:S(2)}, u32[]{:S(2)}) collective-permute-start(bf16[64,128,128]{2,1,0:T(8,128)(2,1)S(1)} %all_to_all.27.chunks_ref), channel_id=1, source_target_pairs={{0,1},{1,0},{2,3},{3,2},{4,5},{5,4},{6,7},{7,6},{8,9},{9,8},{10,11... | collective-permute-start | bytes 6291464 | tf_op jit(solution)/shard_map/ppermute | solution.py:636
  195.7 21.2 %copy-start.29 = (bf16[2,32,512]{2,1,0:T(8,128)(2,1)S(1)}, bf16[2,32,512]{2,1,0:T(8,128)(2,1)}, u32[]{:S(2)}) copy-start(bf16[2,32,512]{2,1,0:T(8,128)(2,1)} %copy-done.28) | copy-start | bytes 196612
  195.7 21.4 %copy-start.27 = (bf16[2,32,512]{2,1,0:T(8,128)(2,1)S(1)}, bf16[2,32,512]{2,1,0:T(8,128)(2,1)}, u32[]{:S(2)}) copy-start(bf16[2,32,512]{2,1,0:T(8,128)(2,1)} %copy-done.26) | copy-start | bytes 196612
  195.7 21.4 %copy-start.25 = (bf16[2,32,512]{2,1,0:T(8,128)(2,1)S(1)}, bf16[2,32,512]{2,1,0:T(8,128)(2,1)}, u32[]{:S(2)}) copy-start(bf16[2,32,512]{2,1,0:T(8,128)(2,1)} %copy-done.24) | copy-start | bytes 196612
  195.7 26.9 %copy-start.23 = (bf16[2,32,512]{2,1,0:T(8,128)(2,1)S(1)}, bf16[2,32,512]{2,1,0:T(8,128)(2,1)}, u32[]{:S(2)}) copy-start(bf16[2,32,512]{2,1,0:T(8,128)(2,1)} %copy-done.22) | copy-start | bytes 196612
  195.7 26.9 %copy-start.21 = (bf16[2,32,512]{2,1,0:T(8,128)(2,1)S(1)}, bf16[2,32,512]{2,1,0:T(8,128)(2,1)}, u32[]{:S(2)}) copy-start(bf16[2,32,512]{2,1,0:T(8,128)(2,1)} %copy-done.20) | copy-start | bytes 196612
  195.7 28.9 %copy-start.19 = (bf16[2,32,512]{2,1,0:T(8,128)(2,1)S(1)}, bf16[2,32,512]{2,1,0:T(8,128)(2,1)}, u32[]{:S(2)}) copy-start(bf16[2,32,512]{2,1,0:T(8,128)(2,1)} %copy-done.18) | copy-start | bytes 196612
  197.7 9.1 %collective-permute-start.11 = (bf16[2,2,16,512]{3,2,1,0:T(8,128)(2,1)S(1)}, bf16[2,2,16,512]{3,2,1,0:T(8,128)(2,1)S(1)}, u32[]{:S(2)}, u32[]{:S(2)}) collective-permute-start(bf16[2,2,16,512]{3,2,1,0:T(8,128)(2,1)S(1)} %get-tuple-element.69), channel_id=1, source_target_pairs={{0,2},{2,4},{4,6},{6,8},{8,10},{10,12},{12,14},{14,0},{1,3},{3,5},... | collective-permute-start | bytes 196616 | tf_op jit(solution)/shard_map/ppermute | solution.py:631
  197.8 9.0 %collective-permute-start.12 = (bf16[2,2,16,512]{3,2,1,0:T(8,128)(2,1)S(1)}, bf16[2,2,16,512]{3,2,1,0:T(8,128)(2,1)S(1)}, u32[]{:S(2)}, u32[]{:S(2)}) collective-permute-start(bf16[2,2,16,512]{3,2,1,0:T(8,128)(2,1)S(1)} %get-tuple-element.70), channel_id=1, source_target_pairs={{0,4},{2,6},{4,8},{6,10},{8,12},{10,14},{12,0},{14,2},{1,5},{3,7},... | collective-permute-start | bytes 196616 | tf_op jit(solution)/shard_map/ppermute | solution.py:631
  199.9 8.5 %collective-permute-start.13 = (bf16[2,2,16,512]{3,2,1,0:T(8,128)(2,1)S(1)}, bf16[2,2,16,512]{3,2,1,0:T(8,128)(2,1)S(1)}, u32[]{:S(2)}, u32[]{:S(2)}) collective-permute-start(bf16[2,2,16,512]{3,2,1,0:T(8,128)(2,1)S(1)} %get-tuple-element.71), channel_id=1, source_target_pairs={{0,6},{2,8},{4,10},{6,12},{8,14},{10,0},{12,2},{14,4},{1,7},{3,9},... | collective-permute-start | bytes 196616 | tf_op jit(solution)/shard_map/ppermute | solution.py:631
  201.5 9.5 %collective-permute-start.14 = (bf16[2,2,16,512]{3,2,1,0:T(8,128)(2,1)S(1)}, bf16[2,2,16,512]{3,2,1,0:T(8,128)(2,1)S(1)}, u32[]{:S(2)}, u32[]{:S(2)}) collective-permute-start(bf16[2,2,16,512]{3,2,1,0:T(8,128)(2,1)S(1)} %get-tuple-element.72), channel_id=1, source_target_pairs={{0,8},{2,10},{4,12},{6,14},{8,0},{10,2},{12,4},{14,6},{1,9},{3,11}... | collective-permute-start | bytes 196616 | tf_op jit(solution)/shard_map/ppermute | solution.py:631
  206.8 5.0 %collective-permute-start.15 = (bf16[2,2,16,512]{3,2,1,0:T(8,128)(2,1)S(1)}, bf16[2,2,16,512]{3,2,1,0:T(8,128)(2,1)S(1)}, u32[]{:S(2)}, u32[]{:S(2)}) collective-permute-start(bf16[2,2,16,512]{3,2,1,0:T(8,128)(2,1)S(1)} %get-tuple-element.73), channel_id=1, source_target_pairs={{0,10},{2,12},{4,14},{6,0},{8,2},{10,4},{12,6},{14,8},{1,11},{3,13... | collective-permute-start | bytes 196616 | tf_op jit(solution)/shard_map/ppermute | solution.py:631
  206.8 5.0 %collective-permute-start.16 = (bf16[2,2,16,512]{3,2,1,0:T(8,128)(2,1)S(1)}, bf16[2,2,16,512]{3,2,1,0:T(8,128)(2,1)S(1)}, u32[]{:S(2)}, u32[]{:S(2)}) collective-permute-start(bf16[2,2,16,512]{3,2,1,0:T(8,128)(2,1)S(1)} %get-tuple-element.74), channel_id=1, source_target_pairs={{0,12},{2,14},{4,0},{6,2},{8,4},{10,6},{12,8},{14,10},{1,13},{3,15... | collective-permute-start | bytes 196616 | tf_op jit(solution)/shard_map/ppermute | solution.py:631
  208.4 5.2 %collective-permute-start.17 = (bf16[2,2,16,512]{3,2,1,0:T(8,128)(2,1)S(1)}, bf16[2,2,16,512]{3,2,1,0:T(8,128)(2,1)S(1)}, u32[]{:S(2)}, u32[]{:S(2)}) collective-permute-start(bf16[2,2,16,512]{3,2,1,0:T(8,128)(2,1)S(1)} %get-tuple-element.75), channel_id=1, source_target_pairs={{0,14},{2,0},{4,2},{6,4},{8,6},{10,8},{12,10},{14,12},{1,15},{3,1}... | collective-permute-start | bytes 196616 | tf_op jit(solution)/shard_map/ppermute | solution.py:631
  214.2 18.7 %collective-permute-start.18 = (bf16[8,2,16,512]{3,2,1,0:T(8,128)(2,1)S(1)}, bf16[8,2,16,512]{3,2,1,0:T(8,128)(2,1)S(1)}, u32[]{:S(2)}, u32[]{:S(2)}) collective-permute-start(bf16[8,2,16,512]{3,2,1,0:T(8,128)(2,1)S(1)} %shard_map.93), channel_id=1, source_target_pairs={{0,1},{1,0},{2,3},{3,2},{4,5},{5,4},{6,7},{7,6},{8,9},{9,8},{10,11... | collective-permute-start | bytes 786440 | tf_op jit(solution)/shard_map/ppermute | solution.py:636
  216.9 5.7 %collective-permute-start.4 = (bf16[2,32,512]{2,1,0:T(8,128)(2,1)S(1)}, bf16[2,32,512]{2,1,0:T(8,128)(2,1)S(1)}, u32[]{:S(2)}, u32[]{:S(2)}) collective-permute-start(bf16[2,32,512]{2,1,0:T(8,128)(2,1)S(1)} %copy-done.29), channel_id=1, source_target_pairs={{0,16},{16,32},{32,48},{48,64},{64,80},{80,96},{96,112},{112,0},{1... | collective-permute-start | bytes 196616 | tf_op jit(solution)/shard_map/ppermute | solution.py:631
  217.1 5.5 %collective-permute-start.5 = (bf16[2,32,512]{2,1,0:T(8,128)(2,1)S(1)}, bf16[2,32,512]{2,1,0:T(8,128)(2,1)S(1)}, u32[]{:S(2)}, u32[]{:S(2)}) collective-permute-start(bf16[2,32,512]{2,1,0:T(8,128)(2,1)S(1)} %copy-done.27), channel_id=1, source_target_pairs={{0,32},{16,48},{32,64},{48,80},{64,96},{80,112},{96,0},{112,16},{1... | collective-permute-start | bytes 196616 | tf_op jit(solution)/shard_map/ppermute | solution.py:631
  217.1 7.5 %collective-permute-start.6 = (bf16[2,32,512]{2,1,0:T(8,128)(2,1)S(1)}, bf16[2,32,512]{2,1,0:T(8,128)(2,1)S(1)}, u32[]{:S(2)}, u32[]{:S(2)}) collective-permute-start(bf16[2,32,512]{2,1,0:T(8,128)(2,1)S(1)} %copy-done.25), channel_id=1, source_target_pairs={{0,48},{16,64},{32,80},{48,96},{64,112},{80,0},{96,16},{112,32},{1... | collective-permute-start | bytes 196616 | tf_op jit(solution)/shard_map/ppermute | solution.py:631
  222.6 4.6 %collective-permute-start.7 = (bf16[2,32,512]{2,1,0:T(8,128)(2,1)S(1)}, bf16[2,32,512]{2,1,0:T(8,128)(2,1)S(1)}, u32[]{:S(2)}, u32[]{:S(2)}) collective-permute-start(bf16[2,32,512]{2,1,0:T(8,128)(2,1)S(1)} %copy-done.23), channel_id=1, source_target_pairs={{0,64},{16,80},{32,96},{48,112},{64,0},{80,16},{96,32},{112,48},{1... | collective-permute-start | bytes 196616 | tf_op jit(solution)/shard_map/ppermute | solution.py:631
  222.6 4.6 %collective-permute-start.8 = (bf16[2,32,512]{2,1,0:T(8,128)(2,1)S(1)}, bf16[2,32,512]{2,1,0:T(8,128)(2,1)S(1)}, u32[]{:S(2)}, u32[]{:S(2)}) collective-permute-start(bf16[2,32,512]{2,1,0:T(8,128)(2,1)S(1)} %copy-done.21), channel_id=1, source_target_pairs={{0,80},{16,96},{32,112},{48,0},{64,16},{80,32},{96,48},{112,64},{1... | collective-permute-start | bytes 196616 | tf_op jit(solution)/shard_map/ppermute | solution.py:631
  224.6 3.1 %collective-permute-start.9 = (bf16[2,32,512]{2,1,0:T(8,128)(2,1)S(1)}, bf16[2,32,512]{2,1,0:T(8,128)(2,1)S(1)}, u32[]{:S(2)}, u32[]{:S(2)}) collective-permute-start(bf16[2,32,512]{2,1,0:T(8,128)(2,1)S(1)} %copy-done.19), channel_id=1, source_target_pairs={{0,96},{16,112},{32,0},{48,16},{64,32},{80,48},{96,64},{112,80},{1... | collective-permute-start | bytes 196616 | tf_op jit(solution)/shard_map/ppermute | solution.py:631
  227.2 3.4 %collective-permute-start.10 = (bf16[2,32,512]{2,1,0:T(8,128)(2,1)S(1)}, bf16[2,32,512]{2,1,0:T(8,128)(2,1)S(1)}, u32[]{:S(2)}, u32[]{:S(2)}) collective-permute-start(bf16[2,32,512]{2,1,0:T(8,128)(2,1)S(1)} %get-tuple-element.61), channel_id=1, source_target_pairs={{0,112},{16,0},{32,16},{48,32},{64,48},{80,64},{96,80},{112,96},{1... | collective-permute-start | bytes 196616 | tf_op jit(solution)/shard_map/ppermute | solution.py:631

commit v3 on v2

--- a/solution.py
+++ b/solution.py
@@ -56,11 +56,11 @@
     return jnp.concatenate([value[:LINE].T, value[LINE:].T], axis=0)
 
 
-def gain_row(keep_ref, block, first, count):
+def gain_row(info_ref, block, first, count):
     head = lax.broadcasted_iota(jnp.int32, (1, count * HEAD), 1) // HEAD
     gain = jnp.zeros((1, count * HEAD), F32)
     for i in range(count):
-        gain = jnp.where(head == i, keep_ref[block, first + i].astype(F32), gain)
+        gain = jnp.where(head == i, info_ref[5 + block * HEADS + first + i].astype(F32), gain)
     return gain
 
 
@@ -102,31 +102,28 @@
     qkv_ref[2] = dot(normed, w_s[2]).astype(BF16)
 
 
-PER_STEP = 2
-
-
-def each_pair(visit):
+def each_pair(visit, per_step=2):
     def step(index, carry):
-        line = index // (N_PAIR // PER_STEP)
-        first = lax.rem(index, N_PAIR // PER_STEP) * PER_STEP
+        line = index // (N_PAIR // per_step)
+        first = lax.rem(index, N_PAIR // per_step) * per_step
         rows = pl.ds(pl.multiple_of(line * LINE, LINE), LINE)
-        for offset in range(PER_STEP):
+        for offset in range(per_step):
             pair = first + offset
             lanes = pl.ds(pl.multiple_of(pair * PAIR, PAIR), PAIR)
             visit(rows, lanes, line * N_PAIR + pair, pair)
         return carry
 
-    lax.fori_loop(0, 2 * N_PAIR // PER_STEP, step, 0)
+    lax.fori_loop(0, 2 * N_PAIR // per_step, step, 0)
 
 
 def row_forward_kernel(
-    keep_ref, x_ref, w_ref, mid_ref, qkv_ref, left_ref,
+    where_ref, x_ref, w_ref, mid_ref, saved_ref,
     mix_s, mid_s, qkv_s, left_s, w_s, w_sem, mid_sem, qkv_sem, left_sem,
 ):
     weights = copies_of(w_ref, w_s, w_sem, 4)
     start_all(weights)
-    saved = copies_of(qkv_s, qkv_ref, qkv_sem, 3)
-    lefts = copies_of(left_s, left_ref, left_sem, 2)
+    saved = copies_of(qkv_s, saved_ref, qkv_sem, 3)
+    lefts = copies_of(left_s, saved_ref.at[3:5], left_sem, 2)
     for rr in range(2):
         u = x_ref[:, rr].astype(F32).reshape(LINE, D)
         left_s[0, rr * LINE : (rr + 1) * LINE, :] = (u * inverse_rms(u)).astype(BF16)
@@ -137,9 +134,9 @@
     def visit(rows, lanes, at, pair):
         probs = softmax(qkv_s[0, rows, lanes], qkv_s[1, rows, lanes]).astype(BF16)
         mixed = pick_halves(dot(probs, qkv_s[2, rows, lanes]))
-        left_s[1, rows, lanes] = (mixed * gain_row(keep_ref, 0, pair * 2, 2)).astype(BF16)
-
-    each_pair(visit)
+        left_s[1, rows, lanes] = (mixed * gain_row(where_ref, 0, pair * 2, 2)).astype(BF16)
+
+    each_pair(visit, 4)
     lefts[1].start()
     weights[3].wait()
     added = dot(left_s[1], w_s[3])
@@ -159,14 +156,14 @@
     wait_all(saved + lefts + sends)
 
 
-def row_prepare_kernel(qkv_ref, left_ref, probs_ref, turned_ref):
+def row_prepare_kernel(saved_ref, probs_ref, turned_ref):
     def visit(rows, lanes, at, pair):
-        probs = softmax(qkv_ref[0, rows, lanes], qkv_ref[1, rows, lanes])
+        probs = softmax(saved_ref[0, rows, lanes], saved_ref[1, rows, lanes])
         probs_ref[at] = probs.astype(BF16)
 
     each_pair(visit)
     for which in range(2):
-        turned_ref[which] = left_ref[which].T
+        turned_ref[which] = saved_ref[3 + which].T
 
 
 def attention_backward(rows, lanes, qkv, da_ref, probs, right_ref):
@@ -201,7 +198,7 @@
 
 
 def row_backward_kernel(
-    where_ref, keep_heads_ref, g_ref, qkv_ref, turned_ref, probs_ref, w_ref,
+    where_ref, g_ref, qkv_ref, turned_ref, probs_ref, w_ref,
     keep_ref, send_ref, right_ref,
     mix_s, da_s, wo_s, qkv_s, turned_s, probs_s, keep_s, send_s, right_s,
     wo_sem, qkv_sem, turned_sem, probs_sem, half_sem, right_sem,
@@ -230,14 +227,14 @@
                 jnp.stack(sides, axis=1).reshape(LINE, 128).astype(BF16)
             )
     weight.wait()
-    gain = gain_row(keep_heads_ref, 0, 0, HEADS)
+    gain = gain_row(where_ref, 0, 0, HEADS)
     da_s[...] = (dot_nt(right_s[3], wo_s[...]) * gain).astype(BF16)
     wait_all(saved + probs)
 
     def visit(rows, lanes, at, pair):
         attention_backward(rows, lanes, qkv_s, da_s, probs_s[at], right_s)
 
-    each_pair(visit)
+    each_pair(visit, 4)
     rights = copies_of(right_s, right_ref, right_sem, 4)
     start_all(rights)
     wait_all(turned)
@@ -266,17 +263,22 @@
         outs[shift][...] = gin_s[lax.rem(chip + shift, 8)]
 
 
-def col_kernel(where_ref, keep_heads_ref, m_ref, w_ref, *refs):
+def col_kernel(where_ref, m_ref, w_ref, *refs):
     parts, got_ref, refs = refs[:4], refs[4], refs[5:]
-    gmid_ref, left_ref, right_ref, u_ref = refs[:4]
-    mix_s, u_s, ulow_s, left_s, right_s, qkv_s, da_s, w_s = refs[4:12]
-    w_sem, left_sem, right_sem, u_sem = refs[12:]
+    gmid_ref, saved_ref = refs[:2]
+    mix_s, u_s, ulow_s, left_s, right_s, qkv_s, da_s, w_s, parts_s, got_s = refs[2:12]
+    w_sem, left_sem, right_sem, u_sem, parts_sem, got_sem = refs[12:]
     mine = where_ref[1]
+    pieces = [
+        pltpu.make_async_copy(parts[i].at[mine], parts_s.at[i], parts_sem.at[i]) for i in range(4)
+    ]
+    pieces.append(pltpu.make_async_copy(got_ref, got_s, got_sem))
+    start_all(pieces)
     weights = copies_of(w_ref, w_s, w_sem, 4)
     for i in (3, 0, 1, 2):
         weights[i].start()
-    lefts = copies_of(left_s, left_ref, left_sem, 2)
-    rights = copies_of(right_s, right_ref, right_sem, 4)
+    rights = copies_of(right_s, saved_ref, right_sem, 4)
+    lefts = copies_of(left_s, saved_ref.at[4:6], left_sem, 2)
     mix_s[...] = m_ref[...].astype(F32).reshape(N_DEV * 16, 128)
     for cc in range(2):
         for rr in range(2):
@@ -289,20 +291,21 @@
                     ]
     u = u_s[...]
     ulow_s[...] = u.astype(BF16)
-    kept_u = pltpu.make_async_copy(ulow_s, u_ref, u_sem)
+    kept_u = pltpu.make_async_copy(ulow_s, saved_ref.at[6], u_sem)
     kept_u.start()
     left_s[0] = (u * inverse_rms(u)).astype(BF16)
     lefts[0].start()
+    wait_all(pieces)
     for shift in range(4):
         source = lax.rem(where_ref[0] + (4 - shift), 4) * 2
-        for grid_row, piece in ((source + mine, parts[shift].at[mine]), (source + (1 - mine), got_ref.at[shift])):
+        for grid_row, piece in ((source + mine, parts_s.at[shift]), (source + (1 - mine), got_s.at[shift])):
             for cc in range(2):
                 for rr in range(2):
                     at = pl.multiple_of(grid_row * 16 + (cc * LINE + rr * 128), 16)
                     right_s[3, pl.ds(at, 16), :] = piece[cc, rr * 16 : (rr + 1) * 16, :]
     rights[3].start()
     weights[3].wait()
-    gain = gain_row(keep_heads_ref, 1, 0, HEADS)
+    gain = gain_row(where_ref, 1, 0, HEADS)
     da_s[...] = (dot_nt(right_s[3], w_s[3]) * gain).astype(BF16)
     project(left_s[0], qkv_s, w_s, weights)
 
@@ -310,9 +313,9 @@
         probs = softmax(qkv_s[0, rows, lanes], qkv_s[1, rows, lanes])
         low = attention_backward(rows, lanes, qkv_s, da_s, probs, right_s)
         mixed = pick_halves(dot(low, qkv_s[2, rows, lanes]))
-        left_s[1, rows, lanes] = (mixed * gain_row(keep_heads_ref, 1, pair * 2, 2)).astype(BF16)
-
-    each_pair(visit)
+        left_s[1, rows, lanes] = (mixed * gain_row(where_ref, 1, pair * 2, 2)).astype(BF16)
+
+    each_pair(visit, 4)
     lefts[1].start()
     start_all(rights[:3])
     for cc in range(2):
@@ -329,17 +332,11 @@
     wait_all(lefts + rights + [kept_u])
 
 
-def col_output_kernel(where_ref, left_ref, right_ref, u_ref, w_ref, *refs):
-    keep_ref, send_ref, outs = refs[0], refs[1], refs[2:10]
-    left_s, right_s, ulow_s, wo_s, turned_s, out_s, keep_s, send_s = refs[10:18]
-    left_sem, right_sem, one_sem, half_sem = refs[18:]
-    lefts = copies_of(left_ref, left_s, left_sem, 2)
-    rights = copies_of(right_ref, right_s, right_sem, 4)
-    others = [
-        pltpu.make_async_copy(w_ref.at[3], wo_s, one_sem.at[0]),
-        pltpu.make_async_copy(u_ref, ulow_s, one_sem.at[1]),
-    ]
-    start_all(lefts + rights + others)
+def col_weights_kernel(where_ref, saved_ref, keep_ref, send_ref, *refs):
+    left_s, right_s, turned_s, keep_s, send_s, left_sem, right_sem, half_sem = refs
+    lefts = copies_of(saved_ref.at[4:6], left_s, left_sem, 2)
+    rights = copies_of(saved_ref, right_s, right_sem, 4)
+    start_all(lefts + rights)
     core = where_ref[4]
     for which in range(2):
         lefts[which].wait()
@@ -351,8 +348,19 @@
     weight_gradients(core, turned_s, right_s, keep_s)
     kept = pltpu.make_async_copy(keep_s, keep_ref, half_sem.at[1])
     kept.start()
-    wait_all(others)
-    out_s[...] = (ulow_s[...].astype(F32) + dot(left_s[1], wo_s[...])).astype(BF16)
+    wait_all([sent, kept])
+
+
+def col_output_kernel(where_ref, saved_ref, w_ref, *refs):
+    outs, (att_s, ulow_s, wo_s, out_s, sem) = refs[:8], refs[8:]
+    copies = [
+        pltpu.make_async_copy(saved_ref.at[5], att_s, sem.at[0]),
+        pltpu.make_async_copy(w_ref.at[3], wo_s, sem.at[1]),
+        pltpu.make_async_copy(saved_ref.at[6], ulow_s, sem.at[2]),
+    ]
+    start_all(copies)
+    wait_all(copies)
+    out_s[...] = (ulow_s[...].astype(F32) + dot(att_s[...], wo_s[...])).astype(BF16)
     me = where_ref[0] * 2 + where_ref[1]
     for shift in range(8):
         start = lax.rem(me + shift, 8) * 16
@@ -360,7 +368,6 @@
             for rr in range(2):
                 at = pl.multiple_of(start + (cc * LINE + rr * 128), 16)
                 outs[shift][cc, rr * 16 : (rr + 1) * 16, :] = out_s[pl.ds(at, 16), :]
-    wait_all([sent, kept])
 
 
 def tile_to_lines_kernel(where_ref, tile_ref, *refs):
@@ -529,8 +536,8 @@
 row_forward = call(
     row_forward_kernel,
     "svh",
-    "hhh",
-    (shape(N_DEV, 16, 128), shape(3, TOK, D), shape(2, TOK, D)),
+    "hh",
+    (shape(N_DEV, 16, 128), shape(5, TOK, D)),
     [
         MIX, pltpu.VMEM((N_DEV, 16, 128), BF16), token_scratch(3), token_scratch(2), *WEIGHTS,
         DMA((4,)), DMA((3,)), DMA((2,)),
@@ -540,11 +547,11 @@
     grant=50,
 )
 row_prepare = call(
-    row_prepare_kernel, "vv", "vv", (shape(8, TOK, LINE), shape(2, D, TOK)), [], ATTEND, 8 * MIB
+    row_prepare_kernel, "v", "vv", (shape(8, TOK, LINE), shape(2, D, TOK)), [], ATTEND, 8 * MIB
 )
 row_backward = call(
     row_backward_kernel,
-    "ssvhhhh",
+    "svhhhh",
     "hhh",
     (HALF, HALF, shape(4, TOK, D)),
     [
@@ -567,29 +574,39 @@
 )
 col_grad = call(
     col_kernel,
-    "ssvh" + "v" * 5,
-    "vhhh",
-    (shape(N_DEV, 16, 128), shape(2, TOK, D), shape(4, TOK, D), shape(TOK, D)),
+    "svh" + "h" * 5,
+    "vh",
+    (shape(N_DEV, 16, 128), shape(7, TOK, D)),
     [
         MIX, token_scratch(dtype=F32), token_scratch(), token_scratch(2), token_scratch(4),
-        token_scratch(3), token_scratch(), *WEIGHTS, DMA((2,)), DMA((4,)), DMA,
+        token_scratch(3), token_scratch(), WEIGHTS[0], pltpu.VMEM((4, 2, 32, D), BF16),
+        pltpu.VMEM((4, 2, 32, D), BF16), DMA((4,)), DMA((2,)), DMA((4,)), DMA, DMA((4,)), DMA,
     ],
     8 * MATMUL + 6 * ATTEND,
     8 * MIB,
-    grant=48,
+    grant=50,
+)
+col_weights = call(
+    col_weights_kernel,
+    "sh",
+    "hh",
+    (HALF, HALF),
+    [
+        token_scratch(2), token_scratch(4), pltpu.VMEM((2, D, TOK), BF16), HALF_S, HALF_S,
+        DMA((2,)), DMA((4,)), DMA((2,)),
+    ],
+    4 * MATMUL,
+    6 * MIB,
+    grant=52,
 )
 col_output = call(
     col_output_kernel,
-    "shhhh",
-    "hh" + "v" * 8,
-    (HALF, HALF) + (LINES,) * 8,
-    [
-        token_scratch(2), token_scratch(4), token_scratch(), pltpu.VMEM((D, D), BF16),
-        pltpu.VMEM((2, D, TOK), BF16), token_scratch(), HALF_S, HALF_S,
-        DMA((2,)), DMA((4,)), DMA((2,)), DMA((2,)),
-    ],
-    5 * MATMUL,
-    7 * MIB,
+    "shh",
+    "v" * 8,
+    (LINES,) * 8,
+    [token_scratch(), token_scratch(), pltpu.VMEM((D, D), BF16), token_scratch(), DMA((3,))],
+    MATMUL,
+    3 * MIB,
     grant=52,
 )
 tile_to_lines = call(tile_to_lines_kernel, "sv", "v" * 4, (PIECE,) * 4, [MIX_TILE], 0, MIB)
@@ -637,25 +654,27 @@
 
 
 def layer(latents, cotangent, w_row, w_col, keep_heads):
-    where = jnp.stack([lax.axis_index(name) for name in AXES]).astype(jnp.int32)
+    where = jnp.concatenate(
+        [jnp.stack([lax.axis_index(name) for name in AXES]), keep_heads.reshape(-1)]
+    ).astype(jnp.int32)
     rows_in = exchange(latents.reshape(16, 2, 16, D), COL)
     grad_pieces = tile_to_lines(where, cotangent)
     grad_parts = shifted(grad_pieces, "y")
     grad_pass = pass_low(where, *grad_parts)
     grad_pass = swap(grad_pass, "zl")
-    mid_send, qkv_row, left_row = row_forward(keep_heads, rows_in, w_row)
+    mid_send, saved_row = row_forward(where, rows_in, w_row)
     mid_lines = exchange(mid_send, BOTH)
-    probs_row, turned_row = row_prepare(qkv_row, left_row)
-    grad_send, left_col, right_col, u_col = col_grad(
-        where, keep_heads, mid_lines, w_col, *grad_parts, grad_pass
+    probs_row, turned_row = row_prepare(saved_row)
+    grad_send, saved_col = col_grad(
+        where, mid_lines, w_col, *grad_parts, grad_pass
     )
     grad_rows = exchange(grad_send, BOTH)
-    keep_col, send_col, *out_pieces = col_output(where, left_col, right_col, u_col, w_col)
+    keep_col, send_col = col_weights(where, saved_col)
     got_col = swap(send_col, "c")
     quarters = pair_sum(where, keep_col, got_col)
     quarters = shifted(quarters, "x")
     keep_row, send_row, right_row = row_backward(
-        where, keep_heads, grad_rows, qkv_row, turned_row, probs_row, w_row
+        where, grad_rows, saved_row, turned_row, probs_row, w_row
     )
     got_row = swap(send_row, "c")
     merged = merge(keep_row, got_row, *quarters)
@@ -667,6 +686,7 @@
     gin_core = pass_core(where, *gin_parts)
     gin_core = swap(gin_core, "c")
     grad_latents = join(where, *gin_parts, gin_core).reshape(32, 16, D)
+    out_pieces = col_output(where, saved_col, w_col)
     out_parts = shifted(out_pieces, ROW)
     output = lines_to_tile(where, *out_parts)
     other = swap(chunks, "c")

time: 244 us -> 238 us (0.975)
  blocking collectives: 82.7 us -> 59.6 us
  waiting for transfers between devices: 41.3 us -> 53.9 us
  starting transfers between devices: 46.3 us -> 56.5 us
  local copies, waits for them, and re-layouts: 15.5 us -> 7.79 us
    all_to_all x3 -> x2, blocking collectives: 82.7 us -> 59.6 us  [exchange(): return lax.all_to_all(values, axes, split_axis=0, concat_axis=0, tiled=True)]
    all_to_all x2 -> x3, waiting for transfers between devices: 0.01 us -> 11.5 us  [exchange(): return lax.all_to_all(values, axes, split_axis=0, concat_axis=0, tiled=True)]
    all_to_all x2 -> x3, starting transfers between devices: 14.4 us -> 24 us  [exchange(): return lax.all_to_all(values, axes, split_axis=0, concat_axis=0, tiled=True)]
    unnamed x64 -> x24, local copies, waits for them, and re-layouts: 15.4 us -> 6.95 us
    pallas_call x5 -> x6, Pallas kernels: 37.6 us -> 38.8 us  [the longest x1 13.2 us: layer(): col_grad(where, mid_lines, w_col, *grad_parts, grad_pass)]
  transfers between devices with their start and end apart: 27 -> 28, of which waited for: 14 -> 16; matrix products, arithmetic and copies ran while one was open for 0% -> 0% of each run, Pallas kernels for 12% -> 13%
where the time goes in v3:
time: 238 us; the launch traced here: 233 us
  blocking collectives  59.6 us (25%)
  starting transfers between devices  56.5 us (24%)
  Pallas kernels  54.7 us (23%)
  waiting for transfers between devices  53.9 us (23%)
  local copies, waits for them, and re-layouts  7.79 us (3%)
    all_to_all x2, blocking collectives, exchange(): return lax.all_to_all(values, axes, split_axis=0, concat_axis=0, tiled=True)  59.6 us
    ppermute x20, waiting for transfers between devices, shifted(): lax.ppermute(pieces[k], axes, [(i, (i + k) % n) for i in range(n)])  36.5 us
    all_to_all x3, starting transfers between devices, exchange(): return lax.all_to_all(values, axes, split_axis=0, concat_axis=0, tiled=True)  24 us
    ppermute x20, starting transfers between devices, shifted(): lax.ppermute(pieces[k], axes, [(i, (i + k) % n) for i in range(n)])  22.1 us
    pallas_call x1, Pallas kernels, layer(): col_grad(where, mid_lines, w_col, *grad_parts, grad_pass)  13.2 us
    all_to_all x3, waiting for transfers between devices, exchange(): return lax.all_to_all(values, axes, split_axis=0, concat_axis=0, tiled=True)  11.5 us
    ppermute x5, starting transfers between devices, swap(): return lax.ppermute(value, axis, [(0, 1), (1, 0)])  10.4 us
    pallas_call x1, Pallas kernels, layer(): row_backward(where, grad_rows, saved_row, turned_row, probs_row, w_row)  9.66 us
  transfers between devices with their start and end apart: 28, of which 16 were waited for; matrix products, arithmetic and copies ran while one was open for 0% of the time, Pallas kernels for 13%

profile of v3, /device:TPU:1, one launch (start us, length us, event | category | flops | bytes accessed | tf_op | source)
XLA Modules:
  0.0 233.5 jit_solution(12553868329972651482)
XLA Ops:
  0.6 9.1 %all-to-all-start = ((bf16[16,2,16,512]{3,2,1,0:T(8,128)(2,1)}), bf16[16,2,16,512]{3,2,1,0:T(8,128)(2,1)S(1)}, u32[]{:S(2)}, u32[]{:S(2)}) async-start(bf16[16,2,16,512]{3,2,1,0:T(8,128)(2,1)} %bitcast.12), calls=%async_computation | async-start | bytes 1048576 | tf_op jit(solution)/shard_map/all_to_all | solution.py:642
  9.8 0.8 reshape.23
  10.6 10.2 %all-to-all-done.x_ref = bf16[16,2,16,512]{3,2,1,0:T(8,128)(2,1)S(1)} async-done(((bf16[16,2,16,512]{3,2,1,0:T(8,128)(2,1)}), bf16[16,2,16,512]{3,2,1,0:T(8,128)(2,1)S(1)}, u32[]{:S(2)}, u32[]{:S(2)}) %all-to-all-start) | async-done | bytes 524320 | tf_op jit(solution)/shard_map/all_to_all | solution.py:642
  20.8 1.6 copy-done.1
  22.4 6.6 %shard_map.84 = (bf16[128,16,128]{2,1,0:T(8,128)(2,1)S(1)}, bf16[5,512,512]{2,1,0:T(8,128)(2,1)}) custom-call(s32[21]{0:T(128)S(1)} %concatenate.3.where_ref, bf16[16,2,16,512]{3,2,1,0:T(8,128)(2,1)S(1)} %all-to-all-done.x_ref, bf16[4,512,512]{2,1,0:T(8,128)(2,1)S(1)} %copy-done.1), custom_call_target="tpu_custom_call" | custom-call | flops 1342177280 | bytes 6291456 | tf_op jit(solution)/shard_map/pallas_call | solution.py:665
  29.0 0.8 copy-done.11
  29.8 6.4 %all-to-all-start.1 = ((bf16[128,16,128]{2,1,0:T(8,128)(2,1)}), bf16[128,16,128]{2,1,0:T(8,128)(2,1)}, u32[]{:S(2)}, u32[]{:S(2)}) async-start(bf16[128,16,128]{2,1,0:T(8,128)(2,1)} %copy-done.11), calls=%async_computation.1 | async-start | bytes 1048576 | tf_op jit(solution)/shard_map/all_to_all | solution.py:642
  36.2 1.2 shard_map.85
  37.5 1.4 collective-permute-start
  38.9 2.5 %collective-permute-start.1 = (bf16[2,2,32,512]{3,2,1,0:T(8,128)(2,1)S(1)}, bf16[2,2,32,512]{3,2,1,0:T(8,128)(2,1)S(1)}, u32[]{:S(2)}, u32[]{:S(2)}) collective-permute-start(bf16[2,2,32,512]{3,2,1,0:T(8,128)(2,1)S(1)} %get-tuple-element.46), channel_id=1, source_target_pairs={{0,64},{32,96},{64,0},{96,32},{1,65},{33,97},{65,1},{97,33},{2,66}... | collective-permute-start | bytes 393224 | tf_op jit(solution)/shard_map/ppermute | solution.py:648
  41.3 1.1 collective-permute-start.2
  42.5 5.2 %collective-permute-done.refs_1_ = bf16[2,2,32,512]{3,2,1,0:T(8,128)(2,1)S(1)} collective-permute-done((bf16[2,2,32,512]{3,2,1,0:T(8,128)(2,1)S(1)}, bf16[2,2,32,512]{3,2,1,0:T(8,128)(2,1)S(1)}, u32[]{:S(2)}, u32[]{:S(2)}) %collective-permute-start) | collective-permute-done | bytes 131104 | tf_op jit(solution)/shard_map/ppermute | solution.py:648
  47.7 3.5 %collective-permute-done.1.refs_2_ = bf16[2,2,32,512]{3,2,1,0:T(8,128)(2,1)S(1)} collective-permute-done((bf16[2,2,32,512]{3,2,1,0:T(8,128)(2,1)S(1)}, bf16[2,2,32,512]{3,2,1,0:T(8,128)(2,1)S(1)}, u32[]{:S(2)}, u32[]{:S(2)}) %collective-permute-start.1) | collective-permute-done | bytes 131104 | tf_op jit(solution)/shard_map/ppermute | solution.py:648
  51.2 0.6 shard_map.86
  51.8 1.7 collective-permute-start.3
  53.5 5.9 %collective-permute-done.3.refs_4_ = bf16[4,2,32,512]{3,2,1,0:T(8,128)(2,1)S(1)} collective-permute-done((bf16[4,2,32,512]{3,2,1,0:T(8,128)(2,1)S(1)}, bf16[4,2,32,512]{3,2,1,0:T(8,128)(2,1)S(1)}, u32[]{:S(2)}, u32[]{:S(2)}) %collective-permute-start.3) | collective-permute-done | bytes 262176 | tf_op jit(solution)/shard_map/ppermute | solution.py:653
  59.4 13.2 %shard_map.87 = (bf16[128,16,128]{2,1,0:T(8,128)(2,1)}, bf16[7,512,512]{2,1,0:T(8,128)(2,1)}) custom-call(s32[21]{0:T(128)S(1)} %concatenate.3.where_ref, bf16[128,16,128]{2,1,0:T(8,128)(2,1)} %all-to-all-done.1.m_ref, bf16[4,512,512]{2,1,0:T(8,128)(2,1)S(1)} %copy-done.3, bf16[2,2,32,512]{3,2,1,0:T(8,128)(2,1)S(1)} %get-tuple-element.44.refs_0_, ...), custom_call_target="tpu_custom_call" | custom-call | flops 2952790016 | bytes 8388608 | tf_op jit(solution)/shard_map/pallas_call | solution.py:668
  72.6 8.4 %all-to-all-start.2 = ((bf16[128,16,128]{2,1,0:T(8,128)(2,1)}), bf16[128,16,128]{2,1,0:T(8,128)(2,1)}, u32[]{:S(2)}, u32[]{:S(2)}) async-start(bf16[128,16,128]{2,1,0:T(8,128)(2,1)} %get-tuple-element.57), calls=%async_computation.2 | async-start | bytes 1048576 | tf_op jit(solution)/shard_map/all_to_all | solution.py:642
  81.1 4.4 %shard_map.95 = (bf16[2,512,512]{2,1,0:T(8,128)(2,1)S(1)}, bf16[2,512,512]{2,1,0:T(8,128)(2,1)}) custom-call(s32[21]{0:T(128)S(1)} %concatenate.3.where_ref, bf16[7,512,512]{2,1,0:T(8,128)(2,1)} %get-tuple-element.48.saved_ref), custom_call_target="tpu_custom_call" | custom-call | flops 1073741824 | bytes 6291456 | tf_op jit(solution)/shard_map/pallas_call | solution.py:672
  85.5 1.0 copy-done.8
  86.5 1.1 collective-permute-start.20
  87.6 2.4 %shard_map.90 = (bf16[8,512,256]{2,1,0:T(8,128)(2,1)S(1)}, bf16[2,512,512]{2,1,0:T(8,128)(2,1)S(1)}) custom-call(bf16[5,512,512]{2,1,0:T(8,128)(2,1)S(1)} %copy-done), custom_call_target="tpu_custom_call" | custom-call | flops 134217728 | bytes 8388608 | tf_op jit(solution)/shard_map/pallas_call | solution.py:667
  90.1 1.3 copy-done.5
  91.4 1.0 copy-done.6
  92.4 1.3 all-to-all-done.2.g_ref
  93.7 1.2 copy-done.7
  95.0 9.7 %shard_map.91 = (bf16[2,512,512]{2,1,0:T(8,128)(2,1)S(1)}, bf16[2,512,512]{2,1,0:T(8,128)(2,1)S(1)}, bf16[4,512,512]{2,1,0:T(8,128)(2,1)}) custom-call(s32[21]{0:T(128)S(1)} %concatenate.3.where_ref, bf16[128,16,128]{2,1,0:T(8,128)(2,1)} %all-to-all-done.2.g_ref, bf16[5,512,512]{2,1,0:T(8,128)(2,1)} %get-tuple-element.58.saved_ref.qkv_ref, ...), custom_call_target="tpu_custom_call" | custom-call | flops 2013265920 | bytes 12582912 | tf_op jit(solution)/shard_map/pallas_call | solution.py:676
  104.6 1.5 collective-permute-start.19
  106.1 1.9 shard_map.96
  108.0 0.4 collective-permute-start.21
  108.4 1.9 collective-permute-start.22
  110.3 0.9 collective-permute-start.23
  111.2 6.4 %collective-permute-done.21.refs_1_ = bf16[256,512]{1,0:T(8,128)(2,1)S(1)} collective-permute-done((bf16[256,512]{1,0:T(8,128)(2,1)S(1)}, bf16[256,512]{1,0:T(8,128)(2,1)S(1)}, u32[]{:S(2)}, u32[]{:S(2)}) %collective-permute-start.21) | collective-permute-done | bytes 262176 | tf_op jit(solution)/shard_map/ppermute | solution.py:648
  117.6 4.7 %collective-permute-done.22.refs_2_ = bf16[256,512]{1,0:T(8,128)(2,1)S(1)} collective-permute-done((bf16[256,512]{1,0:T(8,128)(2,1)S(1)}, bf16[256,512]{1,0:T(8,128)(2,1)S(1)}, u32[]{:S(2)}, u32[]{:S(2)}) %collective-permute-start.22) | collective-permute-done | bytes 262176 | tf_op jit(solution)/shard_map/ppermute | solution.py:648
  122.3 0.8 collective-permute-done.23.refs_3_
  123.1 0.4 shard_map.97
  123.5 27.2 %all_to_all.25.both_ref = bf16[64,80,128]{2,1,0:T(8,128)(2,1)S(1)} all-to-all(bf16[64,80,128]{2,1,0:T(8,128)(2,1)S(1)} %shard_map.97), channel_id=1, replica_groups=mesh['y'=4,'zl'=2,'zh'=2,'x'=4,'c'=2] {'y','zl','zh','x'}, dimensions={0} | all-to-all | bytes 2621440 | tf_op jit(solution)/shard_map/all_to_all | solution.py:642
  150.7 0.4 shard_map.98
  151.1 32.4 %all_to_all.26.chunks_ref = bf16[64,128,128]{2,1,0:T(8,128)(2,1)S(1)} all-to-all(bf16[64,128,128]{2,1,0:T(8,128)(2,1)S(1)} %shard_map.98), channel_id=1, replica_groups=mesh['y'=4,'zl'=2,'zh'=2,'x'=4,'c'=2] {'y','zl','zh','x'}, dimensions={0} | all-to-all | bytes 4194304 | tf_op jit(solution)/shard_map/all_to_all | solution.py:642
  183.5 3.3 %collective-permute-start.24 = (bf16[64,128,128]{2,1,0:T(8,128)(2,1)S(1)}, bf16[64,128,128]{2,1,0:T(8,128)(2,1)S(1)}, u32[]{:S(2)}, u32[]{:S(2)}) collective-permute-start(bf16[64,128,128]{2,1,0:T(8,128)(2,1)S(1)} %all_to_all.26.chunks_ref), channel_id=1, source_target_pairs={{0,1},{1,0},{2,3},{3,2},{4,5},{5,4},{6,7},{7,6},{8,9},{9,8},{10,11... | collective-permute-start | bytes 6291464 | tf_op jit(solution)/shard_map/ppermute | solution.py:653
  186.8 1.9 shard_map.92
  188.9 2.2 collective-permute-start.12
  191.0 1.5 collective-permute-start.13
  192.6 2.4 %collective-permute-start.14 = (bf16[2,2,16,512]{3,2,1,0:T(8,128)(2,1)S(1)}, bf16[2,2,16,512]{3,2,1,0:T(8,128)(2,1)S(1)}, u32[]{:S(2)}, u32[]{:S(2)}) collective-permute-start(bf16[2,2,16,512]{3,2,1,0:T(8,128)(2,1)S(1)} %get-tuple-element.66), channel_id=1, source_target_pairs={{0,8},{2,10},{4,12},{6,14},{8,0},{10,2},{12,4},{14,6},{1,9},{3,11}... | collective-permute-start | bytes 196616 | tf_op jit(solution)/shard_map/ppermute | solution.py:648
  194.9 2.9 %collective-permute-done.11.refs_1_ = bf16[2,2,16,512]{3,2,1,0:T(8,128)(2,1)S(1)} collective-permute-done((bf16[2,2,16,512]{3,2,1,0:T(8,128)(2,1)S(1)}, bf16[2,2,16,512]{3,2,1,0:T(8,128)(2,1)S(1)}, u32[]{:S(2)}, u32[]{:S(2)}) %collective-permute-start.11) | collective-permute-done | bytes 65568 | tf_op jit(solution)/shard_map/ppermute | solution.py:648
  197.9 1.6 collective-permute-start.16
  199.5 2.6 %collective-permute-start.17 = (bf16[2,2,16,512]{3,2,1,0:T(8,128)(2,1)S(1)}, bf16[2,2,16,512]{3,2,1,0:T(8,128)(2,1)S(1)}, u32[]{:S(2)}, u32[]{:S(2)}) collective-permute-start(bf16[2,2,16,512]{3,2,1,0:T(8,128)(2,1)S(1)} %get-tuple-element.69), channel_id=1, source_target_pairs={{0,14},{2,0},{4,2},{6,4},{8,6},{10,8},{12,10},{14,12},{1,15},{3,1}... | collective-permute-start | bytes 196616 | tf_op jit(solution)/shard_map/ppermute | solution.py:648
  202.1 0.8 collective-permute-done.15.refs_5_
  202.9 1.8 collective-permute-done.17.refs_7_
  204.7 0.6 shard_map.93
  205.3 2.7 %collective-permute-start.18 = (bf16[8,2,16,512]{3,2,1,0:T(8,128)(2,1)S(1)}, bf16[8,2,16,512]{3,2,1,0:T(8,128)(2,1)S(1)}, u32[]{:S(2)}, u32[]{:S(2)}) collective-permute-start(bf16[8,2,16,512]{3,2,1,0:T(8,128)(2,1)S(1)} %shard_map.93), channel_id=1, source_target_pairs={{0,1},{1,0},{2,3},{3,2},{4,5},{5,4},{6,7},{7,6},{8,9},{9,8},{10,11... | collective-permute-start | bytes 786440 | tf_op jit(solution)/shard_map/ppermute | solution.py:653
  208.0 2.4 %shard_map.88 = (bf16[2,32,512]{2,1,0:T(8,128)(2,1)S(1)}, bf16[2,32,512]{2,1,0:T(8,128)(2,1)S(1)}, bf16[2,32,512]{2,1,0:T(8,128)(2,1)S(1)}, bf16[2,32,512]{2,1,0...) custom-call(s32[21]{0:T(128)S(1)} %concatenate.3.where_ref, ...), custom_call_target="tpu_custom_call" | custom-call | flops 268435456 | bytes 3145728 | tf_op jit(solution)/shard_map/pallas_call | solution.py:689
  210.7 1.9 collective-permute-start.6
  212.6 3.7 %collective-permute-done.4.refs_1_ = bf16[2,32,512]{2,1,0:T(8,128)(2,1)S(1)} collective-permute-done((bf16[2,32,512]{2,1,0:T(8,128)(2,1)S(1)}, bf16[2,32,512]{2,1,0:T(8,128)(2,1)S(1)}, u32[]{:S(2)}, u32[]{:S(2)}) %collective-permute-start.4) | collective-permute-done | bytes 65568 | tf_op jit(solution)/shard_map/ppermute | solution.py:648
  216.2 0.8 collective-permute-start.8
  217.0 1.2 collective-permute-done.6.refs_3_
  218.2 0.6 collective-permute-start.9
  218.9 2.0 collective-permute-done.7.refs_4_
  220.9 0.5 collective-permute-done.9.refs_6_
  221.4 2.9 %collective-permute-done.10.refs_7_ = bf16[2,32,512]{2,1,0:T(8,128)(2,1)S(1)} collective-permute-done((bf16[2,32,512]{2,1,0:T(8,128)(2,1)S(1)}, bf16[2,32,512]{2,1,0:T(8,128)(2,1)S(1)}, u32[]{:S(2)}, u32[]{:S(2)}) %collective-permute-start.10) | collective-permute-done | bytes 65568 | tf_op jit(solution)/shard_map/ppermute | solution.py:648
  224.3 2.3 shard_map.89
  226.5 1.4 shard_map.94
  227.9 2.7 %widen.2 = (f32[2,1024,512]{2,1,0:T(8,128)}, f32[2,4,256,512]{3,2,1,0:T(8,128)}) custom-call(s32[21]{0:T(128)S(1)} %concatenate.3.where_ref, bf16[64,128,128]{2,1,0:T(8,128)(2,1)S(1)} %all_to_all.26.chunks_ref), custom_call_target="tpu_custom_call" | custom-call | bytes 6291456 | tf_op jit(solution)/shard_map/widen/pallas_call | solution.py:626
  230.6 2.7 %widen.3 = (f32[2,1024,512]{2,1,0:T(8,128)}, f32[2,4,256,512]{3,2,1,0:T(8,128)}) custom-call(s32[21]{0:T(128)S(1)} %concatenate.3.where_ref, bf16[64,128,128]{2,1,0:T(8,128)(2,1)S(1)} %collective-permute-done.24.chunks_ref, f32[2,1024,512]{2,1,0:T(8,128)} %get-tuple-element.78.refs_0_, ...), custom_call_target="tpu_custom_call", output_to_operand_aliasing={{0}: (2, {}), {1}: (3, {})} | custom-call | bytes 6291456 | tf_op jit(solution)/shard_map/widen/pallas_call | solution.py:626
  (37 shorter events, 0.5 us)
Async XLA Ops:
  0.6 20.1 %all-to-all-start = ((bf16[16,2,16,512]{3,2,1,0:T(8,128)(2,1)}), bf16[16,2,16,512]{3,2,1,0:T(8,128)(2,1)S(1)}, u32[]{:S(2)}, u32[]{:S(2)}) async-start(bf16[16,2,16,512]{3,2,1,0:T(8,128)(2,1)} %bitcast.12), calls=%async_computation | async-start | bytes 1048576 | tf_op jit(solution)/shard_map/all_to_all | solution.py:642
  20.8 1.6 copy-start.1
  22.3 13.9 %copy-start.10 = (bf16[32,16,512]{2,1,0:T(8,128)(2,1)S(1)}, bf16[32,16,512]{2,1,0:T(8,128)(2,1)}, u32[]{:S(2)}) copy-start(bf16[32,16,512]{2,1,0:T(8,128)(2,1)} %tile_ref.1) | copy-start | bytes 1572868
  29.0 0.8 copy-start.11
  29.8 29.6 %copy-start.3 = (bf16[4,512,512]{2,1,0:T(8,128)(2,1)S(1)}, bf16[4,512,512]{2,1,0:T(8,128)(2,1)}, u32[]{:S(2)}) copy-start(bf16[4,512,512]{2,1,0:T(8,128)(2,1)} %w_ref.7) | copy-start | bytes 6291460
  29.8 29.6 %all-to-all-start.1 = ((bf16[128,16,128]{2,1,0:T(8,128)(2,1)}), bf16[128,16,128]{2,1,0:T(8,128)(2,1)}, u32[]{:S(2)}, u32[]{:S(2)}) async-start(bf16[128,16,128]{2,1,0:T(8,128)(2,1)} %copy-done.11), calls=%async_computation.1 | async-start | bytes 1048576 | tf_op jit(solution)/shard_map/all_to_all | solution.py:642
  37.5 10.2 %collective-permute-start = (bf16[2,2,32,512]{3,2,1,0:T(8,128)(2,1)S(1)}, bf16[2,2,32,512]{3,2,1,0:T(8,128)(2,1)S(1)}, u32[]{:S(2)}, u32[]{:S(2)}) collective-permute-start(bf16[2,2,32,512]{3,2,1,0:T(8,128)(2,1)S(1)} %get-tuple-element.45), channel_id=1, source_target_pairs={{0,32},{32,64},{64,96},{96,0},{1,33},{33,65},{65,97},{97,1},{2,34}... | collective-permute-start | bytes 393224 | tf_op jit(solution)/shard_map/ppermute | solution.py:648
  38.9 12.3 %collective-permute-start.1 = (bf16[2,2,32,512]{3,2,1,0:T(8,128)(2,1)S(1)}, bf16[2,2,32,512]{3,2,1,0:T(8,128)(2,1)S(1)}, u32[]{:S(2)}, u32[]{:S(2)}) collective-permute-start(bf16[2,2,32,512]{3,2,1,0:T(8,128)(2,1)S(1)} %get-tuple-element.46), channel_id=1, source_target_pairs={{0,64},{32,96},{64,0},{96,32},{1,65},{33,97},{65,1},{97,33},{2,66}... | collective-permute-start | bytes 393224 | tf_op jit(solution)/shard_map/ppermute | solution.py:648
  41.3 9.8 %collective-permute-start.2 = (bf16[2,2,32,512]{3,2,1,0:T(8,128)(2,1)S(1)}, bf16[2,2,32,512]{3,2,1,0:T(8,128)(2,1)S(1)}, u32[]{:S(2)}, u32[]{:S(2)}) collective-permute-start(bf16[2,2,32,512]{3,2,1,0:T(8,128)(2,1)S(1)} %get-tuple-element.47), channel_id=1, source_target_pairs={{0,96},{32,0},{64,32},{96,64},{1,97},{33,1},{65,33},{97,65},{2,98}... | collective-permute-start | bytes 393224 | tf_op jit(solution)/shard_map/ppermute | solution.py:648
  51.8 7.6 %collective-permute-start.3 = (bf16[4,2,32,512]{3,2,1,0:T(8,128)(2,1)S(1)}, bf16[4,2,32,512]{3,2,1,0:T(8,128)(2,1)S(1)}, u32[]{:S(2)}, u32[]{:S(2)}) collective-permute-start(bf16[4,2,32,512]{3,2,1,0:T(8,128)(2,1)S(1)} %shard_map.86), channel_id=1, source_target_pairs={{0,16},{16,0},{1,17},{17,1},{2,18},{18,2},{3,19},{19,3},{4,20},{20... | collective-permute-start | bytes 786440 | tf_op jit(solution)/shard_map/ppermute | solution.py:653
  72.6 21.1 %all-to-all-start.2 = ((bf16[128,16,128]{2,1,0:T(8,128)(2,1)}), bf16[128,16,128]{2,1,0:T(8,128)(2,1)}, u32[]{:S(2)}, u32[]{:S(2)}) async-start(bf16[128,16,128]{2,1,0:T(8,128)(2,1)} %get-tuple-element.57), calls=%async_computation.2 | async-start | bytes 1048576 | tf_op jit(solution)/shard_map/all_to_all | solution.py:642
  81.0 6.6 %copy-start = (bf16[5,512,512]{2,1,0:T(8,128)(2,1)S(1)}, bf16[5,512,512]{2,1,0:T(8,128)(2,1)}, u32[]{:S(2)}) copy-start(bf16[5,512,512]{2,1,0:T(8,128)(2,1)} %get-tuple-element.58.saved_ref.qkv_ref) | copy-start | bytes 7864324
  85.5 1.0 copy-start.8
  86.5 19.7 %collective-permute-start.20 = (bf16[2,512,512]{2,1,0:T(8,128)(2,1)}, bf16[2,512,512]{2,1,0:T(8,128)(2,1)}, u32[]{:S(2)}, u32[]{:S(2)}) collective-permute-start(bf16[2,512,512]{2,1,0:T(8,128)(2,1)} %get-tuple-element.73), channel_id=1, source_target_pairs={{0,1},{1,0},{2,3},{3,2},{4,5},{5,4},{6,7},{7,6},{8,9},{9,8},{10,11... | collective-permute-start | bytes 3145736 | tf_op jit(solution)/shard_map/ppermute | solution.py:653
  90.1 1.4 copy-start.5
  91.4 1.0 copy-start.6
  93.7 1.2 copy-start.7
  95.0 11.2 %copy-start.9 = (bf16[2,512,512]{2,1,0:T(8,128)(2,1)S(1)}, bf16[2,512,512]{2,1,0:T(8,128)(2,1)}, u32[]{:S(2)}) copy-start(bf16[2,512,512]{2,1,0:T(8,128)(2,1)} %copy-done.8) | copy-start | bytes 3145732
  104.6 18.4 %collective-permute-start.19 = (bf16[2,512,512]{2,1,0:T(8,128)(2,1)S(1)}, bf16[2,512,512]{2,1,0:T(8,128)(2,1)S(1)}, u32[]{:S(2)}, u32[]{:S(2)}) collective-permute-start(bf16[2,512,512]{2,1,0:T(8,128)(2,1)S(1)} %get-tuple-element.71), channel_id=1, source_target_pairs={{0,1},{1,0},{2,3},{3,2},{4,5},{5,4},{6,7},{7,6},{8,9},{9,8},{10,11... | collective-permute-start | bytes 3145736 | tf_op jit(solution)/shard_map/ppermute | solution.py:653
  108.0 9.6 %collective-permute-start.21 = (bf16[256,512]{1,0:T(8,128)(2,1)S(1)}, bf16[256,512]{1,0:T(8,128)(2,1)S(1)}, u32[]{:S(2)}, u32[]{:S(2)}) collective-permute-start(bf16[256,512]{1,0:T(8,128)(2,1)S(1)} %get-tuple-element.75), channel_id=1, source_target_pairs={{0,2},{2,4},{4,6},{6,0},{1,3},{3,5},{5,7},{7,1},{8,10},{10,12},{12... | collective-permute-start | bytes 786440 | tf_op jit(solution)/shard_map/ppermute | solution.py:648
  108.4 13.9 %collective-permute-start.22 = (bf16[256,512]{1,0:T(8,128)(2,1)S(1)}, bf16[256,512]{1,0:T(8,128)(2,1)S(1)}, u32[]{:S(2)}, u32[]{:S(2)}) collective-permute-start(bf16[256,512]{1,0:T(8,128)(2,1)S(1)} %get-tuple-element.76), channel_id=1, source_target_pairs={{0,4},{2,6},{4,0},{6,2},{1,5},{3,7},{5,1},{7,3},{8,12},{10,14},{12... | collective-permute-start | bytes 786440 | tf_op jit(solution)/shard_map/ppermute | solution.py:648
  110.3 12.8 %collective-permute-start.23 = (bf16[256,512]{1,0:T(8,128)(2,1)S(1)}, bf16[256,512]{1,0:T(8,128)(2,1)S(1)}, u32[]{:S(2)}, u32[]{:S(2)}) collective-permute-start(bf16[256,512]{1,0:T(8,128)(2,1)S(1)} %get-tuple-element.77), channel_id=1, source_target_pairs={{0,6},{2,0},{4,2},{6,4},{1,7},{3,1},{5,3},{7,5},{8,14},{10,8},{12,... | collective-permute-start | bytes 786440 | tf_op jit(solution)/shard_map/ppermute | solution.py:648
  151.1 35.8 %copy-start.2 = (bf16[4,512,512]{2,1,0:T(8,128)(2,1)S(1)}, bf16[4,512,512]{2,1,0:T(8,128)(2,1)}, u32[]{:S(2)}) copy-start(bf16[4,512,512]{2,1,0:T(8,128)(2,1)} %w_ref.9) | copy-start | bytes 6291460
  151.1 35.7 %copy-start.4 = (bf16[4,512,512]{2,1,0:T(8,128)(2,1)S(1)}, bf16[4,512,512]{2,1,0:T(8,128)(2,1)}, u32[]{:S(2)}) copy-start(bf16[4,512,512]{2,1,0:T(8,128)(2,1)} %get-tuple-element.61.right_ref) | copy-start | bytes 6291460
  183.5 47.1 %collective-permute-start.24 = (bf16[64,128,128]{2,1,0:T(8,128)(2,1)S(1)}, bf16[64,128,128]{2,1,0:T(8,128)(2,1)S(1)}, u32[]{:S(2)}, u32[]{:S(2)}) collective-permute-start(bf16[64,128,128]{2,1,0:T(8,128)(2,1)S(1)} %all_to_all.26.chunks_ref), channel_id=1, source_target_pairs={{0,1},{1,0},{2,3},{3,2},{4,5},{5,4},{6,7},{7,6},{8,9},{9,8},{10,11... | collective-permute-start | bytes 6291464 | tf_op jit(solution)/shard_map/ppermute | solution.py:653
  188.8 9.1 %collective-permute-start.11 = (bf16[2,2,16,512]{3,2,1,0:T(8,128)(2,1)S(1)}, bf16[2,2,16,512]{3,2,1,0:T(8,128)(2,1)S(1)}, u32[]{:S(2)}, u32[]{:S(2)}) collective-permute-start(bf16[2,2,16,512]{3,2,1,0:T(8,128)(2,1)S(1)} %get-tuple-element.63), channel_id=1, source_target_pairs={{0,2},{2,4},{4,6},{6,8},{8,10},{10,12},{12,14},{14,0},{1,3},{3,5},... | collective-permute-start | bytes 196616 | tf_op jit(solution)/shard_map/ppermute | solution.py:648
  188.9 9.0 %collective-permute-start.12 = (bf16[2,2,16,512]{3,2,1,0:T(8,128)(2,1)S(1)}, bf16[2,2,16,512]{3,2,1,0:T(8,128)(2,1)S(1)}, u32[]{:S(2)}, u32[]{:S(2)}) collective-permute-start(bf16[2,2,16,512]{3,2,1,0:T(8,128)(2,1)S(1)} %get-tuple-element.64), channel_id=1, source_target_pairs={{0,4},{2,6},{4,8},{6,10},{8,12},{10,14},{12,0},{14,2},{1,5},{3,7},... | collective-permute-start | bytes 196616 | tf_op jit(solution)/shard_map/ppermute | solution.py:648
  191.0 8.5 %collective-permute-start.13 = (bf16[2,2,16,512]{3,2,1,0:T(8,128)(2,1)S(1)}, bf16[2,2,16,512]{3,2,1,0:T(8,128)(2,1)S(1)}, u32[]{:S(2)}, u32[]{:S(2)}) collective-permute-start(bf16[2,2,16,512]{3,2,1,0:T(8,128)(2,1)S(1)} %get-tuple-element.65), channel_id=1, source_target_pairs={{0,6},{2,8},{4,10},{6,12},{8,14},{10,0},{12,2},{14,4},{1,7},{3,9},... | collective-permute-start | bytes 196616 | tf_op jit(solution)/shard_map/ppermute | solution.py:648
  192.6 9.5 %collective-permute-start.14 = (bf16[2,2,16,512]{3,2,1,0:T(8,128)(2,1)S(1)}, bf16[2,2,16,512]{3,2,1,0:T(8,128)(2,1)S(1)}, u32[]{:S(2)}, u32[]{:S(2)}) collective-permute-start(bf16[2,2,16,512]{3,2,1,0:T(8,128)(2,1)S(1)} %get-tuple-element.66), channel_id=1, source_target_pairs={{0,8},{2,10},{4,12},{6,14},{8,0},{10,2},{12,4},{14,6},{1,9},{3,11}... | collective-permute-start | bytes 196616 | tf_op jit(solution)/shard_map/ppermute | solution.py:648
  197.9 5.0 %collective-permute-start.15 = (bf16[2,2,16,512]{3,2,1,0:T(8,128)(2,1)S(1)}, bf16[2,2,16,512]{3,2,1,0:T(8,128)(2,1)S(1)}, u32[]{:S(2)}, u32[]{:S(2)}) collective-permute-start(bf16[2,2,16,512]{3,2,1,0:T(8,128)(2,1)S(1)} %get-tuple-element.67), channel_id=1, source_target_pairs={{0,10},{2,12},{4,14},{6,0},{8,2},{10,4},{12,6},{14,8},{1,11},{3,13... | collective-permute-start | bytes 196616 | tf_op jit(solution)/shard_map/ppermute | solution.py:648
  197.9 5.0 %collective-permute-start.16 = (bf16[2,2,16,512]{3,2,1,0:T(8,128)(2,1)S(1)}, bf16[2,2,16,512]{3,2,1,0:T(8,128)(2,1)S(1)}, u32[]{:S(2)}, u32[]{:S(2)}) collective-permute-start(bf16[2,2,16,512]{3,2,1,0:T(8,128)(2,1)S(1)} %get-tuple-element.68), channel_id=1, source_target_pairs={{0,12},{2,14},{4,0},{6,2},{8,4},{10,6},{12,8},{14,10},{1,13},{3,15... | collective-permute-start | bytes 196616 | tf_op jit(solution)/shard_map/ppermute | solution.py:648
  199.5 5.2 %collective-permute-start.17 = (bf16[2,2,16,512]{3,2,1,0:T(8,128)(2,1)S(1)}, bf16[2,2,16,512]{3,2,1,0:T(8,128)(2,1)S(1)}, u32[]{:S(2)}, u32[]{:S(2)}) collective-permute-start(bf16[2,2,16,512]{3,2,1,0:T(8,128)(2,1)S(1)} %get-tuple-element.69), channel_id=1, source_target_pairs={{0,14},{2,0},{4,2},{6,4},{8,6},{10,8},{12,10},{14,12},{1,15},{3,1}... | collective-permute-start | bytes 196616 | tf_op jit(solution)/shard_map/ppermute | solution.py:648
  205.3 21.2 %collective-permute-start.18 = (bf16[8,2,16,512]{3,2,1,0:T(8,128)(2,1)S(1)}, bf16[8,2,16,512]{3,2,1,0:T(8,128)(2,1)S(1)}, u32[]{:S(2)}, u32[]{:S(2)}) collective-permute-start(bf16[8,2,16,512]{3,2,1,0:T(8,128)(2,1)S(1)} %shard_map.93), channel_id=1, source_target_pairs={{0,1},{1,0},{2,3},{3,2},{4,5},{5,4},{6,7},{7,6},{8,9},{9,8},{10,11... | collective-permute-start | bytes 786440 | tf_op jit(solution)/shard_map/ppermute | solution.py:653
  210.4 5.8 %collective-permute-start.4 = (bf16[2,32,512]{2,1,0:T(8,128)(2,1)S(1)}, bf16[2,32,512]{2,1,0:T(8,128)(2,1)S(1)}, u32[]{:S(2)}, u32[]{:S(2)}) collective-permute-start(bf16[2,32,512]{2,1,0:T(8,128)(2,1)S(1)} %get-tuple-element.50), channel_id=1, source_target_pairs={{0,16},{16,32},{32,48},{48,64},{64,80},{80,96},{96,112},{112,0},{1... | collective-permute-start | bytes 196616 | tf_op jit(solution)/shard_map/ppermute | solution.py:648
  210.7 5.5 %collective-permute-start.5 = (bf16[2,32,512]{2,1,0:T(8,128)(2,1)S(1)}, bf16[2,32,512]{2,1,0:T(8,128)(2,1)S(1)}, u32[]{:S(2)}, u32[]{:S(2)}) collective-permute-start(bf16[2,32,512]{2,1,0:T(8,128)(2,1)S(1)} %get-tuple-element.51), channel_id=1, source_target_pairs={{0,32},{16,48},{32,64},{48,80},{64,96},{80,112},{96,0},{112,16},{1... | collective-permute-start | bytes 196616 | tf_op jit(solution)/shard_map/ppermute | solution.py:648
  210.7 7.6 %collective-permute-start.6 = (bf16[2,32,512]{2,1,0:T(8,128)(2,1)S(1)}, bf16[2,32,512]{2,1,0:T(8,128)(2,1)S(1)}, u32[]{:S(2)}, u32[]{:S(2)}) collective-permute-start(bf16[2,32,512]{2,1,0:T(8,128)(2,1)S(1)} %get-tuple-element.52), channel_id=1, source_target_pairs={{0,48},{16,64},{32,80},{48,96},{64,112},{80,0},{96,16},{112,32},{1... | collective-permute-start | bytes 196616 | tf_op jit(solution)/shard_map/ppermute | solution.py:648
  216.2 4.6 %collective-permute-start.7 = (bf16[2,32,512]{2,1,0:T(8,128)(2,1)S(1)}, bf16[2,32,512]{2,1,0:T(8,128)(2,1)S(1)}, u32[]{:S(2)}, u32[]{:S(2)}) collective-permute-start(bf16[2,32,512]{2,1,0:T(8,128)(2,1)S(1)} %get-tuple-element.53), channel_id=1, source_target_pairs={{0,64},{16,80},{32,96},{48,112},{64,0},{80,16},{96,32},{112,48},{1... | collective-permute-start | bytes 196616 | tf_op jit(solution)/shard_map/ppermute | solution.py:648
  216.2 4.6 %collective-permute-start.8 = (bf16[2,32,512]{2,1,0:T(8,128)(2,1)S(1)}, bf16[2,32,512]{2,1,0:T(8,128)(2,1)S(1)}, u32[]{:S(2)}, u32[]{:S(2)}) collective-permute-start(bf16[2,32,512]{2,1,0:T(8,128)(2,1)S(1)} %get-tuple-element.54), channel_id=1, source_target_pairs={{0,80},{16,96},{32,112},{48,0},{64,16},{80,32},{96,48},{112,64},{1... | collective-permute-start | bytes 196616 | tf_op jit(solution)/shard_map/ppermute | solution.py:648
  218.2 3.1 %collective-permute-start.9 = (bf16[2,32,512]{2,1,0:T(8,128)(2,1)S(1)}, bf16[2,32,512]{2,1,0:T(8,128)(2,1)S(1)}, u32[]{:S(2)}, u32[]{:S(2)}) collective-permute-start(bf16[2,32,512]{2,1,0:T(8,128)(2,1)S(1)} %get-tuple-element.55), channel_id=1, source_target_pairs={{0,96},{16,112},{32,0},{48,16},{64,32},{80,48},{96,64},{112,80},{1... | collective-permute-start | bytes 196616 | tf_op jit(solution)/shard_map/ppermute | solution.py:648
  220.8 3.4 %collective-permute-start.10 = (bf16[2,32,512]{2,1,0:T(8,128)(2,1)S(1)}, bf16[2,32,512]{2,1,0:T(8,128)(2,1)S(1)}, u32[]{:S(2)}, u32[]{:S(2)}) collective-permute-start(bf16[2,32,512]{2,1,0:T(8,128)(2,1)S(1)} %get-tuple-element.56), channel_id=1, source_target_pairs={{0,112},{16,0},{32,16},{48,32},{64,48},{80,64},{96,80},{112,96},{1... | collective-permute-start | bytes 196616 | tf_op jit(solution)/shard_map/ppermute | solution.py:648

commit v4 on v3

--- a/solution.py
+++ b/solution.py
@@ -199,8 +199,8 @@
 
 def row_backward_kernel(
     where_ref, g_ref, qkv_ref, turned_ref, probs_ref, w_ref,
-    keep_ref, send_ref, right_ref,
-    mix_s, da_s, wo_s, qkv_s, turned_s, probs_s, keep_s, send_s, right_s,
+    send_ref, right_ref,
+    mix_s, da_s, wo_s, qkv_s, turned_s, probs_s, send_s, right_s,
     wo_sem, qkv_sem, turned_sem, probs_sem, half_sem, right_sem,
 ):
     weight = pltpu.make_async_copy(w_ref.at[3], wo_s, wo_sem)
@@ -240,23 +240,31 @@
     wait_all(turned)
     core = where_ref[4]
     weight_gradients(1 - core, turned_s, right_s, send_s)
-    sent = pltpu.make_async_copy(send_s, send_ref, half_sem.at[0])
+    sent = pltpu.make_async_copy(send_s, send_ref, half_sem)
     sent.start()
-    weight_gradients(core, turned_s, right_s, keep_s)
-    kept = pltpu.make_async_copy(keep_s, keep_ref, half_sem.at[1])
-    kept.start()
-    wait_all(rights + [sent, kept])
+    wait_all(rights + [sent])
+
+
+def kept_gradients_kernel(where_ref, turned_ref, right_ref, keep_ref, turned_s, right_s, turned_sem, right_sem):
+    core = where_ref[4]
+    turned = copies_of(turned_ref, turned_s, turned_sem, 2)
+    rights = copies_of(right_ref.at[pl.ds(core * 2, 2)], right_s, right_sem, 2)
+    start_all(turned + rights)
+    wait_all(turned + rights)
+    for j in range(2):
+        keep_ref[j] = dot(turned_s[(core * 2 + j) // 3], right_s[j]).astype(BF16)
 
 
 def row_input_gradient_kernel(where_ref, x_ref, right_ref, w_ref, *refs):
-    outs, w_s, sems, gin_s = refs[:8], refs[8], refs[9], refs[10]
-    copies = copies_of(w_ref, w_s, sems, 3)
-    start_all(copies)
-    wait_all(copies)
+    outs, w_s, right_s, gin_s, w_sem, right_sem = refs[:8], *refs[8:]
+    weights = copies_of(w_ref, w_s, w_sem, 3)
+    rights = copies_of(right_ref, right_s, right_sem, 4)
+    start_all([copy for pair in zip(weights, rights) for copy in pair] + rights[3:])
+    wait_all(weights + rights)
     for rr in range(2):
         rows = slice(rr * LINE, (rr + 1) * LINE)
         u = x_ref[:, rr].astype(F32).reshape(LINE, D)
-        grad_in = input_gradient(u, right_ref, w_s, rows)
+        grad_in = input_gradient(u, right_s, w_s, rows)
         gin_s[:, :, rr] = grad_in.astype(BF16).reshape(8, 2, 16, D)
     chip = where_ref[2] * 4 + where_ref[3]
     for shift in range(8):
@@ -332,23 +340,21 @@
     wait_all(lefts + rights + [kept_u])
 
 
-def col_weights_kernel(where_ref, saved_ref, keep_ref, send_ref, *refs):
-    left_s, right_s, turned_s, keep_s, send_s, left_sem, right_sem, half_sem = refs
+def col_weights_kernel(where_ref, saved_ref, send_ref, turned_ref, *refs):
+    left_s, right_s, turned_s, left_sem, right_sem, turned_sem = refs
+    side = 1 - where_ref[4]
     lefts = copies_of(saved_ref.at[4:6], left_s, left_sem, 2)
-    rights = copies_of(saved_ref, right_s, right_sem, 4)
+    rights = copies_of(saved_ref.at[pl.ds(side * 2, 2)], right_s, right_sem, 2)
     start_all(lefts + rights)
-    core = where_ref[4]
+    turned = copies_of(turned_s, turned_ref, turned_sem, 2)
     for which in range(2):
         lefts[which].wait()
         turned_s[which] = left_s[which].T
+        turned[which].start()
     wait_all(rights)
-    weight_gradients(1 - core, turned_s, right_s, send_s)
-    sent = pltpu.make_async_copy(send_s, send_ref, half_sem.at[0])
-    sent.start()
-    weight_gradients(core, turned_s, right_s, keep_s)
-    kept = pltpu.make_async_copy(keep_s, keep_ref, half_sem.at[1])
-    kept.start()
-    wait_all([sent, kept])
+    for j in range(2):
+        send_ref[j] = dot(turned_s[(side * 2 + j) // 3], right_s[j]).astype(BF16)
+    wait_all(turned)
 
 
 def col_output_kernel(where_ref, saved_ref, w_ref, *refs):
@@ -552,25 +558,39 @@
 row_backward = call(
     row_backward_kernel,
     "svhhhh",
-    "hhh",
-    (HALF, HALF, shape(4, TOK, D)),
+    "hh",
+    (HALF, shape(4, TOK, D)),
     [
         MIX, token_scratch(), pltpu.VMEM((D, D), BF16), token_scratch(3),
-        pltpu.VMEM((2, D, TOK), BF16), pltpu.VMEM((8, TOK, LINE), BF16), HALF_S, HALF_S,
-        token_scratch(4), DMA, DMA((3,)), DMA((2,)), DMA((4,)), DMA((2,)), DMA((4,)),
+        pltpu.VMEM((2, D, TOK), BF16), pltpu.VMEM((8, TOK, LINE), BF16), HALF_S,
+        token_scratch(4), DMA, DMA((3,)), DMA((2,)), DMA((4,)), DMA, DMA((4,)),
     ],
     5 * MATMUL + 5 * ATTEND,
     12 * MIB,
     grant=50,
 )
+kept_gradients = call(
+    kept_gradients_kernel,
+    "shh",
+    "v",
+    HALF,
+    [pltpu.VMEM((2, D, TOK), BF16), token_scratch(2), DMA((2,)), DMA((2,))],
+    2 * MATMUL,
+    3 * MIB,
+    grant=50,
+)
 row_input_gradient = call(
     row_input_gradient_kernel,
-    "svvh",
+    "svhh",
     "v" * 8,
     (shape(2, 2, 16, D),) * 8,
-    [*WEIGHTS, pltpu.VMEM((8, 2, 2, 16, D), BF16)],
+    [
+        pltpu.VMEM((3, D, D), BF16), token_scratch(4), pltpu.VMEM((8, 2, 2, 16, D), BF16),
+        DMA((3,)), DMA((4,)),
+    ],
     3 * MATMUL,
     5 * MIB,
+    grant=50,
 )
 col_grad = call(
     col_kernel,
@@ -589,15 +609,15 @@
 col_weights = call(
     col_weights_kernel,
     "sh",
-    "hh",
-    (HALF, HALF),
+    "vh",
+    (HALF, shape(2, D, TOK)),
     [
-        token_scratch(2), token_scratch(4), pltpu.VMEM((2, D, TOK), BF16), HALF_S, HALF_S,
-        DMA((2,)), DMA((4,)), DMA((2,)),
+        token_scratch(2), token_scratch(2), pltpu.VMEM((2, D, TOK), BF16),
+        DMA((2,)), DMA((2,)), DMA((2,)),
     ],
-    4 * MATMUL,
+    2 * MATMUL,
     6 * MIB,
-    grant=52,
+    grant=50,
 )
 col_output = call(
     col_output_kernel,
@@ -618,7 +638,7 @@
 pair_sum = call(
     pair_sum_kernel, "svv", "v" * 4, (QUARTER,) * 4, [pltpu.VMEM((4, 256, D), BF16)], 0, 3 * MIB,
 )
-merge = call(merge_kernel, "v" * 6, "v", shape(64, 80, 128), [], 0, 4 * MIB)
+merge = call(merge_kernel, "v" * 6, "v", shape(64, 80, 128), [], 0, 4 * MIB, grant=16)
 spread = call(spread_kernel, "v", "v", shape(64, 128, 128), [], 0, 3 * MIB)
 
 
@@ -669,14 +689,14 @@
         where, mid_lines, w_col, *grad_parts, grad_pass
     )
     grad_rows = exchange(grad_send, BOTH)
-    keep_col, send_col = col_weights(where, saved_col)
+    send_col, turned_col = col_weights(where, saved_col)
     got_col = swap(send_col, "c")
+    keep_col = kept_gradients(where, turned_col, saved_col)
     quarters = pair_sum(where, keep_col, got_col)
     quarters = shifted(quarters, "x")
-    keep_row, send_row, right_row = row_backward(
-        where, grad_rows, saved_row, turned_row, probs_row, w_row
-    )
+    send_row, right_row = row_backward(where, grad_rows, saved_row, turned_row, probs_row, w_row)
     got_row = swap(send_row, "c")
+    keep_row = kept_gradients(where, turned_row, right_row)
     merged = merge(keep_row, got_row, *quarters)
     both = exchange(merged, CHIPS)
     totals = spread(both)

time: 238 us -> 240 us (level)
  Pallas kernels: 54.7 us -> 59.6 us
    pallas_call x1 -> x3, Pallas kernels: 4.42 us -> 8.26 us  [the longest x1 3.14 us: layer(): send_col, turned_col = col_weights(where, saved_col)]
    ppermute x20, waiting for transfers between devices: 36.5 us -> 33.9 us  [shifted(): lax.ppermute(pieces[k], axes, [(i, (i + k) % n) for i in range(n)])]
  transfers between devices with their start and end apart: 28 -> 28, of which waited for: 16 -> 16; matrix products, arithmetic and copies ran while one was open for 0% -> 0% of each run, Pallas kernels for 13% -> 15%
where the time goes in v4:
time: 240 us; the launch traced here: 236 us
  Pallas kernels  59.6 us (25%)
  blocking collectives  58.5 us (24%)
  starting transfers between devices  56.4 us (24%)
  waiting for transfers between devices  52.6 us (22%)
  local copies, waits for them, and re-layouts  7.79 us (3%)
    all_to_all x2, blocking collectives, exchange(): return lax.all_to_all(values, axes, split_axis=0, concat_axis=0, tiled=True)  58.5 us
    ppermute x20, waiting for transfers between devices, shifted(): lax.ppermute(pieces[k], axes, [(i, (i + k) % n) for i in range(n)])  33.9 us
    all_to_all x3, starting transfers between devices, exchange(): return lax.all_to_all(values, axes, split_axis=0, concat_axis=0, tiled=True)  24 us
    ppermute x20, starting transfers between devices, shifted(): lax.ppermute(pieces[k], axes, [(i, (i + k) % n) for i in range(n)])  22.1 us
    pallas_call x1, Pallas kernels, layer(): col_grad(where, mid_lines, w_col, *grad_parts, grad_pass)  13.2 us
    all_to_all x3, waiting for transfers between devices, exchange(): return lax.all_to_all(values, axes, split_axis=0, concat_axis=0, tiled=True)  12.8 us
    ppermute x5, starting transfers between devices, swap(): return lax.ppermute(value, axis, [(0, 1), (1, 0)])  10.4 us
    pallas_call x1, Pallas kernels, layer(): row_backward(where, grad_rows, saved_row, turned_row, probs_row, w_row)  9.39 us
  transfers between devices with their start and end apart: 28, of which 16 were waited for; matrix products, arithmetic and copies ran while one was open for 0% of the time, Pallas kernels for 15%

profile of v4, /device:TPU:1, one launch (start us, length us, event | category | flops | bytes accessed | tf_op | source)
XLA Modules:
  0.0 236.0 jit_solution(7964998754075124607)
XLA Ops:
  0.6 9.1 %all-to-all-start = ((bf16[16,2,16,512]{3,2,1,0:T(8,128)(2,1)}), bf16[16,2,16,512]{3,2,1,0:T(8,128)(2,1)S(1)}, u32[]{:S(2)}, u32[]{:S(2)}) async-start(bf16[16,2,16,512]{3,2,1,0:T(8,128)(2,1)} %bitcast.12), calls=%async_computation | async-start | bytes 1048576 | tf_op jit(solution)/shard_map/all_to_all | solution.py:662
  9.8 0.8 reshape.23
  10.6 10.2 %all-to-all-done.x_ref = bf16[16,2,16,512]{3,2,1,0:T(8,128)(2,1)S(1)} async-done(((bf16[16,2,16,512]{3,2,1,0:T(8,128)(2,1)}), bf16[16,2,16,512]{3,2,1,0:T(8,128)(2,1)S(1)}, u32[]{:S(2)}, u32[]{:S(2)}) %all-to-all-start) | async-done | bytes 524320 | tf_op jit(solution)/shard_map/all_to_all | solution.py:662
  20.8 1.6 copy-done.2
  22.4 6.6 %shard_map.84 = (bf16[128,16,128]{2,1,0:T(8,128)(2,1)S(1)}, bf16[5,512,512]{2,1,0:T(8,128)(2,1)}) custom-call(s32[21]{0:T(128)S(1)} %concatenate.3.where_ref, bf16[16,2,16,512]{3,2,1,0:T(8,128)(2,1)S(1)} %all-to-all-done.x_ref, bf16[4,512,512]{2,1,0:T(8,128)(2,1)S(1)} %copy-done.2), custom_call_target="tpu_custom_call" | custom-call | flops 1342177280 | bytes 6291456 | tf_op jit(solution)/shard_map/pallas_call | solution.py:685
  29.0 0.8 copy-done.11
  29.8 6.4 %all-to-all-start.1 = ((bf16[128,16,128]{2,1,0:T(8,128)(2,1)}), bf16[128,16,128]{2,1,0:T(8,128)(2,1)}, u32[]{:S(2)}, u32[]{:S(2)}) async-start(bf16[128,16,128]{2,1,0:T(8,128)(2,1)} %copy-done.11), calls=%async_computation.1 | async-start | bytes 1048576 | tf_op jit(solution)/shard_map/all_to_all | solution.py:662
  36.2 1.2 shard_map.85
  37.5 1.4 collective-permute-start
  38.9 2.5 %collective-permute-start.1 = (bf16[2,2,32,512]{3,2,1,0:T(8,128)(2,1)S(1)}, bf16[2,2,32,512]{3,2,1,0:T(8,128)(2,1)S(1)}, u32[]{:S(2)}, u32[]{:S(2)}) collective-permute-start(bf16[2,2,32,512]{3,2,1,0:T(8,128)(2,1)S(1)} %get-tuple-element.45), channel_id=1, source_target_pairs={{0,64},{32,96},{64,0},{96,32},{1,65},{33,97},{65,1},{97,33},{2,66}... | collective-permute-start | bytes 393224 | tf_op jit(solution)/shard_map/ppermute | solution.py:668
  41.3 1.1 collective-permute-start.2
  42.5 5.2 %collective-permute-done.refs_1_ = bf16[2,2,32,512]{3,2,1,0:T(8,128)(2,1)S(1)} collective-permute-done((bf16[2,2,32,512]{3,2,1,0:T(8,128)(2,1)S(1)}, bf16[2,2,32,512]{3,2,1,0:T(8,128)(2,1)S(1)}, u32[]{:S(2)}, u32[]{:S(2)}) %collective-permute-start) | collective-permute-done | bytes 131104 | tf_op jit(solution)/shard_map/ppermute | solution.py:668
  47.7 3.5 %collective-permute-done.1.refs_2_ = bf16[2,2,32,512]{3,2,1,0:T(8,128)(2,1)S(1)} collective-permute-done((bf16[2,2,32,512]{3,2,1,0:T(8,128)(2,1)S(1)}, bf16[2,2,32,512]{3,2,1,0:T(8,128)(2,1)S(1)}, u32[]{:S(2)}, u32[]{:S(2)}) %collective-permute-start.1) | collective-permute-done | bytes 131104 | tf_op jit(solution)/shard_map/ppermute | solution.py:668
  51.2 0.6 shard_map.86
  51.8 1.7 collective-permute-start.3
  53.5 5.9 %collective-permute-done.3.refs_4_ = bf16[4,2,32,512]{3,2,1,0:T(8,128)(2,1)S(1)} collective-permute-done((bf16[4,2,32,512]{3,2,1,0:T(8,128)(2,1)S(1)}, bf16[4,2,32,512]{3,2,1,0:T(8,128)(2,1)S(1)}, u32[]{:S(2)}, u32[]{:S(2)}) %collective-permute-start.3) | collective-permute-done | bytes 262176 | tf_op jit(solution)/shard_map/ppermute | solution.py:673
  59.4 13.2 %shard_map.87 = (bf16[128,16,128]{2,1,0:T(8,128)(2,1)}, bf16[7,512,512]{2,1,0:T(8,128)(2,1)}) custom-call(s32[21]{0:T(128)S(1)} %concatenate.3.where_ref, bf16[128,16,128]{2,1,0:T(8,128)(2,1)} %all-to-all-done.1.m_ref, bf16[4,512,512]{2,1,0:T(8,128)(2,1)S(1)} %copy-done.6, bf16[2,2,32,512]{3,2,1,0:T(8,128)(2,1)S(1)} %get-tuple-element.43.refs_0_, ...), custom_call_target="tpu_custom_call" | custom-call | flops 2952790016 | bytes 8388608 | tf_op jit(solution)/shard_map/pallas_call | solution.py:688
  72.6 8.4 %all-to-all-start.2 = ((bf16[128,16,128]{2,1,0:T(8,128)(2,1)}), bf16[128,16,128]{2,1,0:T(8,128)(2,1)}, u32[]{:S(2)}, u32[]{:S(2)}) async-start(bf16[128,16,128]{2,1,0:T(8,128)(2,1)} %get-tuple-element.56), calls=%async_computation.2 | async-start | bytes 1048576 | tf_op jit(solution)/shard_map/all_to_all | solution.py:662
  81.1 3.1 %shard_map.96 = (bf16[2,512,512]{2,1,0:T(8,128)(2,1)S(1)}, bf16[2,512,512]{2,1,0:T(8,128)(2,1)S(1)}) custom-call(s32[21]{0:T(128)S(1)} %concatenate.3.where_ref, bf16[7,512,512]{2,1,0:T(8,128)(2,1)} %get-tuple-element.47.saved_ref.right_ref), custom_call_target="tpu_custom_call" | custom-call | flops 536870912 | bytes 6291456 | tf_op jit(solution)/shard_map/pallas_call | solution.py:692
  84.2 1.0 copy-done.8
  85.2 1.1 collective-permute-start.20
  86.3 2.4 %shard_map.90 = (bf16[8,512,256]{2,1,0:T(8,128)(2,1)S(1)}, bf16[2,512,512]{2,1,0:T(8,128)(2,1)S(1)}) custom-call(bf16[5,512,512]{2,1,0:T(8,128)(2,1)S(1)} %copy-done), custom_call_target="tpu_custom_call" | custom-call | flops 134217728 | bytes 8388608 | tf_op jit(solution)/shard_map/pallas_call | solution.py:687
  88.8 1.0 copy-done.3
  89.8 1.3 copy-done.7
  91.1 2.6 %all-to-all-done.2.g_ref = bf16[128,16,128]{2,1,0:T(8,128)(2,1)} async-done(((bf16[128,16,128]{2,1,0:T(8,128)(2,1)}), bf16[128,16,128]{2,1,0:T(8,128)(2,1)}, u32[]{:S(2)}, u32[]{:S(2)}) %all-to-all-start.2) | async-done | bytes 524320 | tf_op jit(solution)/shard_map/all_to_all | solution.py:662
  93.7 1.2 copy-done.4
  95.0 9.4 %shard_map.91 = (bf16[2,512,512]{2,1,0:T(8,128)(2,1)S(1)}, bf16[4,512,512]{2,1,0:T(8,128)(2,1)}) custom-call(s32[21]{0:T(128)S(1)} %concatenate.3.where_ref, bf16[128,16,128]{2,1,0:T(8,128)(2,1)} %all-to-all-done.2.g_ref, bf16[5,512,512]{2,1,0:T(8,128)(2,1)} %get-tuple-element.57.saved_ref.qkv_ref, bf16[2,512,512]{2,1,0:T(8,128)(2,1)S(1)} %copy-done.4, ...), custom_call_target="tpu_custom_call" | custom-call | flops 2013265920 | bytes 12582912 | tf_op jit(solution)/shard_map/pallas_call | solution.py:697
  104.4 1.5 collective-permute-start.19
  105.9 2.6 %shard_map.97.keep_ref = bf16[2,512,512]{2,1,0:T(8,128)(2,1)S(1)} custom-call(s32[21]{0:T(128)S(1)} %concatenate.3.where_ref, bf16[2,512,512]{2,1,0:T(8,128)(2,1)S(1)} %copy-done.9, bf16[7,512,512]{2,1,0:T(8,128)(2,1)} %get-tuple-element.47.saved_ref.right_ref), custom_call_target="tpu_custom_call" | custom-call | flops 536870912 | bytes 3145728 | tf_op jit(solution)/shard_map/pallas_call | solution.py:694
  108.5 1.9 shard_map.98
  110.8 1.9 collective-permute-start.22
  112.7 0.9 collective-permute-start.23
  113.6 2.6 %shard_map.95.keep_ref = bf16[2,512,512]{2,1,0:T(8,128)(2,1)S(1)} custom-call(s32[21]{0:T(128)S(1)} %concatenate.3.where_ref, bf16[2,512,512]{2,1,0:T(8,128)(2,1)S(1)} %copy-done.5, bf16[4,512,512]{2,1,0:T(8,128)(2,1)} %get-tuple-element.60.right_ref), custom_call_target="tpu_custom_call" | custom-call | flops 536870912 | bytes 3145728 | tf_op jit(solution)/shard_map/pallas_call | solution.py:699
  116.2 3.8 %collective-permute-done.21.refs_1_ = bf16[256,512]{1,0:T(8,128)(2,1)S(1)} collective-permute-done((bf16[256,512]{1,0:T(8,128)(2,1)S(1)}, bf16[256,512]{1,0:T(8,128)(2,1)S(1)}, u32[]{:S(2)}, u32[]{:S(2)}) %collective-permute-start.21) | collective-permute-done | bytes 262176 | tf_op jit(solution)/shard_map/ppermute | solution.py:668
  120.0 4.7 %collective-permute-done.22.refs_2_ = bf16[256,512]{1,0:T(8,128)(2,1)S(1)} collective-permute-done((bf16[256,512]{1,0:T(8,128)(2,1)S(1)}, bf16[256,512]{1,0:T(8,128)(2,1)S(1)}, u32[]{:S(2)}, u32[]{:S(2)}) %collective-permute-start.22) | collective-permute-done | bytes 262176 | tf_op jit(solution)/shard_map/ppermute | solution.py:668
  124.7 0.8 collective-permute-done.23.refs_3_
  125.5 0.4 shard_map.99
  125.9 26.0 %all_to_all.25.both_ref = bf16[64,80,128]{2,1,0:T(8,128)(2,1)S(1)} all-to-all(bf16[64,80,128]{2,1,0:T(8,128)(2,1)S(1)} %shard_map.99), channel_id=1, replica_groups=mesh['y'=4,'zl'=2,'zh'=2,'x'=4,'c'=2] {'y','zl','zh','x'}, dimensions={0} | all-to-all | bytes 2621440 | tf_op jit(solution)/shard_map/all_to_all | solution.py:662
  152.3 32.4 %all_to_all.26.chunks_ref = bf16[64,128,128]{2,1,0:T(8,128)(2,1)S(1)} all-to-all(bf16[64,128,128]{2,1,0:T(8,128)(2,1)S(1)} %shard_map.100), channel_id=1, replica_groups=mesh['y'=4,'zl'=2,'zh'=2,'x'=4,'c'=2] {'y','zl','zh','x'}, dimensions={0} | all-to-all | bytes 4194304 | tf_op jit(solution)/shard_map/all_to_all | solution.py:662
  184.8 3.3 %collective-permute-start.24 = (bf16[64,128,128]{2,1,0:T(8,128)(2,1)S(1)}, bf16[64,128,128]{2,1,0:T(8,128)(2,1)S(1)}, u32[]{:S(2)}, u32[]{:S(2)}) collective-permute-start(bf16[64,128,128]{2,1,0:T(8,128)(2,1)S(1)} %all_to_all.26.chunks_ref), channel_id=1, source_target_pairs={{0,1},{1,0},{2,3},{3,2},{4,5},{5,4},{6,7},{7,6},{8,9},{9,8},{10,11... | collective-permute-start | bytes 6291464 | tf_op jit(solution)/shard_map/ppermute | solution.py:673
  188.1 3.2 %shard_map.92 = (bf16[2,2,16,512]{3,2,1,0:T(8,128)(2,1)S(1)}, bf16[2,2,16,512]{3,2,1,0:T(8,128)(2,1)S(1)}, bf16[2,2,16,512]{3,2,1,0:T(8,128)(2,1)S(1)}, bf16[2,2...) custom-call(s32[21]{0:T(128)S(1)} %concatenate.3.where_ref, ...), custom_call_target="tpu_custom_call" | custom-call | flops 805306368 | bytes 5242880 | tf_op jit(solution)/shard_map/pallas_call | solution.py:704
  191.4 2.0 collective-permute-start.12
  193.4 1.7 collective-permute-start.13
  195.1 2.4 %collective-permute-start.14 = (bf16[2,2,16,512]{3,2,1,0:T(8,128)(2,1)S(1)}, bf16[2,2,16,512]{3,2,1,0:T(8,128)(2,1)S(1)}, u32[]{:S(2)}, u32[]{:S(2)}) collective-permute-start(bf16[2,2,16,512]{3,2,1,0:T(8,128)(2,1)S(1)} %get-tuple-element.65), channel_id=1, source_target_pairs={{0,8},{2,10},{4,12},{6,14},{8,0},{10,2},{12,4},{14,6},{1,9},{3,11}... | collective-permute-start | bytes 196616 | tf_op jit(solution)/shard_map/ppermute | solution.py:668
  197.4 3.0 %collective-permute-done.11.refs_1_ = bf16[2,2,16,512]{3,2,1,0:T(8,128)(2,1)S(1)} collective-permute-done((bf16[2,2,16,512]{3,2,1,0:T(8,128)(2,1)S(1)}, bf16[2,2,16,512]{3,2,1,0:T(8,128)(2,1)S(1)}, u32[]{:S(2)}, u32[]{:S(2)}) %collective-permute-start.11) | collective-permute-done | bytes 65568 | tf_op jit(solution)/shard_map/ppermute | solution.py:668
  200.4 1.6 collective-permute-start.16
  202.0 2.6 %collective-permute-start.17 = (bf16[2,2,16,512]{3,2,1,0:T(8,128)(2,1)S(1)}, bf16[2,2,16,512]{3,2,1,0:T(8,128)(2,1)S(1)}, u32[]{:S(2)}, u32[]{:S(2)}) collective-permute-start(bf16[2,2,16,512]{3,2,1,0:T(8,128)(2,1)S(1)} %get-tuple-element.68), channel_id=1, source_target_pairs={{0,14},{2,0},{4,2},{6,4},{8,6},{10,8},{12,10},{14,12},{1,15},{3,1}... | collective-permute-start | bytes 196616 | tf_op jit(solution)/shard_map/ppermute | solution.py:668
  204.6 0.8 collective-permute-done.15.refs_5_
  205.4 1.8 collective-permute-done.17.refs_7_
  207.2 0.6 shard_map.93
  207.8 2.7 %collective-permute-start.18 = (bf16[8,2,16,512]{3,2,1,0:T(8,128)(2,1)S(1)}, bf16[8,2,16,512]{3,2,1,0:T(8,128)(2,1)S(1)}, u32[]{:S(2)}, u32[]{:S(2)}) collective-permute-start(bf16[8,2,16,512]{3,2,1,0:T(8,128)(2,1)S(1)} %shard_map.93), channel_id=1, source_target_pairs={{0,1},{1,0},{2,3},{3,2},{4,5},{5,4},{6,7},{7,6},{8,9},{9,8},{10,11... | collective-permute-start | bytes 786440 | tf_op jit(solution)/shard_map/ppermute | solution.py:673
  210.5 2.4 %shard_map.88 = (bf16[2,32,512]{2,1,0:T(8,128)(2,1)S(1)}, bf16[2,32,512]{2,1,0:T(8,128)(2,1)S(1)}, bf16[2,32,512]{2,1,0:T(8,128)(2,1)S(1)}, bf16[2,32,512]{2,1,0...) custom-call(s32[21]{0:T(128)S(1)} %concatenate.3.where_ref, ...), custom_call_target="tpu_custom_call" | custom-call | flops 268435456 | bytes 3145728 | tf_op jit(solution)/shard_map/pallas_call | solution.py:709
  213.2 1.9 collective-permute-start.6
  215.1 3.7 %collective-permute-done.4.refs_1_ = bf16[2,32,512]{2,1,0:T(8,128)(2,1)S(1)} collective-permute-done((bf16[2,32,512]{2,1,0:T(8,128)(2,1)S(1)}, bf16[2,32,512]{2,1,0:T(8,128)(2,1)S(1)}, u32[]{:S(2)}, u32[]{:S(2)}) %collective-permute-start.4) | collective-permute-done | bytes 65568 | tf_op jit(solution)/shard_map/ppermute | solution.py:668
  218.7 0.8 collective-permute-start.8
  219.5 1.2 collective-permute-done.6.refs_3_
  220.8 0.6 collective-permute-start.9
  221.4 2.0 collective-permute-done.7.refs_4_
  223.4 0.5 collective-permute-done.9.refs_6_
  223.9 2.9 %collective-permute-done.10.refs_7_ = bf16[2,32,512]{2,1,0:T(8,128)(2,1)S(1)} collective-permute-done((bf16[2,32,512]{2,1,0:T(8,128)(2,1)S(1)}, bf16[2,32,512]{2,1,0:T(8,128)(2,1)S(1)}, u32[]{:S(2)}, u32[]{:S(2)}) %collective-permute-start.10) | collective-permute-done | bytes 65568 | tf_op jit(solution)/shard_map/ppermute | solution.py:668
  226.8 2.3 shard_map.89
  229.1 1.4 shard_map.94
  230.4 2.7 %widen.2 = (f32[2,1024,512]{2,1,0:T(8,128)}, f32[2,4,256,512]{3,2,1,0:T(8,128)}) custom-call(s32[21]{0:T(128)S(1)} %concatenate.3.where_ref, bf16[64,128,128]{2,1,0:T(8,128)(2,1)S(1)} %all_to_all.26.chunks_ref), custom_call_target="tpu_custom_call" | custom-call | bytes 6291456 | tf_op jit(solution)/shard_map/widen/pallas_call | solution.py:646
  233.1 2.7 %widen.3 = (f32[2,1024,512]{2,1,0:T(8,128)}, f32[2,4,256,512]{3,2,1,0:T(8,128)}) custom-call(s32[21]{0:T(128)S(1)} %concatenate.3.where_ref, bf16[64,128,128]{2,1,0:T(8,128)(2,1)S(1)} %collective-permute-done.24.chunks_ref, f32[2,1024,512]{2,1,0:T(8,128)} %get-tuple-element.76.refs_0_, ...), custom_call_target="tpu_custom_call", output_to_operand_aliasing={{0}: (2, {}), {1}: (3, {})} | custom-call | bytes 6291456 | tf_op jit(solution)/shard_map/widen/pallas_call | solution.py:646
  (39 shorter events, 1.3 us)
Async XLA Ops:
  0.6 20.1 %all-to-all-start = ((bf16[16,2,16,512]{3,2,1,0:T(8,128)(2,1)}), bf16[16,2,16,512]{3,2,1,0:T(8,128)(2,1)S(1)}, u32[]{:S(2)}, u32[]{:S(2)}) async-start(bf16[16,2,16,512]{3,2,1,0:T(8,128)(2,1)} %bitcast.12), calls=%async_computation | async-start | bytes 1048576 | tf_op jit(solution)/shard_map/all_to_all | solution.py:662
  20.8 1.6 copy-start.2
  22.3 13.9 %copy-start.10 = (bf16[32,16,512]{2,1,0:T(8,128)(2,1)S(1)}, bf16[32,16,512]{2,1,0:T(8,128)(2,1)}, u32[]{:S(2)}) copy-start(bf16[32,16,512]{2,1,0:T(8,128)(2,1)} %tile_ref.1) | copy-start | bytes 1572868
  29.0 0.8 copy-start.11
  29.8 29.6 %copy-start.6 = (bf16[4,512,512]{2,1,0:T(8,128)(2,1)S(1)}, bf16[4,512,512]{2,1,0:T(8,128)(2,1)}, u32[]{:S(2)}) copy-start(bf16[4,512,512]{2,1,0:T(8,128)(2,1)} %w_ref.7) | copy-start | bytes 6291460
  29.8 29.6 %all-to-all-start.1 = ((bf16[128,16,128]{2,1,0:T(8,128)(2,1)}), bf16[128,16,128]{2,1,0:T(8,128)(2,1)}, u32[]{:S(2)}, u32[]{:S(2)}) async-start(bf16[128,16,128]{2,1,0:T(8,128)(2,1)} %copy-done.11), calls=%async_computation.1 | async-start | bytes 1048576 | tf_op jit(solution)/shard_map/all_to_all | solution.py:662
  37.5 10.2 %collective-permute-start = (bf16[2,2,32,512]{3,2,1,0:T(8,128)(2,1)S(1)}, bf16[2,2,32,512]{3,2,1,0:T(8,128)(2,1)S(1)}, u32[]{:S(2)}, u32[]{:S(2)}) collective-permute-start(bf16[2,2,32,512]{3,2,1,0:T(8,128)(2,1)S(1)} %get-tuple-element.44), channel_id=1, source_target_pairs={{0,32},{32,64},{64,96},{96,0},{1,33},{33,65},{65,97},{97,1},{2,34}... | collective-permute-start | bytes 393224 | tf_op jit(solution)/shard_map/ppermute | solution.py:668
  38.9 12.3 %collective-permute-start.1 = (bf16[2,2,32,512]{3,2,1,0:T(8,128)(2,1)S(1)}, bf16[2,2,32,512]{3,2,1,0:T(8,128)(2,1)S(1)}, u32[]{:S(2)}, u32[]{:S(2)}) collective-permute-start(bf16[2,2,32,512]{3,2,1,0:T(8,128)(2,1)S(1)} %get-tuple-element.45), channel_id=1, source_target_pairs={{0,64},{32,96},{64,0},{96,32},{1,65},{33,97},{65,1},{97,33},{2,66}... | collective-permute-start | bytes 393224 | tf_op jit(solution)/shard_map/ppermute | solution.py:668
  41.3 9.8 %collective-permute-start.2 = (bf16[2,2,32,512]{3,2,1,0:T(8,128)(2,1)S(1)}, bf16[2,2,32,512]{3,2,1,0:T(8,128)(2,1)S(1)}, u32[]{:S(2)}, u32[]{:S(2)}) collective-permute-start(bf16[2,2,32,512]{3,2,1,0:T(8,128)(2,1)S(1)} %get-tuple-element.46), channel_id=1, source_target_pairs={{0,96},{32,0},{64,32},{96,64},{1,97},{33,1},{65,33},{97,65},{2,98}... | collective-permute-start | bytes 393224 | tf_op jit(solution)/shard_map/ppermute | solution.py:668
  51.8 7.6 %collective-permute-start.3 = (bf16[4,2,32,512]{3,2,1,0:T(8,128)(2,1)S(1)}, bf16[4,2,32,512]{3,2,1,0:T(8,128)(2,1)S(1)}, u32[]{:S(2)}, u32[]{:S(2)}) collective-permute-start(bf16[4,2,32,512]{3,2,1,0:T(8,128)(2,1)S(1)} %shard_map.86), channel_id=1, source_target_pairs={{0,16},{16,0},{1,17},{17,1},{2,18},{18,2},{3,19},{19,3},{4,20},{20... | collective-permute-start | bytes 786440 | tf_op jit(solution)/shard_map/ppermute | solution.py:673
  72.6 21.1 %all-to-all-start.2 = ((bf16[128,16,128]{2,1,0:T(8,128)(2,1)}), bf16[128,16,128]{2,1,0:T(8,128)(2,1)}, u32[]{:S(2)}, u32[]{:S(2)}) async-start(bf16[128,16,128]{2,1,0:T(8,128)(2,1)} %get-tuple-element.56), calls=%async_computation.2 | async-start | bytes 1048576 | tf_op jit(solution)/shard_map/all_to_all | solution.py:662
  81.0 5.3 %copy-start = (bf16[5,512,512]{2,1,0:T(8,128)(2,1)S(1)}, bf16[5,512,512]{2,1,0:T(8,128)(2,1)}, u32[]{:S(2)}) copy-start(bf16[5,512,512]{2,1,0:T(8,128)(2,1)} %get-tuple-element.57.saved_ref.qkv_ref) | copy-start | bytes 7864324
  84.2 1.0 copy-start.8
  85.2 23.3 %collective-permute-start.20 = (bf16[2,512,512]{2,1,0:T(8,128)(2,1)S(1)}, bf16[2,512,512]{2,1,0:T(8,128)(2,1)}, u32[]{:S(2)}, u32[]{:S(2)}) collective-permute-start(bf16[2,512,512]{2,1,0:T(8,128)(2,1)S(1)} %get-tuple-element.71), channel_id=1, source_target_pairs={{0,1},{1,0},{2,3},{3,2},{4,5},{5,4},{6,7},{7,6},{8,9},{9,8},{10,11... | collective-permute-start | bytes 3145736 | tf_op jit(solution)/shard_map/ppermute | solution.py:673
  88.8 1.0 copy-start.3
  89.8 1.3 copy-start.7
  93.7 1.2 copy-start.4
  95.0 10.9 %copy-start.9 = (bf16[2,512,512]{2,1,0:T(8,128)(2,1)S(1)}, bf16[2,512,512]{2,1,0:T(8,128)(2,1)}, u32[]{:S(2)}) copy-start(bf16[2,512,512]{2,1,0:T(8,128)(2,1)} %copy-done.8) | copy-start | bytes 3145732
  104.4 21.1 %collective-permute-start.19 = (bf16[2,512,512]{2,1,0:T(8,128)(2,1)S(1)}, bf16[2,512,512]{2,1,0:T(8,128)(2,1)S(1)}, u32[]{:S(2)}, u32[]{:S(2)}) collective-permute-start(bf16[2,512,512]{2,1,0:T(8,128)(2,1)S(1)} %get-tuple-element.69), channel_id=1, source_target_pairs={{0,1},{1,0},{2,3},{3,2},{4,5},{5,4},{6,7},{7,6},{8,9},{9,8},{10,11... | collective-permute-start | bytes 3145736 | tf_op jit(solution)/shard_map/ppermute | solution.py:673
  108.4 5.1 %copy-start.5 = (bf16[2,512,512]{2,1,0:T(8,128)(2,1)S(1)}, bf16[2,512,512]{2,1,0:T(8,128)(2,1)}, u32[]{:S(2)}) copy-start(bf16[2,512,512]{2,1,0:T(8,128)(2,1)} %copy-done.3) | copy-start | bytes 3145732
  110.4 9.6 %collective-permute-start.21 = (bf16[256,512]{1,0:T(8,128)(2,1)S(1)}, bf16[256,512]{1,0:T(8,128)(2,1)S(1)}, u32[]{:S(2)}, u32[]{:S(2)}) collective-permute-start(bf16[256,512]{1,0:T(8,128)(2,1)S(1)} %get-tuple-element.73), channel_id=1, source_target_pairs={{0,2},{2,4},{4,6},{6,0},{1,3},{3,5},{5,7},{7,1},{8,10},{10,12},{12... | collective-permute-start | bytes 786440 | tf_op jit(solution)/shard_map/ppermute | solution.py:668
  110.8 13.9 %collective-permute-start.22 = (bf16[256,512]{1,0:T(8,128)(2,1)S(1)}, bf16[256,512]{1,0:T(8,128)(2,1)S(1)}, u32[]{:S(2)}, u32[]{:S(2)}) collective-permute-start(bf16[256,512]{1,0:T(8,128)(2,1)S(1)} %get-tuple-element.74), channel_id=1, source_target_pairs={{0,4},{2,6},{4,0},{6,2},{1,5},{3,7},{5,1},{7,3},{8,12},{10,14},{12... | collective-permute-start | bytes 786440 | tf_op jit(solution)/shard_map/ppermute | solution.py:668
  112.7 12.8 %collective-permute-start.23 = (bf16[256,512]{1,0:T(8,128)(2,1)S(1)}, bf16[256,512]{1,0:T(8,128)(2,1)S(1)}, u32[]{:S(2)}, u32[]{:S(2)}) collective-permute-start(bf16[256,512]{1,0:T(8,128)(2,1)S(1)} %get-tuple-element.75), channel_id=1, source_target_pairs={{0,6},{2,0},{4,2},{6,4},{1,7},{3,1},{5,3},{7,5},{8,14},{10,8},{12,... | collective-permute-start | bytes 786440 | tf_op jit(solution)/shard_map/ppermute | solution.py:668
  152.3 35.7 %copy-start.1 = (bf16[4,512,512]{2,1,0:T(8,128)(2,1)S(1)}, bf16[4,512,512]{2,1,0:T(8,128)(2,1)}, u32[]{:S(2)}) copy-start(bf16[4,512,512]{2,1,0:T(8,128)(2,1)} %get-tuple-element.60.right_ref) | copy-start | bytes 6291460
  184.8 48.3 %collective-permute-start.24 = (bf16[64,128,128]{2,1,0:T(8,128)(2,1)S(1)}, bf16[64,128,128]{2,1,0:T(8,128)(2,1)S(1)}, u32[]{:S(2)}, u32[]{:S(2)}) collective-permute-start(bf16[64,128,128]{2,1,0:T(8,128)(2,1)S(1)} %all_to_all.26.chunks_ref), channel_id=1, source_target_pairs={{0,1},{1,0},{2,3},{3,2},{4,5},{5,4},{6,7},{7,6},{8,9},{9,8},{10,11... | collective-permute-start | bytes 6291464 | tf_op jit(solution)/shard_map/ppermute | solution.py:673
  191.3 9.1 %collective-permute-start.11 = (bf16[2,2,16,512]{3,2,1,0:T(8,128)(2,1)S(1)}, bf16[2,2,16,512]{3,2,1,0:T(8,128)(2,1)S(1)}, u32[]{:S(2)}, u32[]{:S(2)}) collective-permute-start(bf16[2,2,16,512]{3,2,1,0:T(8,128)(2,1)S(1)} %get-tuple-element.62), channel_id=1, source_target_pairs={{0,2},{2,4},{4,6},{6,8},{8,10},{10,12},{12,14},{14,0},{1,3},{3,5},... | collective-permute-start | bytes 196616 | tf_op jit(solution)/shard_map/ppermute | solution.py:668
  191.4 9.0 %collective-permute-start.12 = (bf16[2,2,16,512]{3,2,1,0:T(8,128)(2,1)S(1)}, bf16[2,2,16,512]{3,2,1,0:T(8,128)(2,1)S(1)}, u32[]{:S(2)}, u32[]{:S(2)}) collective-permute-start(bf16[2,2,16,512]{3,2,1,0:T(8,128)(2,1)S(1)} %get-tuple-element.63), channel_id=1, source_target_pairs={{0,4},{2,6},{4,8},{6,10},{8,12},{10,14},{12,0},{14,2},{1,5},{3,7},... | collective-permute-start | bytes 196616 | tf_op jit(solution)/shard_map/ppermute | solution.py:668
  193.4 8.6 %collective-permute-start.13 = (bf16[2,2,16,512]{3,2,1,0:T(8,128)(2,1)S(1)}, bf16[2,2,16,512]{3,2,1,0:T(8,128)(2,1)S(1)}, u32[]{:S(2)}, u32[]{:S(2)}) collective-permute-start(bf16[2,2,16,512]{3,2,1,0:T(8,128)(2,1)S(1)} %get-tuple-element.64), channel_id=1, source_target_pairs={{0,6},{2,8},{4,10},{6,12},{8,14},{10,0},{12,2},{14,4},{1,7},{3,9},... | collective-permute-start | bytes 196616 | tf_op jit(solution)/shard_map/ppermute | solution.py:668
  195.1 9.5 %collective-permute-start.14 = (bf16[2,2,16,512]{3,2,1,0:T(8,128)(2,1)S(1)}, bf16[2,2,16,512]{3,2,1,0:T(8,128)(2,1)S(1)}, u32[]{:S(2)}, u32[]{:S(2)}) collective-permute-start(bf16[2,2,16,512]{3,2,1,0:T(8,128)(2,1)S(1)} %get-tuple-element.65), channel_id=1, source_target_pairs={{0,8},{2,10},{4,12},{6,14},{8,0},{10,2},{12,4},{14,6},{1,9},{3,11}... | collective-permute-start | bytes 196616 | tf_op jit(solution)/shard_map/ppermute | solution.py:668
  200.4 5.0 %collective-permute-start.15 = (bf16[2,2,16,512]{3,2,1,0:T(8,128)(2,1)S(1)}, bf16[2,2,16,512]{3,2,1,0:T(8,128)(2,1)S(1)}, u32[]{:S(2)}, u32[]{:S(2)}) collective-permute-start(bf16[2,2,16,512]{3,2,1,0:T(8,128)(2,1)S(1)} %get-tuple-element.66), channel_id=1, source_target_pairs={{0,10},{2,12},{4,14},{6,0},{8,2},{10,4},{12,6},{14,8},{1,11},{3,13... | collective-permute-start | bytes 196616 | tf_op jit(solution)/shard_map/ppermute | solution.py:668
  200.4 5.0 %collective-permute-start.16 = (bf16[2,2,16,512]{3,2,1,0:T(8,128)(2,1)S(1)}, bf16[2,2,16,512]{3,2,1,0:T(8,128)(2,1)S(1)}, u32[]{:S(2)}, u32[]{:S(2)}) collective-permute-start(bf16[2,2,16,512]{3,2,1,0:T(8,128)(2,1)S(1)} %get-tuple-element.67), channel_id=1, source_target_pairs={{0,12},{2,14},{4,0},{6,2},{8,4},{10,6},{12,8},{14,10},{1,13},{3,15... | collective-permute-start | bytes 196616 | tf_op jit(solution)/shard_map/ppermute | solution.py:668
  202.0 5.2 %collective-permute-start.17 = (bf16[2,2,16,512]{3,2,1,0:T(8,128)(2,1)S(1)}, bf16[2,2,16,512]{3,2,1,0:T(8,128)(2,1)S(1)}, u32[]{:S(2)}, u32[]{:S(2)}) collective-permute-start(bf16[2,2,16,512]{3,2,1,0:T(8,128)(2,1)S(1)} %get-tuple-element.68), channel_id=1, source_target_pairs={{0,14},{2,0},{4,2},{6,4},{8,6},{10,8},{12,10},{14,12},{1,15},{3,1}... | collective-permute-start | bytes 196616 | tf_op jit(solution)/shard_map/ppermute | solution.py:668
  207.8 21.2 %collective-permute-start.18 = (bf16[8,2,16,512]{3,2,1,0:T(8,128)(2,1)S(1)}, bf16[8,2,16,512]{3,2,1,0:T(8,128)(2,1)S(1)}, u32[]{:S(2)}, u32[]{:S(2)}) collective-permute-start(bf16[8,2,16,512]{3,2,1,0:T(8,128)(2,1)S(1)} %shard_map.93), channel_id=1, source_target_pairs={{0,1},{1,0},{2,3},{3,2},{4,5},{5,4},{6,7},{7,6},{8,9},{9,8},{10,11... | collective-permute-start | bytes 786440 | tf_op jit(solution)/shard_map/ppermute | solution.py:673
  212.9 5.8 %collective-permute-start.4 = (bf16[2,32,512]{2,1,0:T(8,128)(2,1)S(1)}, bf16[2,32,512]{2,1,0:T(8,128)(2,1)S(1)}, u32[]{:S(2)}, u32[]{:S(2)}) collective-permute-start(bf16[2,32,512]{2,1,0:T(8,128)(2,1)S(1)} %get-tuple-element.49), channel_id=1, source_target_pairs={{0,16},{16,32},{32,48},{48,64},{64,80},{80,96},{96,112},{112,0},{1... | collective-permute-start | bytes 196616 | tf_op jit(solution)/shard_map/ppermute | solution.py:668
  213.2 5.6 %collective-permute-start.5 = (bf16[2,32,512]{2,1,0:T(8,128)(2,1)S(1)}, bf16[2,32,512]{2,1,0:T(8,128)(2,1)S(1)}, u32[]{:S(2)}, u32[]{:S(2)}) collective-permute-start(bf16[2,32,512]{2,1,0:T(8,128)(2,1)S(1)} %get-tuple-element.50), channel_id=1, source_target_pairs={{0,32},{16,48},{32,64},{48,80},{64,96},{80,112},{96,0},{112,16},{1... | collective-permute-start | bytes 196616 | tf_op jit(solution)/shard_map/ppermute | solution.py:668
  213.2 7.6 %collective-permute-start.6 = (bf16[2,32,512]{2,1,0:T(8,128)(2,1)S(1)}, bf16[2,32,512]{2,1,0:T(8,128)(2,1)S(1)}, u32[]{:S(2)}, u32[]{:S(2)}) collective-permute-start(bf16[2,32,512]{2,1,0:T(8,128)(2,1)S(1)} %get-tuple-element.51), channel_id=1, source_target_pairs={{0,48},{16,64},{32,80},{48,96},{64,112},{80,0},{96,16},{112,32},{1... | collective-permute-start | bytes 196616 | tf_op jit(solution)/shard_map/ppermute | solution.py:668
  218.7 4.6 %collective-permute-start.7 = (bf16[2,32,512]{2,1,0:T(8,128)(2,1)S(1)}, bf16[2,32,512]{2,1,0:T(8,128)(2,1)S(1)}, u32[]{:S(2)}, u32[]{:S(2)}) collective-permute-start(bf16[2,32,512]{2,1,0:T(8,128)(2,1)S(1)} %get-tuple-element.52), channel_id=1, source_target_pairs={{0,64},{16,80},{32,96},{48,112},{64,0},{80,16},{96,32},{112,48},{1... | collective-permute-start | bytes 196616 | tf_op jit(solution)/shard_map/ppermute | solution.py:668
  218.7 4.6 %collective-permute-start.8 = (bf16[2,32,512]{2,1,0:T(8,128)(2,1)S(1)}, bf16[2,32,512]{2,1,0:T(8,128)(2,1)S(1)}, u32[]{:S(2)}, u32[]{:S(2)}) collective-permute-start(bf16[2,32,512]{2,1,0:T(8,128)(2,1)S(1)} %get-tuple-element.53), channel_id=1, source_target_pairs={{0,80},{16,96},{32,112},{48,0},{64,16},{80,32},{96,48},{112,64},{1... | collective-permute-start | bytes 196616 | tf_op jit(solution)/shard_map/ppermute | solution.py:668
  220.8 3.1 %collective-permute-start.9 = (bf16[2,32,512]{2,1,0:T(8,128)(2,1)S(1)}, bf16[2,32,512]{2,1,0:T(8,128)(2,1)S(1)}, u32[]{:S(2)}, u32[]{:S(2)}) collective-permute-start(bf16[2,32,512]{2,1,0:T(8,128)(2,1)S(1)} %get-tuple-element.54), channel_id=1, source_target_pairs={{0,96},{16,112},{32,0},{48,16},{64,32},{80,48},{96,64},{112,80},{1... | collective-permute-start | bytes 196616 | tf_op jit(solution)/shard_map/ppermute | solution.py:668
  223.4 3.4 %collective-permute-start.10 = (bf16[2,32,512]{2,1,0:T(8,128)(2,1)S(1)}, bf16[2,32,512]{2,1,0:T(8,128)(2,1)S(1)}, u32[]{:S(2)}, u32[]{:S(2)}) collective-permute-start(bf16[2,32,512]{2,1,0:T(8,128)(2,1)S(1)} %get-tuple-element.55), channel_id=1, source_target_pairs={{0,112},{16,0},{32,16},{48,32},{64,48},{80,64},{96,80},{112,96},{1... | collective-permute-start | bytes 196616 | tf_op jit(solution)/shard_map/ppermute | solution.py:668

commit v5 on v4

--- a/solution.py
+++ b/solution.py
@@ -75,8 +75,41 @@
     return grown * (1.0 / jnp.sum(grown, axis=-1, keepdims=True))
 
 
-def slot(col_local, group, row_local):
-    return col_local * 8 + group * 2 + row_local
+def picked(rows):
+    return jnp.where(rows == lax.broadcasted_iota(jnp.int32, (TOK, TOK), 1), 1.0, 0.0).astype(BF16)
+
+
+def chunk_row(grid_col, grid_row, row_local, col_local):
+    return ((grid_col * 8 + grid_row) * 2 + row_local) * 2 + col_local
+
+
+def positions():
+    return lax.broadcasted_iota(jnp.int32, (TOK, 1), 0)
+
+
+def chunk_parts():
+    row = positions()
+    return row // 32, (row // 4) % 8, (row // 2) % 2, row % 2
+
+
+def row_tokens_of_chunks():
+    token = positions()
+    return picked(chunk_row((token // 16) % 16, token % 8, token // 256, (token // 8) % 2))
+
+
+def chunks_of_row_tokens():
+    grid_col, grid_row, row_local, col_local = chunk_parts()
+    return picked(row_local * 256 + grid_col * 16 + col_local * 8 + grid_row)
+
+
+def col_tokens_of_chunks():
+    token = positions()
+    return picked(chunk_row(token % 16, (token // 16) % 8, (token // 128) % 2, token // 256))
+
+
+def chunks_of_col_tokens():
+    grid_col, grid_row, row_local, col_local = chunk_parts()
+    return picked(col_local * 256 + row_local * 128 + grid_row * 16 + grid_col)
 
 
 def copies_of(source, target, sems, count):
@@ -118,12 +151,13 @@
 
 def row_forward_kernel(
     where_ref, x_ref, w_ref, mid_ref, saved_ref,
-    mix_s, mid_s, qkv_s, left_s, w_s, w_sem, mid_sem, qkv_sem, left_sem,
+    order_s, mid_s, qkv_s, left_s, w_s, w_sem, mid_sem, qkv_sem, left_sem,
 ):
     weights = copies_of(w_ref, w_s, w_sem, 4)
     start_all(weights)
     saved = copies_of(qkv_s, saved_ref, qkv_sem, 3)
     lefts = copies_of(left_s, saved_ref.at[3:5], left_sem, 2)
+    order_s[...] = chunks_of_row_tokens()
     for rr in range(2):
         u = x_ref[:, rr].astype(F32).reshape(LINE, D)
         left_s[0, rr * LINE : (rr + 1) * LINE, :] = (u * inverse_rms(u)).astype(BF16)
@@ -140,17 +174,16 @@
     lefts[1].start()
     weights[3].wait()
     added = dot(left_s[1], w_s[3])
+    mids = []
     for rr in range(2):
         u = x_ref[:, rr].astype(F32).reshape(LINE, D)
-        mid = (u + added[rr * LINE : (rr + 1) * LINE]).reshape(16, 2, 8, D)
-        for cc in range(2):
-            for group in range(4):
-                piece = mid[:, cc, :, group * 128 : (group + 1) * 128].reshape(128, 128)
-                mix_s[pl.ds(slot(cc, group, rr), 128, stride=16), :] = piece
+        mids.append((u + added[rr * LINE : (rr + 1) * LINE]).astype(BF16))
+    mid = jnp.concatenate(mids, axis=0)
     sends = []
     for part in range(4):
         rows = slice(part * 32, (part + 1) * 32)
-        mid_s[rows] = mix_s[part * 512 : (part + 1) * 512, :].reshape(32, 16, 128).astype(BF16)
+        turned = dot(order_s[part * 128 : (part + 1) * 128, :], mid)
+        mid_s[rows] = turned.astype(BF16).reshape(32, 4, D)
         sends.append(pltpu.make_async_copy(mid_s.at[rows], mid_ref.at[rows], mid_sem.at[part]))
         sends[-1].start()
     wait_all(saved + lefts + sends)
@@ -200,7 +233,7 @@
 def row_backward_kernel(
     where_ref, g_ref, qkv_ref, turned_ref, probs_ref, w_ref,
     send_ref, right_ref,
-    mix_s, da_s, wo_s, qkv_s, turned_s, probs_s, send_s, right_s,
+    da_s, wo_s, qkv_s, turned_s, probs_s, send_s, right_s,
     wo_sem, qkv_sem, turned_sem, probs_sem, half_sem, right_sem,
 ):
     weight = pltpu.make_async_copy(w_ref.at[3], wo_s, wo_sem)
@@ -216,16 +249,7 @@
     start_all(probs)
     turned = copies_of(turned_ref, turned_s, turned_sem, 2)
     start_all(turned)
-    mix_s[...] = g_ref[...].astype(F32).reshape(N_DEV * 16, 128)
-    for rr in range(2):
-        for group in range(4):
-            sides = [
-                mix_s[pl.ds(slot(cc, group, rr), 128, stride=16), :].reshape(16, 8, 128)
-                for cc in range(2)
-            ]
-            right_s[3, rr * LINE : (rr + 1) * LINE, group * 128 : (group + 1) * 128] = (
-                jnp.stack(sides, axis=1).reshape(LINE, 128).astype(BF16)
-            )
+    right_s[3] = dot(row_tokens_of_chunks(), g_ref[...].reshape(TOK, D)).astype(BF16)
     weight.wait()
     gain = gain_row(where_ref, 0, 0, HEADS)
     da_s[...] = (dot_nt(right_s[3], wo_s[...]) * gain).astype(BF16)
@@ -274,7 +298,7 @@
 def col_kernel(where_ref, m_ref, w_ref, *refs):
     parts, got_ref, refs = refs[:4], refs[4], refs[5:]
     gmid_ref, saved_ref = refs[:2]
-    mix_s, u_s, ulow_s, left_s, right_s, qkv_s, da_s, w_s, parts_s, got_s = refs[2:12]
+    order_s, u_s, ulow_s, left_s, right_s, qkv_s, da_s, w_s, parts_s, got_s = refs[2:12]
     w_sem, left_sem, right_sem, u_sem, parts_sem, got_sem = refs[12:]
     mine = where_ref[1]
     pieces = [
@@ -287,16 +311,8 @@
         weights[i].start()
     rights = copies_of(right_s, saved_ref, right_sem, 4)
     lefts = copies_of(left_s, saved_ref.at[4:6], left_sem, 2)
-    mix_s[...] = m_ref[...].astype(F32).reshape(N_DEV * 16, 128)
-    for cc in range(2):
-        for rr in range(2):
-            base = cc * LINE + rr * 128
-            for group in range(4):
-                for grid_row in range(N_ROW):
-                    start = base + grid_row * 16
-                    u_s[start : start + 16, group * 128 : (group + 1) * 128] = mix_s[
-                        pl.ds(grid_row * 16 + slot(cc, group, rr), 16, stride=128), :
-                    ]
+    order_s[...] = chunks_of_col_tokens()
+    u_s[...] = dot(col_tokens_of_chunks(), m_ref[...].reshape(TOK, D))
     u = u_s[...]
     ulow_s[...] = u.astype(BF16)
     kept_u = pltpu.make_async_copy(ulow_s, saved_ref.at[6], u_sem)
@@ -326,17 +342,11 @@
     each_pair(visit, 4)
     lefts[1].start()
     start_all(rights[:3])
-    for cc in range(2):
-        rows = slice(cc * LINE, (cc + 1) * LINE)
-        grad_in = input_gradient(u_s[rows, :], right_s, w_s, rows)
-        for rr in range(2):
-            for group in range(4):
-                for grid_row in range(N_ROW):
-                    start = rr * 128 + grid_row * 16
-                    mix_s[pl.ds(grid_row * 16 + slot(cc, group, rr), 16, stride=128), :] = grad_in[
-                        start : start + 16, group * 128 : (group + 1) * 128
-                    ]
-    gmid_ref[...] = mix_s[...].reshape(N_DEV, 16, 128).astype(BF16)
+    grads = [
+        input_gradient(u_s[rows, :], right_s, w_s, rows).astype(BF16)
+        for rows in (slice(0, LINE), slice(LINE, TOK))
+    ]
+    gmid_ref[...] = dot(order_s[...], jnp.concatenate(grads, axis=0)).astype(BF16).reshape(N_DEV, 4, D)
     wait_all(lefts + rights + [kept_u])
 
 
@@ -522,7 +532,6 @@
 
 MATMUL = 2 * TOK * D * D
 ATTEND = 2 * 16 * LINE * LINE * HEAD
-MIX = pltpu.VMEM((N_DEV * 16, 128), F32)
 MIX_TILE = pltpu.VMEM((4, TOK, 128), F32)
 DMA = pltpu.SemaphoreType.DMA
 WEIGHTS = [pltpu.VMEM((4, D, D), BF16), DMA((4,))]
@@ -543,9 +552,9 @@
     row_forward_kernel,
     "svh",
     "hh",
-    (shape(N_DEV, 16, 128), shape(5, TOK, D)),
+    (shape(N_DEV, 4, D), shape(5, TOK, D)),
     [
-        MIX, pltpu.VMEM((N_DEV, 16, 128), BF16), token_scratch(3), token_scratch(2), *WEIGHTS,
+        token_scratch(), pltpu.VMEM((N_DEV, 4, D), BF16), token_scratch(3), token_scratch(2), *WEIGHTS,
         DMA((4,)), DMA((3,)), DMA((2,)),
     ],
     4 * MATMUL + 2 * ATTEND,
@@ -561,7 +570,7 @@
     "hh",
     (HALF, shape(4, TOK, D)),
     [
-        MIX, token_scratch(), pltpu.VMEM((D, D), BF16), token_scratch(3),
+        token_scratch(), pltpu.VMEM((D, D), BF16), token_scratch(3),
         pltpu.VMEM((2, D, TOK), BF16), pltpu.VMEM((8, TOK, LINE), BF16), HALF_S,
         token_scratch(4), DMA, DMA((3,)), DMA((2,)), DMA((4,)), DMA, DMA((4,)),
     ],
@@ -596,9 +605,9 @@
     col_kernel,
     "svh" + "h" * 5,
     "vh",
-    (shape(N_DEV, 16, 128), shape(7, TOK, D)),
+    (shape(N_DEV, 4, D), shape(7, TOK, D)),
     [
-        MIX, token_scratch(dtype=F32), token_scratch(), token_scratch(2), token_scratch(4),
+        token_scratch(), token_scratch(dtype=F32), token_scratch(), token_scratch(2), token_scratch(4),
         token_scratch(3), token_scratch(), WEIGHTS[0], pltpu.VMEM((4, 2, 32, D), BF16),
         pltpu.VMEM((4, 2, 32, D), BF16), DMA((4,)), DMA((2,)), DMA((4,)), DMA, DMA((4,)), DMA,
     ],
@@ -639,7 +648,7 @@
     pair_sum_kernel, "svv", "v" * 4, (QUARTER,) * 4, [pltpu.VMEM((4, 256, D), BF16)], 0, 3 * MIB,
 )
 merge = call(merge_kernel, "v" * 6, "v", shape(64, 80, 128), [], 0, 4 * MIB, grant=16)
-spread = call(spread_kernel, "v", "v", shape(64, 128, 128), [], 0, 3 * MIB)
+spread = call(spread_kernel, "v", "v", shape(64, 128, 128), [], 0, 3 * MIB, grant=52)
 
 
 def widen(where, chunks, side, *before):

time: 240 us -> 243 us (1.012)
  no operation moved by 1% of the time
where the time goes in v5:
time: 243 us; the launch traced here: 238 us
  Pallas kernels  61.5 us (25%)
  blocking collectives  58.7 us (24%)
  starting transfers between devices  56.7 us (23%)
  waiting for transfers between devices  52.6 us (22%)
  local copies, waits for them, and re-layouts  7.79 us (3%)
    all_to_all x2, blocking collectives, exchange(): return lax.all_to_all(values, axes, split_axis=0, concat_axis=0, tiled=True)  58.7 us
    ppermute x20, waiting for transfers between devices, shifted(): lax.ppermute(pieces[k], axes, [(i, (i + k) % n) for i in range(n)])  33.9 us
    all_to_all x3, starting transfers between devices, exchange(): return lax.all_to_all(values, axes, split_axis=0, concat_axis=0, tiled=True)  24 us
    ppermute x20, starting transfers between devices, shifted(): lax.ppermute(pieces[k], axes, [(i, (i + k) % n) for i in range(n)])  22.1 us
    pallas_call x1, Pallas kernels, layer(): col_grad(where, mid_lines, w_col, *grad_parts, grad_pass)  12.8 us
    all_to_all x3, waiting for transfers between devices, exchange(): return lax.all_to_all(values, axes, split_axis=0, concat_axis=0, tiled=True)  12.8 us
    ppermute x5, starting transfers between devices, swap(): return lax.ppermute(value, axis, [(0, 1), (1, 0)])  10.6 us
    pallas_call x1, Pallas kernels, layer(): row_backward(where, grad_rows, saved_row, turned_row, probs_row, w_row)  9.4 us
  transfers between devices with their start and end apart: 28, of which 16 were waited for; matrix products, arithmetic and copies ran while one was open for 0% of the time, Pallas kernels for 15%

profile of v5, /device:TPU:1, one launch (start us, length us, event | category | flops | bytes accessed | tf_op | source)
XLA Modules:
  0.0 238.3 jit_solution(10571667193401588895)
XLA Ops:
  0.6 9.1 %all-to-all-start = ((bf16[16,2,16,512]{3,2,1,0:T(8,128)(2,1)}), bf16[16,2,16,512]{3,2,1,0:T(8,128)(2,1)S(1)}, u32[]{:S(2)}, u32[]{:S(2)}) async-start(bf16[16,2,16,512]{3,2,1,0:T(8,128)(2,1)} %bitcast.12), calls=%async_computation | async-start | bytes 1048576 | tf_op jit(solution)/shard_map/all_to_all | solution.py:671
  9.8 0.8 reshape.23
  10.6 10.2 %all-to-all-done.x_ref = bf16[16,2,16,512]{3,2,1,0:T(8,128)(2,1)S(1)} async-done(((bf16[16,2,16,512]{3,2,1,0:T(8,128)(2,1)}), bf16[16,2,16,512]{3,2,1,0:T(8,128)(2,1)S(1)}, u32[]{:S(2)}, u32[]{:S(2)}) %all-to-all-start) | async-done | bytes 524320 | tf_op jit(solution)/shard_map/all_to_all | solution.py:671
  20.8 1.6 copy-done.2
  22.4 7.6 %shard_map.84 = (bf16[128,4,512]{2,1,0:T(4,128)(2,1)S(1)}, bf16[5,512,512]{2,1,0:T(8,128)(2,1)}) custom-call(s32[21]{0:T(128)S(1)} %concatenate.3.where_ref, bf16[16,2,16,512]{3,2,1,0:T(8,128)(2,1)S(1)} %all-to-all-done.x_ref, bf16[4,512,512]{2,1,0:T(8,128)(2,1)S(1)} %copy-done.2), custom_call_target="tpu_custom_call" | custom-call | flops 1342177280 | bytes 6291456 | tf_op jit(solution)/shard_map/pallas_call | solution.py:694
  29.9 0.8 copy-done.11
  30.7 6.4 %all-to-all-start.1 = ((bf16[128,4,512]{2,1,0:T(4,128)(2,1)}), bf16[128,4,512]{2,1,0:T(4,128)(2,1)}, u32[]{:S(2)}, u32[]{:S(2)}) async-start(bf16[128,4,512]{2,1,0:T(4,128)(2,1)} %copy-done.11), calls=%async_computation.1 | async-start | bytes 1048576 | tf_op jit(solution)/shard_map/all_to_all | solution.py:671
  37.2 1.2 shard_map.85
  38.4 1.4 collective-permute-start
  39.8 2.5 %collective-permute-start.1 = (bf16[2,2,32,512]{3,2,1,0:T(8,128)(2,1)S(1)}, bf16[2,2,32,512]{3,2,1,0:T(8,128)(2,1)S(1)}, u32[]{:S(2)}, u32[]{:S(2)}) collective-permute-start(bf16[2,2,32,512]{3,2,1,0:T(8,128)(2,1)S(1)} %get-tuple-element.45), channel_id=1, source_target_pairs={{0,64},{32,96},{64,0},{96,32},{1,65},{33,97},{65,1},{97,33},{2,66}... | collective-permute-start | bytes 393224 | tf_op jit(solution)/shard_map/ppermute | solution.py:677
  42.3 1.1 collective-permute-start.2
  43.4 5.2 %collective-permute-done.refs_1_ = bf16[2,2,32,512]{3,2,1,0:T(8,128)(2,1)S(1)} collective-permute-done((bf16[2,2,32,512]{3,2,1,0:T(8,128)(2,1)S(1)}, bf16[2,2,32,512]{3,2,1,0:T(8,128)(2,1)S(1)}, u32[]{:S(2)}, u32[]{:S(2)}) %collective-permute-start) | collective-permute-done | bytes 131104 | tf_op jit(solution)/shard_map/ppermute | solution.py:677
  48.6 3.5 %collective-permute-done.1.refs_2_ = bf16[2,2,32,512]{3,2,1,0:T(8,128)(2,1)S(1)} collective-permute-done((bf16[2,2,32,512]{3,2,1,0:T(8,128)(2,1)S(1)}, bf16[2,2,32,512]{3,2,1,0:T(8,128)(2,1)S(1)}, u32[]{:S(2)}, u32[]{:S(2)}) %collective-permute-start.1) | collective-permute-done | bytes 131104 | tf_op jit(solution)/shard_map/ppermute | solution.py:677
  52.1 0.6 shard_map.86
  52.7 1.7 collective-permute-start.3
  54.4 5.9 %collective-permute-done.3.refs_4_ = bf16[4,2,32,512]{3,2,1,0:T(8,128)(2,1)S(1)} collective-permute-done((bf16[4,2,32,512]{3,2,1,0:T(8,128)(2,1)S(1)}, bf16[4,2,32,512]{3,2,1,0:T(8,128)(2,1)S(1)}, u32[]{:S(2)}, u32[]{:S(2)}) %collective-permute-start.3) | collective-permute-done | bytes 262176 | tf_op jit(solution)/shard_map/ppermute | solution.py:682
  60.3 12.8 %shard_map.87 = (bf16[128,4,512]{2,1,0:T(4,128)(2,1)}, bf16[7,512,512]{2,1,0:T(8,128)(2,1)}) custom-call(s32[21]{0:T(128)S(1)} %concatenate.3.where_ref, bf16[128,4,512]{2,1,0:T(4,128)(2,1)} %all-to-all-done.1.m_ref, bf16[4,512,512]{2,1,0:T(8,128)(2,1)S(1)} %copy-done.6, bf16[2,2,32,512]{3,2,1,0:T(8,128)(2,1)S(1)} %get-tuple-element.43.refs_0_, ...), custom_call_target="tpu_custom_call" | custom-call | flops 2952790016 | bytes 8388608 | tf_op jit(solution)/shard_map/pallas_call | solution.py:697
  73.2 8.4 %all-to-all-start.2 = ((bf16[128,4,512]{2,1,0:T(4,128)(2,1)}), bf16[128,4,512]{2,1,0:T(4,128)(2,1)}, u32[]{:S(2)}, u32[]{:S(2)}) async-start(bf16[128,4,512]{2,1,0:T(4,128)(2,1)} %get-tuple-element.56), calls=%async_computation.2 | async-start | bytes 1048576 | tf_op jit(solution)/shard_map/all_to_all | solution.py:671
  81.6 3.1 %shard_map.96 = (bf16[2,512,512]{2,1,0:T(8,128)(2,1)S(1)}, bf16[2,512,512]{2,1,0:T(8,128)(2,1)S(1)}) custom-call(s32[21]{0:T(128)S(1)} %concatenate.3.where_ref, bf16[7,512,512]{2,1,0:T(8,128)(2,1)} %get-tuple-element.47.saved_ref.right_ref), custom_call_target="tpu_custom_call" | custom-call | flops 536870912 | bytes 6291456 | tf_op jit(solution)/shard_map/pallas_call | solution.py:701
  84.8 1.0 copy-done.8
  85.7 1.1 collective-permute-start.20
  86.9 2.4 %shard_map.90 = (bf16[8,512,256]{2,1,0:T(8,128)(2,1)S(1)}, bf16[2,512,512]{2,1,0:T(8,128)(2,1)S(1)}) custom-call(bf16[5,512,512]{2,1,0:T(8,128)(2,1)S(1)} %copy-done), custom_call_target="tpu_custom_call" | custom-call | flops 134217728 | bytes 8388608 | tf_op jit(solution)/shard_map/pallas_call | solution.py:696
  89.3 1.0 copy-done.3
  90.3 1.3 copy-done.7
  91.7 2.6 %all-to-all-done.2.g_ref = bf16[128,4,512]{2,1,0:T(4,128)(2,1)} async-done(((bf16[128,4,512]{2,1,0:T(4,128)(2,1)}), bf16[128,4,512]{2,1,0:T(4,128)(2,1)}, u32[]{:S(2)}, u32[]{:S(2)}) %all-to-all-start.2) | async-done | bytes 524320 | tf_op jit(solution)/shard_map/all_to_all | solution.py:671
  94.3 1.2 copy-done.4
  95.5 9.4 %shard_map.91 = (bf16[2,512,512]{2,1,0:T(8,128)(2,1)S(1)}, bf16[4,512,512]{2,1,0:T(8,128)(2,1)}) custom-call(s32[21]{0:T(128)S(1)} %concatenate.3.where_ref, bf16[128,4,512]{2,1,0:T(4,128)(2,1)} %all-to-all-done.2.g_ref, bf16[5,512,512]{2,1,0:T(8,128)(2,1)} %get-tuple-element.57.saved_ref.qkv_ref, bf16[2,512,512]{2,1,0:T(8,128)(2,1)S(1)} %copy-done.4, ...), custom_call_target="tpu_custom_call" | custom-call | flops 2013265920 | bytes 12582912 | tf_op jit(solution)/shard_map/pallas_call | solution.py:706
  104.9 1.7 collective-permute-start.19
  106.7 2.6 %shard_map.97.keep_ref = bf16[2,512,512]{2,1,0:T(8,128)(2,1)S(1)} custom-call(s32[21]{0:T(128)S(1)} %concatenate.3.where_ref, bf16[2,512,512]{2,1,0:T(8,128)(2,1)S(1)} %copy-done.9, bf16[7,512,512]{2,1,0:T(8,128)(2,1)} %get-tuple-element.47.saved_ref.right_ref), custom_call_target="tpu_custom_call" | custom-call | flops 536870912 | bytes 3145728 | tf_op jit(solution)/shard_map/pallas_call | solution.py:703
  109.2 1.9 shard_map.98
  111.6 1.9 collective-permute-start.22
  113.5 0.9 collective-permute-start.23
  114.4 2.6 %shard_map.95.keep_ref = bf16[2,512,512]{2,1,0:T(8,128)(2,1)S(1)} custom-call(s32[21]{0:T(128)S(1)} %concatenate.3.where_ref, bf16[2,512,512]{2,1,0:T(8,128)(2,1)S(1)} %copy-done.5, bf16[4,512,512]{2,1,0:T(8,128)(2,1)} %get-tuple-element.60.right_ref), custom_call_target="tpu_custom_call" | custom-call | flops 536870912 | bytes 3145728 | tf_op jit(solution)/shard_map/pallas_call | solution.py:708
  116.9 3.8 %collective-permute-done.21.refs_1_ = bf16[256,512]{1,0:T(8,128)(2,1)S(1)} collective-permute-done((bf16[256,512]{1,0:T(8,128)(2,1)S(1)}, bf16[256,512]{1,0:T(8,128)(2,1)S(1)}, u32[]{:S(2)}, u32[]{:S(2)}) %collective-permute-start.21) | collective-permute-done | bytes 262176 | tf_op jit(solution)/shard_map/ppermute | solution.py:677
  120.8 4.7 %collective-permute-done.22.refs_2_ = bf16[256,512]{1,0:T(8,128)(2,1)S(1)} collective-permute-done((bf16[256,512]{1,0:T(8,128)(2,1)S(1)}, bf16[256,512]{1,0:T(8,128)(2,1)S(1)}, u32[]{:S(2)}, u32[]{:S(2)}) %collective-permute-start.22) | collective-permute-done | bytes 262176 | tf_op jit(solution)/shard_map/ppermute | solution.py:677
  125.5 0.8 collective-permute-done.23.refs_3_
  126.7 26.0 %all_to_all.25.both_ref = bf16[64,80,128]{2,1,0:T(8,128)(2,1)S(1)} all-to-all(bf16[64,80,128]{2,1,0:T(8,128)(2,1)S(1)} %shard_map.99), channel_id=1, replica_groups=mesh['y'=4,'zl'=2,'zh'=2,'x'=4,'c'=2] {'y','zl','zh','x'}, dimensions={0} | all-to-all | bytes 2621440 | tf_op jit(solution)/shard_map/all_to_all | solution.py:671
  152.7 1.7 shard_map.100
  154.4 32.6 %all_to_all.26.chunks_ref = bf16[64,128,128]{2,1,0:T(8,128)(2,1)S(1)} all-to-all(bf16[64,128,128]{2,1,0:T(8,128)(2,1)} %shard_map.100), channel_id=1, replica_groups=mesh['y'=4,'zl'=2,'zh'=2,'x'=4,'c'=2] {'y','zl','zh','x'}, dimensions={0} | all-to-all | bytes 4194304 | tf_op jit(solution)/shard_map/all_to_all | solution.py:671
  187.1 3.3 %collective-permute-start.24 = (bf16[64,128,128]{2,1,0:T(8,128)(2,1)S(1)}, bf16[64,128,128]{2,1,0:T(8,128)(2,1)S(1)}, u32[]{:S(2)}, u32[]{:S(2)}) collective-permute-start(bf16[64,128,128]{2,1,0:T(8,128)(2,1)S(1)} %all_to_all.26.chunks_ref), channel_id=1, source_target_pairs={{0,1},{1,0},{2,3},{3,2},{4,5},{5,4},{6,7},{7,6},{8,9},{9,8},{10,11... | collective-permute-start | bytes 6291464 | tf_op jit(solution)/shard_map/ppermute | solution.py:682
  190.4 3.2 %shard_map.92 = (bf16[2,2,16,512]{3,2,1,0:T(8,128)(2,1)S(1)}, bf16[2,2,16,512]{3,2,1,0:T(8,128)(2,1)S(1)}, bf16[2,2,16,512]{3,2,1,0:T(8,128)(2,1)S(1)}, bf16[2,2...) custom-call(s32[21]{0:T(128)S(1)} %concatenate.3.where_ref, ...), custom_call_target="tpu_custom_call" | custom-call | flops 805306368 | bytes 5242880 | tf_op jit(solution)/shard_map/pallas_call | solution.py:713
  193.7 2.2 collective-permute-start.12
  195.8 1.5 collective-permute-start.13
  197.4 2.4 collective-permute-start.14
  199.7 3.0 %collective-permute-done.11.refs_1_ = bf16[2,2,16,512]{3,2,1,0:T(8,128)(2,1)S(1)} collective-permute-done((bf16[2,2,16,512]{3,2,1,0:T(8,128)(2,1)S(1)}, bf16[2,2,16,512]{3,2,1,0:T(8,128)(2,1)S(1)}, u32[]{:S(2)}, u32[]{:S(2)}) %collective-permute-start.11) | collective-permute-done | bytes 65568 | tf_op jit(solution)/shard_map/ppermute | solution.py:677
  202.7 1.6 collective-permute-start.16
  204.3 2.6 %collective-permute-start.17 = (bf16[2,2,16,512]{3,2,1,0:T(8,128)(2,1)S(1)}, bf16[2,2,16,512]{3,2,1,0:T(8,128)(2,1)S(1)}, u32[]{:S(2)}, u32[]{:S(2)}) collective-permute-start(bf16[2,2,16,512]{3,2,1,0:T(8,128)(2,1)S(1)} %get-tuple-element.68), channel_id=1, source_target_pairs={{0,14},{2,0},{4,2},{6,4},{8,6},{10,8},{12,10},{14,12},{1,15},{3,1}... | collective-permute-start | bytes 196616 | tf_op jit(solution)/shard_map/ppermute | solution.py:677
  206.9 0.8 collective-permute-done.15.refs_5_
  207.7 1.8 collective-permute-done.17.refs_7_
  209.5 0.6 shard_map.93
  210.1 2.7 %collective-permute-start.18 = (bf16[8,2,16,512]{3,2,1,0:T(8,128)(2,1)S(1)}, bf16[8,2,16,512]{3,2,1,0:T(8,128)(2,1)S(1)}, u32[]{:S(2)}, u32[]{:S(2)}) collective-permute-start(bf16[8,2,16,512]{3,2,1,0:T(8,128)(2,1)S(1)} %shard_map.93), channel_id=1, source_target_pairs={{0,1},{1,0},{2,3},{3,2},{4,5},{5,4},{6,7},{7,6},{8,9},{9,8},{10,11... | collective-permute-start | bytes 786440 | tf_op jit(solution)/shard_map/ppermute | solution.py:682
  212.8 2.4 %shard_map.88 = (bf16[2,32,512]{2,1,0:T(8,128)(2,1)S(1)}, bf16[2,32,512]{2,1,0:T(8,128)(2,1)S(1)}, bf16[2,32,512]{2,1,0:T(8,128)(2,1)S(1)}, bf16[2,32,512]{2,1,0...) custom-call(s32[21]{0:T(128)S(1)} %concatenate.3.where_ref, ...), custom_call_target="tpu_custom_call" | custom-call | flops 268435456 | bytes 3145728 | tf_op jit(solution)/shard_map/pallas_call | solution.py:718
  215.5 1.9 collective-permute-start.6
  217.4 3.7 %collective-permute-done.4.refs_1_ = bf16[2,32,512]{2,1,0:T(8,128)(2,1)S(1)} collective-permute-done((bf16[2,32,512]{2,1,0:T(8,128)(2,1)S(1)}, bf16[2,32,512]{2,1,0:T(8,128)(2,1)S(1)}, u32[]{:S(2)}, u32[]{:S(2)}) %collective-permute-start.4) | collective-permute-done | bytes 65568 | tf_op jit(solution)/shard_map/ppermute | solution.py:677
  221.0 0.8 collective-permute-start.8
  221.8 1.2 collective-permute-done.6.refs_3_
  223.0 0.6 collective-permute-start.9
  223.7 2.0 collective-permute-done.7.refs_4_
  225.7 0.5 collective-permute-done.9.refs_6_
  226.2 2.9 %collective-permute-done.10.refs_7_ = bf16[2,32,512]{2,1,0:T(8,128)(2,1)S(1)} collective-permute-done((bf16[2,32,512]{2,1,0:T(8,128)(2,1)S(1)}, bf16[2,32,512]{2,1,0:T(8,128)(2,1)S(1)}, u32[]{:S(2)}, u32[]{:S(2)}) %collective-permute-start.10) | collective-permute-done | bytes 65568 | tf_op jit(solution)/shard_map/ppermute | solution.py:677
  229.1 2.3 shard_map.89
  231.3 1.4 shard_map.94
  232.7 2.7 %widen.2 = (f32[2,1024,512]{2,1,0:T(8,128)}, f32[2,4,256,512]{3,2,1,0:T(8,128)}) custom-call(s32[21]{0:T(128)S(1)} %concatenate.3.where_ref, bf16[64,128,128]{2,1,0:T(8,128)(2,1)S(1)} %all_to_all.26.chunks_ref), custom_call_target="tpu_custom_call" | custom-call | bytes 6291456 | tf_op jit(solution)/shard_map/widen/pallas_call | solution.py:655
  235.4 2.7 %widen.3 = (f32[2,1024,512]{2,1,0:T(8,128)}, f32[2,4,256,512]{3,2,1,0:T(8,128)}) custom-call(s32[21]{0:T(128)S(1)} %concatenate.3.where_ref, bf16[64,128,128]{2,1,0:T(8,128)(2,1)S(1)} %collective-permute-done.24.chunks_ref, f32[2,1024,512]{2,1,0:T(8,128)} %get-tuple-element.76.refs_0_, ...), custom_call_target="tpu_custom_call", output_to_operand_aliasing={{0}: (2, {}), {1}: (3, {})} | custom-call | bytes 6291456 | tf_op jit(solution)/shard_map/widen/pallas_call | solution.py:655
  (39 shorter events, 1.3 us)
Async XLA Ops:
  0.6 20.1 %all-to-all-start = ((bf16[16,2,16,512]{3,2,1,0:T(8,128)(2,1)}), bf16[16,2,16,512]{3,2,1,0:T(8,128)(2,1)S(1)}, u32[]{:S(2)}, u32[]{:S(2)}) async-start(bf16[16,2,16,512]{3,2,1,0:T(8,128)(2,1)} %bitcast.12), calls=%async_computation | async-start | bytes 1048576 | tf_op jit(solution)/shard_map/all_to_all | solution.py:671
  20.8 1.6 copy-start.2
  22.3 14.8 %copy-start.10 = (bf16[32,16,512]{2,1,0:T(8,128)(2,1)S(1)}, bf16[32,16,512]{2,1,0:T(8,128)(2,1)}, u32[]{:S(2)}) copy-start(bf16[32,16,512]{2,1,0:T(8,128)(2,1)} %tile_ref.1) | copy-start | bytes 1572868
  29.9 0.8 copy-start.11
  30.7 29.6 %copy-start.6 = (bf16[4,512,512]{2,1,0:T(8,128)(2,1)S(1)}, bf16[4,512,512]{2,1,0:T(8,128)(2,1)}, u32[]{:S(2)}) copy-start(bf16[4,512,512]{2,1,0:T(8,128)(2,1)} %w_ref.7) | copy-start | bytes 6291460
  30.7 29.6 %all-to-all-start.1 = ((bf16[128,4,512]{2,1,0:T(4,128)(2,1)}), bf16[128,4,512]{2,1,0:T(4,128)(2,1)}, u32[]{:S(2)}, u32[]{:S(2)}) async-start(bf16[128,4,512]{2,1,0:T(4,128)(2,1)} %copy-done.11), calls=%async_computation.1 | async-start | bytes 1048576 | tf_op jit(solution)/shard_map/all_to_all | solution.py:671
  38.4 10.2 %collective-permute-start = (bf16[2,2,32,512]{3,2,1,0:T(8,128)(2,1)S(1)}, bf16[2,2,32,512]{3,2,1,0:T(8,128)(2,1)S(1)}, u32[]{:S(2)}, u32[]{:S(2)}) collective-permute-start(bf16[2,2,32,512]{3,2,1,0:T(8,128)(2,1)S(1)} %get-tuple-element.44), channel_id=1, source_target_pairs={{0,32},{32,64},{64,96},{96,0},{1,33},{33,65},{65,97},{97,1},{2,34}... | collective-permute-start | bytes 393224 | tf_op jit(solution)/shard_map/ppermute | solution.py:677
  39.8 12.3 %collective-permute-start.1 = (bf16[2,2,32,512]{3,2,1,0:T(8,128)(2,1)S(1)}, bf16[2,2,32,512]{3,2,1,0:T(8,128)(2,1)S(1)}, u32[]{:S(2)}, u32[]{:S(2)}) collective-permute-start(bf16[2,2,32,512]{3,2,1,0:T(8,128)(2,1)S(1)} %get-tuple-element.45), channel_id=1, source_target_pairs={{0,64},{32,96},{64,0},{96,32},{1,65},{33,97},{65,1},{97,33},{2,66}... | collective-permute-start | bytes 393224 | tf_op jit(solution)/shard_map/ppermute | solution.py:677
  42.3 9.8 %collective-permute-start.2 = (bf16[2,2,32,512]{3,2,1,0:T(8,128)(2,1)S(1)}, bf16[2,2,32,512]{3,2,1,0:T(8,128)(2,1)S(1)}, u32[]{:S(2)}, u32[]{:S(2)}) collective-permute-start(bf16[2,2,32,512]{3,2,1,0:T(8,128)(2,1)S(1)} %get-tuple-element.46), channel_id=1, source_target_pairs={{0,96},{32,0},{64,32},{96,64},{1,97},{33,1},{65,33},{97,65},{2,98}... | collective-permute-start | bytes 393224 | tf_op jit(solution)/shard_map/ppermute | solution.py:677
  52.7 7.6 %collective-permute-start.3 = (bf16[4,2,32,512]{3,2,1,0:T(8,128)(2,1)S(1)}, bf16[4,2,32,512]{3,2,1,0:T(8,128)(2,1)S(1)}, u32[]{:S(2)}, u32[]{:S(2)}) collective-permute-start(bf16[4,2,32,512]{3,2,1,0:T(8,128)(2,1)S(1)} %shard_map.86), channel_id=1, source_target_pairs={{0,16},{16,0},{1,17},{17,1},{2,18},{18,2},{3,19},{19,3},{4,20},{20... | collective-permute-start | bytes 786440 | tf_op jit(solution)/shard_map/ppermute | solution.py:682
  73.2 21.1 %all-to-all-start.2 = ((bf16[128,4,512]{2,1,0:T(4,128)(2,1)}), bf16[128,4,512]{2,1,0:T(4,128)(2,1)}, u32[]{:S(2)}, u32[]{:S(2)}) async-start(bf16[128,4,512]{2,1,0:T(4,128)(2,1)} %get-tuple-element.56), calls=%async_computation.2 | async-start | bytes 1048576 | tf_op jit(solution)/shard_map/all_to_all | solution.py:671
  81.6 5.3 %copy-start = (bf16[5,512,512]{2,1,0:T(8,128)(2,1)S(1)}, bf16[5,512,512]{2,1,0:T(8,128)(2,1)}, u32[]{:S(2)}) copy-start(bf16[5,512,512]{2,1,0:T(8,128)(2,1)} %get-tuple-element.57.saved_ref.qkv_ref) | copy-start | bytes 7864324
  84.8 1.0 copy-start.8
  85.7 23.5 %collective-permute-start.20 = (bf16[2,512,512]{2,1,0:T(8,128)(2,1)S(1)}, bf16[2,512,512]{2,1,0:T(8,128)(2,1)}, u32[]{:S(2)}, u32[]{:S(2)}) collective-permute-start(bf16[2,512,512]{2,1,0:T(8,128)(2,1)S(1)} %get-tuple-element.71), channel_id=1, source_target_pairs={{0,1},{1,0},{2,3},{3,2},{4,5},{5,4},{6,7},{7,6},{8,9},{9,8},{10,11... | collective-permute-start | bytes 3145736 | tf_op jit(solution)/shard_map/ppermute | solution.py:682
  89.3 1.0 copy-start.3
  90.3 1.3 copy-start.7
  94.3 1.2 copy-start.4
  95.5 11.1 %copy-start.9 = (bf16[2,512,512]{2,1,0:T(8,128)(2,1)S(1)}, bf16[2,512,512]{2,1,0:T(8,128)(2,1)}, u32[]{:S(2)}) copy-start(bf16[2,512,512]{2,1,0:T(8,128)(2,1)} %copy-done.8) | copy-start | bytes 3145732
  104.9 21.4 %collective-permute-start.19 = (bf16[2,512,512]{2,1,0:T(8,128)(2,1)S(1)}, bf16[2,512,512]{2,1,0:T(8,128)(2,1)S(1)}, u32[]{:S(2)}, u32[]{:S(2)}) collective-permute-start(bf16[2,512,512]{2,1,0:T(8,128)(2,1)S(1)} %get-tuple-element.69), channel_id=1, source_target_pairs={{0,1},{1,0},{2,3},{3,2},{4,5},{5,4},{6,7},{7,6},{8,9},{9,8},{10,11... | collective-permute-start | bytes 3145736 | tf_op jit(solution)/shard_map/ppermute | solution.py:682
  109.2 5.1 %copy-start.5 = (bf16[2,512,512]{2,1,0:T(8,128)(2,1)S(1)}, bf16[2,512,512]{2,1,0:T(8,128)(2,1)}, u32[]{:S(2)}) copy-start(bf16[2,512,512]{2,1,0:T(8,128)(2,1)} %copy-done.3) | copy-start | bytes 3145732
  111.2 9.6 %collective-permute-start.21 = (bf16[256,512]{1,0:T(8,128)(2,1)S(1)}, bf16[256,512]{1,0:T(8,128)(2,1)S(1)}, u32[]{:S(2)}, u32[]{:S(2)}) collective-permute-start(bf16[256,512]{1,0:T(8,128)(2,1)S(1)} %get-tuple-element.73), channel_id=1, source_target_pairs={{0,2},{2,4},{4,6},{6,0},{1,3},{3,5},{5,7},{7,1},{8,10},{10,12},{12... | collective-permute-start | bytes 786440 | tf_op jit(solution)/shard_map/ppermute | solution.py:677
  111.6 13.9 %collective-permute-start.22 = (bf16[256,512]{1,0:T(8,128)(2,1)S(1)}, bf16[256,512]{1,0:T(8,128)(2,1)S(1)}, u32[]{:S(2)}, u32[]{:S(2)}) collective-permute-start(bf16[256,512]{1,0:T(8,128)(2,1)S(1)} %get-tuple-element.74), channel_id=1, source_target_pairs={{0,4},{2,6},{4,0},{6,2},{1,5},{3,7},{5,1},{7,3},{8,12},{10,14},{12... | collective-permute-start | bytes 786440 | tf_op jit(solution)/shard_map/ppermute | solution.py:677
  113.5 12.8 %collective-permute-start.23 = (bf16[256,512]{1,0:T(8,128)(2,1)S(1)}, bf16[256,512]{1,0:T(8,128)(2,1)S(1)}, u32[]{:S(2)}, u32[]{:S(2)}) collective-permute-start(bf16[256,512]{1,0:T(8,128)(2,1)S(1)} %get-tuple-element.75), channel_id=1, source_target_pairs={{0,6},{2,0},{4,2},{6,4},{1,7},{3,1},{5,3},{7,5},{8,14},{10,8},{12,... | collective-permute-start | bytes 786440 | tf_op jit(solution)/shard_map/ppermute | solution.py:677
  154.4 35.9 %copy-start.1 = (bf16[4,512,512]{2,1,0:T(8,128)(2,1)S(1)}, bf16[4,512,512]{2,1,0:T(8,128)(2,1)}, u32[]{:S(2)}) copy-start(bf16[4,512,512]{2,1,0:T(8,128)(2,1)} %get-tuple-element.60.right_ref) | copy-start | bytes 6291460
  187.1 48.3 %collective-permute-start.24 = (bf16[64,128,128]{2,1,0:T(8,128)(2,1)S(1)}, bf16[64,128,128]{2,1,0:T(8,128)(2,1)S(1)}, u32[]{:S(2)}, u32[]{:S(2)}) collective-permute-start(bf16[64,128,128]{2,1,0:T(8,128)(2,1)S(1)} %all_to_all.26.chunks_ref), channel_id=1, source_target_pairs={{0,1},{1,0},{2,3},{3,2},{4,5},{5,4},{6,7},{7,6},{8,9},{9,8},{10,11... | collective-permute-start | bytes 6291464 | tf_op jit(solution)/shard_map/ppermute | solution.py:682
  193.6 9.1 %collective-permute-start.11 = (bf16[2,2,16,512]{3,2,1,0:T(8,128)(2,1)S(1)}, bf16[2,2,16,512]{3,2,1,0:T(8,128)(2,1)S(1)}, u32[]{:S(2)}, u32[]{:S(2)}) collective-permute-start(bf16[2,2,16,512]{3,2,1,0:T(8,128)(2,1)S(1)} %get-tuple-element.62), channel_id=1, source_target_pairs={{0,2},{2,4},{4,6},{6,8},{8,10},{10,12},{12,14},{14,0},{1,3},{3,5},... | collective-permute-start | bytes 196616 | tf_op jit(solution)/shard_map/ppermute | solution.py:677
  193.7 9.0 %collective-permute-start.12 = (bf16[2,2,16,512]{3,2,1,0:T(8,128)(2,1)S(1)}, bf16[2,2,16,512]{3,2,1,0:T(8,128)(2,1)S(1)}, u32[]{:S(2)}, u32[]{:S(2)}) collective-permute-start(bf16[2,2,16,512]{3,2,1,0:T(8,128)(2,1)S(1)} %get-tuple-element.63), channel_id=1, source_target_pairs={{0,4},{2,6},{4,8},{6,10},{8,12},{10,14},{12,0},{14,2},{1,5},{3,7},... | collective-permute-start | bytes 196616 | tf_op jit(solution)/shard_map/ppermute | solution.py:677
  195.8 8.5 %collective-permute-start.13 = (bf16[2,2,16,512]{3,2,1,0:T(8,128)(2,1)S(1)}, bf16[2,2,16,512]{3,2,1,0:T(8,128)(2,1)S(1)}, u32[]{:S(2)}, u32[]{:S(2)}) collective-permute-start(bf16[2,2,16,512]{3,2,1,0:T(8,128)(2,1)S(1)} %get-tuple-element.64), channel_id=1, source_target_pairs={{0,6},{2,8},{4,10},{6,12},{8,14},{10,0},{12,2},{14,4},{1,7},{3,9},... | collective-permute-start | bytes 196616 | tf_op jit(solution)/shard_map/ppermute | solution.py:677
  197.4 9.5 %collective-permute-start.14 = (bf16[2,2,16,512]{3,2,1,0:T(8,128)(2,1)S(1)}, bf16[2,2,16,512]{3,2,1,0:T(8,128)(2,1)S(1)}, u32[]{:S(2)}, u32[]{:S(2)}) collective-permute-start(bf16[2,2,16,512]{3,2,1,0:T(8,128)(2,1)S(1)} %get-tuple-element.65), channel_id=1, source_target_pairs={{0,8},{2,10},{4,12},{6,14},{8,0},{10,2},{12,4},{14,6},{1,9},{3,11}... | collective-permute-start | bytes 196616 | tf_op jit(solution)/shard_map/ppermute | solution.py:677
  202.7 5.0 %collective-permute-start.15 = (bf16[2,2,16,512]{3,2,1,0:T(8,128)(2,1)S(1)}, bf16[2,2,16,512]{3,2,1,0:T(8,128)(2,1)S(1)}, u32[]{:S(2)}, u32[]{:S(2)}) collective-permute-start(bf16[2,2,16,512]{3,2,1,0:T(8,128)(2,1)S(1)} %get-tuple-element.66), channel_id=1, source_target_pairs={{0,10},{2,12},{4,14},{6,0},{8,2},{10,4},{12,6},{14,8},{1,11},{3,13... | collective-permute-start | bytes 196616 | tf_op jit(solution)/shard_map/ppermute | solution.py:677
  202.7 5.0 %collective-permute-start.16 = (bf16[2,2,16,512]{3,2,1,0:T(8,128)(2,1)S(1)}, bf16[2,2,16,512]{3,2,1,0:T(8,128)(2,1)S(1)}, u32[]{:S(2)}, u32[]{:S(2)}) collective-permute-start(bf16[2,2,16,512]{3,2,1,0:T(8,128)(2,1)S(1)} %get-tuple-element.67), channel_id=1, source_target_pairs={{0,12},{2,14},{4,0},{6,2},{8,4},{10,6},{12,8},{14,10},{1,13},{3,15... | collective-permute-start | bytes 196616 | tf_op jit(solution)/shard_map/ppermute | solution.py:677
  204.3 5.2 %collective-permute-start.17 = (bf16[2,2,16,512]{3,2,1,0:T(8,128)(2,1)S(1)}, bf16[2,2,16,512]{3,2,1,0:T(8,128)(2,1)S(1)}, u32[]{:S(2)}, u32[]{:S(2)}) collective-permute-start(bf16[2,2,16,512]{3,2,1,0:T(8,128)(2,1)S(1)} %get-tuple-element.68), channel_id=1, source_target_pairs={{0,14},{2,0},{4,2},{6,4},{8,6},{10,8},{12,10},{14,12},{1,15},{3,1}... | collective-permute-start | bytes 196616 | tf_op jit(solution)/shard_map/ppermute | solution.py:677
  210.1 21.2 %collective-permute-start.18 = (bf16[8,2,16,512]{3,2,1,0:T(8,128)(2,1)S(1)}, bf16[8,2,16,512]{3,2,1,0:T(8,128)(2,1)S(1)}, u32[]{:S(2)}, u32[]{:S(2)}) collective-permute-start(bf16[8,2,16,512]{3,2,1,0:T(8,128)(2,1)S(1)} %shard_map.93), channel_id=1, source_target_pairs={{0,1},{1,0},{2,3},{3,2},{4,5},{5,4},{6,7},{7,6},{8,9},{9,8},{10,11... | collective-permute-start | bytes 786440 | tf_op jit(solution)/shard_map/ppermute | solution.py:682
  215.2 5.8 %collective-permute-start.4 = (bf16[2,32,512]{2,1,0:T(8,128)(2,1)S(1)}, bf16[2,32,512]{2,1,0:T(8,128)(2,1)S(1)}, u32[]{:S(2)}, u32[]{:S(2)}) collective-permute-start(bf16[2,32,512]{2,1,0:T(8,128)(2,1)S(1)} %get-tuple-element.49), channel_id=1, source_target_pairs={{0,16},{16,32},{32,48},{48,64},{64,80},{80,96},{96,112},{112,0},{1... | collective-permute-start | bytes 196616 | tf_op jit(solution)/shard_map/ppermute | solution.py:677
  215.5 5.6 %collective-permute-start.5 = (bf16[2,32,512]{2,1,0:T(8,128)(2,1)S(1)}, bf16[2,32,512]{2,1,0:T(8,128)(2,1)S(1)}, u32[]{:S(2)}, u32[]{:S(2)}) collective-permute-start(bf16[2,32,512]{2,1,0:T(8,128)(2,1)S(1)} %get-tuple-element.50), channel_id=1, source_target_pairs={{0,32},{16,48},{32,64},{48,80},{64,96},{80,112},{96,0},{112,16},{1... | collective-permute-start | bytes 196616 | tf_op jit(solution)/shard_map/ppermute | solution.py:677
  215.5 7.6 %collective-permute-start.6 = (bf16[2,32,512]{2,1,0:T(8,128)(2,1)S(1)}, bf16[2,32,512]{2,1,0:T(8,128)(2,1)S(1)}, u32[]{:S(2)}, u32[]{:S(2)}) collective-permute-start(bf16[2,32,512]{2,1,0:T(8,128)(2,1)S(1)} %get-tuple-element.51), channel_id=1, source_target_pairs={{0,48},{16,64},{32,80},{48,96},{64,112},{80,0},{96,16},{112,32},{1... | collective-permute-start | bytes 196616 | tf_op jit(solution)/shard_map/ppermute | solution.py:677
  221.0 4.6 %collective-permute-start.7 = (bf16[2,32,512]{2,1,0:T(8,128)(2,1)S(1)}, bf16[2,32,512]{2,1,0:T(8,128)(2,1)S(1)}, u32[]{:S(2)}, u32[]{:S(2)}) collective-permute-start(bf16[2,32,512]{2,1,0:T(8,128)(2,1)S(1)} %get-tuple-element.52), channel_id=1, source_target_pairs={{0,64},{16,80},{32,96},{48,112},{64,0},{80,16},{96,32},{112,48},{1... | collective-permute-start | bytes 196616 | tf_op jit(solution)/shard_map/ppermute | solution.py:677
  221.0 4.6 %collective-permute-start.8 = (bf16[2,32,512]{2,1,0:T(8,128)(2,1)S(1)}, bf16[2,32,512]{2,1,0:T(8,128)(2,1)S(1)}, u32[]{:S(2)}, u32[]{:S(2)}) collective-permute-start(bf16[2,32,512]{2,1,0:T(8,128)(2,1)S(1)} %get-tuple-element.53), channel_id=1, source_target_pairs={{0,80},{16,96},{32,112},{48,0},{64,16},{80,32},{96,48},{112,64},{1... | collective-permute-start | bytes 196616 | tf_op jit(solution)/shard_map/ppermute | solution.py:677
  223.0 3.1 %collective-permute-start.9 = (bf16[2,32,512]{2,1,0:T(8,128)(2,1)S(1)}, bf16[2,32,512]{2,1,0:T(8,128)(2,1)S(1)}, u32[]{:S(2)}, u32[]{:S(2)}) collective-permute-start(bf16[2,32,512]{2,1,0:T(8,128)(2,1)S(1)} %get-tuple-element.54), channel_id=1, source_target_pairs={{0,96},{16,112},{32,0},{48,16},{64,32},{80,48},{96,64},{112,80},{1... | collective-permute-start | bytes 196616 | tf_op jit(solution)/shard_map/ppermute | solution.py:677
  225.7 3.4 %collective-permute-start.10 = (bf16[2,32,512]{2,1,0:T(8,128)(2,1)S(1)}, bf16[2,32,512]{2,1,0:T(8,128)(2,1)S(1)}, u32[]{:S(2)}, u32[]{:S(2)}) collective-permute-start(bf16[2,32,512]{2,1,0:T(8,128)(2,1)S(1)} %get-tuple-element.55), channel_id=1, source_target_pairs={{0,112},{16,0},{32,16},{48,32},{64,48},{80,64},{96,80},{112,96},{1... | collective-permute-start | bytes 196616 | tf_op jit(solution)/shard_map/ppermute | solution.py:677

commit v6 on v5

--- a/solution.py
+++ b/solution.py
@@ -126,19 +126,18 @@
         copy.wait()
 
 
-def project(normed, qkv_ref, w_s, copies):
-    copies[0].wait()
-    qkv_ref[0] = (dot(normed, w_s[0]).astype(BF16).astype(F32) * SCALE).astype(BF16)
-    copies[1].wait()
-    qkv_ref[1] = dot(normed, w_s[1]).astype(BF16)
-    copies[2].wait()
-    qkv_ref[2] = dot(normed, w_s[2]).astype(BF16)
-
-
-def each_pair(visit, per_step=2):
+def project(normed, qkv_ref, w_ref):
+    qkv_ref[0] = (dot(normed, w_ref[0]).astype(BF16).astype(F32) * SCALE).astype(BF16)
+    qkv_ref[1] = dot(normed, w_ref[1]).astype(BF16)
+    qkv_ref[2] = dot(normed, w_ref[2]).astype(BF16)
+
+
+def each_pair(visit, per_step=2, before=None):
     def step(index, carry):
         line = index // (N_PAIR // per_step)
         first = lax.rem(index, N_PAIR // per_step) * per_step
+        if before is not None:
+            before(line)
         rows = pl.ds(pl.multiple_of(line * LINE, LINE), LINE)
         for offset in range(per_step):
             pair = first + offset
@@ -151,17 +150,15 @@
 
 def row_forward_kernel(
     where_ref, x_ref, w_ref, mid_ref, saved_ref,
-    order_s, mid_s, qkv_s, left_s, w_s, w_sem, mid_sem, qkv_sem, left_sem,
+    order_s, mid_s, qkv_s, left_s, mid_sem, qkv_sem, left_sem,
 ):
-    weights = copies_of(w_ref, w_s, w_sem, 4)
-    start_all(weights)
     saved = copies_of(qkv_s, saved_ref, qkv_sem, 3)
     lefts = copies_of(left_s, saved_ref.at[3:5], left_sem, 2)
     order_s[...] = chunks_of_row_tokens()
     for rr in range(2):
         u = x_ref[:, rr].astype(F32).reshape(LINE, D)
         left_s[0, rr * LINE : (rr + 1) * LINE, :] = (u * inverse_rms(u)).astype(BF16)
-    project(left_s[0], qkv_s, w_s, weights)
+    project(left_s[0], qkv_s, w_ref)
     lefts[0].start()
     start_all(saved)
 
@@ -172,8 +169,7 @@
 
     each_pair(visit, 4)
     lefts[1].start()
-    weights[3].wait()
-    added = dot(left_s[1], w_s[3])
+    added = dot(left_s[1], w_ref[3])
     mids = []
     for rr in range(2):
         u = x_ref[:, rr].astype(F32).reshape(LINE, D)
@@ -240,25 +236,25 @@
     weight.start()
     saved = copies_of(qkv_ref, qkv_s, qkv_sem, 3)
     start_all(saved)
-    probs = [
-        pltpu.make_async_copy(
-            probs_ref.at[i * 2 : (i + 1) * 2], probs_s.at[i * 2 : (i + 1) * 2], probs_sem.at[i]
-        )
-        for i in range(4)
-    ]
-    start_all(probs)
     turned = copies_of(turned_ref, turned_s, turned_sem, 2)
-    start_all(turned)
+
+    def line_probs(line):
+        pairs = pl.ds(line * N_PAIR, N_PAIR)
+        return pltpu.make_async_copy(probs_ref.at[pairs], probs_s.at[pairs], probs_sem.at[line])
+
+    line_probs(0).start()
     right_s[3] = dot(row_tokens_of_chunks(), g_ref[...].reshape(TOK, D)).astype(BF16)
     weight.wait()
     gain = gain_row(where_ref, 0, 0, HEADS)
     da_s[...] = (dot_nt(right_s[3], wo_s[...]) * gain).astype(BF16)
-    wait_all(saved + probs)
+    line_probs(1).start()
+    start_all(turned)
+    wait_all(saved)
 
     def visit(rows, lanes, at, pair):
         attention_backward(rows, lanes, qkv_s, da_s, probs_s[at], right_s)
 
-    each_pair(visit, 4)
+    each_pair(visit, 4, lambda line: line_probs(line).wait())
     rights = copies_of(right_s, right_ref, right_sem, 4)
     start_all(rights)
     wait_all(turned)
@@ -298,17 +294,9 @@
 def col_kernel(where_ref, m_ref, w_ref, *refs):
     parts, got_ref, refs = refs[:4], refs[4], refs[5:]
     gmid_ref, saved_ref = refs[:2]
-    order_s, u_s, ulow_s, left_s, right_s, qkv_s, da_s, w_s, parts_s, got_s = refs[2:12]
-    w_sem, left_sem, right_sem, u_sem, parts_sem, got_sem = refs[12:]
+    order_s, u_s, ulow_s, left_s, right_s, qkv_s, da_s = refs[2:9]
+    left_sem, right_sem, u_sem = refs[9:]
     mine = where_ref[1]
-    pieces = [
-        pltpu.make_async_copy(parts[i].at[mine], parts_s.at[i], parts_sem.at[i]) for i in range(4)
-    ]
-    pieces.append(pltpu.make_async_copy(got_ref, got_s, got_sem))
-    start_all(pieces)
-    weights = copies_of(w_ref, w_s, w_sem, 4)
-    for i in (3, 0, 1, 2):
-        weights[i].start()
     rights = copies_of(right_s, saved_ref, right_sem, 4)
     lefts = copies_of(left_s, saved_ref.at[4:6], left_sem, 2)
     order_s[...] = chunks_of_col_tokens()
@@ -319,19 +307,17 @@
     kept_u.start()
     left_s[0] = (u * inverse_rms(u)).astype(BF16)
     lefts[0].start()
-    wait_all(pieces)
     for shift in range(4):
         source = lax.rem(where_ref[0] + (4 - shift), 4) * 2
-        for grid_row, piece in ((source + mine, parts_s.at[shift]), (source + (1 - mine), got_s.at[shift])):
+        for grid_row, piece in ((source + mine, parts[shift].at[mine]), (source + (1 - mine), got_ref.at[shift])):
             for cc in range(2):
                 for rr in range(2):
                     at = pl.multiple_of(grid_row * 16 + (cc * LINE + rr * 128), 16)
                     right_s[3, pl.ds(at, 16), :] = piece[cc, rr * 16 : (rr + 1) * 16, :]
     rights[3].start()
-    weights[3].wait()
     gain = gain_row(where_ref, 1, 0, HEADS)
-    da_s[...] = (dot_nt(right_s[3], w_s[3]) * gain).astype(BF16)
-    project(left_s[0], qkv_s, w_s, weights)
+    da_s[...] = (dot_nt(right_s[3], w_ref[3]) * gain).astype(BF16)
+    project(left_s[0], qkv_s, w_ref)
 
     def visit(rows, lanes, at, pair):
         probs = softmax(qkv_s[0, rows, lanes], qkv_s[1, rows, lanes])
@@ -343,7 +329,7 @@
     lefts[1].start()
     start_all(rights[:3])
     grads = [
-        input_gradient(u_s[rows, :], right_s, w_s, rows).astype(BF16)
+        input_gradient(u_s[rows, :], right_s, w_ref, rows).astype(BF16)
         for rows in (slice(0, LINE), slice(LINE, TOK))
     ]
     gmid_ref[...] = dot(order_s[...], jnp.concatenate(grads, axis=0)).astype(BF16).reshape(N_DEV, 4, D)
@@ -550,11 +536,11 @@
 
 row_forward = call(
     row_forward_kernel,
-    "svh",
+    "svv",
     "hh",
     (shape(N_DEV, 4, D), shape(5, TOK, D)),
     [
-        token_scratch(), pltpu.VMEM((N_DEV, 4, D), BF16), token_scratch(3), token_scratch(2), *WEIGHTS,
+        token_scratch(), pltpu.VMEM((N_DEV, 4, D), BF16), token_scratch(3), token_scratch(2),
         DMA((4,)), DMA((3,)), DMA((2,)),
     ],
     4 * MATMUL + 2 * ATTEND,
@@ -572,7 +558,7 @@
     [
         token_scratch(), pltpu.VMEM((D, D), BF16), token_scratch(3),
         pltpu.VMEM((2, D, TOK), BF16), pltpu.VMEM((8, TOK, LINE), BF16), HALF_S,
-        token_scratch(4), DMA, DMA((3,)), DMA((2,)), DMA((4,)), DMA, DMA((4,)),
+        token_scratch(4), DMA, DMA((3,)), DMA((2,)), DMA((2,)), DMA, DMA((4,)),
     ],
     5 * MATMUL + 5 * ATTEND,
     12 * MIB,
@@ -603,13 +589,12 @@
 )
 col_grad = call(
     col_kernel,
-    "svh" + "h" * 5,
+    "svv" + "v" * 5,
     "vh",
     (shape(N_DEV, 4, D), shape(7, TOK, D)),
     [
         token_scratch(), token_scratch(dtype=F32), token_scratch(), token_scratch(2), token_scratch(4),
-        token_scratch(3), token_scratch(), WEIGHTS[0], pltpu.VMEM((4, 2, 32, D), BF16),
-        pltpu.VMEM((4, 2, 32, D), BF16), DMA((4,)), DMA((2,)), DMA((4,)), DMA, DMA((4,)), DMA,
+        token_scratch(3), token_scratch(), DMA((2,)), DMA((4,)), DMA,
     ],
     8 * MATMUL + 6 * ATTEND,
     8 * MIB,
@@ -647,7 +632,7 @@
 pair_sum = call(
     pair_sum_kernel, "svv", "v" * 4, (QUARTER,) * 4, [pltpu.VMEM((4, 256, D), BF16)], 0, 3 * MIB,
 )
-merge = call(merge_kernel, "v" * 6, "v", shape(64, 80, 128), [], 0, 4 * MIB, grant=16)
+merge = call(merge_kernel, "v" * 6, "v", shape(64, 80, 128), [], 0, 4 * MIB)
 spread = call(spread_kernel, "v", "v", shape(64, 128, 128), [], 0, 3 * MIB, grant=52)
 
 

time: 243 us -> 240 us (0.988)
  no operation moved by 1% of the time
where the time goes in v6:
time: 240 us; the launch traced here: 235 us
  Pallas kernels  59.1 us (25%)
  blocking collectives  58.7 us (24%)
  starting transfers between devices  56.3 us (23%)
  waiting for transfers between devices  52.6 us (22%)
  local copies, waits for them, and re-layouts  7.79 us (3%)
    all_to_all x2, blocking collectives, exchange(): return lax.all_to_all(values, axes, split_axis=0, concat_axis=0, tiled=True)  58.7 us
    ppermute x20, waiting for transfers between devices, shifted(): lax.ppermute(pieces[k], axes, [(i, (i + k) % n) for i in range(n)])  33.9 us
    all_to_all x3, starting transfers between devices, exchange(): return lax.all_to_all(values, axes, split_axis=0, concat_axis=0, tiled=True)  24 us
    ppermute x20, starting transfers between devices, shifted(): lax.ppermute(pieces[k], axes, [(i, (i + k) % n) for i in range(n)])  22.1 us
    all_to_all x3, waiting for transfers between devices, exchange(): return lax.all_to_all(values, axes, split_axis=0, concat_axis=0, tiled=True)  12.8 us
    pallas_call x1, Pallas kernels, layer(): col_grad(where, mid_lines, w_col, *grad_parts, grad_pass)  11.5 us
    ppermute x5, starting transfers between devices, swap(): return lax.ppermute(value, axis, [(0, 1), (1, 0)])  10.2 us
    pallas_call x1, Pallas kernels, layer(): row_backward(where, grad_rows, saved_row, turned_row, probs_row, w_row)  8.96 us
  transfers between devices with their start and end apart: 28, of which 16 were waited for; matrix products, arithmetic and copies ran while one was open for 0% of the time, Pallas kernels for 15%

profile of v6, /device:TPU:1, one launch (start us, length us, event | category | flops | bytes accessed | tf_op | source)
XLA Modules:
  0.0 235.5 jit_solution(8013235357745079230)
XLA Ops:
  0.6 9.1 %all-to-all-start = ((bf16[16,2,16,512]{3,2,1,0:T(8,128)(2,1)}), bf16[16,2,16,512]{3,2,1,0:T(8,128)(2,1)S(1)}, u32[]{:S(2)}, u32[]{:S(2)}) async-start(bf16[16,2,16,512]{3,2,1,0:T(8,128)(2,1)} %bitcast.12), calls=%async_computation | async-start | bytes 1048576 | tf_op jit(solution)/shard_map/all_to_all | solution.py:656
  9.8 0.8 reshape.23
  10.6 10.2 %all-to-all-done.x_ref = bf16[16,2,16,512]{3,2,1,0:T(8,128)(2,1)S(1)} async-done(((bf16[16,2,16,512]{3,2,1,0:T(8,128)(2,1)}), bf16[16,2,16,512]{3,2,1,0:T(8,128)(2,1)S(1)}, u32[]{:S(2)}, u32[]{:S(2)}) %all-to-all-start) | async-done | bytes 524320 | tf_op jit(solution)/shard_map/all_to_all | solution.py:656
  20.8 1.6 copy-done.2
  22.4 6.9 %shard_map.84 = (bf16[128,4,512]{2,1,0:T(4,128)(2,1)S(1)}, bf16[5,512,512]{2,1,0:T(8,128)(2,1)}) custom-call(s32[21]{0:T(128)S(1)} %concatenate.3.where_ref, bf16[16,2,16,512]{3,2,1,0:T(8,128)(2,1)S(1)} %all-to-all-done.x_ref, bf16[4,512,512]{2,1,0:T(8,128)(2,1)S(1)} %copy-done.2), custom_call_target="tpu_custom_call" | custom-call | flops 1342177280 | bytes 6291456 | tf_op jit(solution)/shard_map/pallas_call | solution.py:679
  29.3 0.8 copy-done.11
  30.1 6.4 %all-to-all-start.1 = ((bf16[128,4,512]{2,1,0:T(4,128)(2,1)}), bf16[128,4,512]{2,1,0:T(4,128)(2,1)}, u32[]{:S(2)}, u32[]{:S(2)}) async-start(bf16[128,4,512]{2,1,0:T(4,128)(2,1)} %copy-done.11), calls=%async_computation.1 | async-start | bytes 1048576 | tf_op jit(solution)/shard_map/all_to_all | solution.py:656
  36.6 1.2 shard_map.85
  37.8 1.4 collective-permute-start
  39.2 2.5 %collective-permute-start.1 = (bf16[2,2,32,512]{3,2,1,0:T(8,128)(2,1)S(1)}, bf16[2,2,32,512]{3,2,1,0:T(8,128)(2,1)S(1)}, u32[]{:S(2)}, u32[]{:S(2)}) collective-permute-start(bf16[2,2,32,512]{3,2,1,0:T(8,128)(2,1)S(1)} %get-tuple-element.45), channel_id=1, source_target_pairs={{0,64},{32,96},{64,0},{96,32},{1,65},{33,97},{65,1},{97,33},{2,66}... | collective-permute-start | bytes 393224 | tf_op jit(solution)/shard_map/ppermute | solution.py:662
  41.7 1.1 collective-permute-start.2
  42.8 5.2 %collective-permute-done.refs_1_ = bf16[2,2,32,512]{3,2,1,0:T(8,128)(2,1)S(1)} collective-permute-done((bf16[2,2,32,512]{3,2,1,0:T(8,128)(2,1)S(1)}, bf16[2,2,32,512]{3,2,1,0:T(8,128)(2,1)S(1)}, u32[]{:S(2)}, u32[]{:S(2)}) %collective-permute-start) | collective-permute-done | bytes 131104 | tf_op jit(solution)/shard_map/ppermute | solution.py:662
  48.0 3.5 %collective-permute-done.1.refs_2_ = bf16[2,2,32,512]{3,2,1,0:T(8,128)(2,1)S(1)} collective-permute-done((bf16[2,2,32,512]{3,2,1,0:T(8,128)(2,1)S(1)}, bf16[2,2,32,512]{3,2,1,0:T(8,128)(2,1)S(1)}, u32[]{:S(2)}, u32[]{:S(2)}) %collective-permute-start.1) | collective-permute-done | bytes 131104 | tf_op jit(solution)/shard_map/ppermute | solution.py:662
  51.5 0.6 shard_map.86
  52.1 1.5 collective-permute-start.3
  53.6 5.9 %collective-permute-done.3.refs_4_ = bf16[4,2,32,512]{3,2,1,0:T(8,128)(2,1)S(1)} collective-permute-done((bf16[4,2,32,512]{3,2,1,0:T(8,128)(2,1)S(1)}, bf16[4,2,32,512]{3,2,1,0:T(8,128)(2,1)S(1)}, u32[]{:S(2)}, u32[]{:S(2)}) %collective-permute-start.3) | collective-permute-done | bytes 262176 | tf_op jit(solution)/shard_map/ppermute | solution.py:667
  59.5 11.5 %shard_map.87 = (bf16[128,4,512]{2,1,0:T(4,128)(2,1)}, bf16[7,512,512]{2,1,0:T(8,128)(2,1)}) custom-call(s32[21]{0:T(128)S(1)} %concatenate.3.where_ref, bf16[128,4,512]{2,1,0:T(4,128)(2,1)} %all-to-all-done.1.m_ref, bf16[4,512,512]{2,1,0:T(8,128)(2,1)S(1)} %copy-done.6, bf16[2,2,32,512]{3,2,1,0:T(8,128)(2,1)S(1)} %get-tuple-element.43.refs_0_, ...), custom_call_target="tpu_custom_call" | custom-call | flops 2952790016 | bytes 8388608 | tf_op jit(solution)/shard_map/pallas_call | solution.py:682
  71.0 8.4 %all-to-all-start.2 = ((bf16[128,4,512]{2,1,0:T(4,128)(2,1)}), bf16[128,4,512]{2,1,0:T(4,128)(2,1)}, u32[]{:S(2)}, u32[]{:S(2)}) async-start(bf16[128,4,512]{2,1,0:T(4,128)(2,1)} %get-tuple-element.56), calls=%async_computation.2 | async-start | bytes 1048576 | tf_op jit(solution)/shard_map/all_to_all | solution.py:656
  79.4 3.1 %shard_map.96 = (bf16[2,512,512]{2,1,0:T(8,128)(2,1)S(1)}, bf16[2,512,512]{2,1,0:T(8,128)(2,1)S(1)}) custom-call(s32[21]{0:T(128)S(1)} %concatenate.3.where_ref, bf16[7,512,512]{2,1,0:T(8,128)(2,1)} %get-tuple-element.47.saved_ref.right_ref), custom_call_target="tpu_custom_call" | custom-call | flops 536870912 | bytes 6291456 | tf_op jit(solution)/shard_map/pallas_call | solution.py:686
  82.6 1.0 copy-done.8
  83.6 1.1 collective-permute-start.20
  84.7 2.4 %shard_map.90 = (bf16[8,512,256]{2,1,0:T(8,128)(2,1)S(1)}, bf16[2,512,512]{2,1,0:T(8,128)(2,1)S(1)}) custom-call(bf16[5,512,512]{2,1,0:T(8,128)(2,1)S(1)} %copy-done), custom_call_target="tpu_custom_call" | custom-call | flops 134217728 | bytes 8388608 | tf_op jit(solution)/shard_map/pallas_call | solution.py:681
  87.2 1.0 copy-done.3
  88.2 1.3 copy-done.7
  89.5 2.6 %all-to-all-done.2.g_ref = bf16[128,4,512]{2,1,0:T(4,128)(2,1)} async-done(((bf16[128,4,512]{2,1,0:T(4,128)(2,1)}), bf16[128,4,512]{2,1,0:T(4,128)(2,1)}, u32[]{:S(2)}, u32[]{:S(2)}) %all-to-all-start.2) | async-done | bytes 524320 | tf_op jit(solution)/shard_map/all_to_all | solution.py:656
  92.1 1.2 copy-done.4
  93.4 9.0 %shard_map.91 = (bf16[2,512,512]{2,1,0:T(8,128)(2,1)S(1)}, bf16[4,512,512]{2,1,0:T(8,128)(2,1)}) custom-call(s32[21]{0:T(128)S(1)} %concatenate.3.where_ref, bf16[128,4,512]{2,1,0:T(4,128)(2,1)} %all-to-all-done.2.g_ref, bf16[5,512,512]{2,1,0:T(8,128)(2,1)} %get-tuple-element.57.saved_ref.qkv_ref, bf16[2,512,512]{2,1,0:T(8,128)(2,1)S(1)} %copy-done.4, ...), custom_call_target="tpu_custom_call" | custom-call | flops 2013265920 | bytes 12582912 | tf_op jit(solution)/shard_map/pallas_call | solution.py:691
  102.3 1.5 collective-permute-start.19
  103.8 2.6 %shard_map.97.keep_ref = bf16[2,512,512]{2,1,0:T(8,128)(2,1)S(1)} custom-call(s32[21]{0:T(128)S(1)} %concatenate.3.where_ref, bf16[2,512,512]{2,1,0:T(8,128)(2,1)S(1)} %copy-done.9, bf16[7,512,512]{2,1,0:T(8,128)(2,1)} %get-tuple-element.47.saved_ref.right_ref), custom_call_target="tpu_custom_call" | custom-call | flops 536870912 | bytes 3145728 | tf_op jit(solution)/shard_map/pallas_call | solution.py:688
  106.4 1.9 shard_map.98
  108.8 1.9 collective-permute-start.22
  110.6 0.9 collective-permute-start.23
  111.6 2.6 %shard_map.95.keep_ref = bf16[2,512,512]{2,1,0:T(8,128)(2,1)S(1)} custom-call(s32[21]{0:T(128)S(1)} %concatenate.3.where_ref, bf16[2,512,512]{2,1,0:T(8,128)(2,1)S(1)} %copy-done.5, bf16[4,512,512]{2,1,0:T(8,128)(2,1)} %get-tuple-element.60.right_ref), custom_call_target="tpu_custom_call" | custom-call | flops 536870912 | bytes 3145728 | tf_op jit(solution)/shard_map/pallas_call | solution.py:693
  114.1 3.9 %collective-permute-done.21.refs_1_ = bf16[256,512]{1,0:T(8,128)(2,1)S(1)} collective-permute-done((bf16[256,512]{1,0:T(8,128)(2,1)S(1)}, bf16[256,512]{1,0:T(8,128)(2,1)S(1)}, u32[]{:S(2)}, u32[]{:S(2)}) %collective-permute-start.21) | collective-permute-done | bytes 262176 | tf_op jit(solution)/shard_map/ppermute | solution.py:662
  118.0 4.7 %collective-permute-done.22.refs_2_ = bf16[256,512]{1,0:T(8,128)(2,1)S(1)} collective-permute-done((bf16[256,512]{1,0:T(8,128)(2,1)S(1)}, bf16[256,512]{1,0:T(8,128)(2,1)S(1)}, u32[]{:S(2)}, u32[]{:S(2)}) %collective-permute-start.22) | collective-permute-done | bytes 262176 | tf_op jit(solution)/shard_map/ppermute | solution.py:662
  122.7 0.8 collective-permute-done.23.refs_3_
  123.9 26.0 %all_to_all.25.both_ref = bf16[64,80,128]{2,1,0:T(8,128)(2,1)S(1)} all-to-all(bf16[64,80,128]{2,1,0:T(8,128)(2,1)S(1)} %shard_map.99), channel_id=1, replica_groups=mesh['y'=4,'zl'=2,'zh'=2,'x'=4,'c'=2] {'y','zl','zh','x'}, dimensions={0} | all-to-all | bytes 2621440 | tf_op jit(solution)/shard_map/all_to_all | solution.py:656
  149.9 1.7 shard_map.100
  151.6 32.6 %all_to_all.26.chunks_ref = bf16[64,128,128]{2,1,0:T(8,128)(2,1)S(1)} all-to-all(bf16[64,128,128]{2,1,0:T(8,128)(2,1)} %shard_map.100), channel_id=1, replica_groups=mesh['y'=4,'zl'=2,'zh'=2,'x'=4,'c'=2] {'y','zl','zh','x'}, dimensions={0} | all-to-all | bytes 4194304 | tf_op jit(solution)/shard_map/all_to_all | solution.py:656
  184.3 3.3 %collective-permute-start.24 = (bf16[64,128,128]{2,1,0:T(8,128)(2,1)S(1)}, bf16[64,128,128]{2,1,0:T(8,128)(2,1)S(1)}, u32[]{:S(2)}, u32[]{:S(2)}) collective-permute-start(bf16[64,128,128]{2,1,0:T(8,128)(2,1)S(1)} %all_to_all.26.chunks_ref), channel_id=1, source_target_pairs={{0,1},{1,0},{2,3},{3,2},{4,5},{5,4},{6,7},{7,6},{8,9},{9,8},{10,11... | collective-permute-start | bytes 6291464 | tf_op jit(solution)/shard_map/ppermute | solution.py:667
  187.6 3.2 %shard_map.92 = (bf16[2,2,16,512]{3,2,1,0:T(8,128)(2,1)S(1)}, bf16[2,2,16,512]{3,2,1,0:T(8,128)(2,1)S(1)}, bf16[2,2,16,512]{3,2,1,0:T(8,128)(2,1)S(1)}, bf16[2,2...) custom-call(s32[21]{0:T(128)S(1)} %concatenate.3.where_ref, ...), custom_call_target="tpu_custom_call" | custom-call | flops 805306368 | bytes 5242880 | tf_op jit(solution)/shard_map/pallas_call | solution.py:698
  190.8 2.2 collective-permute-start.12
  193.0 1.5 collective-permute-start.13
  194.6 2.4 %collective-permute-start.14 = (bf16[2,2,16,512]{3,2,1,0:T(8,128)(2,1)S(1)}, bf16[2,2,16,512]{3,2,1,0:T(8,128)(2,1)S(1)}, u32[]{:S(2)}, u32[]{:S(2)}) collective-permute-start(bf16[2,2,16,512]{3,2,1,0:T(8,128)(2,1)S(1)} %get-tuple-element.65), channel_id=1, source_target_pairs={{0,8},{2,10},{4,12},{6,14},{8,0},{10,2},{12,4},{14,6},{1,9},{3,11}... | collective-permute-start | bytes 196616 | tf_op jit(solution)/shard_map/ppermute | solution.py:662
  196.9 2.9 %collective-permute-done.11.refs_1_ = bf16[2,2,16,512]{3,2,1,0:T(8,128)(2,1)S(1)} collective-permute-done((bf16[2,2,16,512]{3,2,1,0:T(8,128)(2,1)S(1)}, bf16[2,2,16,512]{3,2,1,0:T(8,128)(2,1)S(1)}, u32[]{:S(2)}, u32[]{:S(2)}) %collective-permute-start.11) | collective-permute-done | bytes 65568 | tf_op jit(solution)/shard_map/ppermute | solution.py:662
  199.9 1.6 collective-permute-start.16
  201.5 2.6 %collective-permute-start.17 = (bf16[2,2,16,512]{3,2,1,0:T(8,128)(2,1)S(1)}, bf16[2,2,16,512]{3,2,1,0:T(8,128)(2,1)S(1)}, u32[]{:S(2)}, u32[]{:S(2)}) collective-permute-start(bf16[2,2,16,512]{3,2,1,0:T(8,128)(2,1)S(1)} %get-tuple-element.68), channel_id=1, source_target_pairs={{0,14},{2,0},{4,2},{6,4},{8,6},{10,8},{12,10},{14,12},{1,15},{3,1}... | collective-permute-start | bytes 196616 | tf_op jit(solution)/shard_map/ppermute | solution.py:662
  204.1 0.8 collective-permute-done.15.refs_5_
  204.9 1.8 collective-permute-done.17.refs_7_
  206.7 0.6 shard_map.93
  207.3 2.7 %collective-permute-start.18 = (bf16[8,2,16,512]{3,2,1,0:T(8,128)(2,1)S(1)}, bf16[8,2,16,512]{3,2,1,0:T(8,128)(2,1)S(1)}, u32[]{:S(2)}, u32[]{:S(2)}) collective-permute-start(bf16[8,2,16,512]{3,2,1,0:T(8,128)(2,1)S(1)} %shard_map.93), channel_id=1, source_target_pairs={{0,1},{1,0},{2,3},{3,2},{4,5},{5,4},{6,7},{7,6},{8,9},{9,8},{10,11... | collective-permute-start | bytes 786440 | tf_op jit(solution)/shard_map/ppermute | solution.py:667
  210.0 2.4 %shard_map.88 = (bf16[2,32,512]{2,1,0:T(8,128)(2,1)S(1)}, bf16[2,32,512]{2,1,0:T(8,128)(2,1)S(1)}, bf16[2,32,512]{2,1,0:T(8,128)(2,1)S(1)}, bf16[2,32,512]{2,1,0...) custom-call(s32[21]{0:T(128)S(1)} %concatenate.3.where_ref, ...), custom_call_target="tpu_custom_call" | custom-call | flops 268435456 | bytes 3145728 | tf_op jit(solution)/shard_map/pallas_call | solution.py:703
  212.7 1.9 collective-permute-start.6
  214.5 3.7 %collective-permute-done.4.refs_1_ = bf16[2,32,512]{2,1,0:T(8,128)(2,1)S(1)} collective-permute-done((bf16[2,32,512]{2,1,0:T(8,128)(2,1)S(1)}, bf16[2,32,512]{2,1,0:T(8,128)(2,1)S(1)}, u32[]{:S(2)}, u32[]{:S(2)}) %collective-permute-start.4) | collective-permute-done | bytes 65568 | tf_op jit(solution)/shard_map/ppermute | solution.py:662
  218.2 0.8 collective-permute-start.8
  219.0 1.2 collective-permute-done.6.refs_3_
  220.2 0.6 collective-permute-start.9
  220.9 2.0 collective-permute-done.7.refs_4_
  222.9 0.5 collective-permute-done.9.refs_6_
  223.4 2.9 %collective-permute-done.10.refs_7_ = bf16[2,32,512]{2,1,0:T(8,128)(2,1)S(1)} collective-permute-done((bf16[2,32,512]{2,1,0:T(8,128)(2,1)S(1)}, bf16[2,32,512]{2,1,0:T(8,128)(2,1)S(1)}, u32[]{:S(2)}, u32[]{:S(2)}) %collective-permute-start.10) | collective-permute-done | bytes 65568 | tf_op jit(solution)/shard_map/ppermute | solution.py:662
  226.3 2.3 shard_map.89
  228.5 1.4 shard_map.94
  229.9 2.7 %widen.2 = (f32[2,1024,512]{2,1,0:T(8,128)}, f32[2,4,256,512]{3,2,1,0:T(8,128)}) custom-call(s32[21]{0:T(128)S(1)} %concatenate.3.where_ref, bf16[64,128,128]{2,1,0:T(8,128)(2,1)S(1)} %all_to_all.26.chunks_ref), custom_call_target="tpu_custom_call" | custom-call | bytes 6291456 | tf_op jit(solution)/shard_map/widen/pallas_call | solution.py:640
  232.6 2.7 %widen.3 = (f32[2,1024,512]{2,1,0:T(8,128)}, f32[2,4,256,512]{3,2,1,0:T(8,128)}) custom-call(s32[21]{0:T(128)S(1)} %concatenate.3.where_ref, bf16[64,128,128]{2,1,0:T(8,128)(2,1)S(1)} %collective-permute-done.24.chunks_ref, f32[2,1024,512]{2,1,0:T(8,128)} %get-tuple-element.76.refs_0_, ...), custom_call_target="tpu_custom_call", output_to_operand_aliasing={{0}: (2, {}), {1}: (3, {})} | custom-call | bytes 6291456 | tf_op jit(solution)/shard_map/widen/pallas_call | solution.py:640
  (39 shorter events, 1.3 us)
Async XLA Ops:
  0.6 20.1 %all-to-all-start = ((bf16[16,2,16,512]{3,2,1,0:T(8,128)(2,1)}), bf16[16,2,16,512]{3,2,1,0:T(8,128)(2,1)S(1)}, u32[]{:S(2)}, u32[]{:S(2)}) async-start(bf16[16,2,16,512]{3,2,1,0:T(8,128)(2,1)} %bitcast.12), calls=%async_computation | async-start | bytes 1048576 | tf_op jit(solution)/shard_map/all_to_all | solution.py:656
  20.8 1.6 copy-start.2
  22.3 14.2 %copy-start.10 = (bf16[32,16,512]{2,1,0:T(8,128)(2,1)S(1)}, bf16[32,16,512]{2,1,0:T(8,128)(2,1)}, u32[]{:S(2)}) copy-start(bf16[32,16,512]{2,1,0:T(8,128)(2,1)} %tile_ref.1) | copy-start | bytes 1572868
  29.3 0.8 copy-start.11
  30.1 29.4 %copy-start.6 = (bf16[4,512,512]{2,1,0:T(8,128)(2,1)S(1)}, bf16[4,512,512]{2,1,0:T(8,128)(2,1)}, u32[]{:S(2)}) copy-start(bf16[4,512,512]{2,1,0:T(8,128)(2,1)} %w_ref.7) | copy-start | bytes 6291460
  30.1 29.4 %all-to-all-start.1 = ((bf16[128,4,512]{2,1,0:T(4,128)(2,1)}), bf16[128,4,512]{2,1,0:T(4,128)(2,1)}, u32[]{:S(2)}, u32[]{:S(2)}) async-start(bf16[128,4,512]{2,1,0:T(4,128)(2,1)} %copy-done.11), calls=%async_computation.1 | async-start | bytes 1048576 | tf_op jit(solution)/shard_map/all_to_all | solution.py:656
  37.8 10.2 %collective-permute-start = (bf16[2,2,32,512]{3,2,1,0:T(8,128)(2,1)S(1)}, bf16[2,2,32,512]{3,2,1,0:T(8,128)(2,1)S(1)}, u32[]{:S(2)}, u32[]{:S(2)}) collective-permute-start(bf16[2,2,32,512]{3,2,1,0:T(8,128)(2,1)S(1)} %get-tuple-element.44), channel_id=1, source_target_pairs={{0,32},{32,64},{64,96},{96,0},{1,33},{33,65},{65,97},{97,1},{2,34}... | collective-permute-start | bytes 393224 | tf_op jit(solution)/shard_map/ppermute | solution.py:662
  39.2 12.3 %collective-permute-start.1 = (bf16[2,2,32,512]{3,2,1,0:T(8,128)(2,1)S(1)}, bf16[2,2,32,512]{3,2,1,0:T(8,128)(2,1)S(1)}, u32[]{:S(2)}, u32[]{:S(2)}) collective-permute-start(bf16[2,2,32,512]{3,2,1,0:T(8,128)(2,1)S(1)} %get-tuple-element.45), channel_id=1, source_target_pairs={{0,64},{32,96},{64,0},{96,32},{1,65},{33,97},{65,1},{97,33},{2,66}... | collective-permute-start | bytes 393224 | tf_op jit(solution)/shard_map/ppermute | solution.py:662
  41.7 9.8 %collective-permute-start.2 = (bf16[2,2,32,512]{3,2,1,0:T(8,128)(2,1)S(1)}, bf16[2,2,32,512]{3,2,1,0:T(8,128)(2,1)S(1)}, u32[]{:S(2)}, u32[]{:S(2)}) collective-permute-start(bf16[2,2,32,512]{3,2,1,0:T(8,128)(2,1)S(1)} %get-tuple-element.46), channel_id=1, source_target_pairs={{0,96},{32,0},{64,32},{96,64},{1,97},{33,1},{65,33},{97,65},{2,98}... | collective-permute-start | bytes 393224 | tf_op jit(solution)/shard_map/ppermute | solution.py:662
  52.1 7.4 %collective-permute-start.3 = (bf16[4,2,32,512]{3,2,1,0:T(8,128)(2,1)S(1)}, bf16[4,2,32,512]{3,2,1,0:T(8,128)(2,1)S(1)}, u32[]{:S(2)}, u32[]{:S(2)}) collective-permute-start(bf16[4,2,32,512]{3,2,1,0:T(8,128)(2,1)S(1)} %shard_map.86), channel_id=1, source_target_pairs={{0,16},{16,0},{1,17},{17,1},{2,18},{18,2},{3,19},{19,3},{4,20},{20... | collective-permute-start | bytes 786440 | tf_op jit(solution)/shard_map/ppermute | solution.py:667
  71.0 21.1 %all-to-all-start.2 = ((bf16[128,4,512]{2,1,0:T(4,128)(2,1)}), bf16[128,4,512]{2,1,0:T(4,128)(2,1)}, u32[]{:S(2)}, u32[]{:S(2)}) async-start(bf16[128,4,512]{2,1,0:T(4,128)(2,1)} %get-tuple-element.56), calls=%async_computation.2 | async-start | bytes 1048576 | tf_op jit(solution)/shard_map/all_to_all | solution.py:656
  79.4 5.3 %copy-start = (bf16[5,512,512]{2,1,0:T(8,128)(2,1)S(1)}, bf16[5,512,512]{2,1,0:T(8,128)(2,1)}, u32[]{:S(2)}) copy-start(bf16[5,512,512]{2,1,0:T(8,128)(2,1)} %get-tuple-element.57.saved_ref.qkv_ref) | copy-start | bytes 7864324
  82.6 1.0 copy-start.8
  83.6 22.9 %collective-permute-start.20 = (bf16[2,512,512]{2,1,0:T(8,128)(2,1)S(1)}, bf16[2,512,512]{2,1,0:T(8,128)(2,1)}, u32[]{:S(2)}, u32[]{:S(2)}) collective-permute-start(bf16[2,512,512]{2,1,0:T(8,128)(2,1)S(1)} %get-tuple-element.71), channel_id=1, source_target_pairs={{0,1},{1,0},{2,3},{3,2},{4,5},{5,4},{6,7},{7,6},{8,9},{9,8},{10,11... | collective-permute-start | bytes 3145736 | tf_op jit(solution)/shard_map/ppermute | solution.py:667
  87.2 1.0 copy-start.3
  88.2 1.3 copy-start.7
  92.1 1.2 copy-start.4
  93.4 10.5 %copy-start.9 = (bf16[2,512,512]{2,1,0:T(8,128)(2,1)S(1)}, bf16[2,512,512]{2,1,0:T(8,128)(2,1)}, u32[]{:S(2)}) copy-start(bf16[2,512,512]{2,1,0:T(8,128)(2,1)} %copy-done.8) | copy-start | bytes 3145732
  102.3 21.1 %collective-permute-start.19 = (bf16[2,512,512]{2,1,0:T(8,128)(2,1)S(1)}, bf16[2,512,512]{2,1,0:T(8,128)(2,1)S(1)}, u32[]{:S(2)}, u32[]{:S(2)}) collective-permute-start(bf16[2,512,512]{2,1,0:T(8,128)(2,1)S(1)} %get-tuple-element.69), channel_id=1, source_target_pairs={{0,1},{1,0},{2,3},{3,2},{4,5},{5,4},{6,7},{7,6},{8,9},{9,8},{10,11... | collective-permute-start | bytes 3145736 | tf_op jit(solution)/shard_map/ppermute | solution.py:667
  106.4 5.1 %copy-start.5 = (bf16[2,512,512]{2,1,0:T(8,128)(2,1)S(1)}, bf16[2,512,512]{2,1,0:T(8,128)(2,1)}, u32[]{:S(2)}) copy-start(bf16[2,512,512]{2,1,0:T(8,128)(2,1)} %copy-done.3) | copy-start | bytes 3145732
  108.4 9.6 %collective-permute-start.21 = (bf16[256,512]{1,0:T(8,128)(2,1)S(1)}, bf16[256,512]{1,0:T(8,128)(2,1)S(1)}, u32[]{:S(2)}, u32[]{:S(2)}) collective-permute-start(bf16[256,512]{1,0:T(8,128)(2,1)S(1)} %get-tuple-element.73), channel_id=1, source_target_pairs={{0,2},{2,4},{4,6},{6,0},{1,3},{3,5},{5,7},{7,1},{8,10},{10,12},{12... | collective-permute-start | bytes 786440 | tf_op jit(solution)/shard_map/ppermute | solution.py:662
  108.8 13.9 %collective-permute-start.22 = (bf16[256,512]{1,0:T(8,128)(2,1)S(1)}, bf16[256,512]{1,0:T(8,128)(2,1)S(1)}, u32[]{:S(2)}, u32[]{:S(2)}) collective-permute-start(bf16[256,512]{1,0:T(8,128)(2,1)S(1)} %get-tuple-element.74), channel_id=1, source_target_pairs={{0,4},{2,6},{4,0},{6,2},{1,5},{3,7},{5,1},{7,3},{8,12},{10,14},{12... | collective-permute-start | bytes 786440 | tf_op jit(solution)/shard_map/ppermute | solution.py:662
  110.6 12.8 %collective-permute-start.23 = (bf16[256,512]{1,0:T(8,128)(2,1)S(1)}, bf16[256,512]{1,0:T(8,128)(2,1)S(1)}, u32[]{:S(2)}, u32[]{:S(2)}) collective-permute-start(bf16[256,512]{1,0:T(8,128)(2,1)S(1)} %get-tuple-element.75), channel_id=1, source_target_pairs={{0,6},{2,0},{4,2},{6,4},{1,7},{3,1},{5,3},{7,5},{8,14},{10,8},{12,... | collective-permute-start | bytes 786440 | tf_op jit(solution)/shard_map/ppermute | solution.py:662
  151.6 35.9 %copy-start.1 = (bf16[4,512,512]{2,1,0:T(8,128)(2,1)S(1)}, bf16[4,512,512]{2,1,0:T(8,128)(2,1)}, u32[]{:S(2)}) copy-start(bf16[4,512,512]{2,1,0:T(8,128)(2,1)} %get-tuple-element.60.right_ref) | copy-start | bytes 6291460
  184.3 48.3 %collective-permute-start.24 = (bf16[64,128,128]{2,1,0:T(8,128)(2,1)S(1)}, bf16[64,128,128]{2,1,0:T(8,128)(2,1)S(1)}, u32[]{:S(2)}, u32[]{:S(2)}) collective-permute-start(bf16[64,128,128]{2,1,0:T(8,128)(2,1)S(1)} %all_to_all.26.chunks_ref), channel_id=1, source_target_pairs={{0,1},{1,0},{2,3},{3,2},{4,5},{5,4},{6,7},{7,6},{8,9},{9,8},{10,11... | collective-permute-start | bytes 6291464 | tf_op jit(solution)/shard_map/ppermute | solution.py:667
  190.8 9.1 %collective-permute-start.11 = (bf16[2,2,16,512]{3,2,1,0:T(8,128)(2,1)S(1)}, bf16[2,2,16,512]{3,2,1,0:T(8,128)(2,1)S(1)}, u32[]{:S(2)}, u32[]{:S(2)}) collective-permute-start(bf16[2,2,16,512]{3,2,1,0:T(8,128)(2,1)S(1)} %get-tuple-element.62), channel_id=1, source_target_pairs={{0,2},{2,4},{4,6},{6,8},{8,10},{10,12},{12,14},{14,0},{1,3},{3,5},... | collective-permute-start | bytes 196616 | tf_op jit(solution)/shard_map/ppermute | solution.py:662
  190.8 9.0 %collective-permute-start.12 = (bf16[2,2,16,512]{3,2,1,0:T(8,128)(2,1)S(1)}, bf16[2,2,16,512]{3,2,1,0:T(8,128)(2,1)S(1)}, u32[]{:S(2)}, u32[]{:S(2)}) collective-permute-start(bf16[2,2,16,512]{3,2,1,0:T(8,128)(2,1)S(1)} %get-tuple-element.63), channel_id=1, source_target_pairs={{0,4},{2,6},{4,8},{6,10},{8,12},{10,14},{12,0},{14,2},{1,5},{3,7},... | collective-permute-start | bytes 196616 | tf_op jit(solution)/shard_map/ppermute | solution.py:662
  193.0 8.5 %collective-permute-start.13 = (bf16[2,2,16,512]{3,2,1,0:T(8,128)(2,1)S(1)}, bf16[2,2,16,512]{3,2,1,0:T(8,128)(2,1)S(1)}, u32[]{:S(2)}, u32[]{:S(2)}) collective-permute-start(bf16[2,2,16,512]{3,2,1,0:T(8,128)(2,1)S(1)} %get-tuple-element.64), channel_id=1, source_target_pairs={{0,6},{2,8},{4,10},{6,12},{8,14},{10,0},{12,2},{14,4},{1,7},{3,9},... | collective-permute-start | bytes 196616 | tf_op jit(solution)/shard_map/ppermute | solution.py:662
  194.6 9.5 %collective-permute-start.14 = (bf16[2,2,16,512]{3,2,1,0:T(8,128)(2,1)S(1)}, bf16[2,2,16,512]{3,2,1,0:T(8,128)(2,1)S(1)}, u32[]{:S(2)}, u32[]{:S(2)}) collective-permute-start(bf16[2,2,16,512]{3,2,1,0:T(8,128)(2,1)S(1)} %get-tuple-element.65), channel_id=1, source_target_pairs={{0,8},{2,10},{4,12},{6,14},{8,0},{10,2},{12,4},{14,6},{1,9},{3,11}... | collective-permute-start | bytes 196616 | tf_op jit(solution)/shard_map/ppermute | solution.py:662
  199.9 5.0 %collective-permute-start.15 = (bf16[2,2,16,512]{3,2,1,0:T(8,128)(2,1)S(1)}, bf16[2,2,16,512]{3,2,1,0:T(8,128)(2,1)S(1)}, u32[]{:S(2)}, u32[]{:S(2)}) collective-permute-start(bf16[2,2,16,512]{3,2,1,0:T(8,128)(2,1)S(1)} %get-tuple-element.66), channel_id=1, source_target_pairs={{0,10},{2,12},{4,14},{6,0},{8,2},{10,4},{12,6},{14,8},{1,11},{3,13... | collective-permute-start | bytes 196616 | tf_op jit(solution)/shard_map/ppermute | solution.py:662
  199.9 5.0 %collective-permute-start.16 = (bf16[2,2,16,512]{3,2,1,0:T(8,128)(2,1)S(1)}, bf16[2,2,16,512]{3,2,1,0:T(8,128)(2,1)S(1)}, u32[]{:S(2)}, u32[]{:S(2)}) collective-permute-start(bf16[2,2,16,512]{3,2,1,0:T(8,128)(2,1)S(1)} %get-tuple-element.67), channel_id=1, source_target_pairs={{0,12},{2,14},{4,0},{6,2},{8,4},{10,6},{12,8},{14,10},{1,13},{3,15... | collective-permute-start | bytes 196616 | tf_op jit(solution)/shard_map/ppermute | solution.py:662
  201.5 5.2 %collective-permute-start.17 = (bf16[2,2,16,512]{3,2,1,0:T(8,128)(2,1)S(1)}, bf16[2,2,16,512]{3,2,1,0:T(8,128)(2,1)S(1)}, u32[]{:S(2)}, u32[]{:S(2)}) collective-permute-start(bf16[2,2,16,512]{3,2,1,0:T(8,128)(2,1)S(1)} %get-tuple-element.68), channel_id=1, source_target_pairs={{0,14},{2,0},{4,2},{6,4},{8,6},{10,8},{12,10},{14,12},{1,15},{3,1}... | collective-permute-start | bytes 196616 | tf_op jit(solution)/shard_map/ppermute | solution.py:662
  207.3 21.2 %collective-permute-start.18 = (bf16[8,2,16,512]{3,2,1,0:T(8,128)(2,1)S(1)}, bf16[8,2,16,512]{3,2,1,0:T(8,128)(2,1)S(1)}, u32[]{:S(2)}, u32[]{:S(2)}) collective-permute-start(bf16[8,2,16,512]{3,2,1,0:T(8,128)(2,1)S(1)} %shard_map.93), channel_id=1, source_target_pairs={{0,1},{1,0},{2,3},{3,2},{4,5},{5,4},{6,7},{7,6},{8,9},{9,8},{10,11... | collective-permute-start | bytes 786440 | tf_op jit(solution)/shard_map/ppermute | solution.py:667
  212.4 5.8 %collective-permute-start.4 = (bf16[2,32,512]{2,1,0:T(8,128)(2,1)S(1)}, bf16[2,32,512]{2,1,0:T(8,128)(2,1)S(1)}, u32[]{:S(2)}, u32[]{:S(2)}) collective-permute-start(bf16[2,32,512]{2,1,0:T(8,128)(2,1)S(1)} %get-tuple-element.49), channel_id=1, source_target_pairs={{0,16},{16,32},{32,48},{48,64},{64,80},{80,96},{96,112},{112,0},{1... | collective-permute-start | bytes 196616 | tf_op jit(solution)/shard_map/ppermute | solution.py:662
  212.7 5.6 %collective-permute-start.5 = (bf16[2,32,512]{2,1,0:T(8,128)(2,1)S(1)}, bf16[2,32,512]{2,1,0:T(8,128)(2,1)S(1)}, u32[]{:S(2)}, u32[]{:S(2)}) collective-permute-start(bf16[2,32,512]{2,1,0:T(8,128)(2,1)S(1)} %get-tuple-element.50), channel_id=1, source_target_pairs={{0,32},{16,48},{32,64},{48,80},{64,96},{80,112},{96,0},{112,16},{1... | collective-permute-start | bytes 196616 | tf_op jit(solution)/shard_map/ppermute | solution.py:662
  212.7 7.6 %collective-permute-start.6 = (bf16[2,32,512]{2,1,0:T(8,128)(2,1)S(1)}, bf16[2,32,512]{2,1,0:T(8,128)(2,1)S(1)}, u32[]{:S(2)}, u32[]{:S(2)}) collective-permute-start(bf16[2,32,512]{2,1,0:T(8,128)(2,1)S(1)} %get-tuple-element.51), channel_id=1, source_target_pairs={{0,48},{16,64},{32,80},{48,96},{64,112},{80,0},{96,16},{112,32},{1... | collective-permute-start | bytes 196616 | tf_op jit(solution)/shard_map/ppermute | solution.py:662
  218.2 4.6 %collective-permute-start.7 = (bf16[2,32,512]{2,1,0:T(8,128)(2,1)S(1)}, bf16[2,32,512]{2,1,0:T(8,128)(2,1)S(1)}, u32[]{:S(2)}, u32[]{:S(2)}) collective-permute-start(bf16[2,32,512]{2,1,0:T(8,128)(2,1)S(1)} %get-tuple-element.52), channel_id=1, source_target_pairs={{0,64},{16,80},{32,96},{48,112},{64,0},{80,16},{96,32},{112,48},{1... | collective-permute-start | bytes 196616 | tf_op jit(solution)/shard_map/ppermute | solution.py:662
  218.2 4.6 %collective-permute-start.8 = (bf16[2,32,512]{2,1,0:T(8,128)(2,1)S(1)}, bf16[2,32,512]{2,1,0:T(8,128)(2,1)S(1)}, u32[]{:S(2)}, u32[]{:S(2)}) collective-permute-start(bf16[2,32,512]{2,1,0:T(8,128)(2,1)S(1)} %get-tuple-element.53), channel_id=1, source_target_pairs={{0,80},{16,96},{32,112},{48,0},{64,16},{80,32},{96,48},{112,64},{1... | collective-permute-start | bytes 196616 | tf_op jit(solution)/shard_map/ppermute | solution.py:662
  220.2 3.1 %collective-permute-start.9 = (bf16[2,32,512]{2,1,0:T(8,128)(2,1)S(1)}, bf16[2,32,512]{2,1,0:T(8,128)(2,1)S(1)}, u32[]{:S(2)}, u32[]{:S(2)}) collective-permute-start(bf16[2,32,512]{2,1,0:T(8,128)(2,1)S(1)} %get-tuple-element.54), channel_id=1, source_target_pairs={{0,96},{16,112},{32,0},{48,16},{64,32},{80,48},{96,64},{112,80},{1... | collective-permute-start | bytes 196616 | tf_op jit(solution)/shard_map/ppermute | solution.py:662
  222.8 3.4 %collective-permute-start.10 = (bf16[2,32,512]{2,1,0:T(8,128)(2,1)S(1)}, bf16[2,32,512]{2,1,0:T(8,128)(2,1)S(1)}, u32[]{:S(2)}, u32[]{:S(2)}) collective-permute-start(bf16[2,32,512]{2,1,0:T(8,128)(2,1)S(1)} %get-tuple-element.55), channel_id=1, source_target_pairs={{0,112},{16,0},{32,16},{48,32},{64,48},{80,64},{96,80},{112,96},{1... | collective-permute-start | bytes 196616 | tf_op jit(solution)/shard_map/ppermute | solution.py:662

commit v7 on v6

--- a/solution.py
+++ b/solution.py
@@ -126,13 +126,16 @@
         copy.wait()
 
 
-def project(normed, qkv_ref, w_ref):
+def project(normed, qkv_ref, w_ref, copies=()):
+    wait_all(copies[0:1])
     qkv_ref[0] = (dot(normed, w_ref[0]).astype(BF16).astype(F32) * SCALE).astype(BF16)
+    wait_all(copies[1:2])
     qkv_ref[1] = dot(normed, w_ref[1]).astype(BF16)
+    wait_all(copies[2:3])
     qkv_ref[2] = dot(normed, w_ref[2]).astype(BF16)
 
 
-def each_pair(visit, per_step=2, before=None):
+def each_pair(visit, per_step=2, before=None, after=None):
     def step(index, carry):
         line = index // (N_PAIR // per_step)
         first = lax.rem(index, N_PAIR // per_step) * per_step
@@ -143,6 +146,8 @@
             pair = first + offset
             lanes = pl.ds(pl.multiple_of(pair * PAIR, PAIR), PAIR)
             visit(rows, lanes, line * N_PAIR + pair, pair)
+        if after is not None:
+            after(line)
         return carry
 
     lax.fori_loop(0, 2 * N_PAIR // per_step, step, 0)
@@ -150,15 +155,17 @@
 
 def row_forward_kernel(
     where_ref, x_ref, w_ref, mid_ref, saved_ref,
-    order_s, mid_s, qkv_s, left_s, mid_sem, qkv_sem, left_sem,
+    w_s, order_s, mid_s, qkv_s, left_s, w_sem, mid_sem, qkv_sem, left_sem,
 ):
+    weights = copies_of(w_ref, w_s, w_sem, 4)
+    start_all(weights)
     saved = copies_of(qkv_s, saved_ref, qkv_sem, 3)
     lefts = copies_of(left_s, saved_ref.at[3:5], left_sem, 2)
     order_s[...] = chunks_of_row_tokens()
     for rr in range(2):
         u = x_ref[:, rr].astype(F32).reshape(LINE, D)
         left_s[0, rr * LINE : (rr + 1) * LINE, :] = (u * inverse_rms(u)).astype(BF16)
-    project(left_s[0], qkv_s, w_ref)
+    project(left_s[0], qkv_s, w_s, weights)
     lefts[0].start()
     start_all(saved)
 
@@ -169,7 +176,8 @@
 
     each_pair(visit, 4)
     lefts[1].start()
-    added = dot(left_s[1], w_ref[3])
+    weights[3].wait()
+    added = dot(left_s[1], w_s[3])
     mids = []
     for rr in range(2):
         u = x_ref[:, rr].astype(F32).reshape(LINE, D)
@@ -229,8 +237,8 @@
 def row_backward_kernel(
     where_ref, g_ref, qkv_ref, turned_ref, probs_ref, w_ref,
     send_ref, right_ref,
-    da_s, wo_s, qkv_s, turned_s, probs_s, send_s, right_s,
-    wo_sem, qkv_sem, turned_sem, probs_sem, half_sem, right_sem,
+    da_s, wo_s, qkv_s, turned_s, probs_s, right_s,
+    wo_sem, qkv_sem, turned_sem, probs_sem, grad_sem, right_sem,
 ):
     weight = pltpu.make_async_copy(w_ref.at[3], wo_s, wo_sem)
     weight.start()
@@ -244,6 +252,8 @@
 
     line_probs(0).start()
     right_s[3] = dot(row_tokens_of_chunks(), g_ref[...].reshape(TOK, D)).astype(BF16)
+    grad = pltpu.make_async_copy(right_s.at[3], right_ref.at[3], grad_sem)
+    grad.start()
     weight.wait()
     gain = gain_row(where_ref, 0, 0, HEADS)
     da_s[...] = (dot_nt(right_s[3], wo_s[...]) * gain).astype(BF16)
@@ -254,15 +264,18 @@
     def visit(rows, lanes, at, pair):
         attention_backward(rows, lanes, qkv_s, da_s, probs_s[at], right_s)
 
-    each_pair(visit, 4, lambda line: line_probs(line).wait())
-    rights = copies_of(right_s, right_ref, right_sem, 4)
-    start_all(rights)
+    def line_grads(line):
+        rows = pl.ds(pl.multiple_of(line * LINE, LINE), LINE)
+        return pltpu.make_async_copy(
+            right_s.at[0:3, rows], right_ref.at[0:3, rows], right_sem.at[line]
+        )
+
+    each_pair(
+        visit, 4, lambda line: line_probs(line).wait(), lambda line: line_grads(line).start()
+    )
     wait_all(turned)
-    core = where_ref[4]
-    weight_gradients(1 - core, turned_s, right_s, send_s)
-    sent = pltpu.make_async_copy(send_s, send_ref, half_sem)
-    sent.start()
-    wait_all(rights + [sent])
+    weight_gradients(1 - where_ref[4], turned_s, right_s, send_ref)
+    wait_all([line_grads(0), line_grads(1), grad])
 
 
 def kept_gradients_kernel(where_ref, turned_ref, right_ref, keep_ref, turned_s, right_s, turned_sem, right_sem):
@@ -394,17 +407,12 @@
 
 
 def lines_to_tile_kernel(where_ref, *refs):
-    parts, tile_ref, mix_s = refs[:8], refs[8], refs[9]
-    me = where_ref[0] * 2 + where_ref[1]
-    for group in range(4):
-        lanes = slice(group * 128, (group + 1) * 128)
-        for shift in range(8):
-            peer = lax.rem(me + (8 - shift), 8)
-            for cc in range(2):
-                for rr in range(2):
-                    piece = parts[shift][cc, rr * 16 : (rr + 1) * 16, lanes].astype(F32)
-                    mix_s[group, pl.ds(peer + (rr * 16 + cc * 8), 16, stride=32), :] = piece
-        tile_ref[:, :, lanes] = mix_s[group].astype(BF16).reshape(32, 16, 128)
+    parts, tile_ref = refs[:8], refs[8]
+    row = positions()
+    shift = (where_ref[0] * 2 + where_ref[1] + 8 - row % 8) % 8
+    order = picked(((shift * 2 + (row // 8) % 2) * 2 + (row // 16) % 2) * 16 + row // 32)
+    lines = jnp.concatenate([part[...].reshape(64, D) for part in parts], axis=0)
+    tile_ref[...] = dot(order, lines).astype(BF16).reshape(32, 16, D)
 
 
 def pass_core_kernel(where_ref, *refs):
@@ -527,7 +535,6 @@
 PASS = shape(4, 2, 32, D)
 QUARTER = shape(256, D)
 HALF = shape(2, D, D)
-HALF_S = pltpu.VMEM((2, D, D), BF16)
 
 
 def token_scratch(*lead, dtype=BF16):
@@ -536,16 +543,17 @@
 
 row_forward = call(
     row_forward_kernel,
-    "svv",
+    "svh",
     "hh",
     (shape(N_DEV, 4, D), shape(5, TOK, D)),
     [
-        token_scratch(), pltpu.VMEM((N_DEV, 4, D), BF16), token_scratch(3), token_scratch(2),
+        WEIGHTS[0], token_scratch(), pltpu.VMEM((N_DEV, 4, D), BF16), token_scratch(3),
+        token_scratch(2), WEIGHTS[1],
         DMA((4,)), DMA((3,)), DMA((2,)),
     ],
     4 * MATMUL + 2 * ATTEND,
     6 * MIB,
-    grant=50,
+    grant=51,
 )
 row_prepare = call(
     row_prepare_kernel, "v", "vv", (shape(8, TOK, LINE), shape(2, D, TOK)), [], ATTEND, 8 * MIB
@@ -553,12 +561,12 @@
 row_backward = call(
     row_backward_kernel,
     "svhhhh",
-    "hh",
+    "vh",
     (HALF, shape(4, TOK, D)),
     [
         token_scratch(), pltpu.VMEM((D, D), BF16), token_scratch(3),
-        pltpu.VMEM((2, D, TOK), BF16), pltpu.VMEM((8, TOK, LINE), BF16), HALF_S,
-        token_scratch(4), DMA, DMA((3,)), DMA((2,)), DMA((2,)), DMA, DMA((4,)),
+        pltpu.VMEM((2, D, TOK), BF16), pltpu.VMEM((8, TOK, LINE), BF16),
+        token_scratch(4), DMA, DMA((3,)), DMA((2,)), DMA((2,)), DMA, DMA((2,)),
     ],
     5 * MATMUL + 5 * ATTEND,
     12 * MIB,
@@ -585,7 +593,7 @@
     ],
     3 * MATMUL,
     5 * MIB,
-    grant=50,
+    grant=51,
 )
 col_grad = call(
     col_kernel,
@@ -611,7 +619,7 @@
     ],
     2 * MATMUL,
     6 * MIB,
-    grant=50,
+    grant=54,
 )
 col_output = call(
     col_output_kernel,
@@ -623,16 +631,20 @@
     3 * MIB,
     grant=52,
 )
-tile_to_lines = call(tile_to_lines_kernel, "sv", "v" * 4, (PIECE,) * 4, [MIX_TILE], 0, MIB)
-pass_low = call(pass_low_kernel, "s" + "v" * 4, "v", PASS, [], 0, MIB)
-lines_to_tile = call(lines_to_tile_kernel, "s" + "v" * 8, "v", shape(32, 16, D), [MIX_TILE], 0, MIB)
+tile_to_lines = call(
+    tile_to_lines_kernel, "sv", "v" * 4, (PIECE,) * 4, [MIX_TILE], 0, MIB, grant=48
+)
+pass_low = call(pass_low_kernel, "s" + "v" * 4, "v", PASS, [], 0, MIB, grant=12)
+lines_to_tile = call(
+    lines_to_tile_kernel, "s" + "v" * 8, "v", shape(32, 16, D), [], MATMUL, MIB, grant=48
+)
 CORE_PASS = shape(8, 2, 16, D)
-pass_core = call(pass_core_kernel, "s" + "v" * 8, "v", CORE_PASS, [], 0, MIB)
+pass_core = call(pass_core_kernel, "s" + "v" * 8, "v", CORE_PASS, [], 0, MIB, grant=40)
 join = call(join_kernel, "s" + "v" * 9, "v", shape(8, 2, 2, 16, D), [], 0, MIB)
 pair_sum = call(
     pair_sum_kernel, "svv", "v" * 4, (QUARTER,) * 4, [pltpu.VMEM((4, 256, D), BF16)], 0, 3 * MIB,
 )
-merge = call(merge_kernel, "v" * 6, "v", shape(64, 80, 128), [], 0, 4 * MIB)
+merge = call(merge_kernel, "v" * 6, "v", shape(64, 80, 128), [], 0, 4 * MIB, grant=32)
 spread = call(spread_kernel, "v", "v", shape(64, 128, 128), [], 0, 3 * MIB, grant=52)
 
 

time: 240 us -> 239 us (level)
  local copies, waits for them, and re-layouts: 7.79 us -> 5.22 us
    unnamed x24 -> x22, local copies, waits for them, and re-layouts: 6.94 us -> 4.37 us
  transfers between devices with their start and end apart: 28 -> 28, of which waited for: 16 -> 16; matrix products, arithmetic and copies ran while one was open for 0% -> 0% of each run, Pallas kernels for 15% -> 16%
where the time goes in v7:
time: 239 us; the launch traced here: 235 us
  Pallas kernels  61 us (26%)
  blocking collectives  58.5 us (24%)
  starting transfers between devices  56.6 us (24%)
  waiting for transfers between devices  52.4 us (22%)
  local copies, waits for them, and re-layouts  5.22 us (2%)
    all_to_all x2, blocking collectives, exchange(): return lax.all_to_all(values, axes, split_axis=0, concat_axis=0, tiled=True)  58.5 us
    ppermute x20, waiting for transfers between devices, shifted(): lax.ppermute(pieces[k], axes, [(i, (i + k) % n) for i in range(n)])  33.9 us
    all_to_all x3, starting transfers between devices, exchange(): return lax.all_to_all(values, axes, split_axis=0, concat_axis=0, tiled=True)  24 us
    ppermute x20, starting transfers between devices, shifted(): lax.ppermute(pieces[k], axes, [(i, (i + k) % n) for i in range(n)])  22.1 us
    all_to_all x3, waiting for transfers between devices, exchange(): return lax.all_to_all(values, axes, split_axis=0, concat_axis=0, tiled=True)  12.6 us
    pallas_call x1, Pallas kernels, layer(): col_grad(where, mid_lines, w_col, *grad_parts, grad_pass)  11.5 us
    ppermute x5, starting transfers between devices, swap(): return lax.ppermute(value, axis, [(0, 1), (1, 0)])  10.6 us
    pallas_call x1, Pallas kernels, layer(): row_backward(where, grad_rows, saved_row, turned_row, probs_row, w_row)  8.65 us
  transfers between devices with their start and end apart: 28, of which 16 were waited for; matrix products, arithmetic and copies ran while one was open for 0% of the time, Pallas kernels for 16%

profile of v7, /device:TPU:1, one launch (start us, length us, event | category | flops | bytes accessed | tf_op | source)
XLA Modules:
  0.0 234.9 jit_solution(17197440240058719966)
XLA Ops:
  0.6 9.1 %all-to-all-start = ((bf16[16,2,16,512]{3,2,1,0:T(8,128)(2,1)}), bf16[16,2,16,512]{3,2,1,0:T(8,128)(2,1)S(1)}, u32[]{:S(2)}, u32[]{:S(2)}) async-start(bf16[16,2,16,512]{3,2,1,0:T(8,128)(2,1)} %bitcast.12), calls=%async_computation | async-start | bytes 1048576 | tf_op jit(solution)/shard_map/all_to_all | solution.py:668
  9.8 0.8 reshape.23
  10.6 10.1 %all-to-all-done.x_ref = bf16[16,2,16,512]{3,2,1,0:T(8,128)(2,1)S(1)} async-done(((bf16[16,2,16,512]{3,2,1,0:T(8,128)(2,1)}), bf16[16,2,16,512]{3,2,1,0:T(8,128)(2,1)S(1)}, u32[]{:S(2)}, u32[]{:S(2)}) %all-to-all-start) | async-done | bytes 524320 | tf_op jit(solution)/shard_map/all_to_all | solution.py:668
  20.8 7.9 %shard_map.84 = (bf16[128,4,512]{2,1,0:T(4,128)(2,1)S(1)}, bf16[5,512,512]{2,1,0:T(8,128)(2,1)}) custom-call(s32[21]{0:T(128)S(1)} %concatenate.3.where_ref, bf16[16,2,16,512]{3,2,1,0:T(8,128)(2,1)S(1)} %all-to-all-done.x_ref, bf16[4,512,512]{2,1,0:T(8,128)(2,1)} %w_ref.9), custom_call_target="tpu_custom_call" | custom-call | flops 1342177280 | bytes 6291456 | tf_op jit(solution)/shard_map/pallas_call | solution.py:691
  28.7 0.8 copy-done.8
  29.5 6.4 %all-to-all-start.1 = ((bf16[128,4,512]{2,1,0:T(4,128)(2,1)}), bf16[128,4,512]{2,1,0:T(4,128)(2,1)}, u32[]{:S(2)}, u32[]{:S(2)}) async-start(bf16[128,4,512]{2,1,0:T(4,128)(2,1)} %copy-done.8), calls=%async_computation.1 | async-start | bytes 1048576 | tf_op jit(solution)/shard_map/all_to_all | solution.py:668
  35.9 1.2 shard_map.85
  37.2 1.4 collective-permute-start
  38.6 2.5 %collective-permute-start.1 = (bf16[2,2,32,512]{3,2,1,0:T(8,128)(2,1)S(1)}, bf16[2,2,32,512]{3,2,1,0:T(8,128)(2,1)S(1)}, u32[]{:S(2)}, u32[]{:S(2)}) collective-permute-start(bf16[2,2,32,512]{3,2,1,0:T(8,128)(2,1)S(1)} %get-tuple-element.45), channel_id=1, source_target_pairs={{0,64},{32,96},{64,0},{96,32},{1,65},{33,97},{65,1},{97,33},{2,66}... | collective-permute-start | bytes 393224 | tf_op jit(solution)/shard_map/ppermute | solution.py:674
  41.0 1.1 collective-permute-start.2
  42.2 5.2 %collective-permute-done.refs_1_ = bf16[2,2,32,512]{3,2,1,0:T(8,128)(2,1)S(1)} collective-permute-done((bf16[2,2,32,512]{3,2,1,0:T(8,128)(2,1)S(1)}, bf16[2,2,32,512]{3,2,1,0:T(8,128)(2,1)S(1)}, u32[]{:S(2)}, u32[]{:S(2)}) %collective-permute-start) | collective-permute-done | bytes 131104 | tf_op jit(solution)/shard_map/ppermute | solution.py:674
  47.4 3.5 %collective-permute-done.1.refs_2_ = bf16[2,2,32,512]{3,2,1,0:T(8,128)(2,1)S(1)} collective-permute-done((bf16[2,2,32,512]{3,2,1,0:T(8,128)(2,1)S(1)}, bf16[2,2,32,512]{3,2,1,0:T(8,128)(2,1)S(1)}, u32[]{:S(2)}, u32[]{:S(2)}) %collective-permute-start.1) | collective-permute-done | bytes 131104 | tf_op jit(solution)/shard_map/ppermute | solution.py:674
  50.9 0.6 shard_map.86
  51.5 1.7 collective-permute-start.3
  53.2 5.9 %collective-permute-done.3.refs_4_ = bf16[4,2,32,512]{3,2,1,0:T(8,128)(2,1)S(1)} collective-permute-done((bf16[4,2,32,512]{3,2,1,0:T(8,128)(2,1)S(1)}, bf16[4,2,32,512]{3,2,1,0:T(8,128)(2,1)S(1)}, u32[]{:S(2)}, u32[]{:S(2)}) %collective-permute-start.3) | collective-permute-done | bytes 262176 | tf_op jit(solution)/shard_map/ppermute | solution.py:679
  59.1 11.5 %shard_map.87 = (bf16[128,4,512]{2,1,0:T(4,128)(2,1)}, bf16[7,512,512]{2,1,0:T(8,128)(2,1)}) custom-call(s32[21]{0:T(128)S(1)} %concatenate.3.where_ref, bf16[128,4,512]{2,1,0:T(4,128)(2,1)} %all-to-all-done.1.m_ref, bf16[4,512,512]{2,1,0:T(8,128)(2,1)S(1)} %copy-done.4, bf16[2,2,32,512]{3,2,1,0:T(8,128)(2,1)S(1)} %get-tuple-element.43.refs_0_, ...), custom_call_target="tpu_custom_call" | custom-call | flops 2952790016 | bytes 8388608 | tf_op jit(solution)/shard_map/pallas_call | solution.py:694
  70.6 8.4 %all-to-all-start.2 = ((bf16[128,4,512]{2,1,0:T(4,128)(2,1)}), bf16[128,4,512]{2,1,0:T(4,128)(2,1)}, u32[]{:S(2)}, u32[]{:S(2)}) async-start(bf16[128,4,512]{2,1,0:T(4,128)(2,1)} %get-tuple-element.56), calls=%async_computation.2 | async-start | bytes 1048576 | tf_op jit(solution)/shard_map/all_to_all | solution.py:668
  79.0 4.2 %shard_map.96 = (bf16[2,512,512]{2,1,0:T(8,128)(2,1)}, bf16[2,512,512]{2,1,0:T(8,128)(2,1)}) custom-call(s32[21]{0:T(128)} %copy-done.9, bf16[7,512,512]{2,1,0:T(8,128)(2,1)} %get-tuple-element.47.saved_ref.right_ref), custom_call_target="tpu_custom_call" | custom-call | flops 536870912 | bytes 6291456 | tf_op jit(solution)/shard_map/pallas_call | solution.py:698
  83.2 1.2 collective-permute-start.20
  84.4 2.4 %shard_map.90 = (bf16[8,512,256]{2,1,0:T(8,128)(2,1)S(1)}, bf16[2,512,512]{2,1,0:T(8,128)(2,1)S(1)}) custom-call(bf16[5,512,512]{2,1,0:T(8,128)(2,1)S(1)} %copy-done), custom_call_target="tpu_custom_call" | custom-call | flops 134217728 | bytes 8388608 | tf_op jit(solution)/shard_map/pallas_call | solution.py:693
  86.9 1.0 copy-done.1
  87.9 1.3 copy-done.5
  89.2 2.5 %all-to-all-done.2.g_ref = bf16[128,4,512]{2,1,0:T(4,128)(2,1)} async-done(((bf16[128,4,512]{2,1,0:T(4,128)(2,1)}), bf16[128,4,512]{2,1,0:T(4,128)(2,1)}, u32[]{:S(2)}, u32[]{:S(2)}) %all-to-all-start.2) | async-done | bytes 524320 | tf_op jit(solution)/shard_map/all_to_all | solution.py:668
  91.7 1.2 copy-done.2
  92.9 8.7 %shard_map.91 = (bf16[2,512,512]{2,1,0:T(8,128)(2,1)S(1)}, bf16[4,512,512]{2,1,0:T(8,128)(2,1)}) custom-call(s32[21]{0:T(128)S(1)} %copy-done.10, bf16[128,4,512]{2,1,0:T(4,128)(2,1)} %all-to-all-done.2.g_ref, bf16[5,512,512]{2,1,0:T(8,128)(2,1)} %get-tuple-element.57.saved_ref.qkv_ref, bf16[2,512,512]{2,1,0:T(8,128)(2,1)S(1)} %copy-done.2, ...), custom_call_target="tpu_custom_call" | custom-call | flops 2013265920 | bytes 12582912 | tf_op jit(solution)/shard_map/pallas_call | solution.py:703
  101.6 1.7 collective-permute-start.19
  103.3 2.6 %shard_map.97.keep_ref = bf16[2,512,512]{2,1,0:T(8,128)(2,1)S(1)} custom-call(s32[21]{0:T(128)S(1)} %copy-done.10, bf16[2,512,512]{2,1,0:T(8,128)(2,1)S(1)} %copy-done.6, bf16[7,512,512]{2,1,0:T(8,128)(2,1)} %get-tuple-element.47.saved_ref.right_ref), custom_call_target="tpu_custom_call" | custom-call | flops 536870912 | bytes 3145728 | tf_op jit(solution)/shard_map/pallas_call | solution.py:700
  105.9 1.9 shard_map.98
  107.8 0.4 collective-permute-start.21
  108.2 1.9 collective-permute-start.22
  110.1 0.9 collective-permute-start.23
  111.0 2.6 %shard_map.95.keep_ref = bf16[2,512,512]{2,1,0:T(8,128)(2,1)S(1)} custom-call(s32[21]{0:T(128)S(1)} %copy-done.10, bf16[2,512,512]{2,1,0:T(8,128)(2,1)S(1)} %copy-done.3, bf16[4,512,512]{2,1,0:T(8,128)(2,1)} %get-tuple-element.60.right_ref), custom_call_target="tpu_custom_call" | custom-call | flops 536870912 | bytes 3145728 | tf_op jit(solution)/shard_map/pallas_call | solution.py:705
  113.6 3.9 %collective-permute-done.21.refs_1_ = bf16[256,512]{1,0:T(8,128)(2,1)S(1)} collective-permute-done((bf16[256,512]{1,0:T(8,128)(2,1)S(1)}, bf16[256,512]{1,0:T(8,128)(2,1)S(1)}, u32[]{:S(2)}, u32[]{:S(2)}) %collective-permute-start.21) | collective-permute-done | bytes 262176 | tf_op jit(solution)/shard_map/ppermute | solution.py:674
  117.4 4.7 %collective-permute-done.22.refs_2_ = bf16[256,512]{1,0:T(8,128)(2,1)S(1)} collective-permute-done((bf16[256,512]{1,0:T(8,128)(2,1)S(1)}, bf16[256,512]{1,0:T(8,128)(2,1)S(1)}, u32[]{:S(2)}, u32[]{:S(2)}) %collective-permute-start.22) | collective-permute-done | bytes 262176 | tf_op jit(solution)/shard_map/ppermute | solution.py:674
  122.1 0.8 collective-permute-done.23.refs_3_
  122.9 0.4 shard_map.99
  123.3 26.1 %all_to_all.25.both_ref = bf16[64,80,128]{2,1,0:T(8,128)(2,1)S(1)} all-to-all(bf16[64,80,128]{2,1,0:T(8,128)(2,1)S(1)} %shard_map.99), channel_id=1, replica_groups=mesh['y'=4,'zl'=2,'zh'=2,'x'=4,'c'=2] {'y','zl','zh','x'}, dimensions={0} | all-to-all | bytes 2621440 | tf_op jit(solution)/shard_map/all_to_all | solution.py:668
  149.4 1.7 shard_map.100
  151.1 32.5 %all_to_all.26.chunks_ref = bf16[64,128,128]{2,1,0:T(8,128)(2,1)S(1)} all-to-all(bf16[64,128,128]{2,1,0:T(8,128)(2,1)} %shard_map.100), channel_id=1, replica_groups=mesh['y'=4,'zl'=2,'zh'=2,'x'=4,'c'=2] {'y','zl','zh','x'}, dimensions={0} | all-to-all | bytes 4194304 | tf_op jit(solution)/shard_map/all_to_all | solution.py:668
  183.6 3.2 %collective-permute-start.24 = (bf16[64,128,128]{2,1,0:T(8,128)(2,1)S(1)}, bf16[64,128,128]{2,1,0:T(8,128)(2,1)S(1)}, u32[]{:S(2)}, u32[]{:S(2)}) collective-permute-start(bf16[64,128,128]{2,1,0:T(8,128)(2,1)S(1)} %all_to_all.26.chunks_ref), channel_id=1, source_target_pairs={{0,1},{1,0},{2,3},{3,2},{4,5},{5,4},{6,7},{7,6},{8,9},{9,8},{10,11... | collective-permute-start | bytes 6291464 | tf_op jit(solution)/shard_map/ppermute | solution.py:679
  186.8 3.8 %shard_map.92 = (bf16[2,2,16,512]{3,2,1,0:T(8,128)(2,1)S(1)}, bf16[2,2,16,512]{3,2,1,0:T(8,128)(2,1)S(1)}, bf16[2,2,16,512]{3,2,1,0:T(8,128)(2,1)S(1)}, bf16[2,2...) custom-call(s32[21]{0:T(128)S(1)} %copy-done.10, ...), custom_call_target="tpu_custom_call" | custom-call | flops 805306368 | bytes 5242880 | tf_op jit(solution)/shard_map/pallas_call | solution.py:710
  190.7 2.2 collective-permute-start.12
  192.9 1.5 collective-permute-start.13
  194.4 2.4 %collective-permute-start.14 = (bf16[2,2,16,512]{3,2,1,0:T(8,128)(2,1)S(1)}, bf16[2,2,16,512]{3,2,1,0:T(8,128)(2,1)S(1)}, u32[]{:S(2)}, u32[]{:S(2)}) collective-permute-start(bf16[2,2,16,512]{3,2,1,0:T(8,128)(2,1)S(1)} %get-tuple-element.65), channel_id=1, source_target_pairs={{0,8},{2,10},{4,12},{6,14},{8,0},{10,2},{12,4},{14,6},{1,9},{3,11}... | collective-permute-start | bytes 196616 | tf_op jit(solution)/shard_map/ppermute | solution.py:674
  196.7 3.0 %collective-permute-done.11.refs_1_ = bf16[2,2,16,512]{3,2,1,0:T(8,128)(2,1)S(1)} collective-permute-done((bf16[2,2,16,512]{3,2,1,0:T(8,128)(2,1)S(1)}, bf16[2,2,16,512]{3,2,1,0:T(8,128)(2,1)S(1)}, u32[]{:S(2)}, u32[]{:S(2)}) %collective-permute-start.11) | collective-permute-done | bytes 65568 | tf_op jit(solution)/shard_map/ppermute | solution.py:674
  199.7 1.6 collective-permute-start.16
  201.3 2.6 %collective-permute-start.17 = (bf16[2,2,16,512]{3,2,1,0:T(8,128)(2,1)S(1)}, bf16[2,2,16,512]{3,2,1,0:T(8,128)(2,1)S(1)}, u32[]{:S(2)}, u32[]{:S(2)}) collective-permute-start(bf16[2,2,16,512]{3,2,1,0:T(8,128)(2,1)S(1)} %get-tuple-element.68), channel_id=1, source_target_pairs={{0,14},{2,0},{4,2},{6,4},{8,6},{10,8},{12,10},{14,12},{1,15},{3,1}... | collective-permute-start | bytes 196616 | tf_op jit(solution)/shard_map/ppermute | solution.py:674
  203.9 0.8 collective-permute-done.15.refs_5_
  204.7 1.8 collective-permute-done.17.refs_7_
  206.5 0.6 shard_map.93
  207.1 2.7 %collective-permute-start.18 = (bf16[8,2,16,512]{3,2,1,0:T(8,128)(2,1)S(1)}, bf16[8,2,16,512]{3,2,1,0:T(8,128)(2,1)S(1)}, u32[]{:S(2)}, u32[]{:S(2)}) collective-permute-start(bf16[8,2,16,512]{3,2,1,0:T(8,128)(2,1)S(1)} %shard_map.93), channel_id=1, source_target_pairs={{0,1},{1,0},{2,3},{3,2},{4,5},{5,4},{6,7},{7,6},{8,9},{9,8},{10,11... | collective-permute-start | bytes 786440 | tf_op jit(solution)/shard_map/ppermute | solution.py:679
  209.8 2.4 %shard_map.88 = (bf16[2,32,512]{2,1,0:T(8,128)(2,1)S(1)}, bf16[2,32,512]{2,1,0:T(8,128)(2,1)S(1)}, bf16[2,32,512]{2,1,0:T(8,128)(2,1)S(1)}, bf16[2,32,512]{2,1,0...) custom-call(s32[21]{0:T(128)S(1)} %copy-done.10, ...), custom_call_target="tpu_custom_call" | custom-call | flops 268435456 | bytes 3145728 | tf_op jit(solution)/shard_map/pallas_call | solution.py:715
  212.5 1.9 collective-permute-start.6
  214.4 3.7 %collective-permute-done.4.refs_1_ = bf16[2,32,512]{2,1,0:T(8,128)(2,1)S(1)} collective-permute-done((bf16[2,32,512]{2,1,0:T(8,128)(2,1)S(1)}, bf16[2,32,512]{2,1,0:T(8,128)(2,1)S(1)}, u32[]{:S(2)}, u32[]{:S(2)}) %collective-permute-start.4) | collective-permute-done | bytes 65568 | tf_op jit(solution)/shard_map/ppermute | solution.py:674
  218.0 0.8 collective-permute-start.8
  218.8 1.2 collective-permute-done.6.refs_3_
  220.1 0.6 collective-permute-start.9
  220.7 2.0 collective-permute-done.7.refs_4_
  222.7 0.5 collective-permute-done.9.refs_6_
  223.2 2.9 %collective-permute-done.10.refs_7_ = bf16[2,32,512]{2,1,0:T(8,128)(2,1)S(1)} collective-permute-done((bf16[2,32,512]{2,1,0:T(8,128)(2,1)S(1)}, bf16[2,32,512]{2,1,0:T(8,128)(2,1)S(1)}, u32[]{:S(2)}, u32[]{:S(2)}) %collective-permute-start.10) | collective-permute-done | bytes 65568 | tf_op jit(solution)/shard_map/ppermute | solution.py:674
  226.1 1.9 shard_map.89
  227.9 1.4 shard_map.94
  229.3 2.7 %widen.2 = (f32[2,1024,512]{2,1,0:T(8,128)}, f32[2,4,256,512]{3,2,1,0:T(8,128)}) custom-call(s32[21]{0:T(128)S(1)} %copy-done.10, bf16[64,128,128]{2,1,0:T(8,128)(2,1)S(1)} %all_to_all.26.chunks_ref), custom_call_target="tpu_custom_call" | custom-call | bytes 6291456 | tf_op jit(solution)/shard_map/widen/pallas_call | solution.py:652
  232.0 2.7 %widen.3 = (f32[2,1024,512]{2,1,0:T(8,128)}, f32[2,4,256,512]{3,2,1,0:T(8,128)}) custom-call(s32[21]{0:T(128)S(1)} %copy-done.10, bf16[64,128,128]{2,1,0:T(8,128)(2,1)S(1)} %collective-permute-done.24.chunks_ref, f32[2,1024,512]{2,1,0:T(8,128)} %get-tuple-element.76.refs_0_, ...), custom_call_target="tpu_custom_call", output_to_operand_aliasing={{0}: (2, {}), {1}: (3, {})} | custom-call | bytes 6291456 | tf_op jit(solution)/shard_map/widen/pallas_call | solution.py:652
  (37 shorter events, 0.5 us)
Async XLA Ops:
  0.6 20.1 %all-to-all-start = ((bf16[16,2,16,512]{3,2,1,0:T(8,128)(2,1)}), bf16[16,2,16,512]{3,2,1,0:T(8,128)(2,1)S(1)}, u32[]{:S(2)}, u32[]{:S(2)}) async-start(bf16[16,2,16,512]{3,2,1,0:T(8,128)(2,1)} %bitcast.12), calls=%async_computation | async-start | bytes 1048576 | tf_op jit(solution)/shard_map/all_to_all | solution.py:668
  10.6 48.5 %copy-start.9 = (s32[21]{0:T(128)}, s32[21]{0:T(128)S(1)}, u32[]{:S(2)}) copy-start(s32[21]{0:T(128)S(1)} %concatenate.3.where_ref) | copy-start | bytes 256
  10.6 25.3 %copy-start.7 = (bf16[32,16,512]{2,1,0:T(8,128)(2,1)S(1)}, bf16[32,16,512]{2,1,0:T(8,128)(2,1)}, u32[]{:S(2)}) copy-start(bf16[32,16,512]{2,1,0:T(8,128)(2,1)} %tile_ref.1) | copy-start | bytes 1572868
  28.7 0.8 copy-start.8
  29.5 29.6 %copy-start.4 = (bf16[4,512,512]{2,1,0:T(8,128)(2,1)S(1)}, bf16[4,512,512]{2,1,0:T(8,128)(2,1)}, u32[]{:S(2)}) copy-start(bf16[4,512,512]{2,1,0:T(8,128)(2,1)} %w_ref.7) | copy-start | bytes 6291460
  29.5 29.6 %all-to-all-start.1 = ((bf16[128,4,512]{2,1,0:T(4,128)(2,1)}), bf16[128,4,512]{2,1,0:T(4,128)(2,1)}, u32[]{:S(2)}, u32[]{:S(2)}) async-start(bf16[128,4,512]{2,1,0:T(4,128)(2,1)} %copy-done.8), calls=%async_computation.1 | async-start | bytes 1048576 | tf_op jit(solution)/shard_map/all_to_all | solution.py:668
  37.2 10.2 %collective-permute-start = (bf16[2,2,32,512]{3,2,1,0:T(8,128)(2,1)S(1)}, bf16[2,2,32,512]{3,2,1,0:T(8,128)(2,1)S(1)}, u32[]{:S(2)}, u32[]{:S(2)}) collective-permute-start(bf16[2,2,32,512]{3,2,1,0:T(8,128)(2,1)S(1)} %get-tuple-element.44), channel_id=1, source_target_pairs={{0,32},{32,64},{64,96},{96,0},{1,33},{33,65},{65,97},{97,1},{2,34}... | collective-permute-start | bytes 393224 | tf_op jit(solution)/shard_map/ppermute | solution.py:674
  38.6 12.3 %collective-permute-start.1 = (bf16[2,2,32,512]{3,2,1,0:T(8,128)(2,1)S(1)}, bf16[2,2,32,512]{3,2,1,0:T(8,128)(2,1)S(1)}, u32[]{:S(2)}, u32[]{:S(2)}) collective-permute-start(bf16[2,2,32,512]{3,2,1,0:T(8,128)(2,1)S(1)} %get-tuple-element.45), channel_id=1, source_target_pairs={{0,64},{32,96},{64,0},{96,32},{1,65},{33,97},{65,1},{97,33},{2,66}... | collective-permute-start | bytes 393224 | tf_op jit(solution)/shard_map/ppermute | solution.py:674
  41.0 9.8 %collective-permute-start.2 = (bf16[2,2,32,512]{3,2,1,0:T(8,128)(2,1)S(1)}, bf16[2,2,32,512]{3,2,1,0:T(8,128)(2,1)S(1)}, u32[]{:S(2)}, u32[]{:S(2)}) collective-permute-start(bf16[2,2,32,512]{3,2,1,0:T(8,128)(2,1)S(1)} %get-tuple-element.46), channel_id=1, source_target_pairs={{0,96},{32,0},{64,32},{96,64},{1,97},{33,1},{65,33},{97,65},{2,98}... | collective-permute-start | bytes 393224 | tf_op jit(solution)/shard_map/ppermute | solution.py:674
  51.5 7.6 %collective-permute-start.3 = (bf16[4,2,32,512]{3,2,1,0:T(8,128)(2,1)S(1)}, bf16[4,2,32,512]{3,2,1,0:T(8,128)(2,1)S(1)}, u32[]{:S(2)}, u32[]{:S(2)}) collective-permute-start(bf16[4,2,32,512]{3,2,1,0:T(8,128)(2,1)S(1)} %shard_map.86), channel_id=1, source_target_pairs={{0,16},{16,0},{1,17},{17,1},{2,18},{18,2},{3,19},{19,3},{4,20},{20... | collective-permute-start | bytes 786440 | tf_op jit(solution)/shard_map/ppermute | solution.py:679
  70.6 21.1 %all-to-all-start.2 = ((bf16[128,4,512]{2,1,0:T(4,128)(2,1)}), bf16[128,4,512]{2,1,0:T(4,128)(2,1)}, u32[]{:S(2)}, u32[]{:S(2)}) async-start(bf16[128,4,512]{2,1,0:T(4,128)(2,1)} %get-tuple-element.56), calls=%async_computation.2 | async-start | bytes 1048576 | tf_op jit(solution)/shard_map/all_to_all | solution.py:668
  79.0 5.4 %copy-start = (bf16[5,512,512]{2,1,0:T(8,128)(2,1)S(1)}, bf16[5,512,512]{2,1,0:T(8,128)(2,1)}, u32[]{:S(2)}) copy-start(bf16[5,512,512]{2,1,0:T(8,128)(2,1)} %get-tuple-element.57.saved_ref.qkv_ref) | copy-start | bytes 7864324
  83.2 8.5 %copy-start.10 = (s32[21]{0:T(128)S(1)}, s32[21]{0:T(128)}, u32[]{:S(2)}) copy-start(s32[21]{0:T(128)} %copy-done.9) | copy-start | bytes 256
  83.2 22.7 %collective-permute-start.20 = (bf16[2,512,512]{2,1,0:T(8,128)(2,1)}, bf16[2,512,512]{2,1,0:T(8,128)(2,1)}, u32[]{:S(2)}, u32[]{:S(2)}) collective-permute-start(bf16[2,512,512]{2,1,0:T(8,128)(2,1)} %get-tuple-element.71), channel_id=1, source_target_pairs={{0,1},{1,0},{2,3},{3,2},{4,5},{5,4},{6,7},{7,6},{8,9},{9,8},{10,11... | collective-permute-start | bytes 3145736 | tf_op jit(solution)/shard_map/ppermute | solution.py:679
  86.9 1.0 copy-start.1
  87.9 1.3 copy-start.5
  91.7 1.2 copy-start.2
  92.9 10.4 %copy-start.6 = (bf16[2,512,512]{2,1,0:T(8,128)(2,1)S(1)}, bf16[2,512,512]{2,1,0:T(8,128)(2,1)}, u32[]{:S(2)}) copy-start(bf16[2,512,512]{2,1,0:T(8,128)(2,1)} %get-tuple-element.70.turned_ref) | copy-start | bytes 3145732
  101.6 21.4 %collective-permute-start.19 = (bf16[2,512,512]{2,1,0:T(8,128)(2,1)S(1)}, bf16[2,512,512]{2,1,0:T(8,128)(2,1)S(1)}, u32[]{:S(2)}, u32[]{:S(2)}) collective-permute-start(bf16[2,512,512]{2,1,0:T(8,128)(2,1)S(1)} %get-tuple-element.69), channel_id=1, source_target_pairs={{0,1},{1,0},{2,3},{3,2},{4,5},{5,4},{6,7},{7,6},{8,9},{9,8},{10,11... | collective-permute-start | bytes 3145736 | tf_op jit(solution)/shard_map/ppermute | solution.py:679
  105.9 5.1 %copy-start.3 = (bf16[2,512,512]{2,1,0:T(8,128)(2,1)S(1)}, bf16[2,512,512]{2,1,0:T(8,128)(2,1)}, u32[]{:S(2)}) copy-start(bf16[2,512,512]{2,1,0:T(8,128)(2,1)} %copy-done.1) | copy-start | bytes 3145732
  107.8 9.6 %collective-permute-start.21 = (bf16[256,512]{1,0:T(8,128)(2,1)S(1)}, bf16[256,512]{1,0:T(8,128)(2,1)S(1)}, u32[]{:S(2)}, u32[]{:S(2)}) collective-permute-start(bf16[256,512]{1,0:T(8,128)(2,1)S(1)} %get-tuple-element.73), channel_id=1, source_target_pairs={{0,2},{2,4},{4,6},{6,0},{1,3},{3,5},{5,7},{7,1},{8,10},{10,12},{12... | collective-permute-start | bytes 786440 | tf_op jit(solution)/shard_map/ppermute | solution.py:674
  108.2 13.9 %collective-permute-start.22 = (bf16[256,512]{1,0:T(8,128)(2,1)S(1)}, bf16[256,512]{1,0:T(8,128)(2,1)S(1)}, u32[]{:S(2)}, u32[]{:S(2)}) collective-permute-start(bf16[256,512]{1,0:T(8,128)(2,1)S(1)} %get-tuple-element.74), channel_id=1, source_target_pairs={{0,4},{2,6},{4,0},{6,2},{1,5},{3,7},{5,1},{7,3},{8,12},{10,14},{12... | collective-permute-start | bytes 786440 | tf_op jit(solution)/shard_map/ppermute | solution.py:674
  110.1 12.8 %collective-permute-start.23 = (bf16[256,512]{1,0:T(8,128)(2,1)S(1)}, bf16[256,512]{1,0:T(8,128)(2,1)S(1)}, u32[]{:S(2)}, u32[]{:S(2)}) collective-permute-start(bf16[256,512]{1,0:T(8,128)(2,1)S(1)} %get-tuple-element.75), channel_id=1, source_target_pairs={{0,6},{2,0},{4,2},{6,4},{1,7},{3,1},{5,3},{7,5},{8,14},{10,8},{12,... | collective-permute-start | bytes 786440 | tf_op jit(solution)/shard_map/ppermute | solution.py:674
  183.6 48.4 %collective-permute-start.24 = (bf16[64,128,128]{2,1,0:T(8,128)(2,1)S(1)}, bf16[64,128,128]{2,1,0:T(8,128)(2,1)S(1)}, u32[]{:S(2)}, u32[]{:S(2)}) collective-permute-start(bf16[64,128,128]{2,1,0:T(8,128)(2,1)S(1)} %all_to_all.26.chunks_ref), channel_id=1, source_target_pairs={{0,1},{1,0},{2,3},{3,2},{4,5},{5,4},{6,7},{7,6},{8,9},{9,8},{10,11... | collective-permute-start | bytes 6291464 | tf_op jit(solution)/shard_map/ppermute | solution.py:679
  190.6 9.1 %collective-permute-start.11 = (bf16[2,2,16,512]{3,2,1,0:T(8,128)(2,1)S(1)}, bf16[2,2,16,512]{3,2,1,0:T(8,128)(2,1)S(1)}, u32[]{:S(2)}, u32[]{:S(2)}) collective-permute-start(bf16[2,2,16,512]{3,2,1,0:T(8,128)(2,1)S(1)} %get-tuple-element.62), channel_id=1, source_target_pairs={{0,2},{2,4},{4,6},{6,8},{8,10},{10,12},{12,14},{14,0},{1,3},{3,5},... | collective-permute-start | bytes 196616 | tf_op jit(solution)/shard_map/ppermute | solution.py:674
  190.7 9.0 %collective-permute-start.12 = (bf16[2,2,16,512]{3,2,1,0:T(8,128)(2,1)S(1)}, bf16[2,2,16,512]{3,2,1,0:T(8,128)(2,1)S(1)}, u32[]{:S(2)}, u32[]{:S(2)}) collective-permute-start(bf16[2,2,16,512]{3,2,1,0:T(8,128)(2,1)S(1)} %get-tuple-element.63), channel_id=1, source_target_pairs={{0,4},{2,6},{4,8},{6,10},{8,12},{10,14},{12,0},{14,2},{1,5},{3,7},... | collective-permute-start | bytes 196616 | tf_op jit(solution)/shard_map/ppermute | solution.py:674
  192.9 8.4 %collective-permute-start.13 = (bf16[2,2,16,512]{3,2,1,0:T(8,128)(2,1)S(1)}, bf16[2,2,16,512]{3,2,1,0:T(8,128)(2,1)S(1)}, u32[]{:S(2)}, u32[]{:S(2)}) collective-permute-start(bf16[2,2,16,512]{3,2,1,0:T(8,128)(2,1)S(1)} %get-tuple-element.64), channel_id=1, source_target_pairs={{0,6},{2,8},{4,10},{6,12},{8,14},{10,0},{12,2},{14,4},{1,7},{3,9},... | collective-permute-start | bytes 196616 | tf_op jit(solution)/shard_map/ppermute | solution.py:674
  194.4 9.5 %collective-permute-start.14 = (bf16[2,2,16,512]{3,2,1,0:T(8,128)(2,1)S(1)}, bf16[2,2,16,512]{3,2,1,0:T(8,128)(2,1)S(1)}, u32[]{:S(2)}, u32[]{:S(2)}) collective-permute-start(bf16[2,2,16,512]{3,2,1,0:T(8,128)(2,1)S(1)} %get-tuple-element.65), channel_id=1, source_target_pairs={{0,8},{2,10},{4,12},{6,14},{8,0},{10,2},{12,4},{14,6},{1,9},{3,11}... | collective-permute-start | bytes 196616 | tf_op jit(solution)/shard_map/ppermute | solution.py:674
  199.7 5.0 %collective-permute-start.15 = (bf16[2,2,16,512]{3,2,1,0:T(8,128)(2,1)S(1)}, bf16[2,2,16,512]{3,2,1,0:T(8,128)(2,1)S(1)}, u32[]{:S(2)}, u32[]{:S(2)}) collective-permute-start(bf16[2,2,16,512]{3,2,1,0:T(8,128)(2,1)S(1)} %get-tuple-element.66), channel_id=1, source_target_pairs={{0,10},{2,12},{4,14},{6,0},{8,2},{10,4},{12,6},{14,8},{1,11},{3,13... | collective-permute-start | bytes 196616 | tf_op jit(solution)/shard_map/ppermute | solution.py:674
  199.7 5.0 %collective-permute-start.16 = (bf16[2,2,16,512]{3,2,1,0:T(8,128)(2,1)S(1)}, bf16[2,2,16,512]{3,2,1,0:T(8,128)(2,1)S(1)}, u32[]{:S(2)}, u32[]{:S(2)}) collective-permute-start(bf16[2,2,16,512]{3,2,1,0:T(8,128)(2,1)S(1)} %get-tuple-element.67), channel_id=1, source_target_pairs={{0,12},{2,14},{4,0},{6,2},{8,4},{10,6},{12,8},{14,10},{1,13},{3,15... | collective-permute-start | bytes 196616 | tf_op jit(solution)/shard_map/ppermute | solution.py:674
  201.3 5.2 %collective-permute-start.17 = (bf16[2,2,16,512]{3,2,1,0:T(8,128)(2,1)S(1)}, bf16[2,2,16,512]{3,2,1,0:T(8,128)(2,1)S(1)}, u32[]{:S(2)}, u32[]{:S(2)}) collective-permute-start(bf16[2,2,16,512]{3,2,1,0:T(8,128)(2,1)S(1)} %get-tuple-element.68), channel_id=1, source_target_pairs={{0,14},{2,0},{4,2},{6,4},{8,6},{10,8},{12,10},{14,12},{1,15},{3,1}... | collective-permute-start | bytes 196616 | tf_op jit(solution)/shard_map/ppermute | solution.py:674
  207.1 20.8 %collective-permute-start.18 = (bf16[8,2,16,512]{3,2,1,0:T(8,128)(2,1)S(1)}, bf16[8,2,16,512]{3,2,1,0:T(8,128)(2,1)S(1)}, u32[]{:S(2)}, u32[]{:S(2)}) collective-permute-start(bf16[8,2,16,512]{3,2,1,0:T(8,128)(2,1)S(1)} %shard_map.93), channel_id=1, source_target_pairs={{0,1},{1,0},{2,3},{3,2},{4,5},{5,4},{6,7},{7,6},{8,9},{9,8},{10,11... | collective-permute-start | bytes 786440 | tf_op jit(solution)/shard_map/ppermute | solution.py:679
  212.2 5.8 %collective-permute-start.4 = (bf16[2,32,512]{2,1,0:T(8,128)(2,1)S(1)}, bf16[2,32,512]{2,1,0:T(8,128)(2,1)S(1)}, u32[]{:S(2)}, u32[]{:S(2)}) collective-permute-start(bf16[2,32,512]{2,1,0:T(8,128)(2,1)S(1)} %get-tuple-element.49), channel_id=1, source_target_pairs={{0,16},{16,32},{32,48},{48,64},{64,80},{80,96},{96,112},{112,0},{1... | collective-permute-start | bytes 196616 | tf_op jit(solution)/shard_map/ppermute | solution.py:674
  212.5 5.5 %collective-permute-start.5 = (bf16[2,32,512]{2,1,0:T(8,128)(2,1)S(1)}, bf16[2,32,512]{2,1,0:T(8,128)(2,1)S(1)}, u32[]{:S(2)}, u32[]{:S(2)}) collective-permute-start(bf16[2,32,512]{2,1,0:T(8,128)(2,1)S(1)} %get-tuple-element.50), channel_id=1, source_target_pairs={{0,32},{16,48},{32,64},{48,80},{64,96},{80,112},{96,0},{112,16},{1... | collective-permute-start | bytes 196616 | tf_op jit(solution)/shard_map/ppermute | solution.py:674
  212.5 7.6 %collective-permute-start.6 = (bf16[2,32,512]{2,1,0:T(8,128)(2,1)S(1)}, bf16[2,32,512]{2,1,0:T(8,128)(2,1)S(1)}, u32[]{:S(2)}, u32[]{:S(2)}) collective-permute-start(bf16[2,32,512]{2,1,0:T(8,128)(2,1)S(1)} %get-tuple-element.51), channel_id=1, source_target_pairs={{0,48},{16,64},{32,80},{48,96},{64,112},{80,0},{96,16},{112,32},{1... | collective-permute-start | bytes 196616 | tf_op jit(solution)/shard_map/ppermute | solution.py:674
  218.0 4.6 %collective-permute-start.7 = (bf16[2,32,512]{2,1,0:T(8,128)(2,1)S(1)}, bf16[2,32,512]{2,1,0:T(8,128)(2,1)S(1)}, u32[]{:S(2)}, u32[]{:S(2)}) collective-permute-start(bf16[2,32,512]{2,1,0:T(8,128)(2,1)S(1)} %get-tuple-element.52), channel_id=1, source_target_pairs={{0,64},{16,80},{32,96},{48,112},{64,0},{80,16},{96,32},{112,48},{1... | collective-permute-start | bytes 196616 | tf_op jit(solution)/shard_map/ppermute | solution.py:674
  218.0 4.6 %collective-permute-start.8 = (bf16[2,32,512]{2,1,0:T(8,128)(2,1)S(1)}, bf16[2,32,512]{2,1,0:T(8,128)(2,1)S(1)}, u32[]{:S(2)}, u32[]{:S(2)}) collective-permute-start(bf16[2,32,512]{2,1,0:T(8,128)(2,1)S(1)} %get-tuple-element.53), channel_id=1, source_target_pairs={{0,80},{16,96},{32,112},{48,0},{64,16},{80,32},{96,48},{112,64},{1... | collective-permute-start | bytes 196616 | tf_op jit(solution)/shard_map/ppermute | solution.py:674
  220.1 3.1 %collective-permute-start.9 = (bf16[2,32,512]{2,1,0:T(8,128)(2,1)S(1)}, bf16[2,32,512]{2,1,0:T(8,128)(2,1)S(1)}, u32[]{:S(2)}, u32[]{:S(2)}) collective-permute-start(bf16[2,32,512]{2,1,0:T(8,128)(2,1)S(1)} %get-tuple-element.54), channel_id=1, source_target_pairs={{0,96},{16,112},{32,0},{48,16},{64,32},{80,48},{96,64},{112,80},{1... | collective-permute-start | bytes 196616 | tf_op jit(solution)/shard_map/ppermute | solution.py:674
  222.7 3.4 %collective-permute-start.10 = (bf16[2,32,512]{2,1,0:T(8,128)(2,1)S(1)}, bf16[2,32,512]{2,1,0:T(8,128)(2,1)S(1)}, u32[]{:S(2)}, u32[]{:S(2)}) collective-permute-start(bf16[2,32,512]{2,1,0:T(8,128)(2,1)S(1)} %get-tuple-element.55), channel_id=1, source_target_pairs={{0,112},{16,0},{32,16},{48,32},{64,48},{80,64},{96,80},{112,96},{1... | collective-permute-start | bytes 196616 | tf_op jit(solution)/shard_map/ppermute | solution.py:674

commit v8 on v7

--- a/solution.py
+++ b/solution.py
@@ -299,9 +299,9 @@
         u = x_ref[:, rr].astype(F32).reshape(LINE, D)
         grad_in = input_gradient(u, right_s, w_s, rows)
         gin_s[:, :, rr] = grad_in.astype(BF16).reshape(8, 2, 16, D)
-    chip = where_ref[2] * 4 + where_ref[3]
-    for shift in range(8):
-        outs[shift][...] = gin_s[lax.rem(chip + shift, 8)]
+    for place in range(8):
+        high, x = (where_ref[2] + place // 4) % 2, (where_ref[3] + place % 4) % 4
+        outs[place][...] = gin_s[high * 4 + x]
 
 
 def col_kernel(where_ref, m_ref, w_ref, *refs):
@@ -376,9 +376,9 @@
     start_all(copies)
     wait_all(copies)
     out_s[...] = (ulow_s[...].astype(F32) + dot(att_s[...], wo_s[...])).astype(BF16)
-    me = where_ref[0] * 2 + where_ref[1]
     for shift in range(8):
-        start = lax.rem(me + shift, 8) * 16
+        y, low = (where_ref[0] + shift % 4) % 4, (where_ref[1] + shift // 4) % 2
+        start = (y * 2 + low) * 16
         for cc in range(2):
             for rr in range(2):
                 at = pl.multiple_of(start + (cc * LINE + rr * 128), 16)
@@ -409,7 +409,8 @@
 def lines_to_tile_kernel(where_ref, *refs):
     parts, tile_ref = refs[:8], refs[8]
     row = positions()
-    shift = (where_ref[0] * 2 + where_ref[1] + 8 - row % 8) % 8
+    y, low = (row // 2) % 4, row % 2
+    shift = (where_ref[1] + 2 - low) % 2 * 4 + (where_ref[0] + 4 - y) % 4
     order = picked(((shift * 2 + (row // 8) % 2) * 2 + (row // 16) % 2) * 16 + row // 32)
     lines = jnp.concatenate([part[...].reshape(64, D) for part in parts], axis=0)
     tile_ref[...] = dot(order, lines).astype(BF16).reshape(32, 16, D)
@@ -423,11 +424,11 @@
 
 def join_kernel(where_ref, *refs):
     parts, passed_ref, tile_ref = refs[:8], refs[8], refs[9]
-    chip, core = where_ref[2] * 4 + where_ref[3], where_ref[4]
-    for shift in range(8):
-        source = lax.rem(chip + (8 - shift), 8)
-        tile_ref[source, core] = parts[shift][core]
-        tile_ref[source, 1 - core] = passed_ref[shift]
+    core = where_ref[4]
+    for place in range(8):
+        high, x = (where_ref[2] + place // 4) % 2, (where_ref[3] + 4 - place % 4) % 4
+        tile_ref[high * 4 + x, core] = parts[place][core]
+        tile_ref[high * 4 + x, 1 - core] = passed_ref[place]
 
 
 def pair_sum_kernel(where_ref, keep_ref, got_ref, *refs):
@@ -619,7 +620,7 @@
     ],
     2 * MATMUL,
     6 * MIB,
-    grant=54,
+    grant=50,
 )
 col_output = call(
     col_output_kernel,
@@ -668,11 +669,25 @@
     return lax.all_to_all(values, axes, split_axis=0, concat_axis=0, tiled=True)
 
 
-def shifted(pieces, axes):
+def shifted(pieces, axis):
     n = len(pieces)
     return [pieces[0]] + [
-        lax.ppermute(pieces[k], axes, [(i, (i + k) % n) for i in range(n)]) for k in range(1, n)
+        lax.ppermute(pieces[k], axis, [(i, (i + k) % n) for i in range(n)]) for k in range(1, n)
     ]
+
+
+def moved(pieces, axes, sizes, long_axis):
+    peers = []
+    for place in range(1, 8):
+        steps = (place % 4, place // 4) if long_axis == 0 else (place // 4, place % 4)
+        peers.append(
+            [
+                (i * sizes[1] + j, (i + steps[0]) % sizes[0] * sizes[1] + (j + steps[1]) % sizes[1])
+                for i in range(sizes[0])
+                for j in range(sizes[1])
+            ]
+        )
+    return [pieces[0]] + [lax.ppermute(pieces[k + 1], axes, peers[k]) for k in range(7)]
 
 
 def swap(value, axis):
@@ -708,12 +723,12 @@
     totals = spread(both)
     chunks = exchange(totals, CHIPS)
     gin_pieces = row_input_gradient(where, rows_in, right_row, w_row)
-    gin_parts = shifted(gin_pieces, ("zh", "x"))
+    gin_parts = moved(gin_pieces, ("zh", "x"), (2, 4), 1)
     gin_core = pass_core(where, *gin_parts)
     gin_core = swap(gin_core, "c")
     grad_latents = join(where, *gin_parts, gin_core).reshape(32, 16, D)
     out_pieces = col_output(where, saved_col, w_col)
-    out_parts = shifted(out_pieces, ROW)
+    out_parts = moved(out_pieces, ROW, (4, 2), 0)
     output = lines_to_tile(where, *out_parts)
     other = swap(chunks, "c")
     halves_done = widen(where, chunks, 0)

time: 239 us -> 238 us (level)
  starting transfers between devices: 56.6 us -> 59.3 us
  waiting for transfers between devices: 52.4 us -> 49.7 us
    ppermute x20, starting transfers between devices: 22.1 us -> 25.6 us  [the longest x14 17.4 us: moved(): lax.ppermute(pieces[k + 1], axes, peers[k])]
    ppermute x20, waiting for transfers between devices: 33.9 us -> 31 us  [the longest x6 18 us: shifted(): lax.ppermute(pieces[k], axis, [(i, (i + k) % n) for i in range(n)])]
    unnamed x22 -> x20, local copies, waits for them, and re-layouts: 4.37 us -> 5.35 us
  transfers between devices with their start and end apart: 28 -> 28, of which waited for: 16 -> 15; matrix products, arithmetic and copies ran while one was open for 0% -> 0% of each run, Pallas kernels for 16% -> 15%
where the time goes in v8:
time: 238 us; the launch traced here: 235 us
  Pallas kernels  60.1 us (25%)
  starting transfers between devices  59.3 us (25%)
  blocking collectives  58.5 us (25%)
  waiting for transfers between devices  49.7 us (21%)
  local copies, waits for them, and re-layouts  6.2 us (3%)
    all_to_all x2, blocking collectives, exchange(): return lax.all_to_all(values, axes, split_axis=0, concat_axis=0, tiled=True)  58.5 us
    all_to_all x3, starting transfers between devices, exchange(): return lax.all_to_all(values, axes, split_axis=0, concat_axis=0, tiled=True)  24 us
    ppermute x6, waiting for transfers between devices, shifted(): lax.ppermute(pieces[k], axis, [(i, (i + k) % n) for i in range(n)])  18 us
    ppermute x14, starting transfers between devices, moved(): lax.ppermute(pieces[k + 1], axes, peers[k])  17.4 us
    ppermute x14, waiting for transfers between devices, moved(): lax.ppermute(pieces[k + 1], axes, peers[k])  13 us
    all_to_all x3, waiting for transfers between devices, exchange(): return lax.all_to_all(values, axes, split_axis=0, concat_axis=0, tiled=True)  12.8 us
    pallas_call x1, Pallas kernels, layer(): col_grad(where, mid_lines, w_col, *grad_parts, grad_pass)  11.4 us
    ppermute x5, starting transfers between devices, swap(): return lax.ppermute(value, axis, [(0, 1), (1, 0)])  9.64 us
  transfers between devices with their start and end apart: 28, of which 15 were waited for; matrix products, arithmetic and copies ran while one was open for 0% of the time, Pallas kernels for 15%

profile of v8, /device:TPU:1, one launch (start us, length us, event | category | flops | bytes accessed | tf_op | source)
XLA Modules:
  0.0 234.8 jit_solution(3560468012759036194)
XLA Ops:
  0.6 9.1 %all-to-all-start = ((bf16[16,2,16,512]{3,2,1,0:T(8,128)(2,1)}), bf16[16,2,16,512]{3,2,1,0:T(8,128)(2,1)S(1)}, u32[]{:S(2)}, u32[]{:S(2)}) async-start(bf16[16,2,16,512]{3,2,1,0:T(8,128)(2,1)} %bitcast.12), calls=%async_computation | async-start | bytes 1048576 | tf_op jit(solution)/shard_map/all_to_all | solution.py:669
  9.8 0.8 reshape.23
  10.6 10.1 %all-to-all-done.x_ref = bf16[16,2,16,512]{3,2,1,0:T(8,128)(2,1)S(1)} async-done(((bf16[16,2,16,512]{3,2,1,0:T(8,128)(2,1)}), bf16[16,2,16,512]{3,2,1,0:T(8,128)(2,1)S(1)}, u32[]{:S(2)}, u32[]{:S(2)}) %all-to-all-start) | async-done | bytes 524320 | tf_op jit(solution)/shard_map/all_to_all | solution.py:669
  20.8 7.9 %shard_map.84 = (bf16[128,4,512]{2,1,0:T(4,128)(2,1)S(1)}, bf16[5,512,512]{2,1,0:T(8,128)(2,1)}) custom-call(s32[21]{0:T(128)S(1)} %concatenate.3.where_ref, bf16[16,2,16,512]{3,2,1,0:T(8,128)(2,1)S(1)} %all-to-all-done.x_ref, bf16[4,512,512]{2,1,0:T(8,128)(2,1)} %w_ref.9), custom_call_target="tpu_custom_call" | custom-call | flops 1342177280 | bytes 6291456 | tf_op jit(solution)/shard_map/pallas_call | solution.py:706
  28.7 0.8 copy-done.9
  29.5 6.4 %all-to-all-start.1 = ((bf16[128,4,512]{2,1,0:T(4,128)(2,1)}), bf16[128,4,512]{2,1,0:T(4,128)(2,1)}, u32[]{:S(2)}, u32[]{:S(2)}) async-start(bf16[128,4,512]{2,1,0:T(4,128)(2,1)} %copy-done.9), calls=%async_computation.1 | async-start | bytes 1048576 | tf_op jit(solution)/shard_map/all_to_all | solution.py:669
  35.9 1.2 shard_map.85
  37.2 1.4 collective-permute-start
  38.6 2.5 %collective-permute-start.1 = (bf16[2,2,32,512]{3,2,1,0:T(8,128)(2,1)S(1)}, bf16[2,2,32,512]{3,2,1,0:T(8,128)(2,1)S(1)}, u32[]{:S(2)}, u32[]{:S(2)}) collective-permute-start(bf16[2,2,32,512]{3,2,1,0:T(8,128)(2,1)S(1)} %get-tuple-element.45), channel_id=1, source_target_pairs={{0,64},{32,96},{64,0},{96,32},{1,65},{33,97},{65,1},{97,33},{2,66}... | collective-permute-start | bytes 393224 | tf_op jit(solution)/shard_map/ppermute | solution.py:675
  41.0 1.1 collective-permute-start.2
  42.2 5.2 %collective-permute-done.refs_1_ = bf16[2,2,32,512]{3,2,1,0:T(8,128)(2,1)S(1)} collective-permute-done((bf16[2,2,32,512]{3,2,1,0:T(8,128)(2,1)S(1)}, bf16[2,2,32,512]{3,2,1,0:T(8,128)(2,1)S(1)}, u32[]{:S(2)}, u32[]{:S(2)}) %collective-permute-start) | collective-permute-done | bytes 131104 | tf_op jit(solution)/shard_map/ppermute | solution.py:675
  47.4 3.5 %collective-permute-done.1.refs_2_ = bf16[2,2,32,512]{3,2,1,0:T(8,128)(2,1)S(1)} collective-permute-done((bf16[2,2,32,512]{3,2,1,0:T(8,128)(2,1)S(1)}, bf16[2,2,32,512]{3,2,1,0:T(8,128)(2,1)S(1)}, u32[]{:S(2)}, u32[]{:S(2)}) %collective-permute-start.1) | collective-permute-done | bytes 131104 | tf_op jit(solution)/shard_map/ppermute | solution.py:675
  50.9 0.6 shard_map.86
  51.5 1.7 collective-permute-start.3
  53.2 5.9 %collective-permute-done.3.refs_4_ = bf16[4,2,32,512]{3,2,1,0:T(8,128)(2,1)S(1)} collective-permute-done((bf16[4,2,32,512]{3,2,1,0:T(8,128)(2,1)S(1)}, bf16[4,2,32,512]{3,2,1,0:T(8,128)(2,1)S(1)}, u32[]{:S(2)}, u32[]{:S(2)}) %collective-permute-start.3) | collective-permute-done | bytes 262176 | tf_op jit(solution)/shard_map/ppermute | solution.py:694
  59.1 11.4 %shard_map.87 = (bf16[128,4,512]{2,1,0:T(4,128)(2,1)}, bf16[7,512,512]{2,1,0:T(8,128)(2,1)}) custom-call(s32[21]{0:T(128)S(1)} %concatenate.3.where_ref, bf16[128,4,512]{2,1,0:T(4,128)(2,1)} %all-to-all-done.1.m_ref, bf16[4,512,512]{2,1,0:T(8,128)(2,1)S(1)} %copy-done.4, bf16[2,2,32,512]{3,2,1,0:T(8,128)(2,1)S(1)} %get-tuple-element.43.refs_0_, ...), custom_call_target="tpu_custom_call" | custom-call | flops 2952790016 | bytes 8388608 | tf_op jit(solution)/shard_map/pallas_call | solution.py:709
  70.5 8.4 %all-to-all-start.2 = ((bf16[128,4,512]{2,1,0:T(4,128)(2,1)}), bf16[128,4,512]{2,1,0:T(4,128)(2,1)}, u32[]{:S(2)}, u32[]{:S(2)}) async-start(bf16[128,4,512]{2,1,0:T(4,128)(2,1)} %get-tuple-element.56), calls=%async_computation.2 | async-start | bytes 1048576 | tf_op jit(solution)/shard_map/all_to_all | solution.py:669
  79.0 3.1 %shard_map.96 = (bf16[2,512,512]{2,1,0:T(8,128)(2,1)S(1)}, bf16[2,512,512]{2,1,0:T(8,128)(2,1)S(1)}) custom-call(s32[21]{0:T(128)S(1)} %concatenate.3.where_ref, bf16[7,512,512]{2,1,0:T(8,128)(2,1)} %get-tuple-element.47.saved_ref.right_ref), custom_call_target="tpu_custom_call" | custom-call | flops 536870912 | bytes 6291456 | tf_op jit(solution)/shard_map/pallas_call | solution.py:713
  82.1 1.0 copy-done.6
  83.1 1.1 collective-permute-start.20
  84.3 2.4 %shard_map.90 = (bf16[8,512,256]{2,1,0:T(8,128)(2,1)S(1)}, bf16[2,512,512]{2,1,0:T(8,128)(2,1)S(1)}) custom-call(bf16[5,512,512]{2,1,0:T(8,128)(2,1)S(1)} %copy-done), custom_call_target="tpu_custom_call" | custom-call | flops 134217728 | bytes 8388608 | tf_op jit(solution)/shard_map/pallas_call | solution.py:708
  86.7 1.0 copy-done.1
  87.7 1.3 copy-done.5
  89.1 2.6 %all-to-all-done.2.g_ref = bf16[128,4,512]{2,1,0:T(4,128)(2,1)} async-done(((bf16[128,4,512]{2,1,0:T(4,128)(2,1)}), bf16[128,4,512]{2,1,0:T(4,128)(2,1)}, u32[]{:S(2)}, u32[]{:S(2)}) %all-to-all-start.2) | async-done | bytes 524320 | tf_op jit(solution)/shard_map/all_to_all | solution.py:669
  91.7 1.2 copy-done.2
  92.9 8.7 %shard_map.91 = (bf16[2,512,512]{2,1,0:T(8,128)(2,1)S(1)}, bf16[4,512,512]{2,1,0:T(8,128)(2,1)}) custom-call(s32[21]{0:T(128)S(1)} %concatenate.3.where_ref, bf16[128,4,512]{2,1,0:T(4,128)(2,1)} %all-to-all-done.2.g_ref, bf16[5,512,512]{2,1,0:T(8,128)(2,1)} %get-tuple-element.57.saved_ref.qkv_ref, bf16[2,512,512]{2,1,0:T(8,128)(2,1)S(1)} %copy-done.2, ...), custom_call_target="tpu_custom_call" | custom-call | flops 2013265920 | bytes 12582912 | tf_op jit(solution)/shard_map/pallas_call | solution.py:718
  101.6 1.7 collective-permute-start.19
  103.3 2.6 %shard_map.97.keep_ref = bf16[2,512,512]{2,1,0:T(8,128)(2,1)S(1)} custom-call(s32[21]{0:T(128)S(1)} %concatenate.3.where_ref, bf16[2,512,512]{2,1,0:T(8,128)(2,1)S(1)} %copy-done.7, bf16[7,512,512]{2,1,0:T(8,128)(2,1)} %get-tuple-element.47.saved_ref.right_ref), custom_call_target="tpu_custom_call" | custom-call | flops 536870912 | bytes 3145728 | tf_op jit(solution)/shard_map/pallas_call | solution.py:715
  105.9 1.9 shard_map.98
  108.2 1.9 collective-permute-start.22
  110.1 0.9 collective-permute-start.23
  111.0 2.6 %shard_map.95.keep_ref = bf16[2,512,512]{2,1,0:T(8,128)(2,1)S(1)} custom-call(s32[21]{0:T(128)S(1)} %concatenate.3.where_ref, bf16[2,512,512]{2,1,0:T(8,128)(2,1)S(1)} %copy-done.3, bf16[4,512,512]{2,1,0:T(8,128)(2,1)} %get-tuple-element.60.right_ref), custom_call_target="tpu_custom_call" | custom-call | flops 536870912 | bytes 3145728 | tf_op jit(solution)/shard_map/pallas_call | solution.py:720
  113.6 3.9 %collective-permute-done.21.refs_1_ = bf16[256,512]{1,0:T(8,128)(2,1)S(1)} collective-permute-done((bf16[256,512]{1,0:T(8,128)(2,1)S(1)}, bf16[256,512]{1,0:T(8,128)(2,1)S(1)}, u32[]{:S(2)}, u32[]{:S(2)}) %collective-permute-start.21) | collective-permute-done | bytes 262176 | tf_op jit(solution)/shard_map/ppermute | solution.py:675
  117.5 4.7 %collective-permute-done.22.refs_2_ = bf16[256,512]{1,0:T(8,128)(2,1)S(1)} collective-permute-done((bf16[256,512]{1,0:T(8,128)(2,1)S(1)}, bf16[256,512]{1,0:T(8,128)(2,1)S(1)}, u32[]{:S(2)}, u32[]{:S(2)}) %collective-permute-start.22) | collective-permute-done | bytes 262176 | tf_op jit(solution)/shard_map/ppermute | solution.py:675
  122.2 0.8 collective-permute-done.23.refs_3_
  122.9 0.4 shard_map.99
  123.4 26.0 %all_to_all.25.both_ref = bf16[64,80,128]{2,1,0:T(8,128)(2,1)S(1)} all-to-all(bf16[64,80,128]{2,1,0:T(8,128)(2,1)S(1)} %shard_map.99), channel_id=1, replica_groups=mesh['y'=4,'zl'=2,'zh'=2,'x'=4,'c'=2] {'y','zl','zh','x'}, dimensions={0} | all-to-all | bytes 2621440 | tf_op jit(solution)/shard_map/all_to_all | solution.py:669
  149.4 1.7 shard_map.100
  151.1 32.5 %all_to_all.26.chunks_ref = bf16[64,128,128]{2,1,0:T(8,128)(2,1)S(1)} all-to-all(bf16[64,128,128]{2,1,0:T(8,128)(2,1)} %shard_map.100), channel_id=1, replica_groups=mesh['y'=4,'zl'=2,'zh'=2,'x'=4,'c'=2] {'y','zl','zh','x'}, dimensions={0} | all-to-all | bytes 4194304 | tf_op jit(solution)/shard_map/all_to_all | solution.py:669
  183.6 3.3 %collective-permute-start.24 = (bf16[64,128,128]{2,1,0:T(8,128)(2,1)S(1)}, bf16[64,128,128]{2,1,0:T(8,128)(2,1)S(1)}, u32[]{:S(2)}, u32[]{:S(2)}) collective-permute-start(bf16[64,128,128]{2,1,0:T(8,128)(2,1)S(1)} %all_to_all.26.chunks_ref), channel_id=1, source_target_pairs={{0,1},{1,0},{2,3},{3,2},{4,5},{5,4},{6,7},{7,6},{8,9},{9,8},{10,11... | collective-permute-start | bytes 6291464 | tf_op jit(solution)/shard_map/ppermute | solution.py:694
  186.9 3.8 %shard_map.92 = (bf16[2,2,16,512]{3,2,1,0:T(8,128)(2,1)S(1)}, bf16[2,2,16,512]{3,2,1,0:T(8,128)(2,1)S(1)}, bf16[2,2,16,512]{3,2,1,0:T(8,128)(2,1)S(1)}, bf16[2,2...) custom-call(s32[21]{0:T(128)S(1)} %concatenate.3.where_ref, ...), custom_call_target="tpu_custom_call" | custom-call | flops 805306368 | bytes 5242880 | tf_op jit(solution)/shard_map/pallas_call | solution.py:725
  190.8 2.2 collective-permute-start.12
  193.0 1.2 collective-permute-start.13
  194.2 0.6 collective-permute-start.14
  194.8 1.3 collective-permute-done.11.refs_1_
  196.1 1.0 collective-permute-start.15
  197.1 1.9 collective-permute-start.16
  199.0 3.9 %collective-permute-start.17 = (bf16[2,2,16,512]{3,2,1,0:T(8,128)(2,1)S(1)}, bf16[2,2,16,512]{3,2,1,0:T(8,128)(2,1)S(1)}, u32[]{:S(2)}, u32[]{:S(2)}) collective-permute-start(bf16[2,2,16,512]{3,2,1,0:T(8,128)(2,1)S(1)} %get-tuple-element.68), channel_id=1, source_target_pairs={{0,14},{2,8},{4,10},{6,12},{8,6},{10,0},{12,2},{14,4},{1,15},{3,9}... | collective-permute-start | bytes 196616 | tf_op jit(solution)/shard_map/ppermute | solution.py:690
  203.0 1.1 collective-permute-done.16.refs_6_
  204.1 2.6 %collective-permute-done.17.refs_7_ = bf16[2,2,16,512]{3,2,1,0:T(8,128)(2,1)S(1)} collective-permute-done((bf16[2,2,16,512]{3,2,1,0:T(8,128)(2,1)S(1)}, bf16[2,2,16,512]{3,2,1,0:T(8,128)(2,1)S(1)}, u32[]{:S(2)}, u32[]{:S(2)}) %collective-permute-start.17) | collective-permute-done | bytes 65568 | tf_op jit(solution)/shard_map/ppermute | solution.py:690
  206.7 0.6 shard_map.93
  207.3 1.7 collective-permute-start.18
  209.0 2.4 %shard_map.88 = (bf16[2,32,512]{2,1,0:T(8,128)(2,1)S(1)}, bf16[2,32,512]{2,1,0:T(8,128)(2,1)S(1)}, bf16[2,32,512]{2,1,0:T(8,128)(2,1)S(1)}, bf16[2,32,512]{2,1,0...) custom-call(s32[21]{0:T(128)S(1)} %concatenate.3.where_ref, ...), custom_call_target="tpu_custom_call" | custom-call | flops 268435456 | bytes 3145728 | tf_op jit(solution)/shard_map/pallas_call | solution.py:730
  211.5 1.6 collective-permute-start.5
  213.1 1.0 collective-permute-start.6
  214.2 3.6 %collective-permute-done.4.refs_1_ = bf16[2,32,512]{2,1,0:T(8,128)(2,1)S(1)} collective-permute-done((bf16[2,32,512]{2,1,0:T(8,128)(2,1)S(1)}, bf16[2,32,512]{2,1,0:T(8,128)(2,1)S(1)}, u32[]{:S(2)}, u32[]{:S(2)}) %collective-permute-start.4) | collective-permute-done | bytes 65568 | tf_op jit(solution)/shard_map/ppermute | solution.py:690
  218.0 2.9 %collective-permute-start.9 = (bf16[2,32,512]{2,1,0:T(8,128)(2,1)S(1)}, bf16[2,32,512]{2,1,0:T(8,128)(2,1)S(1)}, u32[]{:S(2)}, u32[]{:S(2)}) collective-permute-start(bf16[2,32,512]{2,1,0:T(8,128)(2,1)S(1)} %get-tuple-element.54), channel_id=1, source_target_pairs={{0,80},{16,64},{32,112},{48,96},{64,16},{80,0},{96,48},{112,32},{1... | collective-permute-start | bytes 196616 | tf_op jit(solution)/shard_map/ppermute | solution.py:690
  221.0 0.6 collective-permute-start.10
  221.6 2.3 collective-permute-done.8.refs_5_
  223.9 2.0 collective-permute-done.10.refs_7_
  225.9 2.0 shard_map.89
  227.9 1.4 shard_map.94
  229.2 2.7 %widen.2 = (f32[2,1024,512]{2,1,0:T(8,128)}, f32[2,4,256,512]{3,2,1,0:T(8,128)}) custom-call(s32[21]{0:T(128)S(1)} %concatenate.3.where_ref, bf16[64,128,128]{2,1,0:T(8,128)(2,1)S(1)} %all_to_all.26.chunks_ref), custom_call_target="tpu_custom_call" | custom-call | bytes 6291456 | tf_op jit(solution)/shard_map/widen/pallas_call | solution.py:653
  231.9 2.7 %widen.3 = (f32[2,1024,512]{2,1,0:T(8,128)}, f32[2,4,256,512]{3,2,1,0:T(8,128)}) custom-call(s32[21]{0:T(128)S(1)} %concatenate.3.where_ref, bf16[64,128,128]{2,1,0:T(8,128)(2,1)S(1)} %collective-permute-done.24.chunks_ref, f32[2,1024,512]{2,1,0:T(8,128)} %get-tuple-element.76.refs_0_, ...), custom_call_target="tpu_custom_call", output_to_operand_aliasing={{0}: (2, {}), {1}: (3, {})} | custom-call | bytes 6291456 | tf_op jit(solution)/shard_map/widen/pallas_call | solution.py:653
  (35 shorter events, 1.0 us)
Async XLA Ops:
  0.6 20.1 %all-to-all-start = ((bf16[16,2,16,512]{3,2,1,0:T(8,128)(2,1)}), bf16[16,2,16,512]{3,2,1,0:T(8,128)(2,1)S(1)}, u32[]{:S(2)}, u32[]{:S(2)}) async-start(bf16[16,2,16,512]{3,2,1,0:T(8,128)(2,1)} %bitcast.12), calls=%async_computation | async-start | bytes 1048576 | tf_op jit(solution)/shard_map/all_to_all | solution.py:669
  10.6 25.3 %copy-start.8 = (bf16[32,16,512]{2,1,0:T(8,128)(2,1)S(1)}, bf16[32,16,512]{2,1,0:T(8,128)(2,1)}, u32[]{:S(2)}) copy-start(bf16[32,16,512]{2,1,0:T(8,128)(2,1)} %tile_ref.1) | copy-start | bytes 1572868
  28.7 0.8 copy-start.9
  29.5 29.6 %copy-start.4 = (bf16[4,512,512]{2,1,0:T(8,128)(2,1)S(1)}, bf16[4,512,512]{2,1,0:T(8,128)(2,1)}, u32[]{:S(2)}) copy-start(bf16[4,512,512]{2,1,0:T(8,128)(2,1)} %w_ref.7) | copy-start | bytes 6291460
  29.5 29.6 %all-to-all-start.1 = ((bf16[128,4,512]{2,1,0:T(4,128)(2,1)}), bf16[128,4,512]{2,1,0:T(4,128)(2,1)}, u32[]{:S(2)}, u32[]{:S(2)}) async-start(bf16[128,4,512]{2,1,0:T(4,128)(2,1)} %copy-done.9), calls=%async_computation.1 | async-start | bytes 1048576 | tf_op jit(solution)/shard_map/all_to_all | solution.py:669
  37.2 10.2 %collective-permute-start = (bf16[2,2,32,512]{3,2,1,0:T(8,128)(2,1)S(1)}, bf16[2,2,32,512]{3,2,1,0:T(8,128)(2,1)S(1)}, u32[]{:S(2)}, u32[]{:S(2)}) collective-permute-start(bf16[2,2,32,512]{3,2,1,0:T(8,128)(2,1)S(1)} %get-tuple-element.44), channel_id=1, source_target_pairs={{0,32},{32,64},{64,96},{96,0},{1,33},{33,65},{65,97},{97,1},{2,34}... | collective-permute-start | bytes 393224 | tf_op jit(solution)/shard_map/ppermute | solution.py:675
  38.6 12.3 %collective-permute-start.1 = (bf16[2,2,32,512]{3,2,1,0:T(8,128)(2,1)S(1)}, bf16[2,2,32,512]{3,2,1,0:T(8,128)(2,1)S(1)}, u32[]{:S(2)}, u32[]{:S(2)}) collective-permute-start(bf16[2,2,32,512]{3,2,1,0:T(8,128)(2,1)S(1)} %get-tuple-element.45), channel_id=1, source_target_pairs={{0,64},{32,96},{64,0},{96,32},{1,65},{33,97},{65,1},{97,33},{2,66}... | collective-permute-start | bytes 393224 | tf_op jit(solution)/shard_map/ppermute | solution.py:675
  41.0 9.8 %collective-permute-start.2 = (bf16[2,2,32,512]{3,2,1,0:T(8,128)(2,1)S(1)}, bf16[2,2,32,512]{3,2,1,0:T(8,128)(2,1)S(1)}, u32[]{:S(2)}, u32[]{:S(2)}) collective-permute-start(bf16[2,2,32,512]{3,2,1,0:T(8,128)(2,1)S(1)} %get-tuple-element.46), channel_id=1, source_target_pairs={{0,96},{32,0},{64,32},{96,64},{1,97},{33,1},{65,33},{97,65},{2,98}... | collective-permute-start | bytes 393224 | tf_op jit(solution)/shard_map/ppermute | solution.py:675
  51.5 7.6 %collective-permute-start.3 = (bf16[4,2,32,512]{3,2,1,0:T(8,128)(2,1)S(1)}, bf16[4,2,32,512]{3,2,1,0:T(8,128)(2,1)S(1)}, u32[]{:S(2)}, u32[]{:S(2)}) collective-permute-start(bf16[4,2,32,512]{3,2,1,0:T(8,128)(2,1)S(1)} %shard_map.86), channel_id=1, source_target_pairs={{0,16},{16,0},{1,17},{17,1},{2,18},{18,2},{3,19},{19,3},{4,20},{20... | collective-permute-start | bytes 786440 | tf_op jit(solution)/shard_map/ppermute | solution.py:694
  70.5 21.1 %all-to-all-start.2 = ((bf16[128,4,512]{2,1,0:T(4,128)(2,1)}), bf16[128,4,512]{2,1,0:T(4,128)(2,1)}, u32[]{:S(2)}, u32[]{:S(2)}) async-start(bf16[128,4,512]{2,1,0:T(4,128)(2,1)} %get-tuple-element.56), calls=%async_computation.2 | async-start | bytes 1048576 | tf_op jit(solution)/shard_map/all_to_all | solution.py:669
  79.0 5.3 %copy-start = (bf16[5,512,512]{2,1,0:T(8,128)(2,1)S(1)}, bf16[5,512,512]{2,1,0:T(8,128)(2,1)}, u32[]{:S(2)}) copy-start(bf16[5,512,512]{2,1,0:T(8,128)(2,1)} %get-tuple-element.57.saved_ref.qkv_ref) | copy-start | bytes 7864324
  82.1 1.0 copy-start.6
  83.1 22.8 %collective-permute-start.20 = (bf16[2,512,512]{2,1,0:T(8,128)(2,1)S(1)}, bf16[2,512,512]{2,1,0:T(8,128)(2,1)}, u32[]{:S(2)}, u32[]{:S(2)}) collective-permute-start(bf16[2,512,512]{2,1,0:T(8,128)(2,1)S(1)} %get-tuple-element.71), channel_id=1, source_target_pairs={{0,1},{1,0},{2,3},{3,2},{4,5},{5,4},{6,7},{7,6},{8,9},{9,8},{10,11... | collective-permute-start | bytes 3145736 | tf_op jit(solution)/shard_map/ppermute | solution.py:694
  86.7 1.0 copy-start.1
  87.7 1.3 copy-start.5
  91.7 1.2 copy-start.2
  92.9 10.4 %copy-start.7 = (bf16[2,512,512]{2,1,0:T(8,128)(2,1)S(1)}, bf16[2,512,512]{2,1,0:T(8,128)(2,1)}, u32[]{:S(2)}) copy-start(bf16[2,512,512]{2,1,0:T(8,128)(2,1)} %copy-done.6) | copy-start | bytes 3145732
  101.6 21.4 %collective-permute-start.19 = (bf16[2,512,512]{2,1,0:T(8,128)(2,1)S(1)}, bf16[2,512,512]{2,1,0:T(8,128)(2,1)S(1)}, u32[]{:S(2)}, u32[]{:S(2)}) collective-permute-start(bf16[2,512,512]{2,1,0:T(8,128)(2,1)S(1)} %get-tuple-element.69), channel_id=1, source_target_pairs={{0,1},{1,0},{2,3},{3,2},{4,5},{5,4},{6,7},{7,6},{8,9},{9,8},{10,11... | collective-permute-start | bytes 3145736 | tf_op jit(solution)/shard_map/ppermute | solution.py:694
  105.9 5.1 %copy-start.3 = (bf16[2,512,512]{2,1,0:T(8,128)(2,1)S(1)}, bf16[2,512,512]{2,1,0:T(8,128)(2,1)}, u32[]{:S(2)}) copy-start(bf16[2,512,512]{2,1,0:T(8,128)(2,1)} %copy-done.1) | copy-start | bytes 3145732
  107.9 9.6 %collective-permute-start.21 = (bf16[256,512]{1,0:T(8,128)(2,1)S(1)}, bf16[256,512]{1,0:T(8,128)(2,1)S(1)}, u32[]{:S(2)}, u32[]{:S(2)}) collective-permute-start(bf16[256,512]{1,0:T(8,128)(2,1)S(1)} %get-tuple-element.73), channel_id=1, source_target_pairs={{0,2},{2,4},{4,6},{6,0},{1,3},{3,5},{5,7},{7,1},{8,10},{10,12},{12... | collective-permute-start | bytes 786440 | tf_op jit(solution)/shard_map/ppermute | solution.py:675
  108.2 13.9 %collective-permute-start.22 = (bf16[256,512]{1,0:T(8,128)(2,1)S(1)}, bf16[256,512]{1,0:T(8,128)(2,1)S(1)}, u32[]{:S(2)}, u32[]{:S(2)}) collective-permute-start(bf16[256,512]{1,0:T(8,128)(2,1)S(1)} %get-tuple-element.74), channel_id=1, source_target_pairs={{0,4},{2,6},{4,0},{6,2},{1,5},{3,7},{5,1},{7,3},{8,12},{10,14},{12... | collective-permute-start | bytes 786440 | tf_op jit(solution)/shard_map/ppermute | solution.py:675
  110.1 12.8 %collective-permute-start.23 = (bf16[256,512]{1,0:T(8,128)(2,1)S(1)}, bf16[256,512]{1,0:T(8,128)(2,1)S(1)}, u32[]{:S(2)}, u32[]{:S(2)}) collective-permute-start(bf16[256,512]{1,0:T(8,128)(2,1)S(1)} %get-tuple-element.75), channel_id=1, source_target_pairs={{0,6},{2,0},{4,2},{6,4},{1,7},{3,1},{5,3},{7,5},{8,14},{10,8},{12,... | collective-permute-start | bytes 786440 | tf_op jit(solution)/shard_map/ppermute | solution.py:675
  183.6 48.3 %collective-permute-start.24 = (bf16[64,128,128]{2,1,0:T(8,128)(2,1)S(1)}, bf16[64,128,128]{2,1,0:T(8,128)(2,1)S(1)}, u32[]{:S(2)}, u32[]{:S(2)}) collective-permute-start(bf16[64,128,128]{2,1,0:T(8,128)(2,1)S(1)} %all_to_all.26.chunks_ref), channel_id=1, source_target_pairs={{0,1},{1,0},{2,3},{3,2},{4,5},{5,4},{6,7},{7,6},{8,9},{9,8},{10,11... | collective-permute-start | bytes 6291464 | tf_op jit(solution)/shard_map/ppermute | solution.py:694
  190.7 5.4 %collective-permute-start.11 = (bf16[2,2,16,512]{3,2,1,0:T(8,128)(2,1)S(1)}, bf16[2,2,16,512]{3,2,1,0:T(8,128)(2,1)S(1)}, u32[]{:S(2)}, u32[]{:S(2)}) collective-permute-start(bf16[2,2,16,512]{3,2,1,0:T(8,128)(2,1)S(1)} %get-tuple-element.62), channel_id=1, source_target_pairs={{0,2},{2,4},{4,6},{6,0},{8,10},{10,12},{12,14},{14,8},{1,3},{3,5},... | collective-permute-start | bytes 196616 | tf_op jit(solution)/shard_map/ppermute | solution.py:690
  190.8 6.3 %collective-permute-start.12 = (bf16[2,2,16,512]{3,2,1,0:T(8,128)(2,1)S(1)}, bf16[2,2,16,512]{3,2,1,0:T(8,128)(2,1)S(1)}, u32[]{:S(2)}, u32[]{:S(2)}) collective-permute-start(bf16[2,2,16,512]{3,2,1,0:T(8,128)(2,1)S(1)} %get-tuple-element.63), channel_id=1, source_target_pairs={{0,4},{2,6},{4,0},{6,2},{8,12},{10,14},{12,8},{14,10},{1,5},{3,7},... | collective-permute-start | bytes 196616 | tf_op jit(solution)/shard_map/ppermute | solution.py:690
  193.0 6.1 %collective-permute-start.13 = (bf16[2,2,16,512]{3,2,1,0:T(8,128)(2,1)S(1)}, bf16[2,2,16,512]{3,2,1,0:T(8,128)(2,1)S(1)}, u32[]{:S(2)}, u32[]{:S(2)}) collective-permute-start(bf16[2,2,16,512]{3,2,1,0:T(8,128)(2,1)S(1)} %get-tuple-element.64), channel_id=1, source_target_pairs={{0,6},{2,0},{4,2},{6,4},{8,14},{10,8},{12,10},{14,12},{1,7},{3,1},... | collective-permute-start | bytes 196616 | tf_op jit(solution)/shard_map/ppermute | solution.py:690
  194.2 8.8 %collective-permute-start.14 = (bf16[2,2,16,512]{3,2,1,0:T(8,128)(2,1)S(1)}, bf16[2,2,16,512]{3,2,1,0:T(8,128)(2,1)S(1)}, u32[]{:S(2)}, u32[]{:S(2)}) collective-permute-start(bf16[2,2,16,512]{3,2,1,0:T(8,128)(2,1)S(1)} %get-tuple-element.65), channel_id=1, source_target_pairs={{0,8},{2,10},{4,12},{6,14},{8,0},{10,2},{12,4},{14,6},{1,9},{3,11}... | collective-permute-start | bytes 196616 | tf_op jit(solution)/shard_map/ppermute | solution.py:690
  196.1 6.9 %collective-permute-start.15 = (bf16[2,2,16,512]{3,2,1,0:T(8,128)(2,1)S(1)}, bf16[2,2,16,512]{3,2,1,0:T(8,128)(2,1)S(1)}, u32[]{:S(2)}, u32[]{:S(2)}) collective-permute-start(bf16[2,2,16,512]{3,2,1,0:T(8,128)(2,1)S(1)} %get-tuple-element.66), channel_id=1, source_target_pairs={{0,10},{2,12},{4,14},{6,8},{8,2},{10,4},{12,6},{14,0},{1,11},{3,13... | collective-permute-start | bytes 196616 | tf_op jit(solution)/shard_map/ppermute | solution.py:690
  197.1 7.0 %collective-permute-start.16 = (bf16[2,2,16,512]{3,2,1,0:T(8,128)(2,1)S(1)}, bf16[2,2,16,512]{3,2,1,0:T(8,128)(2,1)S(1)}, u32[]{:S(2)}, u32[]{:S(2)}) collective-permute-start(bf16[2,2,16,512]{3,2,1,0:T(8,128)(2,1)S(1)} %get-tuple-element.67), channel_id=1, source_target_pairs={{0,12},{2,14},{4,8},{6,10},{8,4},{10,6},{12,0},{14,2},{1,13},{3,15... | collective-permute-start | bytes 196616 | tf_op jit(solution)/shard_map/ppermute | solution.py:690
  199.0 7.7 %collective-permute-start.17 = (bf16[2,2,16,512]{3,2,1,0:T(8,128)(2,1)S(1)}, bf16[2,2,16,512]{3,2,1,0:T(8,128)(2,1)S(1)}, u32[]{:S(2)}, u32[]{:S(2)}) collective-permute-start(bf16[2,2,16,512]{3,2,1,0:T(8,128)(2,1)S(1)} %get-tuple-element.68), channel_id=1, source_target_pairs={{0,14},{2,8},{4,10},{6,12},{8,6},{10,0},{12,2},{14,4},{1,15},{3,9}... | collective-permute-start | bytes 196616 | tf_op jit(solution)/shard_map/ppermute | solution.py:690
  207.3 20.6 %collective-permute-start.18 = (bf16[8,2,16,512]{3,2,1,0:T(8,128)(2,1)S(1)}, bf16[8,2,16,512]{3,2,1,0:T(8,128)(2,1)S(1)}, u32[]{:S(2)}, u32[]{:S(2)}) collective-permute-start(bf16[8,2,16,512]{3,2,1,0:T(8,128)(2,1)S(1)} %shard_map.93), channel_id=1, source_target_pairs={{0,1},{1,0},{2,3},{3,2},{4,5},{5,4},{6,7},{7,6},{8,9},{9,8},{10,11... | collective-permute-start | bytes 786440 | tf_op jit(solution)/shard_map/ppermute | solution.py:694
  211.4 6.3 %collective-permute-start.4 = (bf16[2,32,512]{2,1,0:T(8,128)(2,1)S(1)}, bf16[2,32,512]{2,1,0:T(8,128)(2,1)S(1)}, u32[]{:S(2)}, u32[]{:S(2)}) collective-permute-start(bf16[2,32,512]{2,1,0:T(8,128)(2,1)S(1)} %get-tuple-element.49), channel_id=1, source_target_pairs={{0,32},{16,48},{32,64},{48,80},{64,96},{80,112},{96,0},{112,16},{1... | collective-permute-start | bytes 196616 | tf_op jit(solution)/shard_map/ppermute | solution.py:690
  211.5 6.4 %collective-permute-start.5 = (bf16[2,32,512]{2,1,0:T(8,128)(2,1)S(1)}, bf16[2,32,512]{2,1,0:T(8,128)(2,1)S(1)}, u32[]{:S(2)}, u32[]{:S(2)}) collective-permute-start(bf16[2,32,512]{2,1,0:T(8,128)(2,1)S(1)} %get-tuple-element.50), channel_id=1, source_target_pairs={{0,64},{16,80},{32,96},{48,112},{64,0},{80,16},{96,32},{112,48},{1... | collective-permute-start | bytes 196616 | tf_op jit(solution)/shard_map/ppermute | solution.py:690
  213.1 4.9 %collective-permute-start.6 = (bf16[2,32,512]{2,1,0:T(8,128)(2,1)S(1)}, bf16[2,32,512]{2,1,0:T(8,128)(2,1)S(1)}, u32[]{:S(2)}, u32[]{:S(2)}) collective-permute-start(bf16[2,32,512]{2,1,0:T(8,128)(2,1)S(1)} %get-tuple-element.51), channel_id=1, source_target_pairs={{0,96},{16,112},{32,0},{48,16},{64,32},{80,48},{96,64},{112,80},{1... | collective-permute-start | bytes 196616 | tf_op jit(solution)/shard_map/ppermute | solution.py:690
  217.8 3.2 %collective-permute-start.7 = (bf16[2,32,512]{2,1,0:T(8,128)(2,1)S(1)}, bf16[2,32,512]{2,1,0:T(8,128)(2,1)S(1)}, u32[]{:S(2)}, u32[]{:S(2)}) collective-permute-start(bf16[2,32,512]{2,1,0:T(8,128)(2,1)S(1)} %get-tuple-element.52), channel_id=1, source_target_pairs={{0,16},{16,0},{32,48},{48,32},{64,80},{80,64},{96,112},{112,96},{1... | collective-permute-start | bytes 196616 | tf_op jit(solution)/shard_map/ppermute | solution.py:690
  218.0 5.9 %collective-permute-start.8 = (bf16[2,32,512]{2,1,0:T(8,128)(2,1)S(1)}, bf16[2,32,512]{2,1,0:T(8,128)(2,1)S(1)}, u32[]{:S(2)}, u32[]{:S(2)}) collective-permute-start(bf16[2,32,512]{2,1,0:T(8,128)(2,1)S(1)} %get-tuple-element.53), channel_id=1, source_target_pairs={{0,48},{16,32},{32,80},{48,64},{64,112},{80,96},{96,16},{112,0},{1... | collective-permute-start | bytes 196616 | tf_op jit(solution)/shard_map/ppermute | solution.py:690
  218.0 5.8 %collective-permute-start.9 = (bf16[2,32,512]{2,1,0:T(8,128)(2,1)S(1)}, bf16[2,32,512]{2,1,0:T(8,128)(2,1)S(1)}, u32[]{:S(2)}, u32[]{:S(2)}) collective-permute-start(bf16[2,32,512]{2,1,0:T(8,128)(2,1)S(1)} %get-tuple-element.54), channel_id=1, source_target_pairs={{0,80},{16,64},{32,112},{48,96},{64,16},{80,0},{96,48},{112,32},{1... | collective-permute-start | bytes 196616 | tf_op jit(solution)/shard_map/ppermute | solution.py:690
  221.0 4.9 %collective-permute-start.10 = (bf16[2,32,512]{2,1,0:T(8,128)(2,1)S(1)}, bf16[2,32,512]{2,1,0:T(8,128)(2,1)S(1)}, u32[]{:S(2)}, u32[]{:S(2)}) collective-permute-start(bf16[2,32,512]{2,1,0:T(8,128)(2,1)S(1)} %get-tuple-element.55), channel_id=1, source_target_pairs={{0,112},{16,96},{32,16},{48,0},{64,48},{80,32},{96,80},{112,64},{1... | collective-permute-start | bytes 196616 | tf_op jit(solution)/shard_map/ppermute | solution.py:690

commit v9 on v8

--- a/solution.py
+++ b/solution.py
@@ -289,7 +289,7 @@
 
 
 def row_input_gradient_kernel(where_ref, x_ref, right_ref, w_ref, *refs):
-    outs, w_s, right_s, gin_s, w_sem, right_sem = refs[:8], *refs[8:]
+    outs, w_s, right_s, gin_s, w_sem, right_sem = refs[:4], *refs[4:]
     weights = copies_of(w_ref, w_s, w_sem, 3)
     rights = copies_of(right_ref, right_s, right_sem, 4)
     start_all([copy for pair in zip(weights, rights) for copy in pair] + rights[3:])
@@ -299,9 +299,9 @@
         u = x_ref[:, rr].astype(F32).reshape(LINE, D)
         grad_in = input_gradient(u, right_s, w_s, rows)
         gin_s[:, :, rr] = grad_in.astype(BF16).reshape(8, 2, 16, D)
-    for place in range(8):
-        high, x = (where_ref[2] + place // 4) % 2, (where_ref[3] + place % 4) % 4
-        outs[place][...] = gin_s[high * 4 + x]
+    for shift in range(4):
+        for high in range(2):
+            outs[shift][high] = gin_s[high * 4 + (where_ref[3] + shift) % 4]
 
 
 def col_kernel(where_ref, m_ref, w_ref, *refs):
@@ -416,19 +416,29 @@
     tile_ref[...] = dot(order, lines).astype(BF16).reshape(32, 16, D)
 
 
+def pass_high_kernel(where_ref, *refs):
+    parts, pass_ref = refs[:4], refs[4]
+    for shift in range(4):
+        pass_ref[shift] = parts[shift][1 - where_ref[2]]
+
+
 def pass_core_kernel(where_ref, *refs):
-    parts, pass_ref = refs[:8], refs[8]
-    for shift in range(8):
-        pass_ref[shift] = parts[shift][1 - where_ref[4]]
+    parts, got_ref, pass_ref = refs[:4], refs[4], refs[5]
+    high, other = where_ref[2], 1 - where_ref[4]
+    for shift in range(4):
+        pass_ref[0, shift] = parts[shift][high, other]
+        pass_ref[1, shift] = got_ref[shift, other]
 
 
 def join_kernel(where_ref, *refs):
-    parts, passed_ref, tile_ref = refs[:8], refs[8], refs[9]
-    core = where_ref[4]
-    for place in range(8):
-        high, x = (where_ref[2] + place // 4) % 2, (where_ref[3] + 4 - place % 4) % 4
-        tile_ref[high * 4 + x, core] = parts[place][core]
-        tile_ref[high * 4 + x, 1 - core] = passed_ref[place]
+    parts, got_ref, passed_ref, tile_ref = refs[:4], refs[4], refs[5], refs[6]
+    high, core = where_ref[2], where_ref[4]
+    for shift in range(4):
+        source = (where_ref[3] + 4 - shift) % 4
+        tile_ref[high, source, core] = parts[shift][high, core]
+        tile_ref[1 - high, source, core] = got_ref[shift, core]
+        tile_ref[high, source, 1 - core] = passed_ref[0, shift]
+        tile_ref[1 - high, source, 1 - core] = passed_ref[1, shift]
 
 
 def pair_sum_kernel(where_ref, keep_ref, got_ref, *refs):
@@ -586,8 +596,8 @@
 row_input_gradient = call(
     row_input_gradient_kernel,
     "svhh",
-    "v" * 8,
-    (shape(2, 2, 16, D),) * 8,
+    "v" * 4,
+    (shape(2, 2, 2, 16, D),) * 4,
     [
         pltpu.VMEM((3, D, D), BF16), token_scratch(4), pltpu.VMEM((8, 2, 2, 16, D), BF16),
         DMA((3,)), DMA((4,)),
@@ -639,9 +649,11 @@
 lines_to_tile = call(
     lines_to_tile_kernel, "s" + "v" * 8, "v", shape(32, 16, D), [], MATMUL, MIB, grant=48
 )
-CORE_PASS = shape(8, 2, 16, D)
-pass_core = call(pass_core_kernel, "s" + "v" * 8, "v", CORE_PASS, [], 0, MIB, grant=40)
-join = call(join_kernel, "s" + "v" * 9, "v", shape(8, 2, 2, 16, D), [], 0, MIB)
+CHIP_PASS = shape(4, 2, 2, 16, D)
+CORE_PASS = shape(2, 4, 2, 16, D)
+pass_high = call(pass_high_kernel, "s" + "v" * 4, "v", CHIP_PASS, [], 0, MIB)
+pass_core = call(pass_core_kernel, "s" + "v" * 5, "v", CORE_PASS, [], 0, MIB, grant=40)
+join = call(join_kernel, "s" + "v" * 6, "v", shape(2, 4, 2, 2, 16, D), [], 0, MIB)
 pair_sum = call(
     pair_sum_kernel, "svv", "v" * 4, (QUARTER,) * 4, [pltpu.VMEM((4, 256, D), BF16)], 0, 3 * MIB,
 )
@@ -723,10 +735,12 @@
     totals = spread(both)
     chunks = exchange(totals, CHIPS)
     gin_pieces = row_input_gradient(where, rows_in, right_row, w_row)
-    gin_parts = moved(gin_pieces, ("zh", "x"), (2, 4), 1)
-    gin_core = pass_core(where, *gin_parts)
+    gin_parts = shifted(gin_pieces, "x")
+    gin_high = pass_high(where, *gin_parts)
+    gin_got = swap(gin_high, "zh")
+    gin_core = pass_core(where, *gin_parts, gin_got)
     gin_core = swap(gin_core, "c")
-    grad_latents = join(where, *gin_parts, gin_core).reshape(32, 16, D)
+    grad_latents = join(where, *gin_parts, gin_got, gin_core).reshape(32, 16, D)
     out_pieces = col_output(where, saved_col, w_col)
     out_parts = moved(out_pieces, ROW, (4, 2), 0)
     output = lines_to_tile(where, *out_parts)

time: 238 us -> 240 us (level)
  waiting for transfers between devices: 49.7 us -> 57.2 us
  starting transfers between devices: 59.3 us -> 53.8 us
    ppermute x14 -> x7, starting transfers between devices: 17.4 us -> 6.75 us  [moved(): lax.ppermute(pieces[k + 1], axes, peers[k])]
    ppermute x5 -> x6, waiting for transfers between devices: 5.91 us -> 12.8 us  [swap(): return lax.ppermute(value, axis, [(0, 1), (1, 0)])]
    ppermute x6 -> x9, waiting for transfers between devices: 18 us -> 24 us  [shifted(): lax.ppermute(pieces[k], axis, [(i, (i + k) % n) for i in range(n)])]
    ppermute x14 -> x7, waiting for transfers between devices: 13 us -> 7.6 us  [moved(): lax.ppermute(pieces[k + 1], axes, peers[k])]
    ppermute x6 -> x9, starting transfers between devices: 8.18 us -> 11.6 us  [shifted(): lax.ppermute(pieces[k], axis, [(i, (i + k) % n) for i in range(n)])]
    ppermute x5 -> x6, starting transfers between devices: 9.64 us -> 11.4 us  [swap(): return lax.ppermute(value, axis, [(0, 1), (1, 0)])]
  transfers between devices with their start and end apart: 28 -> 25, of which waited for: 15 -> 16; matrix products, arithmetic and copies ran while one was open for 0% -> 0% of each run, Pallas kernels for 15% -> 15%
where the time goes in v9:
time: 240 us; the launch traced here: 237 us
  Pallas kernels  60.6 us (25%)
  blocking collectives  58.5 us (24%)
  waiting for transfers between devices  57.2 us (24%)
  starting transfers between devices  53.8 us (22%)
  local copies, waits for them, and re-layouts  6.16 us (3%)
    all_to_all x2, blocking collectives, exchange(): return lax.all_to_all(values, axes, split_axis=0, concat_axis=0, tiled=True)  58.5 us
    ppermute x9, waiting for transfers between devices, shifted(): lax.ppermute(pieces[k], axis, [(i, (i + k) % n) for i in range(n)])  24 us
    all_to_all x3, starting transfers between devices, exchange(): return lax.all_to_all(values, axes, split_axis=0, concat_axis=0, tiled=True)  24 us
    all_to_all x3, waiting for transfers between devices, exchange(): return lax.all_to_all(values, axes, split_axis=0, concat_axis=0, tiled=True)  12.8 us
    ppermute x6, waiting for transfers between devices, swap(): return lax.ppermute(value, axis, [(0, 1), (1, 0)])  12.8 us
    ppermute x9, starting transfers between devices, shifted(): lax.ppermute(pieces[k], axis, [(i, (i + k) % n) for i in range(n)])  11.6 us
    pallas_call x1, Pallas kernels, layer(): col_grad(where, mid_lines, w_col, *grad_parts, grad_pass)  11.4 us
    ppermute x6, starting transfers between devices, swap(): return lax.ppermute(value, axis, [(0, 1), (1, 0)])  11.4 us
  transfers between devices with their start and end apart: 25, of which 16 were waited for; matrix products, arithmetic and copies ran while one was open for 0% of the time, Pallas kernels for 15%

profile of v9, /device:TPU:1, one launch (start us, length us, event | category | flops | bytes accessed | tf_op | source)
XLA Modules:
  0.0 237.4 jit_solution(10583546973539981509)
XLA Ops:
  0.6 9.1 %all-to-all-start = ((bf16[16,2,16,512]{3,2,1,0:T(8,128)(2,1)}), bf16[16,2,16,512]{3,2,1,0:T(8,128)(2,1)S(1)}, u32[]{:S(2)}, u32[]{:S(2)}) async-start(bf16[16,2,16,512]{3,2,1,0:T(8,128)(2,1)} %bitcast.11), calls=%async_computation | async-start | bytes 1048576 | tf_op jit(solution)/shard_map/all_to_all | solution.py:681
  9.8 0.8 reshape.23
  10.6 10.1 %all-to-all-done.x_ref = bf16[16,2,16,512]{3,2,1,0:T(8,128)(2,1)S(1)} async-done(((bf16[16,2,16,512]{3,2,1,0:T(8,128)(2,1)}), bf16[16,2,16,512]{3,2,1,0:T(8,128)(2,1)S(1)}, u32[]{:S(2)}, u32[]{:S(2)}) %all-to-all-start) | async-done | bytes 524320 | tf_op jit(solution)/shard_map/all_to_all | solution.py:681
  20.8 7.9 %shard_map.84 = (bf16[128,4,512]{2,1,0:T(4,128)(2,1)S(1)}, bf16[5,512,512]{2,1,0:T(8,128)(2,1)}) custom-call(s32[21]{0:T(128)S(1)} %concatenate.3.where_ref, bf16[16,2,16,512]{3,2,1,0:T(8,128)(2,1)S(1)} %all-to-all-done.x_ref, bf16[4,512,512]{2,1,0:T(8,128)(2,1)} %w_ref.9), custom_call_target="tpu_custom_call" | custom-call | flops 1342177280 | bytes 6291456 | tf_op jit(solution)/shard_map/pallas_call | solution.py:718
  28.7 0.8 copy-done.9
  29.5 6.4 %all-to-all-start.1 = ((bf16[128,4,512]{2,1,0:T(4,128)(2,1)}), bf16[128,4,512]{2,1,0:T(4,128)(2,1)}, u32[]{:S(2)}, u32[]{:S(2)}) async-start(bf16[128,4,512]{2,1,0:T(4,128)(2,1)} %copy-done.9), calls=%async_computation.1 | async-start | bytes 1048576 | tf_op jit(solution)/shard_map/all_to_all | solution.py:681
  35.9 1.2 shard_map.85
  37.2 1.4 collective-permute-start
  38.6 2.5 %collective-permute-start.1 = (bf16[2,2,32,512]{3,2,1,0:T(8,128)(2,1)S(1)}, bf16[2,2,32,512]{3,2,1,0:T(8,128)(2,1)S(1)}, u32[]{:S(2)}, u32[]{:S(2)}) collective-permute-start(bf16[2,2,32,512]{3,2,1,0:T(8,128)(2,1)S(1)} %get-tuple-element.41), channel_id=1, source_target_pairs={{0,64},{32,96},{64,0},{96,32},{1,65},{33,97},{65,1},{97,33},{2,66}... | collective-permute-start | bytes 393224 | tf_op jit(solution)/shard_map/ppermute | solution.py:687
  41.0 1.1 collective-permute-start.2
  42.2 5.2 %collective-permute-done.refs_1_ = bf16[2,2,32,512]{3,2,1,0:T(8,128)(2,1)S(1)} collective-permute-done((bf16[2,2,32,512]{3,2,1,0:T(8,128)(2,1)S(1)}, bf16[2,2,32,512]{3,2,1,0:T(8,128)(2,1)S(1)}, u32[]{:S(2)}, u32[]{:S(2)}) %collective-permute-start) | collective-permute-done | bytes 131104 | tf_op jit(solution)/shard_map/ppermute | solution.py:687
  47.4 3.5 %collective-permute-done.1.refs_2_ = bf16[2,2,32,512]{3,2,1,0:T(8,128)(2,1)S(1)} collective-permute-done((bf16[2,2,32,512]{3,2,1,0:T(8,128)(2,1)S(1)}, bf16[2,2,32,512]{3,2,1,0:T(8,128)(2,1)S(1)}, u32[]{:S(2)}, u32[]{:S(2)}) %collective-permute-start.1) | collective-permute-done | bytes 131104 | tf_op jit(solution)/shard_map/ppermute | solution.py:687
  50.9 0.6 shard_map.86
  51.5 1.7 collective-permute-start.3
  53.2 5.9 %collective-permute-done.3.refs_4_ = bf16[4,2,32,512]{3,2,1,0:T(8,128)(2,1)S(1)} collective-permute-done((bf16[4,2,32,512]{3,2,1,0:T(8,128)(2,1)S(1)}, bf16[4,2,32,512]{3,2,1,0:T(8,128)(2,1)S(1)}, u32[]{:S(2)}, u32[]{:S(2)}) %collective-permute-start.3) | collective-permute-done | bytes 262176 | tf_op jit(solution)/shard_map/ppermute | solution.py:706
  59.1 11.4 %shard_map.87 = (bf16[128,4,512]{2,1,0:T(4,128)(2,1)}, bf16[7,512,512]{2,1,0:T(8,128)(2,1)}) custom-call(s32[21]{0:T(128)S(1)} %concatenate.3.where_ref, bf16[128,4,512]{2,1,0:T(4,128)(2,1)} %all-to-all-done.1.m_ref, bf16[4,512,512]{2,1,0:T(8,128)(2,1)S(1)} %copy-done.4, bf16[2,2,32,512]{3,2,1,0:T(8,128)(2,1)S(1)} %get-tuple-element.39.refs_0_, ...), custom_call_target="tpu_custom_call" | custom-call | flops 2952790016 | bytes 8388608 | tf_op jit(solution)/shard_map/pallas_call | solution.py:721
  70.5 8.4 %all-to-all-start.2 = ((bf16[128,4,512]{2,1,0:T(4,128)(2,1)}), bf16[128,4,512]{2,1,0:T(4,128)(2,1)}, u32[]{:S(2)}, u32[]{:S(2)}) async-start(bf16[128,4,512]{2,1,0:T(4,128)(2,1)} %get-tuple-element.52), calls=%async_computation.2 | async-start | bytes 1048576 | tf_op jit(solution)/shard_map/all_to_all | solution.py:681
  79.0 3.1 %shard_map.97 = (bf16[2,512,512]{2,1,0:T(8,128)(2,1)S(1)}, bf16[2,512,512]{2,1,0:T(8,128)(2,1)S(1)}) custom-call(s32[21]{0:T(128)S(1)} %concatenate.3.where_ref, bf16[7,512,512]{2,1,0:T(8,128)(2,1)} %get-tuple-element.43.saved_ref.right_ref), custom_call_target="tpu_custom_call" | custom-call | flops 536870912 | bytes 6291456 | tf_op jit(solution)/shard_map/pallas_call | solution.py:725
  82.1 1.0 copy-done.6
  83.1 1.1 collective-permute-start.17
  84.2 2.4 %shard_map.90 = (bf16[8,512,256]{2,1,0:T(8,128)(2,1)S(1)}, bf16[2,512,512]{2,1,0:T(8,128)(2,1)S(1)}) custom-call(bf16[5,512,512]{2,1,0:T(8,128)(2,1)S(1)} %copy-done), custom_call_target="tpu_custom_call" | custom-call | flops 134217728 | bytes 8388608 | tf_op jit(solution)/shard_map/pallas_call | solution.py:720
  86.7 1.0 copy-done.1
  87.7 1.3 copy-done.5
  89.0 2.6 %all-to-all-done.2.g_ref = bf16[128,4,512]{2,1,0:T(4,128)(2,1)} async-done(((bf16[128,4,512]{2,1,0:T(4,128)(2,1)}), bf16[128,4,512]{2,1,0:T(4,128)(2,1)}, u32[]{:S(2)}, u32[]{:S(2)}) %all-to-all-start.2) | async-done | bytes 524320 | tf_op jit(solution)/shard_map/all_to_all | solution.py:681
  91.7 1.2 copy-done.2
  92.9 8.7 %shard_map.91 = (bf16[2,512,512]{2,1,0:T(8,128)(2,1)S(1)}, bf16[4,512,512]{2,1,0:T(8,128)(2,1)}) custom-call(s32[21]{0:T(128)S(1)} %concatenate.3.where_ref, bf16[128,4,512]{2,1,0:T(4,128)(2,1)} %all-to-all-done.2.g_ref, bf16[5,512,512]{2,1,0:T(8,128)(2,1)} %get-tuple-element.53.saved_ref.qkv_ref, bf16[2,512,512]{2,1,0:T(8,128)(2,1)S(1)} %copy-done.2, ...), custom_call_target="tpu_custom_call" | custom-call | flops 2013265920 | bytes 12582912 | tf_op jit(solution)/shard_map/pallas_call | solution.py:730
  101.6 1.7 collective-permute-start.16
  103.3 2.6 %shard_map.98.keep_ref = bf16[2,512,512]{2,1,0:T(8,128)(2,1)S(1)} custom-call(s32[21]{0:T(128)S(1)} %concatenate.3.where_ref, bf16[2,512,512]{2,1,0:T(8,128)(2,1)S(1)} %copy-done.7, bf16[7,512,512]{2,1,0:T(8,128)(2,1)} %get-tuple-element.43.saved_ref.right_ref), custom_call_target="tpu_custom_call" | custom-call | flops 536870912 | bytes 3145728 | tf_op jit(solution)/shard_map/pallas_call | solution.py:727
  105.9 1.9 shard_map.99
  108.2 1.9 collective-permute-start.19
  110.1 0.9 collective-permute-start.20
  111.0 2.6 %shard_map.96.keep_ref = bf16[2,512,512]{2,1,0:T(8,128)(2,1)S(1)} custom-call(s32[21]{0:T(128)S(1)} %concatenate.3.where_ref, bf16[2,512,512]{2,1,0:T(8,128)(2,1)S(1)} %copy-done.3, bf16[4,512,512]{2,1,0:T(8,128)(2,1)} %get-tuple-element.56.right_ref), custom_call_target="tpu_custom_call" | custom-call | flops 536870912 | bytes 3145728 | tf_op jit(solution)/shard_map/pallas_call | solution.py:732
  113.6 3.9 %collective-permute-done.18.refs_1_ = bf16[256,512]{1,0:T(8,128)(2,1)S(1)} collective-permute-done((bf16[256,512]{1,0:T(8,128)(2,1)S(1)}, bf16[256,512]{1,0:T(8,128)(2,1)S(1)}, u32[]{:S(2)}, u32[]{:S(2)}) %collective-permute-start.18) | collective-permute-done | bytes 262176 | tf_op jit(solution)/shard_map/ppermute | solution.py:687
  117.5 4.7 %collective-permute-done.19.refs_2_ = bf16[256,512]{1,0:T(8,128)(2,1)S(1)} collective-permute-done((bf16[256,512]{1,0:T(8,128)(2,1)S(1)}, bf16[256,512]{1,0:T(8,128)(2,1)S(1)}, u32[]{:S(2)}, u32[]{:S(2)}) %collective-permute-start.19) | collective-permute-done | bytes 262176 | tf_op jit(solution)/shard_map/ppermute | solution.py:687
  122.2 0.8 collective-permute-done.20.refs_3_
  123.0 0.4 shard_map.100
  123.4 26.0 %all_to_all.25.both_ref = bf16[64,80,128]{2,1,0:T(8,128)(2,1)S(1)} all-to-all(bf16[64,80,128]{2,1,0:T(8,128)(2,1)S(1)} %shard_map.100), channel_id=1, replica_groups=mesh['y'=4,'zl'=2,'zh'=2,'x'=4,'c'=2] {'y','zl','zh','x'}, dimensions={0} | all-to-all | bytes 2621440 | tf_op jit(solution)/shard_map/all_to_all | solution.py:681
  149.4 1.7 shard_map.101
  151.1 32.5 %all_to_all.26.chunks_ref = bf16[64,128,128]{2,1,0:T(8,128)(2,1)S(1)} all-to-all(bf16[64,128,128]{2,1,0:T(8,128)(2,1)} %shard_map.101), channel_id=1, replica_groups=mesh['y'=4,'zl'=2,'zh'=2,'x'=4,'c'=2] {'y','zl','zh','x'}, dimensions={0} | all-to-all | bytes 4194304 | tf_op jit(solution)/shard_map/all_to_all | solution.py:681
  183.6 3.3 %collective-permute-start.21 = (bf16[64,128,128]{2,1,0:T(8,128)(2,1)S(1)}, bf16[64,128,128]{2,1,0:T(8,128)(2,1)S(1)}, u32[]{:S(2)}, u32[]{:S(2)}) collective-permute-start(bf16[64,128,128]{2,1,0:T(8,128)(2,1)S(1)} %all_to_all.26.chunks_ref), channel_id=1, source_target_pairs={{0,1},{1,0},{2,3},{3,2},{4,5},{5,4},{6,7},{7,6},{8,9},{9,8},{10,11... | collective-permute-start | bytes 6291464 | tf_op jit(solution)/shard_map/ppermute | solution.py:706
  186.9 3.8 %shard_map.92 = (bf16[2,2,2,16,512]{4,3,2,1,0:T(8,128)(2,1)S(1)}, bf16[2,2,2,16,512]{4,3,2,1,0:T(8,128)(2,1)S(1)}, bf16[2,2,2,16,512]{4,3,2,1,0:T(8,128)(2,1)S(1)}, bf16[2,2,2,16,512]{4,3,2,1,0:T(8,128)(2,1)S(1)}) custom-call(s32[21]{0:T(128)S(1)} %concatenate.3.where_ref, bf16[16,2,16,512]{3,2,1,0:T(8,128)(2,1)S(1)} %all-to-all-done.x_ref, ...), custom_call_target="tpu_custom_call" | custom-call | flops 805306368 | bytes 5242880 | tf_op jit(solution)/shard_map/pallas_call | solution.py:737
  190.8 2.2 collective-permute-start.12
  193.0 1.2 collective-permute-start.13
  194.2 3.3 %collective-permute-done.11.refs_1_ = bf16[2,2,2,16,512]{4,3,2,1,0:T(8,128)(2,1)S(1)} collective-permute-done((bf16[2,2,2,16,512]{4,3,2,1,0:T(8,128)(2,1)S(1)}, bf16[2,2,2,16,512]{4,3,2,1,0:T(8,128)(2,1)S(1)}, u32[]{:S(2)}, u32[]{:S(2)}) %collective-permute-start.11) | collective-permute-done | bytes 131104 | tf_op jit(solution)/shard_map/ppermute | solution.py:687
  197.5 1.9 collective-permute-done.12.refs_2_
  199.4 0.8 collective-permute-done.13.refs_3_
  200.2 0.6 shard_map.93
  200.8 1.4 collective-permute-start.14
  202.2 6.9 %collective-permute-done.14.refs_4_ = bf16[4,2,2,16,512]{4,3,2,1,0:T(8,128)(2,1)S(1)} collective-permute-done((bf16[4,2,2,16,512]{4,3,2,1,0:T(8,128)(2,1)S(1)}, bf16[4,2,2,16,512]{4,3,2,1,0:T(8,128)(2,1)S(1)}, u32[]{:S(2)}, u32[]{:S(2)}) %collective-permute-start.14) | collective-permute-done | bytes 262176 | tf_op jit(solution)/shard_map/ppermute | solution.py:706
  209.1 0.6 shard_map.94
  209.6 2.1 collective-permute-start.15
  211.7 2.4 %shard_map.88 = (bf16[2,32,512]{2,1,0:T(8,128)(2,1)S(1)}, bf16[2,32,512]{2,1,0:T(8,128)(2,1)S(1)}, bf16[2,32,512]{2,1,0:T(8,128)(2,1)S(1)}, bf16[2,32,512]{2,1,0...) custom-call(s32[21]{0:T(128)S(1)} %concatenate.3.where_ref, ...), custom_call_target="tpu_custom_call" | custom-call | flops 268435456 | bytes 3145728 | tf_op jit(solution)/shard_map/pallas_call | solution.py:744
  214.1 0.4 collective-permute-start.4
  214.6 1.6 collective-permute-start.5
  216.2 0.9 collective-permute-start.6
  217.0 3.4 %collective-permute-done.4.refs_1_ = bf16[2,32,512]{2,1,0:T(8,128)(2,1)S(1)} collective-permute-done((bf16[2,32,512]{2,1,0:T(8,128)(2,1)S(1)}, bf16[2,32,512]{2,1,0:T(8,128)(2,1)S(1)}, u32[]{:S(2)}, u32[]{:S(2)}) %collective-permute-start.4) | collective-permute-done | bytes 65568 | tf_op jit(solution)/shard_map/ppermute | solution.py:702
  220.7 2.9 %collective-permute-start.9 = (bf16[2,32,512]{2,1,0:T(8,128)(2,1)S(1)}, bf16[2,32,512]{2,1,0:T(8,128)(2,1)S(1)}, u32[]{:S(2)}, u32[]{:S(2)}) collective-permute-start(bf16[2,32,512]{2,1,0:T(8,128)(2,1)S(1)} %get-tuple-element.50), channel_id=1, source_target_pairs={{0,80},{16,64},{32,112},{48,96},{64,16},{80,0},{96,48},{112,32},{1... | collective-permute-start | bytes 196616 | tf_op jit(solution)/shard_map/ppermute | solution.py:702
  223.7 0.9 collective-permute-start.10
  224.6 2.1 collective-permute-done.8.refs_5_
  226.7 1.8 collective-permute-done.10.refs_7_
  228.5 2.0 shard_map.89
  230.5 1.4 shard_map.95
  231.9 2.7 %widen.2 = (f32[2,1024,512]{2,1,0:T(8,128)}, f32[2,4,256,512]{3,2,1,0:T(8,128)}) custom-call(s32[21]{0:T(128)S(1)} %concatenate.3.where_ref, bf16[64,128,128]{2,1,0:T(8,128)(2,1)S(1)} %all_to_all.26.chunks_ref), custom_call_target="tpu_custom_call" | custom-call | bytes 6291456 | tf_op jit(solution)/shard_map/widen/pallas_call | solution.py:665
  234.5 2.7 %widen.3 = (f32[2,1024,512]{2,1,0:T(8,128)}, f32[2,4,256,512]{3,2,1,0:T(8,128)}) custom-call(s32[21]{0:T(128)S(1)} %concatenate.3.where_ref, bf16[64,128,128]{2,1,0:T(8,128)(2,1)S(1)} %collective-permute-done.21.chunks_ref, f32[2,1024,512]{2,1,0:T(8,128)} %get-tuple-element.68.refs_0_, ...), custom_call_target="tpu_custom_call", output_to_operand_aliasing={{0}: (2, {}), {1}: (3, {})} | custom-call | bytes 6291456 | tf_op jit(solution)/shard_map/widen/pallas_call | solution.py:665
  (30 shorter events, 0.9 us)
Async XLA Ops:
  0.6 20.1 %all-to-all-start = ((bf16[16,2,16,512]{3,2,1,0:T(8,128)(2,1)}), bf16[16,2,16,512]{3,2,1,0:T(8,128)(2,1)S(1)}, u32[]{:S(2)}, u32[]{:S(2)}) async-start(bf16[16,2,16,512]{3,2,1,0:T(8,128)(2,1)} %bitcast.11), calls=%async_computation | async-start | bytes 1048576 | tf_op jit(solution)/shard_map/all_to_all | solution.py:681
  10.6 25.3 %copy-start.8 = (bf16[32,16,512]{2,1,0:T(8,128)(2,1)S(1)}, bf16[32,16,512]{2,1,0:T(8,128)(2,1)}, u32[]{:S(2)}) copy-start(bf16[32,16,512]{2,1,0:T(8,128)(2,1)} %tile_ref.1) | copy-start | bytes 1572868
  28.7 0.8 copy-start.9
  29.5 29.6 %copy-start.4 = (bf16[4,512,512]{2,1,0:T(8,128)(2,1)S(1)}, bf16[4,512,512]{2,1,0:T(8,128)(2,1)}, u32[]{:S(2)}) copy-start(bf16[4,512,512]{2,1,0:T(8,128)(2,1)} %w_ref.7) | copy-start | bytes 6291460
  29.5 29.6 %all-to-all-start.1 = ((bf16[128,4,512]{2,1,0:T(4,128)(2,1)}), bf16[128,4,512]{2,1,0:T(4,128)(2,1)}, u32[]{:S(2)}, u32[]{:S(2)}) async-start(bf16[128,4,512]{2,1,0:T(4,128)(2,1)} %copy-done.9), calls=%async_computation.1 | async-start | bytes 1048576 | tf_op jit(solution)/shard_map/all_to_all | solution.py:681
  37.2 10.2 %collective-permute-start = (bf16[2,2,32,512]{3,2,1,0:T(8,128)(2,1)S(1)}, bf16[2,2,32,512]{3,2,1,0:T(8,128)(2,1)S(1)}, u32[]{:S(2)}, u32[]{:S(2)}) collective-permute-start(bf16[2,2,32,512]{3,2,1,0:T(8,128)(2,1)S(1)} %get-tuple-element.40), channel_id=1, source_target_pairs={{0,32},{32,64},{64,96},{96,0},{1,33},{33,65},{65,97},{97,1},{2,34}... | collective-permute-start | bytes 393224 | tf_op jit(solution)/shard_map/ppermute | solution.py:687
  38.6 12.3 %collective-permute-start.1 = (bf16[2,2,32,512]{3,2,1,0:T(8,128)(2,1)S(1)}, bf16[2,2,32,512]{3,2,1,0:T(8,128)(2,1)S(1)}, u32[]{:S(2)}, u32[]{:S(2)}) collective-permute-start(bf16[2,2,32,512]{3,2,1,0:T(8,128)(2,1)S(1)} %get-tuple-element.41), channel_id=1, source_target_pairs={{0,64},{32,96},{64,0},{96,32},{1,65},{33,97},{65,1},{97,33},{2,66}... | collective-permute-start | bytes 393224 | tf_op jit(solution)/shard_map/ppermute | solution.py:687
  41.0 9.8 %collective-permute-start.2 = (bf16[2,2,32,512]{3,2,1,0:T(8,128)(2,1)S(1)}, bf16[2,2,32,512]{3,2,1,0:T(8,128)(2,1)S(1)}, u32[]{:S(2)}, u32[]{:S(2)}) collective-permute-start(bf16[2,2,32,512]{3,2,1,0:T(8,128)(2,1)S(1)} %get-tuple-element.42), channel_id=1, source_target_pairs={{0,96},{32,0},{64,32},{96,64},{1,97},{33,1},{65,33},{97,65},{2,98}... | collective-permute-start | bytes 393224 | tf_op jit(solution)/shard_map/ppermute | solution.py:687
  51.5 7.6 %collective-permute-start.3 = (bf16[4,2,32,512]{3,2,1,0:T(8,128)(2,1)S(1)}, bf16[4,2,32,512]{3,2,1,0:T(8,128)(2,1)S(1)}, u32[]{:S(2)}, u32[]{:S(2)}) collective-permute-start(bf16[4,2,32,512]{3,2,1,0:T(8,128)(2,1)S(1)} %shard_map.86), channel_id=1, source_target_pairs={{0,16},{16,0},{1,17},{17,1},{2,18},{18,2},{3,19},{19,3},{4,20},{20... | collective-permute-start | bytes 786440 | tf_op jit(solution)/shard_map/ppermute | solution.py:706
  70.5 21.1 %all-to-all-start.2 = ((bf16[128,4,512]{2,1,0:T(4,128)(2,1)}), bf16[128,4,512]{2,1,0:T(4,128)(2,1)}, u32[]{:S(2)}, u32[]{:S(2)}) async-start(bf16[128,4,512]{2,1,0:T(4,128)(2,1)} %get-tuple-element.52), calls=%async_computation.2 | async-start | bytes 1048576 | tf_op jit(solution)/shard_map/all_to_all | solution.py:681
  79.0 5.3 %copy-start = (bf16[5,512,512]{2,1,0:T(8,128)(2,1)S(1)}, bf16[5,512,512]{2,1,0:T(8,128)(2,1)}, u32[]{:S(2)}) copy-start(bf16[5,512,512]{2,1,0:T(8,128)(2,1)} %get-tuple-element.53.saved_ref.qkv_ref) | copy-start | bytes 7864324
  82.1 1.0 copy-start.6
  83.1 22.8 %collective-permute-start.17 = (bf16[2,512,512]{2,1,0:T(8,128)(2,1)S(1)}, bf16[2,512,512]{2,1,0:T(8,128)(2,1)}, u32[]{:S(2)}, u32[]{:S(2)}) collective-permute-start(bf16[2,512,512]{2,1,0:T(8,128)(2,1)S(1)} %get-tuple-element.63), channel_id=1, source_target_pairs={{0,1},{1,0},{2,3},{3,2},{4,5},{5,4},{6,7},{7,6},{8,9},{9,8},{10,11... | collective-permute-start | bytes 3145736 | tf_op jit(solution)/shard_map/ppermute | solution.py:706
  86.7 1.0 copy-start.1
  87.7 1.3 copy-start.5
  91.7 1.2 copy-start.2
  92.9 10.4 %copy-start.7 = (bf16[2,512,512]{2,1,0:T(8,128)(2,1)S(1)}, bf16[2,512,512]{2,1,0:T(8,128)(2,1)}, u32[]{:S(2)}) copy-start(bf16[2,512,512]{2,1,0:T(8,128)(2,1)} %copy-done.6) | copy-start | bytes 3145732
  101.6 21.4 %collective-permute-start.16 = (bf16[2,512,512]{2,1,0:T(8,128)(2,1)S(1)}, bf16[2,512,512]{2,1,0:T(8,128)(2,1)S(1)}, u32[]{:S(2)}, u32[]{:S(2)}) collective-permute-start(bf16[2,512,512]{2,1,0:T(8,128)(2,1)S(1)} %get-tuple-element.61), channel_id=1, source_target_pairs={{0,1},{1,0},{2,3},{3,2},{4,5},{5,4},{6,7},{7,6},{8,9},{9,8},{10,11... | collective-permute-start | bytes 3145736 | tf_op jit(solution)/shard_map/ppermute | solution.py:706
  105.9 5.1 %copy-start.3 = (bf16[2,512,512]{2,1,0:T(8,128)(2,1)S(1)}, bf16[2,512,512]{2,1,0:T(8,128)(2,1)}, u32[]{:S(2)}) copy-start(bf16[2,512,512]{2,1,0:T(8,128)(2,1)} %copy-done.1) | copy-start | bytes 3145732
  107.9 9.6 %collective-permute-start.18 = (bf16[256,512]{1,0:T(8,128)(2,1)S(1)}, bf16[256,512]{1,0:T(8,128)(2,1)S(1)}, u32[]{:S(2)}, u32[]{:S(2)}) collective-permute-start(bf16[256,512]{1,0:T(8,128)(2,1)S(1)} %get-tuple-element.65), channel_id=1, source_target_pairs={{0,2},{2,4},{4,6},{6,0},{1,3},{3,5},{5,7},{7,1},{8,10},{10,12},{12... | collective-permute-start | bytes 786440 | tf_op jit(solution)/shard_map/ppermute | solution.py:687
  108.2 13.9 %collective-permute-start.19 = (bf16[256,512]{1,0:T(8,128)(2,1)S(1)}, bf16[256,512]{1,0:T(8,128)(2,1)S(1)}, u32[]{:S(2)}, u32[]{:S(2)}) collective-permute-start(bf16[256,512]{1,0:T(8,128)(2,1)S(1)} %get-tuple-element.66), channel_id=1, source_target_pairs={{0,4},{2,6},{4,0},{6,2},{1,5},{3,7},{5,1},{7,3},{8,12},{10,14},{12... | collective-permute-start | bytes 786440 | tf_op jit(solution)/shard_map/ppermute | solution.py:687
  110.1 12.8 %collective-permute-start.20 = (bf16[256,512]{1,0:T(8,128)(2,1)S(1)}, bf16[256,512]{1,0:T(8,128)(2,1)S(1)}, u32[]{:S(2)}, u32[]{:S(2)}) collective-permute-start(bf16[256,512]{1,0:T(8,128)(2,1)S(1)} %get-tuple-element.67), channel_id=1, source_target_pairs={{0,6},{2,0},{4,2},{6,4},{1,7},{3,1},{5,3},{7,5},{8,14},{10,8},{12,... | collective-permute-start | bytes 786440 | tf_op jit(solution)/shard_map/ppermute | solution.py:687
  183.6 50.9 %collective-permute-start.21 = (bf16[64,128,128]{2,1,0:T(8,128)(2,1)S(1)}, bf16[64,128,128]{2,1,0:T(8,128)(2,1)S(1)}, u32[]{:S(2)}, u32[]{:S(2)}) collective-permute-start(bf16[64,128,128]{2,1,0:T(8,128)(2,1)S(1)} %all_to_all.26.chunks_ref), channel_id=1, source_target_pairs={{0,1},{1,0},{2,3},{3,2},{4,5},{5,4},{6,7},{7,6},{8,9},{9,8},{10,11... | collective-permute-start | bytes 6291464 | tf_op jit(solution)/shard_map/ppermute | solution.py:706
  190.7 6.8 %collective-permute-start.11 = (bf16[2,2,2,16,512]{4,3,2,1,0:T(8,128)(2,1)S(1)}, bf16[2,2,2,16,512]{4,3,2,1,0:T(8,128)(2,1)S(1)}, u32[]{:S(2)}, u32[]{:S(2)}) collective-permute-start(bf16[2,2,2,16,512]{4,3,2,1,0:T(8,128)(2,1)S(1)} %get-tuple-element.58), channel_id=1, source_target_pairs={{0,2},{2,4},{4,6},{6,0},{1,3},{3,5},{5,7},{7,1},{8,10},{10,12},{12... | collective-permute-start | bytes 393224 | tf_op jit(solution)/shard_map/ppermute | solution.py:687
  190.8 8.6 %collective-permute-start.12 = (bf16[2,2,2,16,512]{4,3,2,1,0:T(8,128)(2,1)S(1)}, bf16[2,2,2,16,512]{4,3,2,1,0:T(8,128)(2,1)S(1)}, u32[]{:S(2)}, u32[]{:S(2)}) collective-permute-start(bf16[2,2,2,16,512]{4,3,2,1,0:T(8,128)(2,1)S(1)} %get-tuple-element.59), channel_id=1, source_target_pairs={{0,4},{2,6},{4,0},{6,2},{1,5},{3,7},{5,1},{7,3},{8,12},{10,14},{12... | collective-permute-start | bytes 393224 | tf_op jit(solution)/shard_map/ppermute | solution.py:687
  193.0 7.2 %collective-permute-start.13 = (bf16[2,2,2,16,512]{4,3,2,1,0:T(8,128)(2,1)S(1)}, bf16[2,2,2,16,512]{4,3,2,1,0:T(8,128)(2,1)S(1)}, u32[]{:S(2)}, u32[]{:S(2)}) collective-permute-start(bf16[2,2,2,16,512]{4,3,2,1,0:T(8,128)(2,1)S(1)} %get-tuple-element.60), channel_id=1, source_target_pairs={{0,6},{2,0},{4,2},{6,4},{1,7},{3,1},{5,3},{7,5},{8,14},{10,8},{12,... | collective-permute-start | bytes 393224 | tf_op jit(solution)/shard_map/ppermute | solution.py:687
  200.8 8.3 %collective-permute-start.14 = (bf16[4,2,2,16,512]{4,3,2,1,0:T(8,128)(2,1)S(1)}, bf16[4,2,2,16,512]{4,3,2,1,0:T(8,128)(2,1)S(1)}, u32[]{:S(2)}, u32[]{:S(2)}) collective-permute-start(bf16[4,2,2,16,512]{4,3,2,1,0:T(8,128)(2,1)S(1)} %shard_map.93), channel_id=1, source_target_pairs={{0,8},{8,0},{1,9},{9,1},{2,10},{10,2},{3,11},{11,3},{4,12},{12,4},... | collective-permute-start | bytes 786440 | tf_op jit(solution)/shard_map/ppermute | solution.py:706
  209.6 20.8 %collective-permute-start.15 = (bf16[2,4,2,16,512]{4,3,2,1,0:T(8,128)(2,1)S(1)}, bf16[2,4,2,16,512]{4,3,2,1,0:T(8,128)(2,1)S(1)}, u32[]{:S(2)}, u32[]{:S(2)}) collective-permute-start(bf16[2,4,2,16,512]{4,3,2,1,0:T(8,128)(2,1)S(1)} %shard_map.94), channel_id=1, source_target_pairs={{0,1},{1,0},{2,3},{3,2},{4,5},{5,4},{6,7},{7,6},{8,9},{9,8},{10,11... | collective-permute-start | bytes 786440 | tf_op jit(solution)/shard_map/ppermute | solution.py:706
  214.1 6.3 %collective-permute-start.4 = (bf16[2,32,512]{2,1,0:T(8,128)(2,1)S(1)}, bf16[2,32,512]{2,1,0:T(8,128)(2,1)S(1)}, u32[]{:S(2)}, u32[]{:S(2)}) collective-permute-start(bf16[2,32,512]{2,1,0:T(8,128)(2,1)S(1)} %get-tuple-element.45), channel_id=1, source_target_pairs={{0,32},{16,48},{32,64},{48,80},{64,96},{80,112},{96,0},{112,16},{1... | collective-permute-start | bytes 196616 | tf_op jit(solution)/shard_map/ppermute | solution.py:702
  214.6 5.9 %collective-permute-start.5 = (bf16[2,32,512]{2,1,0:T(8,128)(2,1)S(1)}, bf16[2,32,512]{2,1,0:T(8,128)(2,1)S(1)}, u32[]{:S(2)}, u32[]{:S(2)}) collective-permute-start(bf16[2,32,512]{2,1,0:T(8,128)(2,1)S(1)} %get-tuple-element.46), channel_id=1, source_target_pairs={{0,64},{16,80},{32,96},{48,112},{64,0},{80,16},{96,32},{112,48},{1... | collective-permute-start | bytes 196616 | tf_op jit(solution)/shard_map/ppermute | solution.py:702
  216.2 4.5 %collective-permute-start.6 = (bf16[2,32,512]{2,1,0:T(8,128)(2,1)S(1)}, bf16[2,32,512]{2,1,0:T(8,128)(2,1)S(1)}, u32[]{:S(2)}, u32[]{:S(2)}) collective-permute-start(bf16[2,32,512]{2,1,0:T(8,128)(2,1)S(1)} %get-tuple-element.47), channel_id=1, source_target_pairs={{0,96},{16,112},{32,0},{48,16},{64,32},{80,48},{96,64},{112,80},{1... | collective-permute-start | bytes 196616 | tf_op jit(solution)/shard_map/ppermute | solution.py:702
  220.4 3.2 %collective-permute-start.7 = (bf16[2,32,512]{2,1,0:T(8,128)(2,1)S(1)}, bf16[2,32,512]{2,1,0:T(8,128)(2,1)S(1)}, u32[]{:S(2)}, u32[]{:S(2)}) collective-permute-start(bf16[2,32,512]{2,1,0:T(8,128)(2,1)S(1)} %get-tuple-element.48), channel_id=1, source_target_pairs={{0,16},{16,0},{32,48},{48,32},{64,80},{80,64},{96,112},{112,96},{1... | collective-permute-start | bytes 196616 | tf_op jit(solution)/shard_map/ppermute | solution.py:702
  220.4 6.2 %collective-permute-start.8 = (bf16[2,32,512]{2,1,0:T(8,128)(2,1)S(1)}, bf16[2,32,512]{2,1,0:T(8,128)(2,1)S(1)}, u32[]{:S(2)}, u32[]{:S(2)}) collective-permute-start(bf16[2,32,512]{2,1,0:T(8,128)(2,1)S(1)} %get-tuple-element.49), channel_id=1, source_target_pairs={{0,48},{16,32},{32,80},{48,64},{64,112},{80,96},{96,16},{112,0},{1... | collective-permute-start | bytes 196616 | tf_op jit(solution)/shard_map/ppermute | solution.py:702
  220.7 6.0 %collective-permute-start.9 = (bf16[2,32,512]{2,1,0:T(8,128)(2,1)S(1)}, bf16[2,32,512]{2,1,0:T(8,128)(2,1)S(1)}, u32[]{:S(2)}, u32[]{:S(2)}) collective-permute-start(bf16[2,32,512]{2,1,0:T(8,128)(2,1)S(1)} %get-tuple-element.50), channel_id=1, source_target_pairs={{0,80},{16,64},{32,112},{48,96},{64,16},{80,0},{96,48},{112,32},{1... | collective-permute-start | bytes 196616 | tf_op jit(solution)/shard_map/ppermute | solution.py:702
  223.7 4.8 %collective-permute-start.10 = (bf16[2,32,512]{2,1,0:T(8,128)(2,1)S(1)}, bf16[2,32,512]{2,1,0:T(8,128)(2,1)S(1)}, u32[]{:S(2)}, u32[]{:S(2)}) collective-permute-start(bf16[2,32,512]{2,1,0:T(8,128)(2,1)S(1)} %get-tuple-element.51), channel_id=1, source_target_pairs={{0,112},{16,96},{32,16},{48,0},{64,48},{80,32},{96,80},{112,64},{1... | collective-permute-start | bytes 196616 | tf_op jit(solution)/shard_map/ppermute | solution.py:702
